TPU v7x, 32 devices: a whole 2x2x4 slice. The times are simulated.
32 devices in a mesh: groups: 2 (over y), band: 4 (over x, core), sect: 4 (over z).
Axes of the slice: x: 2, y: 2, z: 4, core: 2. Of those that a mesh axis runs over, the one named last changes fastest.
Arguments:
- state_field: bfloat16 [198, 128, 512], P('groups', 'band', 'sect'), parts along dimension 0, may hold values from -6 to 6
- conv_in_weight: bfloat16 [9, 128, 99], replicated, may hold values from -0.1875 to 0.1875
- conv_in_bias: float32 [128], replicated, may hold values from -3 to 3
- conv_out_weight: bfloat16 [9, 99, 128], replicated, may hold values from -0.1875 to 0.1875
- conv_out_bias: float32 [99], replicated, may hold values from -3 to 3
- patch_anchor: int32 [32, 2], P('groups'), parts along dimension 0, may hold values from 0 to 480, as said below
- patch_noise: bfloat16 [32, 2, 99, 1024], P(('groups', 'band', 'sect')), parts along dimension 0, may hold values from -6 to 6
- denoise_in_weight: bfloat16 [9, 128, 99], replicated, may hold values from -0.1875 to 0.1875
- step_bias: float32 [2, 128], replicated, may hold values from -3 to 3
- denoise_out_weight: bfloat16 [9, 99, 128], replicated, may hold values from -0.1875 to 0.1875
- denoise_bias: float32 [99], replicated, may hold values from -3 to 3
Outputs:
- next_field: bfloat16 [198, 128, 512], P('groups', 'band', 'sect'), parts along dimension 0
There are 2 independent parts, one for each index of `groups`. A program takes and returns all parts, laid end to end along the dimension named above; an argument that names none is the same for every part. Nothing has to cross between parts.
Inputs may be any that keep to these rules, and one draw needn't show every extreme that they name: `patch_anchor`: patches p * 1 to p + 1 - 1 are denoised by the device at position p of band+sect, band first. Each patch's anchor column lies in the columns of its reader's sector, its anchor row at most 96 and its anchor column at most 480. Among the patches of one sector, at most 2 have anchor rows in one band's rows, and in every sector some band holds exactly 2.
All inputs are finite; a program needn't handle non-finite values.
Results may differ from a plain program's by a relative error of at most 0.0049.
Values may be sent and summed in bfloat16 or wider, within the bound.
No kernel may reach another device: no remote copies, remote signals or barrier semaphores. Data moves between devices by JAX's collectives and lax.ppermute only.
A program may use at most 64 MiB of HBM per device.

v0:
```python
import jax
import jax.numpy as jnp
from jax import lax
from jax.experimental import pallas as pl
from jax.experimental.pallas import tpu as pltpu
from jax.sharding import PartitionSpec as P

SIDE = 32
WIDE = SIDE + 4
PER_TILE = 3
TILES = WIDE // PER_TILE
LANES = 128
REACH = SIDE + 2
HALF = jnp.bfloat16
FULL = jnp.float32


def shift_from(block, axis, distance):
    count = lax.axis_size(axis)
    route = [(i - distance, i) for i in range(count) if 0 <= i - distance < count]
    return lax.ppermute(block, axis, route)


def swap(block, axis, bit):
    count = lax.axis_size(axis)
    return lax.ppermute(block, axis, [(i, i ^ bit) for i in range(count)])


def run(body, outs, ins, scratch, name, micros=1.0, scalars=1, limit=24):
    smem = pl.BlockSpec(memory_space=pltpu.SMEM)
    vmem = pl.BlockSpec(memory_space=pltpu.VMEM)
    return pl.pallas_call(
        body,
        out_shape=outs,
        in_specs=[smem] * scalars + [vmem] * (len(ins) - scalars),
        out_specs=[vmem] * len(outs),
        scratch_shapes=scratch,
        name=name,
        cost_estimate=pl.CostEstimate(
            flops=int(micros * 1.15e9), bytes_accessed=1024, transcendentals=0
        ),
        compiler_params=pltpu.CompilerParams(vmem_limit_bytes=limit * 1024 * 1024),
    )(*ins)


def slot_at(who_ref, at_ref, j, sects, rows, cols):
    reader = jnp.bitwise_xor(who_ref[0], j) * sects + who_ref[1]
    return at_ref[reader, 0] - who_ref[0] * rows, at_ref[reader, 1] - who_ref[1] * cols


def like(shape, dtype=HALF):
    return jax.ShapeDtypeStruct(shape, dtype)


def lane_index(shape):
    return lax.broadcasted_iota(jnp.int32, shape, len(shape) - 1)


def pack(state):
    channels, rows, cols = state.shape
    padded = -(-channels // 8) * 8
    deep = -(-padded // 16) * 16
    span = -(-rows * REACH // LANES)

    def body(state_ref, rows_ref, right_ref, left_ref, flat):
        flat[:channels] = state_ref[...]
        flat[channels:] = jnp.zeros((deep - channels, rows, cols), HALF)
        turned = jnp.swapaxes(flat[...], 0, 1)
        rows_ref[...] = turned
        lane = lane_index((deep, LANES))
        none = jnp.zeros((deep, LANES), HALF)
        tiles = [None] * span
        rim = none
        for r in range(rows):
            row = turned[r]
            at, off = divmod(r * REACH, LANES)
            moved = row if off == 0 else pltpu.roll(row, off, 1)
            if tiles[at] is None:
                tiles[at] = moved
            else:
                tiles[at] = jnp.where(lane >= off, moved, tiles[at])
            if off + REACH > LANES:
                tiles[at + 1] = moved
            moved = pltpu.roll(row, (2 * r + 2) % LANES, 1)
            rim = jnp.where((lane >= 2 * r) & (lane < 2 * r + 2), moved, rim)
        for at in range(span):
            right_ref[:, at * LANES : (at + 1) * LANES] = tiles[at][:padded]
        left_ref[...] = rim[:padded]

    return run(
        body,
        [like((rows, deep, cols)), like((padded, span * LANES)), like((padded, LANES))],
        [state],
        [pltpu.VMEM((deep, rows, cols), HALF)],
        "pack",
        micros=3.0,
        scalars=0,
    )


def prep(weights, noise):
    steps, channels, cells = noise.shape
    count = len(weights)
    tile_rows = LANES // SIDE

    def body(*refs):
        ins, noise_ref, outs, noise_out = refs[:count], refs[count], refs[count + 1 : -1], refs[-1]
        for w_ref, o_ref in zip(ins, outs):
            _, made, used = w_ref.shape
            o_ref[...] = jnp.zeros(o_ref.shape, HALF)
            for v in range(2):
                for a in range(3):
                    for b in range(3):
                        at = (3 * (a + v) + b) * LANES
                        o_ref[v * LANES : v * LANES + made, at : at + used] = w_ref[3 * a + b]
        for k in range(steps):
            for t in range(cells // LANES):
                block = noise_ref[k, :, t * LANES : (t + 1) * LANES].astype(FULL)
                block = jnp.concatenate(
                    [block, jnp.zeros((LANES - channels, LANES), FULL)], axis=0
                ).T.astype(HALF)
                for m in range(tile_rows):
                    r = t * tile_rows + m
                    noise_out[
                        k, r // 2 * SIDE : (r // 2 + 1) * SIDE, r % 2 * LANES : (r % 2 + 1) * LANES
                    ] = block[m * SIDE : (m + 1) * SIDE]

    made = [like((2 * LANES, 12 * LANES))] * count + [like((steps, cells // 2, 2 * LANES))]
    out = run(body, made, [*weights, noise], [], "prep", micros=4.0, scalars=0)
    return out[:count], out[count]


def extract(who, anchor, by_row, right, left, bands, sects):
    rows, deep, cols = by_row.shape
    padded = right.shape[0]
    width = cols + LANES
    batch = 4 if bands % 4 == 0 else bands
    chunk = 4

    def body(who_ref, at_ref, rows_ref, right_ref, left_ref,
             keep_ref, send_ref, ext_ref, top_ref, low_ref, ext, picked):
        lane = lane_index((padded, LANES))
        ext[:, padded:, :] = jnp.zeros((rows, deep - padded, width), HALF)
        ext[:, :, :cols] = rows_ref[...]
        rim = left_ref[...]
        none = jnp.zeros((padded, LANES), HALF)
        for r in range(rows):
            at, off = divmod(r * REACH, LANES)
            piece = right_ref[:, at * LANES : (at + 1) * LANES]
            if off:
                piece = pltpu.roll(piece, LANES - off, 1)
            if off + REACH > LANES:
                after = right_ref[:, (at + 1) * LANES : (at + 2) * LANES]
                piece = jnp.where(lane < LANES - off, piece, pltpu.roll(after, LANES - off, 1))
            turned = pltpu.roll(rim, (LANES - 2 - 2 * r) % LANES, 1)
            piece = jnp.where(lane < REACH, piece, jnp.where(lane >= LANES - 2, turned, none))
            ext[r, :padded, cols:] = piece
        ext_ref[...] = ext[...]
        top_ref[...] = ext[:2]
        low_ref[...] = ext[rows - 2 :]
        for first in range(0, bands, batch):
            picks = []
            for j in range(first, first + batch):
                col0 = slot_at(who_ref, at_ref, j, sects, rows, cols)[1] - 2
                source = lax.broadcasted_iota(jnp.int32, (width, LANES), 0)
                target = lane_index((width, LANES))
                inner = target
                for m in range(1, PER_TILE):
                    inner = jnp.where(target >= WIDE * m, target - WIDE * m, inner)
                want = jnp.bitwise_and(inner + col0, width - 1)
                picks.append(jnp.where(source == want, 1.0, 0.0).astype(HALF))
            pick = jnp.concatenate(picks, axis=1)

            def select(c, carry):
                view = ext[pl.ds(c * chunk, chunk)].reshape(chunk * deep, width)
                picked[pl.ds(c * chunk, chunk)] = jnp.dot(
                    view, pick, preferred_element_type=FULL
                ).reshape(chunk, deep, batch * LANES)
                return carry

            lax.fori_loop(0, rows // chunk, select, 0)
            for j in range(first, first + batch):
                out_ref = send_ref if j % 2 else keep_ref
                row0 = slot_at(who_ref, at_ref, j, sects, rows, cols)[0] - 2
                inside = (row0 > -WIDE) & (row0 < rows)

                @pl.when(inside)
                def _(j=j, row0=row0, out_ref=out_ref, first=first):
                    lanes = slice((j - first) * LANES, (j - first + 1) * LANES)
                    zone = lane_index((padded, LANES))
                    for t in range(TILES):
                        total = jnp.zeros((padded, LANES), FULL)
                        for m in range(PER_TILE):
                            r = row0 + t * PER_TILE + m
                            low = jnp.where((r >= 0) & (r < rows), WIDE * m, width)
                            keep = (zone >= low) & (zone < WIDE * (m + 1))
                            value = picked[jnp.clip(r, 0, rows - 1), :padded, lanes]
                            total = jnp.where(keep, value, total)
                        out_ref[j // 2, :, t * LANES : (t + 1) * LANES] = total.astype(HALF)

                @pl.when(jnp.logical_not(inside))
                def _(j=j, out_ref=out_ref):
                    out_ref[j // 2] = jnp.zeros((padded, TILES * LANES), HALF)

    part = like((bands // 2, padded, TILES * LANES))
    edge = like((2, deep, width))
    return run(
        body,
        [part, part, like((rows, deep, width)), edge, edge],
        [who, anchor, by_row, right, left],
        [pltpu.VMEM((rows, deep, width), HALF), pltpu.VMEM((rows, deep, batch * LANES), FULL)],
        "extract",
        micros=3.0,
        scalars=2,
    )


def pair_bias(bias):
    line = jnp.pad(bias, ((0, LANES - bias.shape[0]),))
    return jnp.concatenate([line, line])[None, :]


def product(view, weight):
    return lax.dot_general(
        view, weight, (((1,), (1,)), ((), ())), preferred_element_type=FULL
    )


def gather_pairs(shifted, first, count):
    view = jnp.concatenate(
        [shifted[b, pl.ds(first + u, count), v] for u in (0, 1) for v in (0, 1) for b in (0, 1, 2)],
        axis=-1,
    )
    return view.reshape(count * view.shape[1], view.shape[2])


def silu(value):
    return value / (1.0 + jnp.exp(-value))


def patch_step(who, anchor, addends, noise, weights, biases, step_bias, sects, limits):
    padded = addends[0].shape[1]
    steps = noise.shape[0]
    half = SIDE // 2
    loose = 48

    def body(*refs):
        who_ref, at_ref = refs[:2]
        parts = refs[2 : 2 + len(addends)]
        mine = who_ref[0] * sects + who_ref[1]
        row0, col0 = at_ref[mine, 0], at_ref[mine, 1]
        (noise_ref, w_in, w_out, d_in, d_out, b_in, b_out, b_step, b_den, out_ref,
         flat, state_sh, hid, hid_sh, pad, pad_sh, corr) = refs[2 + len(addends) :]
        for t in range(TILES):
            lanes = slice(t * LANES, (t + 1) * LANES)
            tile = parts[0][0, :, lanes].astype(FULL)
            for part in parts[1:]:
                tile = tile + part[0, :, lanes].astype(FULL)
            tile = jnp.concatenate([tile, jnp.zeros((LANES - padded, LANES), FULL)], axis=0)
            flat[lanes, :] = tile.T
        for i in range(WIDE):
            t, m = divmod(i, PER_TILE)
            off = t * LANES + m * WIDE
            for b in range(3):
                state_sh[b, i // 2, i % 2] = flat[off + b : off + b + loose, :].astype(HALF)
        pairs = half + 1
        value = product(gather_pairs(state_sh, 0, pairs), w_in[...])
        value = silu(value + b_in[...]).reshape(pairs, loose, 2 * LANES)
        pair = lax.broadcasted_iota(jnp.int32, value.shape, 0)
        col = lax.broadcasted_iota(jnp.int32, value.shape, 1)
        odd = (lane_index(value.shape) >= LANES).astype(jnp.int32)
        grid_row = row0 - 1 + 2 * pair + odd
        grid_col = col0 - 1 + col
        keep = (
            (grid_row >= 0) & (grid_row < limits[0])
            & (grid_col >= 0) & (grid_col < limits[1]) & (col < SIDE + 2)
        )
        value = jnp.where(keep, value, 0.0)
        hid[:, 0] = value[:, :, :LANES]
        hid[:, 1] = value[:, :, LANES:]
        for b in range(3):
            hid_sh[b] = hid[:, :, b : b + SIDE, :].astype(HALF)
        value = product(gather_pairs(hid_sh, 0, half), w_out[...])
        center = jnp.concatenate(
            [state_sh[2, 1 : 1 + half, v, :SIDE, :] for v in (0, 1)], axis=-1
        ).astype(FULL).reshape(half * SIDE, 2 * LANES)
        mean = (center + value + b_out[...]).astype(HALF).astype(FULL)
        state = mean + noise_ref[0].astype(FULL)
        pad[...] = jnp.zeros(pad.shape, FULL)

        def conv(source, weight):
            shaped = source.reshape(half, SIDE, 2 * LANES)
            pad[:half, 1, 8 : 8 + SIDE] = shaped[:, :, :LANES]
            pad[1:, 0, 8 : 8 + SIDE] = shaped[:, :, LANES:]
            for b in range(3):
                pad_sh[b] = pad[:, :, 7 + b : 7 + b + SIDE, :].astype(HALF)
            return product(gather_pairs(pad_sh, 0, half), weight[...])

        for step in range(steps):
            inner = silu(conv(state, d_in) + b_step[step : step + 1])
            state = state - 0.5 * (conv(inner, d_out) + b_den[...])
            if step + 1 < steps:
                state = state + 0.5 * noise_ref[step + 1].astype(FULL)
        change = (state - mean).reshape(half, SIDE, 2 * LANES)
        corr[:, 0] = change[:, :, :LANES]
        corr[:, 1] = change[:, :, LANES:]
        cells = corr[...].reshape(SIDE * SIDE, LANES)
        for t in range(SIDE * SIDE // LANES):
            lanes = slice(t * LANES, (t + 1) * LANES)
            out_ref[:, lanes] = cells[lanes].T[:padded].astype(HALF)

    return run(
        body,
        [like((padded, SIDE * SIDE))],
        [who, anchor, *addends, noise, *weights, *biases[:2], step_bias, biases[2]],
        [
            pltpu.VMEM((TILES * LANES, LANES), FULL),
            pltpu.VMEM((3, WIDE // 2, 2, loose, LANES), HALF),
            pltpu.VMEM((half + 1, 2, loose, LANES), FULL),
            pltpu.VMEM((3, half + 1, 2, SIDE, LANES), HALF),
            pltpu.VMEM((half + 1, 2, loose, LANES), FULL),
            pltpu.VMEM((3, half + 1, 2, SIDE, LANES), HALF),
            pltpu.VMEM((half, 2, SIDE, LANES), FULL),
        ],
        "patch",
        micros=8.0,
        scalars=2,
    )[0]


def grid_mean(who, ext, rim, lower, padded, weights, biases, limits):
    rows, deep, width = ext.shape
    cols = width - LANES
    loose = cols + 16
    made = rows // 2
    pairs_in, pairs_out = made // 4 + 1, made // 4
    hidden_pairs = made // 2 + 1
    if hidden_pairs % pairs_in:
        hidden_pairs += pairs_in - hidden_pairs % pairs_in
    state_pairs = hidden_pairs + 1
    base = rows - made - 2 if lower else -2

    def body(who_ref, ext_ref, rim_ref, w_in, w_out, b_in, b_out, out_ref,
             line, state_sh, hid, hid_sh):
        row0 = who_ref[0] * rows + base + 1
        col0 = who_ref[1] * cols - 1

        def spread(i, v, slot, source):
            value = source.astype(FULL)
            if deep < LANES:
                value = jnp.concatenate([value, jnp.zeros((LANES - deep, width), FULL)], axis=0)
            value = value.T
            line[slot, 8 : 8 + cols] = value[:cols]
            line[slot, 8 + cols :] = value[cols : cols + 16]
            line[slot, :8] = value[width - 8 :]
            for b in range(3):
                state_sh[b, i, v] = line[slot, 6 + b : 6 + b + loose, :].astype(HALF)

        for pair in range(made // 2 + 2, state_pairs):
            for b in range(3):
                state_sh[b, pair] = jnp.zeros((2, loose, LANES), HALF)
        edge = made // 2 + 1 if lower else 0
        for v in range(2):
            spread(edge, v, v, rim_ref[v])
        skip = 0 if lower else 1

        def spread_rows(i, carry):
            for v in range(2):
                spread(i + skip, v, v, ext_ref[2 * (i + skip) + v + base])
            return carry

        lax.fori_loop(0, made // 2 + 1, spread_rows, 0)

        def first(chunk, carry):
            start = chunk * pairs_in
            value = product(gather_pairs(state_sh, start, pairs_in), w_in[...])
            value = silu(value + b_in[...]).reshape(pairs_in, loose, 2 * LANES)
            pair = lax.broadcasted_iota(jnp.int32, value.shape, 0)
            col = lax.broadcasted_iota(jnp.int32, value.shape, 1)
            odd = (lane_index(value.shape) >= LANES).astype(jnp.int32)
            grid_row = row0 + 2 * (start + pair) + odd
            grid_col = col0 + col
            keep = (
                (grid_row >= 0) & (grid_row < limits[0])
                & (grid_col >= 0) & (grid_col < limits[1])
            )
            value = jnp.where(keep, value, 0.0)
            hid[:, 0] = value[:, :, :LANES]
            hid[:, 1] = value[:, :, LANES:]
            for b in range(3):
                hid_sh[b, pl.ds(start, pairs_in)] = hid[:, :, b : b + cols, :].astype(HALF)
            return carry

        lax.fori_loop(0, hidden_pairs // pairs_in, first, 0)

        def second(chunk, carry):
            start = chunk * pairs_out
            value = product(gather_pairs(hid_sh, start, pairs_out), w_out[...]) + b_out[...]
            value = value.reshape(pairs_out, cols, 2 * LANES)
            for k in range(pairs_out):
                for v in range(2):
                    center = state_sh[2, start + k + 1, v, :cols, :].astype(FULL)
                    mean = center + value[k, :, v * LANES : (v + 1) * LANES]
                    out_ref[2 * (start + k) + v] = mean.T[:padded].astype(HALF)
            return carry

        lax.fori_loop(0, made // 2 // pairs_out, second, 0)

    return run(
        body,
        [like((made, padded, cols))],
        [who, ext, rim, *weights, *biases],
        [
            pltpu.VMEM((2, loose + 8, LANES), FULL),
            pltpu.VMEM((3, state_pairs, 2, loose, LANES), HALF),
            pltpu.VMEM((pairs_in, 2, loose, LANES), FULL),
            pltpu.VMEM((3, hidden_pairs, 2, cols, LANES), HALF),
        ],
        "mean_low" if lower else "mean_top",
        micros=5.0,
    )[0]


def spill(who, anchor, pieces, sources, sects, rows, cols):
    padded = pieces[0].shape[-2]

    def body(who_ref, at_ref, *refs):
        out_ref, total = refs[-2:]
        lane = lane_index((padded, LANES))
        none = jnp.zeros((padded, LANES), HALF)
        total[...] = jnp.zeros(total.shape, FULL)
        for piece, j in zip(refs, sources):
            row0, col0 = slot_at(who_ref, at_ref, j, sects, rows, cols)

            @pl.when(col0 > cols - SIDE)
            def _(piece=piece, row0=row0, col0=col0):
                def one(r, carry):
                    i = r - row0
                    source = pl.multiple_of((i // 4) * LANES, LANES)
                    target = pl.multiple_of((r // 4) * LANES, LANES)
                    low = SIDE * (r % 4)
                    turn = jnp.bitwise_and(low - SIDE * (i % 4) + col0 - cols, LANES - 1)
                    value = pltpu.roll(piece[:, pl.ds(source, LANES)], turn, 1)
                    keep = (lane >= low) & (lane < low + col0 - (cols - SIDE))
                    total[:, pl.ds(target, LANES)] += jnp.where(keep, value, none).astype(FULL)
                    return carry

                lax.fori_loop(jnp.maximum(row0, 0), jnp.minimum(row0 + SIDE, rows), one, 0)

        out_ref[...] = total[...].astype(HALF)

    shape = (padded, rows * SIDE)
    return run(
        body, [like(shape)], [who, anchor, *pieces], [pltpu.VMEM(shape, FULL)], "spill",
        micros=1.5, scalars=2,
    )[0]


def canvas(who, anchor, pieces, sources, sects, rows, cols):
    padded = pieces[0].shape[-2]
    total = anchor.shape[0]

    def body(who_ref, at_ref, *refs):
        out_ref, inverse_ref = refs[-2:]
        lane = lane_index((padded, LANES))
        none = jnp.zeros((padded, LANES), HALF)
        out_ref[...] = jnp.zeros(out_ref.shape, FULL)
        for piece, j in zip(refs, sources):
            row0, col0 = slot_at(who_ref, at_ref, j, sects, rows, cols)

            def one(k, carry, piece=piece, row0=row0, col0=col0):
                value = piece[:, pl.ds(pl.multiple_of(k * LANES, LANES), LANES)]
                for m in range(4):
                    r = row0 + 4 * k + m
                    low = jnp.where((r >= 0) & (r < rows), col0, 2 * LANES)
                    moved = pltpu.roll(value, jnp.bitwise_and(col0 - SIDE * m, LANES - 1), 1)
                    keep = (lane >= low) & (lane < col0 + SIDE)
                    out_ref[jnp.clip(r, 0, rows - 1)] += jnp.where(keep, moved, none).astype(FULL)
                return carry

            start = jnp.clip(-row0, 0, SIDE) // 4
            stop = (jnp.clip(rows - row0, 0, SIDE) + 3) // 4
            lax.fori_loop(start, stop, one, 0)
        row = lax.broadcasted_iota(jnp.int32, (rows, cols), 0) + who_ref[0] * rows
        col = lane_index((rows, cols)) + who_ref[1] * cols

        def cover(p, count):
            down, across = row - at_ref[p, 0], col - at_ref[p, 1]
            hit = (down >= 0) & (down < SIDE) & (across >= 0) & (across < SIDE)
            return count + jnp.where(hit, 1.0, 0.0)

        count = lax.fori_loop(0, total, cover, jnp.zeros((rows, cols), FULL))
        inverse_ref[...] = 1.0 / jnp.maximum(count, 1.0)

    return run(
        body, [like((rows, padded, cols), FULL), like((rows, cols), FULL)],
        [who, anchor, *pieces], [], "canvas", micros=2.5, scalars=2,
    )


def finish(means, summed, arrived, inverse, channels):
    rows, padded, cols = summed.shape
    deep = -(-padded // 16) * 16
    half = means[0].shape[0]

    def body(top_ref, low_ref, sum_ref, spill_ref, inverse_ref, out_ref, flat):
        lane = lane_index((padded, LANES))
        none = jnp.zeros((padded, LANES), HALF)
        flat[:, padded:] = jnp.zeros((rows, deep - padded, cols), HALF)
        for r in range(rows):
            at, low = divmod(r * SIDE, LANES)
            extra = spill_ref[:, at * LANES : (at + 1) * LANES]
            if low:
                extra = pltpu.roll(extra, LANES - low, 1)
            extra = jnp.where(lane < SIDE, extra, none).astype(FULL)
            mean = top_ref[r] if r < half else low_ref[r - half]
            value = mean.astype(FULL) + (sum_ref[r] + extra) * inverse_ref[r : r + 1]
            flat[r, :padded] = value.astype(HALF)
        out_ref[...] = jnp.swapaxes(flat[...], 0, 1)[:channels]

    return run(
        body,
        [like((channels, rows, cols))],
        [*means, summed, arrived, inverse],
        [pltpu.VMEM((rows, deep, cols), HALF)],
        "finish",
        micros=3.0,
        scalars=0,
    )[0]


def per_device(
    state_field,
    conv_in_weight,
    conv_in_bias,
    conv_out_weight,
    conv_out_bias,
    patch_anchor,
    patch_noise,
    denoise_in_weight,
    step_bias,
    denoise_out_weight,
    denoise_bias,
):
    bands = lax.axis_size("band")
    sects = lax.axis_size("sect")
    channels, rows, cols = state_field.shape
    limits = (rows * bands, cols * sects)
    who = jnp.stack([lax.axis_index("band"), lax.axis_index("sect")]).astype(jnp.int32)

    by_row, right_rim, left_rim = pack(state_field)
    padded = right_rim.shape[0]
    right = shift_from(right_rim, "sect", -1)
    left = shift_from(left_rim, "sect", 1)

    made, noise = prep(
        [conv_in_weight, conv_out_weight, denoise_in_weight, denoise_out_weight], patch_noise[0]
    )
    biases = [pair_bias(b) for b in (conv_in_bias, conv_out_bias, denoise_bias)]
    step_lines = jnp.concatenate([step_bias, step_bias], axis=-1)

    kept, sent, ext, top, low = extract(
        who, patch_anchor, by_row, right, left, bands, sects
    )
    got = swap(sent, "band", 1)
    addends = [kept, got]
    bit = 2
    parts = None
    while bit < bands:
        parts = kept + got if parts is None else parts[0::2] + got
        got = swap(parts[1::2], "band", bit)
        addends.append(got)
        bit *= 2
    above = shift_from(low, "band", 1)
    below = shift_from(top, "band", -1)
    correction = patch_step(
        who, patch_anchor, addends, noise, made, biases, step_lines, sects, limits
    )
    pieces = [correction]
    sources = [0]
    bit = bands // 2
    while bit:
        pieces += [swap(piece, "band", bit) for piece in pieces]
        sources += [s ^ bit for s in sources]
        bit //= 2
    means = [
        grid_mean(who, ext, rim, lower, padded, made[:2], biases[:2], limits)
        for lower, rim in ((False, above), (True, below))
    ]
    arrived = shift_from(
        spill(who, patch_anchor, pieces, sources, sects, rows, cols), "sect", 1
    )
    summed, inverse = canvas(who, patch_anchor, pieces, sources, sects, rows, cols)
    return finish(means, summed, arrived, inverse, channels)


def solution(mesh):
    placed = (
        P("groups", "band", "sect"),
        P(),
        P(),
        P(),
        P(),
        P("groups", None),
        P(("groups", "band", "sect"), None, None, None),
        P(),
        P(),
        P(),
        P(),
    )
    return jax.shard_map(
        per_device,
        mesh=mesh,
        in_specs=placed,
        out_specs=P("groups", "band", "sect"),
        check_vma=False,
    )
```

profile of v0, /device:TPU:11, one launch (start us, length us, event | category | flops | bytes accessed | tf_op | source)
XLA Modules:
  0.0 64.3 jit_solution(4520104099890174171)
XLA Ops:
  0.0 1.1 %copy-done = bf16[99,32,128]{2,1,0:T(8,128)(2,1)S(1)} copy-done((bf16[99,32,128]{2,1,0:T(8,128)(2,1)S(1)}, bf16[99,32,128]{2,1,0:T(8,128)(2,1)}, u32[]{:S(2)}) %copy-start) | copy-done | bytes 811032
  1.1 0.8 %pack.1 = (bf16[32,112,128]{2,1,0:T(8,128)(2,1)S(1)}, bf16[104,1152]{1,0:T(8,128)(2,1)S(1)}, bf16[104,128]{1,0:T(8,128)(2,1)S(1)}) custom-call(bf16[99,32,128]{2,1,0:T(8,128)(2,1)S(1)} %copy-done), custom_call_target="tpu_custom_call" | custom-call | flops 3449999872 | bytes 1024 | tf_op jit(solution)/shard_map/pack/pallas_call | solution.py:32
  1.9 0.0 copy-start.5
  1.9 0.9 %copy-done.5 = bf16[32,112,128]{2,1,0:T(8,128)(2,1)} copy-done((bf16[32,112,128]{2,1,0:T(8,128)(2,1)}, bf16[32,112,128]{2,1,0:T(8,128)(2,1)S(1)}, u32[]{:S(2)}) %copy-start.5) | copy-done | bytes 917528
  2.8 2.1 %collective-permute-start = (bf16[104,1152]{1,0:T(8,128)(2,1)S(1)}, bf16[104,1152]{1,0:T(8,128)(2,1)S(1)}, u32[]{:S(2)}, u32[]{:S(2)}) collective-permute-start(bf16[104,1152]{1,0:T(8,128)(2,1)S(1)} %get-tuple-element.21), channel_id=1, source_target_pairs={{1,0},{2,1},{3,2},{5,4},{6,5},{7,6},{9,8},{10,9},{11,10},{13,12},{... | collective-permute-start | bytes 718856 | tf_op jit(solution)/shard_map/ppermute | solution.py:21
  4.9 3.2 %collective-permute-start.1 = (bf16[104,128]{1,0:T(8,128)(2,1)S(1)}, bf16[104,128]{1,0:T(8,128)(2,1)S(1)}, u32[]{:S(2)}, u32[]{:S(2)}) collective-permute-start(bf16[104,128]{1,0:T(8,128)(2,1)S(1)} %get-tuple-element.22), channel_id=1, source_target_pairs={{0,1},{1,2},{2,3},{4,5},{5,6},{6,7},{8,9},{9,10},{10,11},{12,13},{... | collective-permute-start | bytes 79880 | tf_op jit(solution)/shard_map/ppermute | solution.py:21
  8.1 0.1 pad_add_fusion.who_ref.refs_0_
  8.2 0.0 copy-done.9
  8.2 0.1 copy.12.at_ref.refs_1_
  8.3 1.5 %collective-permute-done.1.left_ref = bf16[104,128]{1,0:T(8,128)(2,1)S(1)} collective-permute-done((bf16[104,128]{1,0:T(8,128)(2,1)S(1)}, bf16[104,128]{1,0:T(8,128)(2,1)S(1)}, u32[]{:S(2)}, u32[]{:S(2)}) %collective-permute-start.1) | collective-permute-done | bytes 26656 | tf_op jit(solution)/shard_map/ppermute | solution.py:21
  9.8 1.6 %collective-permute-done.right_ref = bf16[104,1152]{1,0:T(8,128)(2,1)S(1)} collective-permute-done((bf16[104,1152]{1,0:T(8,128)(2,1)S(1)}, bf16[104,1152]{1,0:T(8,128)(2,1)S(1)}, u32[]{:S(2)}, u32[]{:S(2)}) %collective-permute-start) | collective-permute-done | bytes 239648 | tf_op jit(solution)/shard_map/ppermute | solution.py:21
  11.4 1.2 %copy-done.6 = bf16[32,112,128]{2,1,0:T(8,128)(2,1)S(1)} copy-done((bf16[32,112,128]{2,1,0:T(8,128)(2,1)S(1)}, bf16[32,112,128]{2,1,0:T(8,128)(2,1)}, u32[]{:S(2)}) %copy-start.6) | copy-done | bytes 917528
  12.6 4.3 %extract.1 = (bf16[2,104,1536]{2,1,0:T(8,128)(2,1)S(1)}, bf16[2,104,1536]{2,1,0:T(8,128)(2,1)S(1)}, bf16[32,112,256]{2,1,0:T(8,128)(2,1)S(1)}, bf16[2,112,256]{2,1,0:T(8,128)(2,1)S(1)}, bf16[2,112,256]{2,1,0:T(8,128)(2,1)S(1)}) custom-call(s32[2]{0:T(128)S(1)} %pad_add_fusion.who_ref.refs_0_, s32[16,2]{1,0:T(8,128)S(1)} %copy.12.at_ref.refs_1_, ...), custom_call_target="tpu_custom_call" | custom-call | flops 3449999872 | bytes 1024 | tf_op jit(solution)/shard_map/extract/pallas_call | solution.py:32
  16.9 0.0 copy-start.3
  16.9 1.2 %copy-done.3 = bf16[32,112,256]{2,1,0:T(8,128)(2,1)} copy-done((bf16[32,112,256]{2,1,0:T(8,128)(2,1)}, bf16[32,112,256]{2,1,0:T(8,128)(2,1)S(1)}, u32[]{:S(2)}) %copy-start.3) | copy-done | bytes 1835032
  18.2 0.0 copy-start.1
  18.2 0.0 copy-start.2
  18.2 2.1 %collective-permute-start.4 = (bf16[2,104,1536]{2,1,0:T(8,128)(2,1)S(1)}, bf16[2,104,1536]{2,1,0:T(8,128)(2,1)S(1)}, u32[]{:S(2)}, u32[]{:S(2)}) collective-permute-start(bf16[2,104,1536]{2,1,0:T(8,128)(2,1)S(1)} %get-tuple-element.29), channel_id=1, source_target_pairs={{0,4},{4,0},{8,12},{12,8},{1,5},{5,1},{9,13},{13,9},{2,6},{6,2},{1... | collective-permute-start | bytes 1916936 | tf_op jit(solution)/shard_map/ppermute | solution.py:26
  20.3 0.0 copy-done.7
  20.3 0.2 copy.14.refs_0_
  20.5 0.0 copy-done.8
  20.5 0.2 copy.15.refs_2_
  20.7 1.1 %copy.20 = bf16[1,2,99,1024]{3,2,1,0:T(8,128)(2,1)S(1)} copy(bf16[1,2,99,1024]{3,1,2,0:T(2,128)(2,1)} %param.17) | data formatting | bytes 811008 | tf_op args[6]
  21.8 0.0 copy-done.11
  21.8 0.0 copy-done.12
  21.9 0.0 copy-done.13
  21.9 0.0 collective-permute-done.4.refs_3_
  22.0 0.1 collective-permute-start.5
  22.1 0.7 %prep.1 = (bf16[256,1536]{1,0:T(8,128)(2,1)S(1)}, bf16[256,1536]{1,0:T(8,128)(2,1)S(1)}, bf16[256,1536]{1,0:T(8,128)(2,1)S(1)}, bf16[256,1536]{1,0:T(8,128)(2,1)S(1)}, bf16[2,512,256]{2,1,0:T(8,128)(2,1)S(1)}) custom-call(bf16[9,128,99]{2,1,0:T(8,128)(2,1)S(1)} %copy.14.refs_0_, bf16[9,99,128]{2,1,0:T(8,128)(2,1)S(1)} %copy-done.1, ...), custom_call_target="tpu_custom_call" | custom-call | flops 4600000000 | bytes 1024 | tf_op jit(solution)/shard_map/prep/pallas_call | solution.py:32
  22.8 1.3 %collective-permute-start.2 = (bf16[2,112,256]{2,1,0:T(8,128)(2,1)S(1)}, bf16[2,112,256]{2,1,0:T(8,128)(2,1)S(1)}, u32[]{:S(2)}, u32[]{:S(2)}) collective-permute-start(bf16[2,112,256]{2,1,0:T(8,128)(2,1)S(1)} %get-tuple-element.24), channel_id=1, source_target_pairs={{0,4},{4,8},{8,12},{1,5},{5,9},{9,13},{2,6},{6,10},{10,14},{3,7},{... | collective-permute-start | bytes 344072 | tf_op jit(solution)/shard_map/ppermute | solution.py:21
  24.1 3.0 %collective-permute-start.3 = (bf16[2,112,256]{2,1,0:T(8,128)(2,1)S(1)}, bf16[2,112,256]{2,1,0:T(8,128)(2,1)S(1)}, u32[]{:S(2)}, u32[]{:S(2)}) collective-permute-start(bf16[2,112,256]{2,1,0:T(8,128)(2,1)S(1)} %get-tuple-element.27), channel_id=1, source_target_pairs={{4,0},{8,4},{12,8},{5,1},{9,5},{13,9},{6,2},{10,6},{14,10},{7,3},{... | collective-permute-start | bytes 344072 | tf_op jit(solution)/shard_map/ppermute | solution.py:21
  27.1 3.7 %collective-permute-done.5.refs_4_ = bf16[1,104,1536]{2,1,0:T(8,128)(2,1)S(1)} collective-permute-done((bf16[1,104,1536]{2,1,0:T(8,128)(2,1)S(1)}, bf16[1,104,1536]{2,1,0:T(8,128)(2,1)S(1)}, u32[]{:S(2)}, u32[]{:S(2)}) %collective-permute-start.5) | collective-permute-done | bytes 319520 | tf_op jit(solution)/shard_map/ppermute | solution.py:26
  30.8 6.6 %patch.1.refs_0_ = bf16[104,1024]{1,0:T(8,128)(2,1)S(1)} custom-call(s32[2]{0:T(128)S(1)} %pad_add_fusion.who_ref.refs_0_, s32[16,2]{1,0:T(8,128)S(1)} %copy.12.at_ref.refs_1_, bf16[2,104,1536]{2,1,0:T(8,128)(2,1)S(1)} %get-tuple-element.28.refs_2_, bf16[2,104,1536]{2,1,0:T(8,128)(2,1)S(1)} %collective-permute-done.4.refs_3_, ...), custom_call_target="tpu_custom_call" | custom-call | flops 9200000000 | bytes 1024 | tf_op jit(solution)/shard_map/patch/pallas_call | solution.py:32
  37.3 0.3 collective-permute-start.6
  37.7 0.0 collective-permute-done.2.rim_ref
  37.7 5.2 %mean_top.1.top_ref = bf16[16,104,128]{2,1,0:T(8,128)(2,1)S(1)} custom-call(s32[2]{0:T(128)S(1)} %pad_add_fusion.who_ref.refs_0_, bf16[32,112,256]{2,1,0:T(8,128)(2,1)S(1)} %copy-done.4, bf16[2,112,256]{2,1,0:T(8,128)(2,1)S(1)} %collective-permute-done.2.rim_ref, bf16[256,1536]{1,0:T(8,128)(2,1)S(1)} %get-tuple-element.25.w_in.refs_6_, ...), custom_call_target="tpu_custom_call" | custom-call | flops 5750000128 | bytes 1024 | tf_op jit(solution)/shard_map/mean_top/pallas_call | solution.py:32
  42.9 1.9 %collective-permute-start.7 = (bf16[104,1024]{1,0:T(8,128)(2,1)S(1)}, bf16[104,1024]{1,0:T(8,128)(2,1)S(1)}, u32[]{:S(2)}, u32[]{:S(2)}) collective-permute-start(bf16[104,1024]{1,0:T(8,128)(2,1)S(1)} %patch.1.refs_0_), channel_id=1, source_target_pairs={{0,4},{4,0},{8,12},{12,8},{1,5},{5,1},{9,13},{13,9},{2,6},{6,2},{1... | collective-permute-start | bytes 638984 | tf_op jit(solution)/shard_map/ppermute | solution.py:26
  44.7 0.0 collective-permute-done.6.refs_1_
  44.7 0.6 collective-permute-start.8
  45.3 0.0 collective-permute-done.3.rim_ref
  45.3 5.1 %mean_low.1.low_ref = bf16[16,104,128]{2,1,0:T(8,128)(2,1)S(1)} custom-call(s32[2]{0:T(128)S(1)} %pad_add_fusion.who_ref.refs_0_, bf16[32,112,256]{2,1,0:T(8,128)(2,1)S(1)} %copy-done.4, bf16[2,112,256]{2,1,0:T(8,128)(2,1)S(1)} %collective-permute-done.3.rim_ref, bf16[256,1536]{1,0:T(8,128)(2,1)S(1)} %get-tuple-element.25.w_in.refs_6_, ...), custom_call_target="tpu_custom_call" | custom-call | flops 5750000128 | bytes 1024 | tf_op jit(solution)/shard_map/mean_low/pallas_call | solution.py:32
  50.4 0.0 collective-permute-done.7.refs_2_
  50.4 0.0 collective-permute-done.8.refs_3_
  50.5 3.4 %spill.1 = bf16[104,1024]{1,0:T(8,128)(2,1)S(1)} custom-call(s32[2]{0:T(128)S(1)} %pad_add_fusion.who_ref.refs_0_, s32[16,2]{1,0:T(8,128)S(1)} %copy.12.at_ref.refs_1_, bf16[104,1024]{1,0:T(8,128)(2,1)S(1)} %patch.1.refs_0_, bf16[104,1024]{1,0:T(8,128)(2,1)S(1)} %collective-permute-done.6.refs_1_, bf16[104,1024]{1,0:T(8,128)(2,1)S(1)} %collective-permute-done.7.refs_2_, ...), custom_call_target="tpu_custom_call" | custom-call | flops 1724999936 | bytes 1024 | tf_op jit(solution)/shard_map/spill/pallas_call | solution.py:32
  53.8 1.9 %collective-permute-start.9 = (bf16[104,1024]{1,0:T(8,128)(2,1)S(1)}, bf16[104,1024]{1,0:T(8,128)(2,1)S(1)}, u32[]{:S(2)}, u32[]{:S(2)}) collective-permute-start(bf16[104,1024]{1,0:T(8,128)(2,1)S(1)} %spill.1), channel_id=1, source_target_pairs={{0,1},{1,2},{2,3},{4,5},{5,6},{6,7},{8,9},{9,10},{10,11},{12,13},{... | collective-permute-start | bytes 638984 | tf_op jit(solution)/shard_map/ppermute | solution.py:21
  55.7 2.7 %canvas.1 = (f32[32,104,128]{2,1,0:T(8,128)S(1)}, f32[32,128]{1,0:T(8,128)S(1)}) custom-call(s32[2]{0:T(128)S(1)} %pad_add_fusion.who_ref.refs_0_, s32[16,2]{1,0:T(8,128)S(1)} %copy.12.at_ref.refs_1_, bf16[104,1024]{1,0:T(8,128)(2,1)S(1)} %patch.1.refs_0_, bf16[104,1024]{1,0:T(8,128)(2,1)S(1)} %collective-permute-done.6.refs_1_, ...), custom_call_target="tpu_custom_call" | custom-call | flops 2875000064 | bytes 1024 | tf_op jit(solution)/shard_map/canvas/pallas_call | solution.py:32
  58.4 4.3 %collective-permute-done.9.spill_ref = bf16[104,1024]{1,0:T(8,128)(2,1)S(1)} collective-permute-done((bf16[104,1024]{1,0:T(8,128)(2,1)S(1)}, bf16[104,1024]{1,0:T(8,128)(2,1)S(1)}, u32[]{:S(2)}, u32[]{:S(2)}) %collective-permute-start.9) | collective-permute-done | bytes 213024 | tf_op jit(solution)/shard_map/ppermute | solution.py:21
  62.7 1.7 %finish.1 = bf16[99,32,128]{2,1,0:T(8,128)(2,1)} custom-call(bf16[16,104,128]{2,1,0:T(8,128)(2,1)S(1)} %mean_top.1.top_ref, bf16[16,104,128]{2,1,0:T(8,128)(2,1)S(1)} %mean_low.1.low_ref, f32[32,104,128]{2,1,0:T(8,128)S(1)} %get-tuple-element.33.sum_ref, bf16[104,1024]{1,0:T(8,128)(2,1)S(1)} %collective-permute-done.9.spill_ref, ...), custom_call_target="tpu_custom_call" | custom-call | flops 3449999872 | bytes 1024 | tf_op jit(solution)/shard_map/finish/pallas_call | solution.py:32
  (21 shorter events, 0.1 us)
Async XLA Ops:
  0.0 1.1 %copy-start = (bf16[99,32,128]{2,1,0:T(8,128)(2,1)S(1)}, bf16[99,32,128]{2,1,0:T(8,128)(2,1)}, u32[]{:S(2)}) copy-start(bf16[99,32,128]{2,1,0:T(8,128)(2,1)} %state_ref.1) | copy-start | bytes 2433028
  1.1 7.1 %copy-start.9 = (s32[16,2]{0,1:T(2,128)S(1)}, s32[16,2]{0,1:T(2,128)}, u32[]{:S(2)}) copy-start(s32[16,2]{0,1:T(2,128)} %param.16) | copy-start | bytes 388
  1.9 0.9 %copy-start.5 = (bf16[32,112,128]{2,1,0:T(8,128)(2,1)}, bf16[32,112,128]{2,1,0:T(8,128)(2,1)S(1)}, u32[]{:S(2)}) copy-start(bf16[32,112,128]{2,1,0:T(8,128)(2,1)S(1)} %get-tuple-element.20.rows_ref) | copy-start | bytes 2752516
  2.8 8.6 %collective-permute-start = (bf16[104,1152]{1,0:T(8,128)(2,1)S(1)}, bf16[104,1152]{1,0:T(8,128)(2,1)S(1)}, u32[]{:S(2)}, u32[]{:S(2)}) collective-permute-start(bf16[104,1152]{1,0:T(8,128)(2,1)S(1)} %get-tuple-element.21), channel_id=1, source_target_pairs={{1,0},{2,1},{3,2},{5,4},{6,5},{7,6},{9,8},{10,9},{11,10},{13,12},{... | collective-permute-start | bytes 718856 | tf_op jit(solution)/shard_map/ppermute | solution.py:21
  4.9 4.9 %collective-permute-start.1 = (bf16[104,128]{1,0:T(8,128)(2,1)S(1)}, bf16[104,128]{1,0:T(8,128)(2,1)S(1)}, u32[]{:S(2)}, u32[]{:S(2)}) collective-permute-start(bf16[104,128]{1,0:T(8,128)(2,1)S(1)} %get-tuple-element.22), channel_id=1, source_target_pairs={{0,1},{1,2},{2,3},{4,5},{5,6},{6,7},{8,9},{9,10},{10,11},{12,13},{... | collective-permute-start | bytes 79880 | tf_op jit(solution)/shard_map/ppermute | solution.py:21
  11.4 1.2 %copy-start.6 = (bf16[32,112,128]{2,1,0:T(8,128)(2,1)S(1)}, bf16[32,112,128]{2,1,0:T(8,128)(2,1)}, u32[]{:S(2)}) copy-start(bf16[32,112,128]{2,1,0:T(8,128)(2,1)} %copy-done.5) | copy-start | bytes 2752516
  12.6 7.6 %copy-start.7 = (bf16[9,128,99]{1,2,0:T(8,128)(2,1)S(1)}, bf16[9,128,99]{1,2,0:T(8,128)(2,1)}, u32[]{:S(2)}) copy-start(bf16[9,128,99]{1,2,0:T(8,128)(2,1)} %param.12) | copy-start | bytes 684292
  12.6 7.9 %copy-start.8 = (bf16[9,128,99]{1,2,0:T(8,128)(2,1)S(1)}, bf16[9,128,99]{1,2,0:T(8,128)(2,1)}, u32[]{:S(2)}) copy-start(bf16[9,128,99]{1,2,0:T(8,128)(2,1)} %param.18) | copy-start | bytes 684292
  16.9 1.3 %copy-start.3 = (bf16[32,112,256]{2,1,0:T(8,128)(2,1)}, bf16[32,112,256]{2,1,0:T(8,128)(2,1)S(1)}, u32[]{:S(2)}) copy-start(bf16[32,112,256]{2,1,0:T(8,128)(2,1)S(1)} %get-tuple-element.23.ext_ref) | copy-start | bytes 5505028
  18.1 3.7 %copy-start.11 = (f32[99]{0:T(128)S(1)}, f32[99]{0:T(128)}, u32[]{:S(2)}) copy-start(f32[99]{0:T(128)} %param.15) | copy-start | bytes 1192
  18.2 3.7 %copy-start.12 = (f32[99]{0:T(128)S(1)}, f32[99]{0:T(128)}, u32[]{:S(2)}) copy-start(f32[99]{0:T(128)} %param.21) | copy-start | bytes 1192
  18.2 3.7 %copy-start.13 = (f32[128]{0:T(128)S(1)}, f32[128]{0:T(128)}, u32[]{:S(2)}) copy-start(f32[128]{0:T(128)} %param.13) | copy-start | bytes 1540
  18.2 3.8 %copy-start.10 = (f32[2,128]{1,0:T(2,128)S(1)}, f32[2,128]{1,0:T(2,128)}, u32[]{:S(2)}) copy-start(f32[2,128]{1,0:T(2,128)} %param.19) | copy-start | bytes 3076
  18.2 3.9 %copy-start.1 = (bf16[9,99,128]{2,1,0:T(8,128)(2,1)S(1)}, bf16[9,99,128]{2,1,0:T(8,128)(2,1)}, u32[]{:S(2)}) copy-start(bf16[9,99,128]{2,1,0:T(8,128)(2,1)} %refs_1_.2) | copy-start | bytes 684292
  18.2 3.9 %copy-start.2 = (bf16[9,99,128]{2,1,0:T(8,128)(2,1)S(1)}, bf16[9,99,128]{2,1,0:T(8,128)(2,1)}, u32[]{:S(2)}) copy-start(bf16[9,99,128]{2,1,0:T(8,128)(2,1)} %refs_3_.1) | copy-start | bytes 684292
  18.2 3.8 %collective-permute-start.4 = (bf16[2,104,1536]{2,1,0:T(8,128)(2,1)S(1)}, bf16[2,104,1536]{2,1,0:T(8,128)(2,1)S(1)}, u32[]{:S(2)}, u32[]{:S(2)}) collective-permute-start(bf16[2,104,1536]{2,1,0:T(8,128)(2,1)S(1)} %get-tuple-element.29), channel_id=1, source_target_pairs={{0,4},{4,0},{8,12},{12,8},{1,5},{5,1},{9,13},{13,9},{2,6},{6,2},{1... | collective-permute-start | bytes 1916936 | tf_op jit(solution)/shard_map/ppermute | solution.py:26
  22.0 8.8 %collective-permute-start.5 = (bf16[1,104,1536]{2,1,0:T(8,128)(2,1)S(1)}, bf16[1,104,1536]{2,1,0:T(8,128)(2,1)S(1)}, u32[]{:S(2)}, u32[]{:S(2)}) collective-permute-start(bf16[1,104,1536]{2,1,0:T(8,128)(2,1)S(1)} %slice_add_fusion), channel_id=1, source_target_pairs={{0,8},{4,12},{8,0},{12,4},{1,9},{5,13},{9,1},{13,5},{2,10},{6,14},... | collective-permute-start | bytes 958472 | tf_op jit(solution)/shard_map/ppermute | solution.py:26
  22.8 14.9 %collective-permute-start.2 = (bf16[2,112,256]{2,1,0:T(8,128)(2,1)S(1)}, bf16[2,112,256]{2,1,0:T(8,128)(2,1)S(1)}, u32[]{:S(2)}, u32[]{:S(2)}) collective-permute-start(bf16[2,112,256]{2,1,0:T(8,128)(2,1)S(1)} %get-tuple-element.24), channel_id=1, source_target_pairs={{0,4},{4,8},{8,12},{1,5},{5,9},{9,13},{2,6},{6,10},{10,14},{3,7},{... | collective-permute-start | bytes 344072 | tf_op jit(solution)/shard_map/ppermute | solution.py:21
  24.1 21.3 %collective-permute-start.3 = (bf16[2,112,256]{2,1,0:T(8,128)(2,1)S(1)}, bf16[2,112,256]{2,1,0:T(8,128)(2,1)S(1)}, u32[]{:S(2)}, u32[]{:S(2)}) collective-permute-start(bf16[2,112,256]{2,1,0:T(8,128)(2,1)S(1)} %get-tuple-element.27), channel_id=1, source_target_pairs={{4,0},{8,4},{12,8},{5,1},{9,5},{13,9},{6,2},{10,6},{14,10},{7,3},{... | collective-permute-start | bytes 344072 | tf_op jit(solution)/shard_map/ppermute | solution.py:21
  30.8 6.9 %copy-start.4 = (bf16[32,112,256]{2,1,0:T(8,128)(2,1)S(1)}, bf16[32,112,256]{2,1,0:T(8,128)(2,1)}, u32[]{:S(2)}) copy-start(bf16[32,112,256]{2,1,0:T(8,128)(2,1)} %copy-done.3) | copy-start | bytes 5505028
  37.3 7.4 %collective-permute-start.6 = (bf16[104,1024]{1,0:T(8,128)(2,1)S(1)}, bf16[104,1024]{1,0:T(8,128)(2,1)S(1)}, u32[]{:S(2)}, u32[]{:S(2)}) collective-permute-start(bf16[104,1024]{1,0:T(8,128)(2,1)S(1)} %patch.1.refs_0_), channel_id=1, source_target_pairs={{0,8},{4,12},{8,0},{12,4},{1,9},{5,13},{9,1},{13,5},{2,10},{6,14},... | collective-permute-start | bytes 638984 | tf_op jit(solution)/shard_map/ppermute | solution.py:26
  42.9 7.6 %collective-permute-start.7 = (bf16[104,1024]{1,0:T(8,128)(2,1)S(1)}, bf16[104,1024]{1,0:T(8,128)(2,1)S(1)}, u32[]{:S(2)}, u32[]{:S(2)}) collective-permute-start(bf16[104,1024]{1,0:T(8,128)(2,1)S(1)} %patch.1.refs_0_), channel_id=1, source_target_pairs={{0,4},{4,0},{8,12},{12,8},{1,5},{5,1},{9,13},{13,9},{2,6},{6,2},{1... | collective-permute-start | bytes 638984 | tf_op jit(solution)/shard_map/ppermute | solution.py:26
  44.7 5.7 %collective-permute-start.8 = (bf16[104,1024]{1,0:T(8,128)(2,1)S(1)}, bf16[104,1024]{1,0:T(8,128)(2,1)S(1)}, u32[]{:S(2)}, u32[]{:S(2)}) collective-permute-start(bf16[104,1024]{1,0:T(8,128)(2,1)S(1)} %collective-permute-done.6.refs_1_), channel_id=1, source_target_pairs={{0,4},{4,0},{8,12},{12,8},{1,5},{5,1},{9,13},{13,9},{2,6},{6,2},{1... | collective-permute-start | bytes 638984 | tf_op jit(solution)/shard_map/ppermute | solution.py:26
  53.8 8.9 %collective-permute-start.9 = (bf16[104,1024]{1,0:T(8,128)(2,1)S(1)}, bf16[104,1024]{1,0:T(8,128)(2,1)S(1)}, u32[]{:S(2)}, u32[]{:S(2)}) collective-permute-start(bf16[104,1024]{1,0:T(8,128)(2,1)S(1)} %spill.1), channel_id=1, source_target_pairs={{0,1},{1,2},{2,3},{4,5},{5,6},{6,7},{8,9},{9,10},{10,11},{12,13},{... | collective-permute-start | bytes 638984 | tf_op jit(solution)/shard_map/ppermute | solution.py:21
where the time goes:
time: 64.4 us; the launch traced here: 64.3 us
  Pallas kernels  30.2 us (47%)
  starting transfers between devices  16.5 us (26%)
  waiting for transfers between devices  11.1 us (17%)
  local copies, waits for them, and re-layouts  6.18 us (10%)
    pallas_call x9, Pallas kernels, run(): pl.pallas_call(body, out_shape=outs, in_specs=[smem] * scalars + [vmem] *...  30.2 us
    ppermute x5, starting transfers between devices, shift_from(): return lax.ppermute(block, axis, route)  11.5 us
    ppermute x5, waiting for transfers between devices, shift_from(): return lax.ppermute(block, axis, route)  7.4 us
    unnamed x32, local copies, waits for them, and re-layouts  6.17 us
    ppermute x5, starting transfers between devices, swap(): return lax.ppermute(block, axis, [(i, i ^ bit) for i in range(count)])  4.93 us
    ppermute x5, waiting for transfers between devices, swap(): return lax.ppermute(block, axis, [(i, i ^ bit) for i in range(count)])  3.7 us
  transfers between devices with their start and end apart: 10, of which 4 were waited for; matrix products, arithmetic and copies ran while one was open for 3% of the time, Pallas kernels for 31%

commit v1 on v0

--- a/solution.py
+++ b/solution.py
@@ -5,12 +5,14 @@
 from jax.experimental.pallas import tpu as pltpu
 from jax.sharding import PartitionSpec as P
 
+
 SIDE = 32
 WIDE = SIDE + 4
 PER_TILE = 3
 TILES = WIDE // PER_TILE
 LANES = 128
 REACH = SIDE + 2
+CHUNKS = 1
 HALF = jnp.bfloat16
 FULL = jnp.float32
 
@@ -26,7 +28,7 @@
     return lax.ppermute(block, axis, [(i, i ^ bit) for i in range(count)])
 
 
-def run(body, outs, ins, scratch, name, micros=1.0, scalars=1, limit=24):
+def run(body, outs, ins, scratch, micros=1.0, scalars=1, limit=16):
     smem = pl.BlockSpec(memory_space=pltpu.SMEM)
     vmem = pl.BlockSpec(memory_space=pltpu.VMEM)
     return pl.pallas_call(
@@ -35,7 +37,6 @@
         in_specs=[smem] * scalars + [vmem] * (len(ins) - scalars),
         out_specs=[vmem] * len(outs),
         scratch_shapes=scratch,
-        name=name,
         cost_estimate=pl.CostEstimate(
             flops=int(micros * 1.15e9), bytes_accessed=1024, transcendentals=0
         ),
@@ -56,21 +57,24 @@
     return lax.broadcasted_iota(jnp.int32, shape, len(shape) - 1)
 
 
-def pack(state):
+def turn_rows(state_ref, flat):
+    channels = state_ref.shape[0]
+    flat[:channels] = state_ref[...]
+    flat[channels:] = jnp.zeros((flat.shape[0] - channels,) + flat.shape[1:], HALF)
+    return jnp.swapaxes(flat[...], 0, 1)
+
+
+def pack(who, anchor, state):
     channels, rows, cols = state.shape
     padded = -(-channels // 8) * 8
     deep = -(-padded // 16) * 16
     span = -(-rows * REACH // LANES)
 
-    def body(state_ref, rows_ref, right_ref, left_ref, flat):
-        flat[:channels] = state_ref[...]
-        flat[channels:] = jnp.zeros((deep - channels, rows, cols), HALF)
-        turned = jnp.swapaxes(flat[...], 0, 1)
-        rows_ref[...] = turned
+    def body(who_ref, at_ref, state_ref, right_ref, left_ref, flat):
+        turned = turn_rows(state_ref, flat)
         lane = lane_index((deep, LANES))
-        none = jnp.zeros((deep, LANES), HALF)
         tiles = [None] * span
-        rim = none
+        rim = jnp.zeros((deep, LANES), HALF)
         for r in range(rows):
             row = turned[r]
             at, off = divmod(r * REACH, LANES)
@@ -89,30 +93,38 @@
 
     return run(
         body,
-        [like((rows, deep, cols)), like((padded, span * LANES)), like((padded, LANES))],
-        [state],
+        [like((padded, span * LANES)), like((padded, LANES))],
+        [who, anchor, state],
         [pltpu.VMEM((deep, rows, cols), HALF)],
-        "pack",
-        micros=3.0,
-        scalars=0,
-    )
-
-
-def prep(weights, noise):
+        micros=1.0,
+        scalars=2,
+    )
+
+
+def prep(weights, biases, noise):
     steps, channels, cells = noise.shape
     count = len(weights)
     tile_rows = LANES // SIDE
+    lines = len(biases)
 
     def body(*refs):
-        ins, noise_ref, outs, noise_out = refs[:count], refs[count], refs[count + 1 : -1], refs[-1]
-        for w_ref, o_ref in zip(ins, outs):
-            _, made, used = w_ref.shape
+        ins, lines_in, noise_ref = refs[:count], refs[count : count + lines], refs[count + lines]
+        outs = refs[count + lines + 1 :]
+        lines_out, noise_out = outs[count : count + lines], outs[count + lines]
+        for k, (w_ref, o_ref) in enumerate(zip(ins, outs)):
+            _, down, across = w_ref.shape
             o_ref[...] = jnp.zeros(o_ref.shape, HALF)
             for v in range(2):
                 for a in range(3):
                     for b in range(3):
-                        at = (3 * (a + v) + b) * LANES
-                        o_ref[v * LANES : v * LANES + made, at : at + used] = w_ref[3 * a + b]
+                        tap = (3 * (a + v) + b) * LANES
+                        row, col = (v * LANES, tap) if k % 2 else (tap, v * LANES)
+                        o_ref[row : row + down, col : col + across] = w_ref[3 * a + b]
+        for line_ref, o_ref in zip(lines_in, lines_out):
+            used = line_ref.shape[1]
+            o_ref[...] = jnp.zeros(o_ref.shape, FULL)
+            o_ref[:, :used] = line_ref[...]
+            o_ref[:, LANES : LANES + used] = line_ref[...]
         for k in range(steps):
             for t in range(cells // LANES):
                 block = noise_ref[k, :, t * LANES : (t + 1) * LANES].astype(FULL)
@@ -125,23 +137,37 @@
                         k, r // 2 * SIDE : (r // 2 + 1) * SIDE, r % 2 * LANES : (r % 2 + 1) * LANES
                     ] = block[m * SIDE : (m + 1) * SIDE]
 
-    made = [like((2 * LANES, 12 * LANES))] * count + [like((steps, cells // 2, 2 * LANES))]
-    out = run(body, made, [*weights, noise], [], "prep", micros=4.0, scalars=0)
-    return out[:count], out[count]
-
-
-def extract(who, anchor, by_row, right, left, bands, sects):
-    rows, deep, cols = by_row.shape
+    sizes = [(12 * LANES, 2 * LANES), (2 * LANES, 12 * LANES)]
+    made = [like(sizes[k % 2]) for k in range(count)]
+    made += [like((line.shape[0], 2 * LANES), FULL) for line in biases]
+    made += [like((steps, cells // 2, 2 * LANES))]
+    out = run(body, made, [*weights, *biases, noise], [], micros=2.0, scalars=0)
+    return out[:count], out[count : count + lines], out[count + lines]
+
+
+def add_parts(kept, got, keep_odd):
+    count, padded, lanes = kept.shape
+
+    def body(kept_ref, got_ref, out_ref):
+        for k in range(count // 2):
+            out_ref[k] = kept_ref[2 * k + keep_odd] + got_ref[2 * k + keep_odd]
+
+    return run(body, [like((count // 2, padded, lanes))], [kept, got], [], micros=0.3, scalars=0)[0]
+
+
+def extract(who, anchor, state, right, left, bands, sects):
+    _, rows, cols = state.shape
     padded = right.shape[0]
+    deep = -(-padded // 16) * 16
     width = cols + LANES
     batch = 4 if bands % 4 == 0 else bands
     chunk = 4
 
-    def body(who_ref, at_ref, rows_ref, right_ref, left_ref,
-             keep_ref, send_ref, ext_ref, top_ref, low_ref, ext, picked):
+    def body(who_ref, at_ref, state_ref, right_ref, left_ref,
+             keep_ref, send_ref, top_ref, low_ref, flat, ext, picked):
         lane = lane_index((padded, LANES))
         ext[:, padded:, :] = jnp.zeros((rows, deep - padded, width), HALF)
-        ext[:, :, :cols] = rows_ref[...]
+        ext[:, :, :cols] = turn_rows(state_ref, flat)
         rim = left_ref[...]
         none = jnp.zeros((padded, LANES), HALF)
         for r in range(rows):
@@ -155,7 +181,6 @@
             turned = pltpu.roll(rim, (LANES - 2 - 2 * r) % LANES, 1)
             piece = jnp.where(lane < REACH, piece, jnp.where(lane >= LANES - 2, turned, none))
             ext[r, :padded, cols:] = piece
-        ext_ref[...] = ext[...]
         top_ref[...] = ext[:2]
         low_ref[...] = ext[rows - 2 :]
         for first in range(0, bands, batch):
@@ -206,23 +231,18 @@
     edge = like((2, deep, width))
     return run(
         body,
-        [part, part, like((rows, deep, width)), edge, edge],
-        [who, anchor, by_row, right, left],
-        [pltpu.VMEM((rows, deep, width), HALF), pltpu.VMEM((rows, deep, batch * LANES), FULL)],
-        "extract",
+        [part, part, edge, edge],
+        [who, anchor, state, right, left],
+        [pltpu.VMEM((deep, rows, cols), HALF), pltpu.VMEM((rows, deep, width), HALF), pltpu.VMEM((rows, deep, batch * LANES), FULL)],
         micros=3.0,
         scalars=2,
     )
 
 
-def pair_bias(bias):
-    line = jnp.pad(bias, ((0, LANES - bias.shape[0]),))
-    return jnp.concatenate([line, line])[None, :]
-
-
 def product(view, weight):
+    turned = weight.shape[0] == 2 * LANES
     return lax.dot_general(
-        view, weight, (((1,), (1,)), ((), ())), preferred_element_type=FULL
+        view, weight, (((1,), (1 if turned else 0,)), ((), ())), preferred_element_type=FULL
     )
 
 
@@ -250,7 +270,7 @@
         mine = who_ref[0] * sects + who_ref[1]
         row0, col0 = at_ref[mine, 0], at_ref[mine, 1]
         (noise_ref, w_in, w_out, d_in, d_out, b_in, b_out, b_step, b_den, out_ref,
-         flat, state_sh, hid, hid_sh, pad, pad_sh, corr) = refs[2 + len(addends) :]
+         flat, state_sh, hid, hid_sh, pad, pad_sh, corr, state) = refs[2 + len(addends) :]
         for t in range(TILES):
             lanes = slice(t * LANES, (t + 1) * LANES)
             tile = parts[0][0, :, lanes].astype(FULL)
@@ -285,23 +305,43 @@
             [state_sh[2, 1 : 1 + half, v, :SIDE, :] for v in (0, 1)], axis=-1
         ).astype(FULL).reshape(half * SIDE, 2 * LANES)
         mean = (center + value + b_out[...]).astype(HALF).astype(FULL)
-        state = mean + noise_ref[0].astype(FULL)
+        state[...] = mean + noise_ref[0].astype(FULL)
         pad[...] = jnp.zeros(pad.shape, FULL)
-
-        def conv(source, weight):
-            shaped = source.reshape(half, SIDE, 2 * LANES)
-            pad[:half, 1, 8 : 8 + SIDE] = shaped[:, :, :LANES]
-            pad[1:, 0, 8 : 8 + SIDE] = shaped[:, :, LANES:]
+        deal = half // CHUNKS
+        trips = jnp.where(who_ref[0] >= 0, CHUNKS, 0)
+
+        def fill(source, first, count):
+            shaped = source.reshape(count, SIDE, 2 * LANES)
+            pad[pl.ds(first, count), 1, 8 : 8 + SIDE] = shaped[:, :, :LANES]
+            pad[pl.ds(first + 1, count), 0, 8 : 8 + SIDE] = shaped[:, :, LANES:]
+
+        def shift():
             for b in range(3):
                 pad_sh[b] = pad[:, :, 7 + b : 7 + b + SIDE, :].astype(HALF)
-            return product(gather_pairs(pad_sh, 0, half), weight[...])
 
         for step in range(steps):
-            inner = silu(conv(state, d_in) + b_step[step : step + 1])
-            state = state - 0.5 * (conv(inner, d_out) + b_den[...])
-            if step + 1 < steps:
-                state = state + 0.5 * noise_ref[step + 1].astype(FULL)
-        change = (state - mean).reshape(half, SIDE, 2 * LANES)
+            fill(state[...], 0, half)
+            shift()
+
+            def first(c, carry, step=step):
+                value = product(gather_pairs(pad_sh, c * deal, deal), d_in[...])
+                fill(silu(value + b_step[step : step + 1]), c * deal, deal)
+                return carry
+
+            lax.fori_loop(0, trips, first, 0)
+            shift()
+
+            def second(c, carry, step=step):
+                value = product(gather_pairs(pad_sh, c * deal, deal), d_out[...])
+                cells = pl.ds(pl.multiple_of(c * deal * SIDE, deal * SIDE), deal * SIDE)
+                value = state[cells] - 0.5 * (value + b_den[...])
+                if step + 1 < steps:
+                    value = value + 0.5 * noise_ref[step + 1, cells].astype(FULL)
+                state[cells] = value
+                return carry
+
+            lax.fori_loop(0, trips, second, 0)
+        change = (state[...] - mean).reshape(half, SIDE, 2 * LANES)
         corr[:, 0] = change[:, :, :LANES]
         corr[:, 1] = change[:, :, LANES:]
         cells = corr[...].reshape(SIDE * SIDE, LANES)
@@ -321,16 +361,19 @@
             pltpu.VMEM((half + 1, 2, loose, LANES), FULL),
             pltpu.VMEM((3, half + 1, 2, SIDE, LANES), HALF),
             pltpu.VMEM((half, 2, SIDE, LANES), FULL),
+            pltpu.VMEM((half * SIDE, 2 * LANES), FULL),
         ],
-        "patch",
         micros=8.0,
         scalars=2,
     )[0]
 
 
-def grid_mean(who, ext, rim, lower, padded, weights, biases, limits):
-    rows, deep, width = ext.shape
-    cols = width - LANES
+def grid_mean(who, state, right, left, rim, lower, weights, biases, limits):
+    _, rows, cols = state.shape
+    padded = right.shape[0]
+    deep = -(-padded // 16) * 16
+    width = cols + LANES
+    span = right.shape[1]
     loose = cols + 16
     made = rows // 2
     pairs_in, pairs_out = made // 4 + 1, made // 4
@@ -340,33 +383,49 @@
     state_pairs = hidden_pairs + 1
     base = rows - made - 2 if lower else -2
 
-    def body(who_ref, ext_ref, rim_ref, w_in, w_out, b_in, b_out, out_ref,
-             line, state_sh, hid, hid_sh):
+    def body(who_ref, state_ref, right_ref, left_ref, rim_ref, w_in, w_out, b_in, b_out, out_ref,
+             flat, turned, after, before, line, state_sh, hid, hid_sh):
         row0 = who_ref[0] * rows + base + 1
         col0 = who_ref[1] * cols - 1
 
-        def spread(i, v, slot, source):
-            value = source.astype(FULL)
-            if deep < LANES:
-                value = jnp.concatenate([value, jnp.zeros((LANES - deep, width), FULL)], axis=0)
-            value = value.T
-            line[slot, 8 : 8 + cols] = value[:cols]
-            line[slot, 8 + cols :] = value[cols : cols + 16]
-            line[slot, :8] = value[width - 8 :]
+        turned[:, :deep] = turn_rows(state_ref, flat)
+        turned[:, deep:] = jnp.zeros((rows, LANES - deep, cols), HALF)
+
+        def upright(value):
+            value = value.astype(FULL)
+            return jnp.concatenate(
+                [value, jnp.zeros((LANES - value.shape[0], value.shape[1]), FULL)], axis=0
+            ).T
+
+        for t in range(span // LANES):
+            lanes = slice(t * LANES, (t + 1) * LANES)
+            after[lanes] = upright(right_ref[:, lanes])
+        before[...] = upright(left_ref[...])
+        line[...] = jnp.zeros(line.shape, FULL)
+
+        def shift(i, v):
             for b in range(3):
-                state_sh[b, i, v] = line[slot, 6 + b : 6 + b + loose, :].astype(HALF)
+                state_sh[b, i, v] = line[v, 6 + b : 6 + b + loose, :].astype(HALF)
 
         for pair in range(made // 2 + 2, state_pairs):
             for b in range(3):
                 state_sh[b, pair] = jnp.zeros((2, loose, LANES), HALF)
         edge = made // 2 + 1 if lower else 0
         for v in range(2):
-            spread(edge, v, v, rim_ref[v])
+            value = upright(rim_ref[v])
+            line[v, 8 : 8 + cols] = value[:cols]
+            line[v, 8 + cols :] = value[cols : cols + 16]
+            line[v, :8] = value[width - 8 :]
+            shift(edge, v)
         skip = 0 if lower else 1
 
         def spread_rows(i, carry):
             for v in range(2):
-                spread(i + skip, v, v, ext_ref[2 * (i + skip) + v + base])
+                r = 2 * (i + skip) + v + base
+                line[v, 8 : 8 + cols] = turned[r].astype(FULL).T
+                line[v, 8 + cols : 10 + cols] = after[pl.ds(r * REACH, 2)]
+                line[v, 6:8] = before[pl.ds(2 * r, 2)]
+                shift(i + skip, v)
             return carry
 
         lax.fori_loop(0, made // 2 + 1, spread_rows, 0)
@@ -409,14 +468,17 @@
     return run(
         body,
         [like((made, padded, cols))],
-        [who, ext, rim, *weights, *biases],
+        [who, state, right, left, rim, *weights, *biases],
         [
+            pltpu.VMEM((deep, rows, cols), HALF),
+            pltpu.VMEM((rows, LANES, cols), HALF),
+            pltpu.VMEM((span, LANES), FULL),
+            pltpu.VMEM((LANES, LANES), FULL),
             pltpu.VMEM((2, loose + 8, LANES), FULL),
             pltpu.VMEM((3, state_pairs, 2, loose, LANES), HALF),
             pltpu.VMEM((pairs_in, 2, loose, LANES), FULL),
             pltpu.VMEM((3, hidden_pairs, 2, cols, LANES), HALF),
         ],
-        "mean_low" if lower else "mean_top",
         micros=5.0,
     )[0]
 
@@ -451,7 +513,7 @@
 
     shape = (padded, rows * SIDE)
     return run(
-        body, [like(shape)], [who, anchor, *pieces], [pltpu.VMEM(shape, FULL)], "spill",
+        body, [like(shape)], [who, anchor, *pieces], [pltpu.VMEM(shape, FULL)],
         micros=1.5, scalars=2,
     )[0]
 
@@ -494,7 +556,7 @@
 
     return run(
         body, [like((rows, padded, cols), FULL), like((rows, cols), FULL)],
-        [who, anchor, *pieces], [], "canvas", micros=2.5, scalars=2,
+        [who, anchor, *pieces], [], micros=2.5, scalars=2,
     )
 
 
@@ -523,13 +585,12 @@
         [like((channels, rows, cols))],
         [*means, summed, arrived, inverse],
         [pltpu.VMEM((rows, deep, cols), HALF)],
-        "finish",
         micros=3.0,
         scalars=0,
     )[0]
 
 
-def per_device(
+def step(
     state_field,
     conv_in_weight,
     conv_in_bias,
@@ -548,27 +609,30 @@
     limits = (rows * bands, cols * sects)
     who = jnp.stack([lax.axis_index("band"), lax.axis_index("sect")]).astype(jnp.int32)
 
-    by_row, right_rim, left_rim = pack(state_field)
-    padded = right_rim.shape[0]
+    right_rim, left_rim = pack(who, patch_anchor, state_field)
     right = shift_from(right_rim, "sect", -1)
     left = shift_from(left_rim, "sect", 1)
 
-    made, noise = prep(
-        [conv_in_weight, conv_out_weight, denoise_in_weight, denoise_out_weight], patch_noise[0]
-    )
-    biases = [pair_bias(b) for b in (conv_in_bias, conv_out_bias, denoise_bias)]
-    step_lines = jnp.concatenate([step_bias, step_bias], axis=-1)
-
-    kept, sent, ext, top, low = extract(
-        who, patch_anchor, by_row, right, left, bands, sects
-    )
+    made, lines, noise = prep(
+        [
+            conv_in_weight.transpose(0, 2, 1),
+            conv_out_weight,
+            denoise_in_weight.transpose(0, 2, 1),
+            denoise_out_weight,
+        ],
+        [conv_in_bias[None, :], conv_out_bias[None, :], denoise_bias[None, :], step_bias],
+        patch_noise[0],
+    )
+    biases, step_lines = lines[:3], lines[3]
+
+    kept, sent, top, low = extract(who, patch_anchor, state_field, right, left, bands, sects)
     got = swap(sent, "band", 1)
     addends = [kept, got]
     bit = 2
-    parts = None
     while bit < bands:
-        parts = kept + got if parts is None else parts[0::2] + got
-        got = swap(parts[1::2], "band", bit)
+        odd = add_parts(kept, got, 1)
+        kept = add_parts(kept, got, 0) if 2 * bit < bands else kept
+        got = swap(odd, "band", bit)
         addends.append(got)
         bit *= 2
     above = shift_from(low, "band", 1)
@@ -580,18 +644,24 @@
     sources = [0]
     bit = bands // 2
     while bit:
-        pieces += [swap(piece, "band", bit) for piece in pieces]
+        fresh = []
+        for piece in pieces:
+            fresh.append(swap(piece, "band", bit))
+        pieces += fresh
         sources += [s ^ bit for s in sources]
         bit //= 2
-    means = [
-        grid_mean(who, ext, rim, lower, padded, made[:2], biases[:2], limits)
-        for lower, rim in ((False, above), (True, below))
-    ]
-    arrived = shift_from(
-        spill(who, patch_anchor, pieces, sources, sects, rows, cols), "sect", 1
-    )
+
+    def grid(lower, rim):
+        return grid_mean(
+            who, state_field, right, left, rim, lower, made[:2], biases[:2], limits
+        )
+
+    top_mean = grid(False, above)
+    low_mean = grid(True, below)
+    spilled = spill(who, patch_anchor, pieces, sources, sects, rows, cols)
+    arrived = shift_from(spilled, "sect", 1)
     summed, inverse = canvas(who, patch_anchor, pieces, sources, sects, rows, cols)
-    return finish(means, summed, arrived, inverse, channels)
+    return finish([top_mean, low_mean], summed, arrived, inverse, channels)
 
 
 def solution(mesh):
@@ -609,7 +679,7 @@
         P(),
     )
     return jax.shard_map(
-        per_device,
+        step,
         mesh=mesh,
         in_specs=placed,
         out_specs=P("groups", "band", "sect"),

time: 64.4 us -> 63.1 us (0.980)
  the two profiles are of different devices: /device:TPU:11 before, /device:TPU:18 now
where the time goes in v1:
time: 63.1 us; the launch traced here: 62.2 us
  Pallas kernels  30.2 us (48%)
  waiting for transfers between devices  15.6 us (25%)
  starting transfers between devices  14.1 us (22%)
  local copies, waits for them, and re-layouts  2.04 us (3%)
    pallas_call x10, Pallas kernels, run(): pl.pallas_call(body, out_shape=outs, in_specs=[smem] * scalars + [vmem] *...  30.2 us
    ppermute x5, starting transfers between devices, shift_from(): return lax.ppermute(block, axis, route)  13.3 us
    ppermute x5, waiting for transfers between devices, shift_from(): return lax.ppermute(block, axis, route)  9.45 us
    ppermute x5, waiting for transfers between devices, swap(): return lax.ppermute(block, axis, [(i, i ^ bit) for i in range(count)])  6.1 us
    unnamed x24, local copies, waits for them, and re-layouts  2.04 us
  transfers between devices with their start and end apart: 10, of which 6 were waited for; matrix products, arithmetic and copies ran while one was open for 0% of the time, Pallas kernels for 32%

profile of v1, /device:TPU:18, one launch (start us, length us, event | category | flops | bytes accessed | tf_op | source)
XLA Modules:
  0.0 62.2 jit_solution(2301523971359128938)
XLA Ops:
  0.0 0.8 %copy.12.at_ref.refs_1_ = s32[16,2]{1,0:T(8,128)S(1)} copy(s32[16,2]{0,1:T(2,128)} %param.16) | data formatting | bytes 256 | tf_op args[5]
  0.8 0.1 pad_add_fusion.who_ref.refs_0_
  0.8 1.1 %copy-done = bf16[99,32,128]{2,1,0:T(8,128)(2,1)S(1)} copy-done((bf16[99,32,128]{2,1,0:T(8,128)(2,1)S(1)}, bf16[99,32,128]{2,1,0:T(8,128)(2,1)}, u32[]{:S(2)}) %copy-start) | copy-done | bytes 811032
  2.0 1.3 %shard_map.109 = (bf16[104,1152]{1,0:T(8,128)(2,1)S(1)}, bf16[104,128]{1,0:T(8,128)(2,1)S(1)}) custom-call(s32[2]{0:T(128)S(1)} %pad_add_fusion.who_ref.refs_0_, s32[16,2]{1,0:T(8,128)S(1)} %copy.12.at_ref.refs_1_, bf16[99,32,128]{2,1,0:T(8,128)(2,1)S(1)} %copy-done), custom_call_target="tpu_custom_call" | custom-call | flops 1150000000 | bytes 1024 | tf_op jit(solution)/shard_map/pallas_call | solution.py:34
  3.3 2.4 %collective-permute-start = (bf16[104,1152]{1,0:T(8,128)(2,1)S(1)}, bf16[104,1152]{1,0:T(8,128)(2,1)S(1)}, u32[]{:S(2)}, u32[]{:S(2)}) collective-permute-start(bf16[104,1152]{1,0:T(8,128)(2,1)S(1)} %get-tuple-element.22), channel_id=1, source_target_pairs={{1,0},{2,1},{3,2},{5,4},{6,5},{7,6},{9,8},{10,9},{11,10},{13,12},{... | collective-permute-start | bytes 718856 | tf_op jit(solution)/shard_map/ppermute | solution.py:23
  5.7 3.5 %collective-permute-start.1 = (bf16[104,128]{1,0:T(8,128)(2,1)S(1)}, bf16[104,128]{1,0:T(8,128)(2,1)S(1)}, u32[]{:S(2)}, u32[]{:S(2)}) collective-permute-start(bf16[104,128]{1,0:T(8,128)(2,1)S(1)} %get-tuple-element.23), channel_id=1, source_target_pairs={{0,1},{1,2},{2,3},{4,5},{5,6},{6,7},{8,9},{9,10},{10,11},{12,13},{... | collective-permute-start | bytes 79880 | tf_op jit(solution)/shard_map/ppermute | solution.py:23
  9.2 2.2 %collective-permute-done.1.left_ref = bf16[104,128]{1,0:T(8,128)(2,1)S(1)} collective-permute-done((bf16[104,128]{1,0:T(8,128)(2,1)S(1)}, bf16[104,128]{1,0:T(8,128)(2,1)S(1)}, u32[]{:S(2)}, u32[]{:S(2)}) %collective-permute-start.1) | collective-permute-done | bytes 26656 | tf_op jit(solution)/shard_map/ppermute | solution.py:23
  11.4 1.3 %collective-permute-done.right_ref = bf16[104,1152]{1,0:T(8,128)(2,1)S(1)} collective-permute-done((bf16[104,1152]{1,0:T(8,128)(2,1)S(1)}, bf16[104,1152]{1,0:T(8,128)(2,1)S(1)}, u32[]{:S(2)}, u32[]{:S(2)}) %collective-permute-start) | collective-permute-done | bytes 239648 | tf_op jit(solution)/shard_map/ppermute | solution.py:23
  12.8 4.6 %shard_map.110 = (bf16[2,104,1536]{2,1,0:T(8,128)(2,1)S(1)}, bf16[2,104,1536]{2,1,0:T(8,128)(2,1)S(1)}, bf16[2,112,256]{2,1,0:T(8,128)(2,1)S(1)}, bf16[2,112,256]{2,1,0:T(8,128)(2,1)S(1)}) custom-call(s32[2]{0:T(128)S(1)} %pad_add_fusion.who_ref.refs_0_, s32[16,2]{1,0:T(8,128)S(1)} %copy.12.at_ref.refs_1_, bf16[99,32,128]{2,1,0:T(8,128)(2,1)S(1)} %copy-done, ...), custom_call_target="tpu_custom_call" | custom-call | flops 3449999872 | bytes 1024 | tf_op jit(solution)/shard_map/pallas_call | solution.py:34
  17.4 0.0 copy-start.10
  17.4 0.0 copy-start.2
  17.4 0.0 copy-start.3
  17.5 0.0 copy-start.4
  17.5 0.0 copy-start.5
  17.5 0.0 copy-start.6
  17.5 0.0 copy-start.7
  17.5 0.0 copy-start.8
  17.5 0.0 copy-start.9
  17.5 0.1 collective-permute-start.4
  17.6 2.1 %collective-permute-done.4.got_ref.refs_3_ = bf16[2,104,1536]{2,1,0:T(8,128)(2,1)S(1)} collective-permute-done((bf16[2,104,1536]{2,1,0:T(8,128)(2,1)S(1)}, bf16[2,104,1536]{2,1,0:T(8,128)(2,1)S(1)}, u32[]{:S(2)}, u32[]{:S(2)}) %collective-permute-start.4) | collective-permute-done | bytes 639008 | tf_op jit(solution)/shard_map/ppermute | solution.py:28
  19.7 0.1 collective-permute-start.5
  19.8 0.0 copy-done.10
  19.8 0.1 copy.19
  19.9 0.0 copy-done.2
  19.9 0.0 copy-done.3
  20.0 0.0 copy-done.4
  20.0 0.0 copy-done.5
  20.0 0.6 %shard_map.111 = (bf16[1536,256]{1,0:T(8,128)(2,1)S(1)}, bf16[256,1536]{1,0:T(8,128)(2,1)S(1)}, bf16[1536,256]{1,0:T(8,128)(2,1)S(1)}, bf16[256,1536]{1,0:T(8,12...) custom-call(bf16[9,99,128]{2,1,0:T(8,128)(2,1)S(1)} %bitcast.11, ...), custom_call_target="tpu_custom_call" | custom-call | flops 2300000000 | bytes 1024 | tf_op jit(solution)/shard_map/pallas_call | solution.py:34
  20.7 2.0 %collective-permute-start.2 = (bf16[2,112,256]{2,1,0:T(8,128)(2,1)S(1)}, bf16[2,112,256]{2,1,0:T(8,128)(2,1)S(1)}, u32[]{:S(2)}, u32[]{:S(2)}) collective-permute-start(bf16[2,112,256]{2,1,0:T(8,128)(2,1)S(1)} %get-tuple-element.24), channel_id=1, source_target_pairs={{0,4},{4,8},{8,12},{1,5},{5,9},{9,13},{2,6},{6,10},{10,14},{3,7},{... | collective-permute-start | bytes 344072 | tf_op jit(solution)/shard_map/ppermute | solution.py:23
  22.7 3.6 %collective-permute-start.3 = (bf16[2,112,256]{2,1,0:T(8,128)(2,1)S(1)}, bf16[2,112,256]{2,1,0:T(8,128)(2,1)S(1)}, u32[]{:S(2)}, u32[]{:S(2)}) collective-permute-start(bf16[2,112,256]{2,1,0:T(8,128)(2,1)S(1)} %get-tuple-element.29), channel_id=1, source_target_pairs={{4,0},{8,4},{12,8},{5,1},{9,5},{13,9},{6,2},{10,6},{14,10},{7,3},{... | collective-permute-start | bytes 344072 | tf_op jit(solution)/shard_map/ppermute | solution.py:23
  26.2 3.9 %collective-permute-done.5.refs_4_ = bf16[1,104,1536]{2,1,0:T(8,128)(2,1)S(1)} collective-permute-done((bf16[1,104,1536]{2,1,0:T(8,128)(2,1)S(1)}, bf16[1,104,1536]{2,1,0:T(8,128)(2,1)S(1)}, u32[]{:S(2)}, u32[]{:S(2)}) %collective-permute-start.5) | collective-permute-done | bytes 319520 | tf_op jit(solution)/shard_map/ppermute | solution.py:28
  30.2 5.9 %shard_map.115.refs_0_ = bf16[104,1024]{1,0:T(8,128)(2,1)S(1)} custom-call(s32[2]{0:T(128)S(1)} %pad_add_fusion.who_ref.refs_0_, s32[16,2]{1,0:T(8,128)S(1)} %copy.12.at_ref.refs_1_, bf16[2,104,1536]{2,1,0:T(8,128)(2,1)S(1)} %get-tuple-element.30.kept_ref.refs_2_, bf16[2,104,1536]{2,1,0:T(8,128)(2,1)S(1)} %collective-permute-done.4.got_ref.refs_3_, ...), custom_call_target="tpu_custom_call" | custom-call | flops 9200000000 | bytes 1024 | tf_op jit(solution)/shard_map/pallas_call | solution.py:34
  36.1 0.1 collective-permute-start.6
  36.2 0.0 collective-permute-done.3.rim_ref
  36.2 0.0 copy-done.1
  36.2 5.6 %shard_map.113.low_ref = bf16[16,104,128]{2,1,0:T(8,128)(2,1)S(1)} custom-call(s32[2]{0:T(128)S(1)} %pad_add_fusion.who_ref.refs_0_, bf16[99,32,128]{2,1,0:T(8,128)(2,1)S(1)} %copy-done.1, bf16[104,1152]{1,0:T(8,128)(2,1)S(1)} %collective-permute-done.right_ref, bf16[104,128]{1,0:T(8,128)(2,1)S(1)} %collective-permute-done.1.left_ref, ...), custom_call_target="tpu_custom_call" | custom-call | flops 5750000128 | bytes 1024 | tf_op jit(solution)/shard_map/pallas_call | solution.py:34
  41.9 0.1 collective-permute-start.7
  41.9 0.1 collective-permute-done.6.refs_1_
  42.0 0.4 collective-permute-start.8
  42.4 0.0 collective-permute-done.2.rim_ref
  42.4 5.6 %shard_map.112.top_ref = bf16[16,104,128]{2,1,0:T(8,128)(2,1)S(1)} custom-call(s32[2]{0:T(128)S(1)} %pad_add_fusion.who_ref.refs_0_, bf16[99,32,128]{2,1,0:T(8,128)(2,1)S(1)} %copy-done.1, bf16[104,1152]{1,0:T(8,128)(2,1)S(1)} %collective-permute-done.right_ref, bf16[104,128]{1,0:T(8,128)(2,1)S(1)} %collective-permute-done.1.left_ref, ...), custom_call_target="tpu_custom_call" | custom-call | flops 5750000128 | bytes 1024 | tf_op jit(solution)/shard_map/pallas_call | solution.py:34
  48.1 0.0 collective-permute-done.7.refs_2_
  48.1 0.0 collective-permute-done.8.refs_3_
  48.1 2.8 %shard_map.117 = bf16[104,1024]{1,0:T(8,128)(2,1)S(1)} custom-call(s32[2]{0:T(128)S(1)} %pad_add_fusion.who_ref.refs_0_, s32[16,2]{1,0:T(8,128)S(1)} %copy.12.at_ref.refs_1_, bf16[104,1024]{1,0:T(8,128)(2,1)S(1)} %shard_map.115.refs_0_, bf16[104,1024]{1,0:T(8,128)(2,1)S(1)} %collective-permute-done.6.refs_1_, ...), custom_call_target="tpu_custom_call" | custom-call | flops 1724999936 | bytes 1024 | tf_op jit(solution)/shard_map/pallas_call | solution.py:34
  51.0 1.9 %collective-permute-start.9 = (bf16[104,1024]{1,0:T(8,128)(2,1)S(1)}, bf16[104,1024]{1,0:T(8,128)(2,1)S(1)}, u32[]{:S(2)}, u32[]{:S(2)}) collective-permute-start(bf16[104,1024]{1,0:T(8,128)(2,1)S(1)} %shard_map.117), channel_id=1, source_target_pairs={{0,1},{1,2},{2,3},{4,5},{5,6},{6,7},{8,9},{9,10},{10,11},{12,13},{... | collective-permute-start | bytes 638984 | tf_op jit(solution)/shard_map/ppermute | solution.py:23
  52.9 1.8 %shard_map.116 = (f32[32,104,128]{2,1,0:T(8,128)S(1)}, f32[32,128]{1,0:T(8,128)S(1)}) custom-call(s32[2]{0:T(128)S(1)} %pad_add_fusion.who_ref.refs_0_, s32[16,2]{1,0:T(8,128)S(1)} %copy.12.at_ref.refs_1_, bf16[104,1024]{1,0:T(8,128)(2,1)S(1)} %shard_map.115.refs_0_, bf16[104,1024]{1,0:T(8,128)(2,1)S(1)} %collective-permute-done.6.refs_1_, ...), custom_call_target="tpu_custom_call" | custom-call | flops 2875000064 | bytes 1024 | tf_op jit(solution)/shard_map/pallas_call | solution.py:34
  54.7 5.9 %collective-permute-done.9.spill_ref = bf16[104,1024]{1,0:T(8,128)(2,1)S(1)} collective-permute-done((bf16[104,1024]{1,0:T(8,128)(2,1)S(1)}, bf16[104,1024]{1,0:T(8,128)(2,1)S(1)}, u32[]{:S(2)}, u32[]{:S(2)}) %collective-permute-start.9) | collective-permute-done | bytes 213024 | tf_op jit(solution)/shard_map/ppermute | solution.py:23
  60.6 1.7 %shard_map.118 = bf16[99,32,128]{2,1,0:T(8,128)(2,1)} custom-call(bf16[16,104,128]{2,1,0:T(8,128)(2,1)S(1)} %shard_map.112.top_ref, bf16[16,104,128]{2,1,0:T(8,128)(2,1)S(1)} %shard_map.113.low_ref, f32[32,104,128]{2,1,0:T(8,128)S(1)} %get-tuple-element.37.sum_ref, bf16[104,1024]{1,0:T(8,128)(2,1)S(1)} %collective-permute-done.9.spill_ref, ...), custom_call_target="tpu_custom_call" | custom-call | flops 3449999872 | bytes 1024 | tf_op jit(solution)/shard_map/pallas_call | solution.py:34
  (7 shorter events, 0.0 us)
Async XLA Ops:
  0.8 1.1 %copy-start = (bf16[99,32,128]{2,1,0:T(8,128)(2,1)S(1)}, bf16[99,32,128]{2,1,0:T(8,128)(2,1)}, u32[]{:S(2)}) copy-start(bf16[99,32,128]{2,1,0:T(8,128)(2,1)} %state_ref.7) | copy-start | bytes 2433028
  3.3 9.5 %collective-permute-start = (bf16[104,1152]{1,0:T(8,128)(2,1)S(1)}, bf16[104,1152]{1,0:T(8,128)(2,1)S(1)}, u32[]{:S(2)}, u32[]{:S(2)}) collective-permute-start(bf16[104,1152]{1,0:T(8,128)(2,1)S(1)} %get-tuple-element.22), channel_id=1, source_target_pairs={{1,0},{2,1},{3,2},{5,4},{6,5},{7,6},{9,8},{10,9},{11,10},{13,12},{... | collective-permute-start | bytes 718856 | tf_op jit(solution)/shard_map/ppermute | solution.py:23
  5.7 5.7 %collective-permute-start.1 = (bf16[104,128]{1,0:T(8,128)(2,1)S(1)}, bf16[104,128]{1,0:T(8,128)(2,1)S(1)}, u32[]{:S(2)}, u32[]{:S(2)}) collective-permute-start(bf16[104,128]{1,0:T(8,128)(2,1)S(1)} %get-tuple-element.23), channel_id=1, source_target_pairs={{0,1},{1,2},{2,3},{4,5},{5,6},{6,7},{8,9},{9,10},{10,11},{12,13},{... | collective-permute-start | bytes 79880 | tf_op jit(solution)/shard_map/ppermute | solution.py:23
  17.4 2.4 %copy-start.10 = (bf16[1,2,99,1024]{3,1,2,0:T(2,128)(2,1)S(1)}, bf16[1,2,99,1024]{3,1,2,0:T(2,128)(2,1)}, u32[]{:S(2)}) copy-start(bf16[1,2,99,1024]{3,1,2,0:T(2,128)(2,1)} %param.17) | copy-start | bytes 1216516
  17.4 2.5 %copy-start.2 = (bf16[9,128,99]{1,2,0:T(8,128)(2,1)S(1)}, bf16[9,128,99]{1,2,0:T(8,128)(2,1)}, u32[]{:S(2)}) copy-start(bf16[9,128,99]{1,2,0:T(8,128)(2,1)} %param.12) | copy-start | bytes 684292
  17.4 2.5 %copy-start.3 = (bf16[9,99,128]{2,1,0:T(8,128)(2,1)S(1)}, bf16[9,99,128]{2,1,0:T(8,128)(2,1)}, u32[]{:S(2)}) copy-start(bf16[9,99,128]{2,1,0:T(8,128)(2,1)} %refs_1_.2) | copy-start | bytes 684292
  17.5 2.5 %copy-start.4 = (bf16[9,128,99]{1,2,0:T(8,128)(2,1)S(1)}, bf16[9,128,99]{1,2,0:T(8,128)(2,1)}, u32[]{:S(2)}) copy-start(bf16[9,128,99]{1,2,0:T(8,128)(2,1)} %param.18) | copy-start | bytes 684292
  17.5 2.5 %copy-start.5 = (bf16[9,99,128]{2,1,0:T(8,128)(2,1)S(1)}, bf16[9,99,128]{2,1,0:T(8,128)(2,1)}, u32[]{:S(2)}) copy-start(bf16[9,99,128]{2,1,0:T(8,128)(2,1)} %refs_3_.1) | copy-start | bytes 684292
  17.5 2.5 %copy-start.6 = (f32[2,128]{1,0:T(2,128)S(1)}, f32[2,128]{1,0:T(2,128)}, u32[]{:S(2)}) copy-start(f32[2,128]{1,0:T(2,128)} %refs_7_.1) | copy-start | bytes 3076
  17.5 2.5 %copy-start.7 = (f32[128]{0:T(128)S(1)}, f32[128]{0:T(128)}, u32[]{:S(2)}) copy-start(f32[128]{0:T(128)} %param.13) | copy-start | bytes 1540
  17.5 2.5 %copy-start.8 = (f32[99]{0:T(128)S(1)}, f32[99]{0:T(128)}, u32[]{:S(2)}) copy-start(f32[99]{0:T(128)} %param.15) | copy-start | bytes 1192
  17.5 2.5 %copy-start.9 = (f32[99]{0:T(128)S(1)}, f32[99]{0:T(128)}, u32[]{:S(2)}) copy-start(f32[99]{0:T(128)} %param.21) | copy-start | bytes 1192
  17.5 2.1 %collective-permute-start.4 = (bf16[2,104,1536]{2,1,0:T(8,128)(2,1)S(1)}, bf16[2,104,1536]{2,1,0:T(8,128)(2,1)S(1)}, u32[]{:S(2)}, u32[]{:S(2)}) collective-permute-start(bf16[2,104,1536]{2,1,0:T(8,128)(2,1)S(1)} %get-tuple-element.31), channel_id=1, source_target_pairs={{0,4},{4,0},{8,12},{12,8},{1,5},{5,1},{9,13},{13,9},{2,6},{6,2},{1... | collective-permute-start | bytes 1916936 | tf_op jit(solution)/shard_map/ppermute | solution.py:28
  19.7 10.5 %collective-permute-start.5 = (bf16[1,104,1536]{2,1,0:T(8,128)(2,1)S(1)}, bf16[1,104,1536]{2,1,0:T(8,128)(2,1)S(1)}, u32[]{:S(2)}, u32[]{:S(2)}) collective-permute-start(bf16[1,104,1536]{2,1,0:T(8,128)(2,1)S(1)} %shard_map.114), channel_id=1, source_target_pairs={{0,8},{4,12},{8,0},{12,4},{1,9},{5,13},{9,1},{13,5},{2,10},{6,14},... | collective-permute-start | bytes 958472 | tf_op jit(solution)/shard_map/ppermute | solution.py:28
  20.7 21.8 %collective-permute-start.2 = (bf16[2,112,256]{2,1,0:T(8,128)(2,1)S(1)}, bf16[2,112,256]{2,1,0:T(8,128)(2,1)S(1)}, u32[]{:S(2)}, u32[]{:S(2)}) collective-permute-start(bf16[2,112,256]{2,1,0:T(8,128)(2,1)S(1)} %get-tuple-element.24), channel_id=1, source_target_pairs={{0,4},{4,8},{8,12},{1,5},{5,9},{9,13},{2,6},{6,10},{10,14},{3,7},{... | collective-permute-start | bytes 344072 | tf_op jit(solution)/shard_map/ppermute | solution.py:23
  22.7 13.5 %collective-permute-start.3 = (bf16[2,112,256]{2,1,0:T(8,128)(2,1)S(1)}, bf16[2,112,256]{2,1,0:T(8,128)(2,1)S(1)}, u32[]{:S(2)}, u32[]{:S(2)}) collective-permute-start(bf16[2,112,256]{2,1,0:T(8,128)(2,1)S(1)} %get-tuple-element.29), channel_id=1, source_target_pairs={{4,0},{8,4},{12,8},{5,1},{9,5},{13,9},{6,2},{10,6},{14,10},{7,3},{... | collective-permute-start | bytes 344072 | tf_op jit(solution)/shard_map/ppermute | solution.py:23
  30.2 6.0 %copy-start.1 = (bf16[99,32,128]{2,1,0:T(8,128)(2,1)S(1)}, bf16[99,32,128]{2,1,0:T(8,128)(2,1)}, u32[]{:S(2)}) copy-start(bf16[99,32,128]{2,1,0:T(8,128)(2,1)} %state_ref.7) | copy-start | bytes 2433028
  36.1 5.9 %collective-permute-start.6 = (bf16[104,1024]{1,0:T(8,128)(2,1)S(1)}, bf16[104,1024]{1,0:T(8,128)(2,1)S(1)}, u32[]{:S(2)}, u32[]{:S(2)}) collective-permute-start(bf16[104,1024]{1,0:T(8,128)(2,1)S(1)} %shard_map.115.refs_0_), channel_id=1, source_target_pairs={{0,8},{4,12},{8,0},{12,4},{1,9},{5,13},{9,1},{13,5},{2,10},{6,14},... | collective-permute-start | bytes 638984 | tf_op jit(solution)/shard_map/ppermute | solution.py:28
  41.9 6.2 %collective-permute-start.7 = (bf16[104,1024]{1,0:T(8,128)(2,1)S(1)}, bf16[104,1024]{1,0:T(8,128)(2,1)S(1)}, u32[]{:S(2)}, u32[]{:S(2)}) collective-permute-start(bf16[104,1024]{1,0:T(8,128)(2,1)S(1)} %shard_map.115.refs_0_), channel_id=1, source_target_pairs={{0,4},{4,0},{8,12},{12,8},{1,5},{5,1},{9,13},{13,9},{2,6},{6,2},{1... | collective-permute-start | bytes 638984 | tf_op jit(solution)/shard_map/ppermute | solution.py:28
  42.0 6.1 %collective-permute-start.8 = (bf16[104,1024]{1,0:T(8,128)(2,1)S(1)}, bf16[104,1024]{1,0:T(8,128)(2,1)S(1)}, u32[]{:S(2)}, u32[]{:S(2)}) collective-permute-start(bf16[104,1024]{1,0:T(8,128)(2,1)S(1)} %collective-permute-done.6.refs_1_), channel_id=1, source_target_pairs={{0,4},{4,0},{8,12},{12,8},{1,5},{5,1},{9,13},{13,9},{2,6},{6,2},{1... | collective-permute-start | bytes 638984 | tf_op jit(solution)/shard_map/ppermute | solution.py:28
  51.0 9.6 %collective-permute-start.9 = (bf16[104,1024]{1,0:T(8,128)(2,1)S(1)}, bf16[104,1024]{1,0:T(8,128)(2,1)S(1)}, u32[]{:S(2)}, u32[]{:S(2)}) collective-permute-start(bf16[104,1024]{1,0:T(8,128)(2,1)S(1)} %shard_map.117), channel_id=1, source_target_pairs={{0,1},{1,2},{2,3},{4,5},{5,6},{6,7},{8,9},{9,10},{10,11},{12,13},{... | collective-permute-start | bytes 638984 | tf_op jit(solution)/shard_map/ppermute | solution.py:23

commit v2 on v1

--- a/solution.py
+++ b/solution.py
@@ -46,7 +46,7 @@
 
 def slot_at(who_ref, at_ref, j, sects, rows, cols):
     reader = jnp.bitwise_xor(who_ref[0], j) * sects + who_ref[1]
-    return at_ref[reader, 0] - who_ref[0] * rows, at_ref[reader, 1] - who_ref[1] * cols
+    return at_ref[0, reader] - who_ref[0] * rows, at_ref[1, reader] - who_ref[1] * cols
 
 
 def like(shape, dtype=HALF):
@@ -70,8 +70,9 @@
     deep = -(-padded // 16) * 16
     span = -(-rows * REACH // LANES)
 
-    def body(who_ref, at_ref, state_ref, right_ref, left_ref, flat):
+    def body(who_ref, at_ref, state_ref, right_ref, left_ref, rows_ref, flat):
         turned = turn_rows(state_ref, flat)
+        rows_ref[...] = turned
         lane = lane_index((deep, LANES))
         tiles = [None] * span
         rim = jnp.zeros((deep, LANES), HALF)
@@ -93,7 +94,7 @@
 
     return run(
         body,
-        [like((padded, span * LANES)), like((padded, LANES))],
+        [like((padded, span * LANES)), like((padded, LANES)), like((rows, deep, cols))],
         [who, anchor, state],
         [pltpu.VMEM((deep, rows, cols), HALF)],
         micros=1.0,
@@ -101,16 +102,18 @@
     )
 
 
-def prep(weights, biases, noise):
+def prep(who, anchor, weights, biases, noise, bands, sects, rows, cols):
     steps, channels, cells = noise.shape
     count = len(weights)
     tile_rows = LANES // SIDE
     lines = len(biases)
-
-    def body(*refs):
+    width = cols + LANES
+
+    def body(who_ref, at_ref, *refs):
         ins, lines_in, noise_ref = refs[:count], refs[count : count + lines], refs[count + lines]
         outs = refs[count + lines + 1 :]
         lines_out, noise_out = outs[count : count + lines], outs[count + lines]
+        pick_ref, place_ref = outs[count + lines + 1 :]
         for k, (w_ref, o_ref) in enumerate(zip(ins, outs)):
             _, down, across = w_ref.shape
             o_ref[...] = jnp.zeros(o_ref.shape, HALF)
@@ -136,13 +139,30 @@
                     noise_out[
                         k, r // 2 * SIDE : (r // 2 + 1) * SIDE, r % 2 * LANES : (r % 2 + 1) * LANES
                     ] = block[m * SIDE : (m + 1) * SIDE]
+        source = lax.broadcasted_iota(jnp.int32, (width, LANES), 0)
+        inner = lane_index((width, LANES))
+        for _ in range(1, PER_TILE):
+            inner = jnp.where(inner >= WIDE, inner - WIDE, inner)
+        cell = lax.broadcasted_iota(jnp.int32, (LANES, 2 * LANES), 0)
+        target = lane_index((LANES, 2 * LANES))
+        for j in range(bands):
+            row0, col0 = slot_at(who_ref, at_ref, j, sects, rows, cols)
+            want = jnp.bitwise_and(inner + (col0 - 2), width - 1)
+            pick_ref[:, j * LANES : (j + 1) * LANES] = jnp.where(source == want, 1.0, 0.0).astype(HALF)
+            across = jnp.bitwise_and(cell, SIDE - 1) + col0
+            for m in range(tile_rows):
+                turn = jnp.bitwise_and(m - row0, tile_rows - 1)
+                there = jnp.where(across < cols, across, across - cols + LANES + m * SIDE)
+                hit = (target == there) & (cell >= turn * SIDE) & (cell < (turn + 1) * SIDE)
+                place_ref[m, j * LANES : (j + 1) * LANES] = jnp.where(hit, 1.0, 0.0).astype(HALF)
 
     sizes = [(12 * LANES, 2 * LANES), (2 * LANES, 12 * LANES)]
     made = [like(sizes[k % 2]) for k in range(count)]
     made += [like((line.shape[0], 2 * LANES), FULL) for line in biases]
     made += [like((steps, cells // 2, 2 * LANES))]
-    out = run(body, made, [*weights, *biases, noise], [], micros=2.0, scalars=0)
-    return out[:count], out[count : count + lines], out[count + lines]
+    made += [like((width, bands * LANES)), like((tile_rows, bands * LANES, 2 * LANES))]
+    out = run(body, made, [who, anchor, *weights, *biases, noise], [], micros=2.5, scalars=2)
+    return out[:count], out[count : count + lines], *out[count + lines :]
 
 
 def add_parts(kept, got, keep_odd):
@@ -155,19 +175,18 @@
     return run(body, [like((count // 2, padded, lanes))], [kept, got], [], micros=0.3, scalars=0)[0]
 
 
-def extract(who, anchor, state, right, left, bands, sects):
-    _, rows, cols = state.shape
+def extract(who, anchor, turned, right, left, pick, bands, sects):
+    rows, deep, cols = turned.shape
     padded = right.shape[0]
-    deep = -(-padded // 16) * 16
     width = cols + LANES
     batch = 4 if bands % 4 == 0 else bands
     chunk = 4
 
-    def body(who_ref, at_ref, state_ref, right_ref, left_ref,
-             keep_ref, send_ref, top_ref, low_ref, flat, ext, picked):
+    def body(who_ref, at_ref, rows_ref, right_ref, left_ref, pick_ref,
+             keep_ref, send_ref, top_ref, low_ref, ext, picked):
         lane = lane_index((padded, LANES))
         ext[:, padded:, :] = jnp.zeros((rows, deep - padded, width), HALF)
-        ext[:, :, :cols] = turn_rows(state_ref, flat)
+        ext[:, :, :cols] = rows_ref[...]
         rim = left_ref[...]
         none = jnp.zeros((padded, LANES), HALF)
         for r in range(rows):
@@ -184,22 +203,12 @@
         top_ref[...] = ext[:2]
         low_ref[...] = ext[rows - 2 :]
         for first in range(0, bands, batch):
-            picks = []
-            for j in range(first, first + batch):
-                col0 = slot_at(who_ref, at_ref, j, sects, rows, cols)[1] - 2
-                source = lax.broadcasted_iota(jnp.int32, (width, LANES), 0)
-                target = lane_index((width, LANES))
-                inner = target
-                for m in range(1, PER_TILE):
-                    inner = jnp.where(target >= WIDE * m, target - WIDE * m, inner)
-                want = jnp.bitwise_and(inner + col0, width - 1)
-                picks.append(jnp.where(source == want, 1.0, 0.0).astype(HALF))
-            pick = jnp.concatenate(picks, axis=1)
-
-            def select(c, carry):
+            chosen = slice(first * LANES, (first + batch) * LANES)
+
+            def select(c, carry, chosen=chosen):
                 view = ext[pl.ds(c * chunk, chunk)].reshape(chunk * deep, width)
                 picked[pl.ds(c * chunk, chunk)] = jnp.dot(
-                    view, pick, preferred_element_type=FULL
+                    view, pick_ref[:, chosen], preferred_element_type=FULL
                 ).reshape(chunk, deep, batch * LANES)
                 return carry
 
@@ -232,8 +241,8 @@
     return run(
         body,
         [part, part, edge, edge],
-        [who, anchor, state, right, left],
-        [pltpu.VMEM((deep, rows, cols), HALF), pltpu.VMEM((rows, deep, width), HALF), pltpu.VMEM((rows, deep, batch * LANES), FULL)],
+        [who, anchor, turned, right, left, pick],
+        [pltpu.VMEM((rows, deep, width), HALF), pltpu.VMEM((rows, deep, batch * LANES), FULL)],
         micros=3.0,
         scalars=2,
     )
@@ -268,7 +277,7 @@
         who_ref, at_ref = refs[:2]
         parts = refs[2 : 2 + len(addends)]
         mine = who_ref[0] * sects + who_ref[1]
-        row0, col0 = at_ref[mine, 0], at_ref[mine, 1]
+        row0, col0 = at_ref[0, mine], at_ref[1, mine]
         (noise_ref, w_in, w_out, d_in, d_out, b_in, b_out, b_step, b_den, out_ref,
          flat, state_sh, hid, hid_sh, pad, pad_sh, corr, state) = refs[2 + len(addends) :]
         for t in range(TILES):
@@ -368,12 +377,54 @@
     )[0]
 
 
-def grid_mean(who, state, right, left, rim, lower, weights, biases, limits):
-    _, rows, cols = state.shape
-    padded = right.shape[0]
-    deep = -(-padded // 16) * 16
-    width = cols + LANES
+def spread(turned, right, left):
+    rows, _, cols = turned.shape
     span = right.shape[1]
+    loose = cols + 16
+
+    def body(rows_ref, right_ref, left_ref, out_ref, after, before, line):
+        def upright(value):
+            value = value.astype(FULL)
+            return jnp.concatenate(
+                [value, jnp.zeros((LANES - value.shape[0], value.shape[1]), FULL)], axis=0
+            ).T
+
+        for t in range(span // LANES):
+            lanes = slice(t * LANES, (t + 1) * LANES)
+            after[lanes] = upright(right_ref[:, lanes])
+        before[...] = upright(left_ref[...])
+        line[...] = jnp.zeros(line.shape, FULL)
+
+        def spread_rows(i, carry):
+            for v in range(2):
+                r = 2 * i + v
+                line[v, 8 : 8 + cols] = upright(rows_ref[r])
+                line[v, 8 + cols : 10 + cols] = after[pl.ds(r * REACH, 2)]
+                line[v, 6:8] = before[pl.ds(2 * r, 2)]
+                for b in range(3):
+                    out_ref[b, i, v] = line[v, 6 + b : 6 + b + loose, :].astype(HALF)
+            return carry
+
+        lax.fori_loop(0, rows // 2, spread_rows, 0)
+
+    return run(
+        body,
+        [like((3, rows // 2, 2, loose, LANES))],
+        [turned, right, left],
+        [
+            pltpu.VMEM((span, LANES), FULL),
+            pltpu.VMEM((LANES, LANES), FULL),
+            pltpu.VMEM((2, loose + 8, LANES), FULL),
+        ],
+        micros=2.5,
+        scalars=0,
+    )[0]
+
+
+def grid_mean(who, shifted, rim, lower, padded, weights, biases, limits):
+    rows = 2 * shifted.shape[1]
+    _, deep, width = rim.shape
+    cols = width - LANES
     loose = cols + 16
     made = rows // 2
     pairs_in, pairs_out = made // 4 + 1, made // 4
@@ -383,52 +434,29 @@
     state_pairs = hidden_pairs + 1
     base = rows - made - 2 if lower else -2
 
-    def body(who_ref, state_ref, right_ref, left_ref, rim_ref, w_in, w_out, b_in, b_out, out_ref,
-             flat, turned, after, before, line, state_sh, hid, hid_sh):
+    def body(who_ref, shifted_ref, rim_ref, w_in, w_out, b_in, b_out, out_ref,
+             line, state_sh, hid, hid_sh):
         row0 = who_ref[0] * rows + base + 1
         col0 = who_ref[1] * cols - 1
-
-        turned[:, :deep] = turn_rows(state_ref, flat)
-        turned[:, deep:] = jnp.zeros((rows, LANES - deep, cols), HALF)
-
-        def upright(value):
-            value = value.astype(FULL)
-            return jnp.concatenate(
-                [value, jnp.zeros((LANES - value.shape[0], value.shape[1]), FULL)], axis=0
-            ).T
-
-        for t in range(span // LANES):
-            lanes = slice(t * LANES, (t + 1) * LANES)
-            after[lanes] = upright(right_ref[:, lanes])
-        before[...] = upright(left_ref[...])
-        line[...] = jnp.zeros(line.shape, FULL)
-
-        def shift(i, v):
-            for b in range(3):
-                state_sh[b, i, v] = line[v, 6 + b : 6 + b + loose, :].astype(HALF)
 
         for pair in range(made // 2 + 2, state_pairs):
             for b in range(3):
                 state_sh[b, pair] = jnp.zeros((2, loose, LANES), HALF)
         edge = made // 2 + 1 if lower else 0
+        skip = 0 if lower else 1
+        given = made // 2 + 1
+        at = (rows - made) // 2 - 1 if lower else 0
+        for b in range(3):
+            state_sh[b, skip : skip + given] = shifted_ref[b, at : at + given]
         for v in range(2):
-            value = upright(rim_ref[v])
+            value = jnp.concatenate(
+                [rim_ref[v].astype(FULL), jnp.zeros((LANES - deep, width), FULL)], axis=0
+            ).T
             line[v, 8 : 8 + cols] = value[:cols]
             line[v, 8 + cols :] = value[cols : cols + 16]
             line[v, :8] = value[width - 8 :]
-            shift(edge, v)
-        skip = 0 if lower else 1
-
-        def spread_rows(i, carry):
-            for v in range(2):
-                r = 2 * (i + skip) + v + base
-                line[v, 8 : 8 + cols] = turned[r].astype(FULL).T
-                line[v, 8 + cols : 10 + cols] = after[pl.ds(r * REACH, 2)]
-                line[v, 6:8] = before[pl.ds(2 * r, 2)]
-                shift(i + skip, v)
-            return carry
-
-        lax.fori_loop(0, made // 2 + 1, spread_rows, 0)
+            for b in range(3):
+                state_sh[b, edge, v] = line[v, 6 + b : 6 + b + loose, :].astype(HALF)
 
         def first(chunk, carry):
             start = chunk * pairs_in
@@ -468,86 +496,59 @@
     return run(
         body,
         [like((made, padded, cols))],
-        [who, state, right, left, rim, *weights, *biases],
+        [who, shifted, rim, *weights, *biases],
         [
-            pltpu.VMEM((deep, rows, cols), HALF),
-            pltpu.VMEM((rows, LANES, cols), HALF),
-            pltpu.VMEM((span, LANES), FULL),
-            pltpu.VMEM((LANES, LANES), FULL),
             pltpu.VMEM((2, loose + 8, LANES), FULL),
             pltpu.VMEM((3, state_pairs, 2, loose, LANES), HALF),
             pltpu.VMEM((pairs_in, 2, loose, LANES), FULL),
             pltpu.VMEM((3, hidden_pairs, 2, cols, LANES), HALF),
         ],
-        micros=5.0,
+        micros=3.5,
     )[0]
 
 
-def spill(who, anchor, pieces, sources, sects, rows, cols):
+def canvas(who, anchor, pieces, sources, place, sects, rows, cols):
     padded = pieces[0].shape[-2]
+    deep = -(-padded // 16) * 16
+    total = anchor.shape[1]
+    slots = len(pieces)
+    tile_rows = LANES // SIDE
+    groups = rows // tile_rows
 
     def body(who_ref, at_ref, *refs):
-        out_ref, total = refs[-2:]
-        lane = lane_index((padded, LANES))
+        place_ref, spill_ref, out_ref, inverse_ref, view = refs[slots:]
         none = jnp.zeros((padded, LANES), HALF)
-        total[...] = jnp.zeros(total.shape, FULL)
         for piece, j in zip(refs, sources):
-            row0, col0 = slot_at(who_ref, at_ref, j, sects, rows, cols)
-
-            @pl.when(col0 > cols - SIDE)
-            def _(piece=piece, row0=row0, col0=col0):
-                def one(r, carry):
-                    i = r - row0
-                    source = pl.multiple_of((i // 4) * LANES, LANES)
-                    target = pl.multiple_of((r // 4) * LANES, LANES)
-                    low = SIDE * (r % 4)
-                    turn = jnp.bitwise_and(low - SIDE * (i % 4) + col0 - cols, LANES - 1)
-                    value = pltpu.roll(piece[:, pl.ds(source, LANES)], turn, 1)
-                    keep = (lane >= low) & (lane < low + col0 - (cols - SIDE))
-                    total[:, pl.ds(target, LANES)] += jnp.where(keep, value, none).astype(FULL)
-                    return carry
-
-                lax.fori_loop(jnp.maximum(row0, 0), jnp.minimum(row0 + SIDE, rows), one, 0)
-
-        out_ref[...] = total[...].astype(HALF)
-
-    shape = (padded, rows * SIDE)
-    return run(
-        body, [like(shape)], [who, anchor, *pieces], [pltpu.VMEM(shape, FULL)],
-        micros=1.5, scalars=2,
-    )[0]
-
-
-def canvas(who, anchor, pieces, sources, sects, rows, cols):
-    padded = pieces[0].shape[-2]
-    total = anchor.shape[0]
-
-    def body(who_ref, at_ref, *refs):
-        out_ref, inverse_ref = refs[-2:]
-        lane = lane_index((padded, LANES))
-        none = jnp.zeros((padded, LANES), HALF)
-        out_ref[...] = jnp.zeros(out_ref.shape, FULL)
-        for piece, j in zip(refs, sources):
-            row0, col0 = slot_at(who_ref, at_ref, j, sects, rows, cols)
-
-            def one(k, carry, piece=piece, row0=row0, col0=col0):
-                value = piece[:, pl.ds(pl.multiple_of(k * LANES, LANES), LANES)]
-                for m in range(4):
-                    r = row0 + 4 * k + m
-                    low = jnp.where((r >= 0) & (r < rows), col0, 2 * LANES)
-                    moved = pltpu.roll(value, jnp.bitwise_and(col0 - SIDE * m, LANES - 1), 1)
-                    keep = (lane >= low) & (lane < col0 + SIDE)
-                    out_ref[jnp.clip(r, 0, rows - 1)] += jnp.where(keep, moved, none).astype(FULL)
-                return carry
-
-            start = jnp.clip(-row0, 0, SIDE) // 4
-            stop = (jnp.clip(rows - row0, 0, SIDE) + 3) // 4
-            lax.fori_loop(start, stop, one, 0)
+            lanes = slice(j * LANES, (j + 1) * LANES)
+            row0 = slot_at(who_ref, at_ref, j, sects, rows, cols)[0]
+            for r in range(rows):
+                i = r - row0
+                tile = jnp.clip(jnp.right_shift(i, tile_rows.bit_length() - 1), 0, SIDE // tile_rows - 1)
+                value = piece[:, pl.ds(pl.multiple_of(tile * LANES, LANES), LANES)]
+                inside = (i >= 0) & (i < SIDE)
+                view[r % tile_rows, r // tile_rows, :padded, lanes] = jnp.where(
+                    inside, value, none
+                )
+        view[:, :, padded:, :] = jnp.zeros(
+            (tile_rows, groups, deep - padded, slots * LANES), HALF
+        )
+        spilled = None
+        for m in range(tile_rows):
+            value = jnp.dot(
+                view[m].reshape(groups * deep, slots * LANES), place_ref[m],
+                preferred_element_type=FULL,
+            ).reshape(groups, deep, 2 * LANES)
+            for k in range(groups):
+                out_ref[k * tile_rows + m] = value[k, :padded, :LANES]
+            part = value[:, :padded, LANES:]
+            spilled = part if spilled is None else spilled + part
+        for k in range(groups):
+            spill_ref[:, k * LANES : (k + 1) * LANES] = spilled[k].astype(HALF)
         row = lax.broadcasted_iota(jnp.int32, (rows, cols), 0) + who_ref[0] * rows
         col = lane_index((rows, cols)) + who_ref[1] * cols
 
         def cover(p, count):
-            down, across = row - at_ref[p, 0], col - at_ref[p, 1]
+            down, across = row - at_ref[0, p], col - at_ref[1, p]
             hit = (down >= 0) & (down < SIDE) & (across >= 0) & (across < SIDE)
             return count + jnp.where(hit, 1.0, 0.0)
 
@@ -555,8 +556,16 @@
         inverse_ref[...] = 1.0 / jnp.maximum(count, 1.0)
 
     return run(
-        body, [like((rows, padded, cols), FULL), like((rows, cols), FULL)],
-        [who, anchor, *pieces], [], micros=2.5, scalars=2,
+        body,
+        [
+            like((padded, rows * SIDE)),
+            like((rows, padded, cols), FULL),
+            like((rows, cols), FULL),
+        ],
+        [who, anchor, *pieces, place],
+        [pltpu.VMEM((tile_rows, groups, deep, slots * LANES), HALF)],
+        micros=1.5,
+        scalars=2,
     )
 
 
@@ -609,11 +618,15 @@
     limits = (rows * bands, cols * sects)
     who = jnp.stack([lax.axis_index("band"), lax.axis_index("sect")]).astype(jnp.int32)
 
-    right_rim, left_rim = pack(who, patch_anchor, state_field)
+    anchor = patch_anchor.T
+
+    right_rim, left_rim, turned = pack(who, anchor, state_field)
     right = shift_from(right_rim, "sect", -1)
     left = shift_from(left_rim, "sect", 1)
 
-    made, lines, noise = prep(
+    made, lines, noise, pick, place = prep(
+        who,
+        anchor,
         [
             conv_in_weight.transpose(0, 2, 1),
             conv_out_weight,
@@ -622,10 +635,14 @@
         ],
         [conv_in_bias[None, :], conv_out_bias[None, :], denoise_bias[None, :], step_bias],
         patch_noise[0],
+        bands,
+        sects,
+        rows,
+        cols,
     )
     biases, step_lines = lines[:3], lines[3]
 
-    kept, sent, top, low = extract(who, patch_anchor, state_field, right, left, bands, sects)
+    kept, sent, top, low = extract(who, anchor, turned, right, left, pick, bands, sects)
     got = swap(sent, "band", 1)
     addends = [kept, got]
     bit = 2
@@ -637,9 +654,7 @@
         bit *= 2
     above = shift_from(low, "band", 1)
     below = shift_from(top, "band", -1)
-    correction = patch_step(
-        who, patch_anchor, addends, noise, made, biases, step_lines, sects, limits
-    )
+    correction = patch_step(who, anchor, addends, noise, made, biases, step_lines, sects, limits)
     pieces = [correction]
     sources = [0]
     bit = bands // 2
@@ -651,16 +666,14 @@
         sources += [s ^ bit for s in sources]
         bit //= 2
 
-    def grid(lower, rim):
-        return grid_mean(
-            who, state_field, right, left, rim, lower, made[:2], biases[:2], limits
-        )
-
-    top_mean = grid(False, above)
-    low_mean = grid(True, below)
-    spilled = spill(who, patch_anchor, pieces, sources, sects, rows, cols)
+    shifted = spread(turned, right, left)
+    padded = right.shape[0]
+    top_mean = grid_mean(who, shifted, above, False, padded, made[:2], biases[:2], limits)
+    low_mean = grid_mean(who, shifted, below, True, padded, made[:2], biases[:2], limits)
+    spilled, summed, inverse = canvas(
+        who, anchor, pieces, sources, place, sects, rows, cols
+    )
     arrived = shift_from(spilled, "sect", 1)
-    summed, inverse = canvas(who, patch_anchor, pieces, sources, sects, rows, cols)
     return finish([top_mean, low_mean], summed, arrived, inverse, channels)
 
 

time: 63.1 us -> 59.3 us (0.940)
  Pallas kernels: 30.2 us -> 27.4 us
    ppermute x5, waiting for transfers between devices: 9.45 us -> 4.82 us  [shift_from(): return lax.ppermute(block, axis, route)]
    ppermute x5, waiting for transfers between devices: 6.1 us -> 10.7 us  [swap(): return lax.ppermute(block, axis, [(i, i ^ bit) for i in range(count)])]
    pallas_call x10, Pallas kernels: 30.2 us -> 27.4 us  [run(): pl.pallas_call(body, out_shape=outs, in_specs=[smem] * scalars + [vmem] *...]
    unnamed x24 -> x25, local copies, waits for them, and re-layouts: 2.04 us -> 1.94 us
  transfers between devices with their start and end apart: 10 -> 10, of which waited for: 6 -> 6; matrix products, arithmetic and copies ran while one was open for 0% -> 0% of each run, Pallas kernels for 32% -> 34%
where the time goes in v2:
time: 59.3 us; the launch traced here: 58.8 us
  Pallas kernels  27.4 us (46%)
  waiting for transfers between devices  15.5 us (26%)
  starting transfers between devices  13.6 us (23%)
  local copies, waits for them, and re-layouts  1.94 us (3%)
    pallas_call x10, Pallas kernels, run(): pl.pallas_call(body, out_shape=outs, in_specs=[smem] * scalars + [vmem] *...  27.4 us
    ppermute x5, starting transfers between devices, shift_from(): return lax.ppermute(block, axis, route)  13.2 us
    ppermute x5, waiting for transfers between devices, swap(): return lax.ppermute(block, axis, [(i, i ^ bit) for i in range(count)])  10.7 us
    ppermute x5, waiting for transfers between devices, shift_from(): return lax.ppermute(block, axis, route)  4.82 us
    unnamed x25, local copies, waits for them, and re-layouts  1.94 us
  transfers between devices with their start and end apart: 10, of which 6 were waited for; matrix products, arithmetic and copies ran while one was open for 0% of the time, Pallas kernels for 34%

profile of v2, /device:TPU:18, one launch (start us, length us, event | category | flops | bytes accessed | tf_op | source)
XLA Modules:
  0.0 58.8 jit_solution(4966355076871352814)
XLA Ops:
  0.0 0.0 copy-start.8
  0.0 0.0 copy-start.9
  0.0 0.0 copy-start.5
  0.0 0.1 pad_add_fusion.who_ref.refs_0_
  0.1 1.1 %copy-done = bf16[99,32,128]{2,1,0:T(8,128)(2,1)S(1)} copy-done((bf16[99,32,128]{2,1,0:T(8,128)(2,1)S(1)}, bf16[99,32,128]{2,1,0:T(8,128)(2,1)}, u32[]{:S(2)}) %copy-start) | copy-done | bytes 811032
  1.2 0.7 %copy-done.6 = s32[16,2]{0,1:T(2,128)S(1)} copy-done((s32[16,2]{0,1:T(2,128)S(1)}, s32[16,2]{0,1:T(2,128)}, u32[]{:S(2)}) %copy-start.6) | copy-done | bytes 152
  1.9 0.0 copy-start.4
  1.9 1.3 %shard_map.109 = (bf16[104,1152]{1,0:T(8,128)(2,1)S(1)}, bf16[104,128]{1,0:T(8,128)(2,1)S(1)}, bf16[32,112,128]{2,1,0:T(8,128)(2,1)S(1)}) custom-call(s32[2]{0:T(128)S(1)} %pad_add_fusion.who_ref.refs_0_, s32[2,16]{1,0:T(2,128)S(1)} %bitcast.14, bf16[99,32,128]{2,1,0:T(8,128)(2,1)S(1)} %copy-done), custom_call_target="tpu_custom_call" | custom-call | flops 1150000000 | bytes 1024 | tf_op jit(solution)/shard_map/pallas_call | solution.py:34
  3.3 2.4 %collective-permute-start = (bf16[104,1152]{1,0:T(8,128)(2,1)S(1)}, bf16[104,1152]{1,0:T(8,128)(2,1)S(1)}, u32[]{:S(2)}, u32[]{:S(2)}) collective-permute-start(bf16[104,1152]{1,0:T(8,128)(2,1)S(1)} %get-tuple-element.27), channel_id=1, source_target_pairs={{1,0},{2,1},{3,2},{5,4},{6,5},{7,6},{9,8},{10,9},{11,10},{13,12},{... | collective-permute-start | bytes 718856 | tf_op jit(solution)/shard_map/ppermute | solution.py:23
  5.6 3.5 %collective-permute-start.1 = (bf16[104,128]{1,0:T(8,128)(2,1)S(1)}, bf16[104,128]{1,0:T(8,128)(2,1)S(1)}, u32[]{:S(2)}, u32[]{:S(2)}) collective-permute-start(bf16[104,128]{1,0:T(8,128)(2,1)S(1)} %get-tuple-element.28), channel_id=1, source_target_pairs={{0,1},{1,2},{2,3},{4,5},{5,6},{6,7},{8,9},{9,10},{10,11},{12,13},{... | collective-permute-start | bytes 79880 | tf_op jit(solution)/shard_map/ppermute | solution.py:23
  9.1 0.0 copy-done.11
  9.1 0.1 copy.14
  9.2 0.0 copy-done.8
  9.2 0.0 copy-done.9
  9.2 0.0 copy-done.10
  9.3 0.0 copy-done.5
  9.3 0.0 copy-done.1
  9.3 0.0 copy-done.2
  9.3 0.0 copy-done.3
  9.3 0.0 copy-done.4
  9.3 2.0 %shard_map.111 = (bf16[1536,256]{1,0:T(8,128)(2,1)S(1)}, bf16[256,1536]{1,0:T(8,128)(2,1)S(1)}, bf16[1536,256]{1,0:T(8,128)(2,1)S(1)}, bf16[256,1536]{1,0:T(8,12...) custom-call(s32[2]{0:T(128)S(1)} %pad_add_fusion.who_ref.refs_0_, ...), custom_call_target="tpu_custom_call" | custom-call | flops 2875000064 | bytes 1024 | tf_op jit(solution)/shard_map/pallas_call | solution.py:34
  11.3 0.1 collective-permute-done.1.left_ref
  11.4 1.3 %collective-permute-done.right_ref = bf16[104,1152]{1,0:T(8,128)(2,1)S(1)} collective-permute-done((bf16[104,1152]{1,0:T(8,128)(2,1)S(1)}, bf16[104,1152]{1,0:T(8,128)(2,1)S(1)}, u32[]{:S(2)}, u32[]{:S(2)}) %collective-permute-start) | collective-permute-done | bytes 239648 | tf_op jit(solution)/shard_map/ppermute | solution.py:23
  12.7 4.3 %shard_map.112 = (bf16[2,104,1536]{2,1,0:T(8,128)(2,1)S(1)}, bf16[2,104,1536]{2,1,0:T(8,128)(2,1)S(1)}, bf16[2,112,256]{2,1,0:T(8,128)(2,1)S(1)}, bf16[2,112,256]{2,1,0:T(8,128)(2,1)S(1)}) custom-call(s32[2]{0:T(128)S(1)} %pad_add_fusion.who_ref.refs_0_, s32[2,16]{1,0:T(2,128)S(1)} %bitcast.16, bf16[32,112,128]{2,1,0:T(8,128)(2,1)S(1)} %get-tuple-element.26.rows_ref, ...), custom_call_target="tpu_custom_call" | custom-call | flops 3449999872 | bytes 1024 | tf_op jit(solution)/shard_map/pallas_call | solution.py:34
  17.0 0.1 collective-permute-start.4
  17.1 2.1 %collective-permute-done.4.got_ref.refs_3_ = bf16[2,104,1536]{2,1,0:T(8,128)(2,1)S(1)} collective-permute-done((bf16[2,104,1536]{2,1,0:T(8,128)(2,1)S(1)}, bf16[2,104,1536]{2,1,0:T(8,128)(2,1)S(1)}, u32[]{:S(2)}, u32[]{:S(2)}) %collective-permute-start.4) | collective-permute-done | bytes 639008 | tf_op jit(solution)/shard_map/ppermute | solution.py:28
  19.2 0.1 collective-permute-start.5
  19.3 3.3 %collective-permute-start.3 = (bf16[2,112,256]{2,1,0:T(8,128)(2,1)S(1)}, bf16[2,112,256]{2,1,0:T(8,128)(2,1)S(1)}, u32[]{:S(2)}, u32[]{:S(2)}) collective-permute-start(bf16[2,112,256]{2,1,0:T(8,128)(2,1)S(1)} %get-tuple-element.35), channel_id=1, source_target_pairs={{4,0},{8,4},{12,8},{5,1},{9,5},{13,9},{6,2},{10,6},{14,10},{7,3},{... | collective-permute-start | bytes 344072 | tf_op jit(solution)/shard_map/ppermute | solution.py:23
  22.6 1.9 %collective-permute-start.2 = (bf16[2,112,256]{2,1,0:T(8,128)(2,1)S(1)}, bf16[2,112,256]{2,1,0:T(8,128)(2,1)S(1)}, u32[]{:S(2)}, u32[]{:S(2)}) collective-permute-start(bf16[2,112,256]{2,1,0:T(8,128)(2,1)S(1)} %get-tuple-element.30), channel_id=1, source_target_pairs={{0,4},{4,8},{8,12},{1,5},{5,9},{9,13},{2,6},{6,10},{10,14},{3,7},{... | collective-permute-start | bytes 344072 | tf_op jit(solution)/shard_map/ppermute | solution.py:23
  24.6 5.1 %collective-permute-done.5.refs_4_ = bf16[1,104,1536]{2,1,0:T(8,128)(2,1)S(1)} collective-permute-done((bf16[1,104,1536]{2,1,0:T(8,128)(2,1)S(1)}, bf16[1,104,1536]{2,1,0:T(8,128)(2,1)S(1)}, u32[]{:S(2)}, u32[]{:S(2)}) %collective-permute-start.5) | collective-permute-done | bytes 319520 | tf_op jit(solution)/shard_map/ppermute | solution.py:28
  29.7 5.8 %shard_map.116.refs_0_ = bf16[104,1024]{1,0:T(8,128)(2,1)S(1)} custom-call(s32[2]{0:T(128)S(1)} %pad_add_fusion.who_ref.refs_0_, s32[2,16]{1,0:T(2,128)S(1)} %bitcast.17, bf16[2,104,1536]{2,1,0:T(8,128)(2,1)S(1)} %get-tuple-element.36.kept_ref.refs_2_, bf16[2,104,1536]{2,1,0:T(8,128)(2,1)S(1)} %collective-permute-done.4.got_ref.refs_3_, ...), custom_call_target="tpu_custom_call" | custom-call | flops 9200000000 | bytes 1024 | tf_op jit(solution)/shard_map/pallas_call | solution.py:34
  35.4 0.1 collective-permute-start.6
  35.5 2.2 %shard_map.110.shifted_ref = bf16[3,16,2,144,128]{4,3,2,1,0:T(8,128)(2,1)S(1)} custom-call(bf16[32,112,128]{2,1,0:T(8,128)(2,1)S(1)} %get-tuple-element.26.rows_ref, bf16[104,1152]{1,0:T(8,128)(2,1)S(1)} %collective-permute-done.right_ref, bf16[104,128]{1,0:T(8,128)(2,1)S(1)} %collective-permute-done.1.left_ref), custom_call_target="tpu_custom_call" | custom-call | flops 2875000064 | bytes 1024 | tf_op jit(solution)/shard_map/pallas_call | solution.py:34
  37.7 0.0 copy-start.7
  37.7 0.1 collective-permute-start.7
  37.8 3.6 %collective-permute-done.6.refs_1_ = bf16[104,1024]{1,0:T(8,128)(2,1)S(1)} collective-permute-done((bf16[104,1024]{1,0:T(8,128)(2,1)S(1)}, bf16[104,1024]{1,0:T(8,128)(2,1)S(1)}, u32[]{:S(2)}, u32[]{:S(2)}) %collective-permute-start.6) | collective-permute-done | bytes 213024 | tf_op jit(solution)/shard_map/ppermute | solution.py:28
  41.4 0.0 collective-permute-start.8
  41.4 0.0 collective-permute-done.3.rim_ref
  41.4 4.0 %shard_map.114.low_ref = bf16[16,104,128]{2,1,0:T(8,128)(2,1)S(1)} custom-call(s32[2]{0:T(128)S(1)} %pad_add_fusion.who_ref.refs_0_, bf16[3,16,2,144,128]{4,3,2,1,0:T(8,128)(2,1)S(1)} %shard_map.110.shifted_ref, bf16[2,112,256]{2,1,0:T(8,128)(2,1)S(1)} %collective-permute-done.3.rim_ref, bf16[1536,256]{1,0:T(8,128)(2,1)S(1)} %get-tuple-element.31.w_in.refs_6_, ...), custom_call_target="tpu_custom_call" | custom-call | flops 4024999936 | bytes 1024 | tf_op jit(solution)/shard_map/pallas_call | solution.py:34
  45.4 0.0 collective-permute-done.7.refs_2_
  45.4 0.0 collective-permute-done.8.refs_3_
  45.4 0.0 copy-done.7
  45.4 2.1 %shard_map.117 = (bf16[104,1024]{1,0:T(8,128)(2,1)S(1)}, f32[32,104,128]{2,1,0:T(8,128)S(1)}, f32[32,128]{1,0:T(8,128)S(1)}) custom-call(s32[2]{0:T(128)S(1)} %pad_add_fusion.who_ref.refs_0_, s32[2,16]{1,0:T(2,128)S(1)} %bitcast.18, bf16[104,1024]{1,0:T(8,128)(2,1)S(1)} %shard_map.116.refs_0_, bf16[104,1024]{1,0:T(8,128)(2,1)S(1)} %collective-permute-done.6.refs_1_, ...), custom_call_target="tpu_custom_call" | custom-call | flops 1724999936 | bytes 1024 | tf_op jit(solution)/shard_map/pallas_call | solution.py:34
  47.5 2.2 %collective-permute-start.9 = (bf16[104,1024]{1,0:T(8,128)(2,1)S(1)}, bf16[104,1024]{1,0:T(8,128)(2,1)S(1)}, u32[]{:S(2)}, u32[]{:S(2)}) collective-permute-start(bf16[104,1024]{1,0:T(8,128)(2,1)S(1)} %get-tuple-element.45), channel_id=1, source_target_pairs={{0,1},{1,2},{2,3},{4,5},{5,6},{6,7},{8,9},{9,10},{10,11},{12,13},{... | collective-permute-start | bytes 638984 | tf_op jit(solution)/shard_map/ppermute | solution.py:23
  49.7 0.0 collective-permute-done.2.rim_ref
  49.7 4.0 %shard_map.113.top_ref = bf16[16,104,128]{2,1,0:T(8,128)(2,1)S(1)} custom-call(s32[2]{0:T(128)S(1)} %pad_add_fusion.who_ref.refs_0_, bf16[3,16,2,144,128]{4,3,2,1,0:T(8,128)(2,1)S(1)} %shard_map.110.shifted_ref, bf16[2,112,256]{2,1,0:T(8,128)(2,1)S(1)} %collective-permute-done.2.rim_ref, bf16[1536,256]{1,0:T(8,128)(2,1)S(1)} %get-tuple-element.31.w_in.refs_6_, ...), custom_call_target="tpu_custom_call" | custom-call | flops 4024999936 | bytes 1024 | tf_op jit(solution)/shard_map/pallas_call | solution.py:34
  53.7 3.4 %collective-permute-done.9.spill_ref = bf16[104,1024]{1,0:T(8,128)(2,1)S(1)} collective-permute-done((bf16[104,1024]{1,0:T(8,128)(2,1)S(1)}, bf16[104,1024]{1,0:T(8,128)(2,1)S(1)}, u32[]{:S(2)}, u32[]{:S(2)}) %collective-permute-start.9) | collective-permute-done | bytes 213024 | tf_op jit(solution)/shard_map/ppermute | solution.py:23
  57.1 1.6 %shard_map.118 = bf16[99,32,128]{2,1,0:T(8,128)(2,1)} custom-call(bf16[16,104,128]{2,1,0:T(8,128)(2,1)S(1)} %shard_map.113.top_ref, bf16[16,104,128]{2,1,0:T(8,128)(2,1)S(1)} %shard_map.114.low_ref, f32[32,104,128]{2,1,0:T(8,128)S(1)} %get-tuple-element.44.sum_ref, bf16[104,1024]{1,0:T(8,128)(2,1)S(1)} %collective-permute-done.9.spill_ref, ...), custom_call_target="tpu_custom_call" | custom-call | flops 3449999872 | bytes 1024 | tf_op jit(solution)/shard_map/pallas_call | solution.py:34
  (8 shorter events, 0.1 us)
Async XLA Ops:
  0.0 9.2 %copy-start.8 = (f32[128]{0:T(128)S(1)}, f32[128]{0:T(128)}, u32[]{:S(2)}) copy-start(f32[128]{0:T(128)} %param.13) | copy-start | bytes 1540
  0.0 9.2 %copy-start.9 = (f32[99]{0:T(128)S(1)}, f32[99]{0:T(128)}, u32[]{:S(2)}) copy-start(f32[99]{0:T(128)} %param.15) | copy-start | bytes 1192
  0.0 9.2 %copy-start.10 = (f32[99]{0:T(128)S(1)}, f32[99]{0:T(128)}, u32[]{:S(2)}) copy-start(f32[99]{0:T(128)} %param.21) | copy-start | bytes 1192
  0.0 9.2 %copy-start.5 = (f32[2,128]{1,0:T(2,128)S(1)}, f32[2,128]{1,0:T(2,128)}, u32[]{:S(2)}) copy-start(f32[2,128]{1,0:T(2,128)} %refs_7_.1) | copy-start | bytes 3076
  0.1 1.1 %copy-start = (bf16[99,32,128]{2,1,0:T(8,128)(2,1)S(1)}, bf16[99,32,128]{2,1,0:T(8,128)(2,1)}, u32[]{:S(2)}) copy-start(bf16[99,32,128]{2,1,0:T(8,128)(2,1)} %state_ref.1) | copy-start | bytes 2433028
  1.2 0.7 %copy-start.6 = (s32[16,2]{0,1:T(2,128)S(1)}, s32[16,2]{0,1:T(2,128)}, u32[]{:S(2)}) copy-start(s32[16,2]{0,1:T(2,128)} %param.16) | copy-start | bytes 388
  1.9 7.2 %copy-start.11 = (bf16[1,2,99,1024]{3,1,2,0:T(2,128)(2,1)S(1)}, bf16[1,2,99,1024]{3,1,2,0:T(2,128)(2,1)}, u32[]{:S(2)}) copy-start(bf16[1,2,99,1024]{3,1,2,0:T(2,128)(2,1)} %param.17) | copy-start | bytes 1216516
  1.9 7.3 %copy-start.1 = (bf16[9,128,99]{1,2,0:T(8,128)(2,1)S(1)}, bf16[9,128,99]{1,2,0:T(8,128)(2,1)}, u32[]{:S(2)}) copy-start(bf16[9,128,99]{1,2,0:T(8,128)(2,1)} %param.12) | copy-start | bytes 684292
  1.9 7.4 %copy-start.2 = (bf16[9,99,128]{2,1,0:T(8,128)(2,1)S(1)}, bf16[9,99,128]{2,1,0:T(8,128)(2,1)}, u32[]{:S(2)}) copy-start(bf16[9,99,128]{2,1,0:T(8,128)(2,1)} %refs_1_.1) | copy-start | bytes 684292
  1.9 7.4 %copy-start.3 = (bf16[9,128,99]{1,2,0:T(8,128)(2,1)S(1)}, bf16[9,128,99]{1,2,0:T(8,128)(2,1)}, u32[]{:S(2)}) copy-start(bf16[9,128,99]{1,2,0:T(8,128)(2,1)} %param.18) | copy-start | bytes 684292
  1.9 7.4 %copy-start.4 = (bf16[9,99,128]{2,1,0:T(8,128)(2,1)S(1)}, bf16[9,99,128]{2,1,0:T(8,128)(2,1)}, u32[]{:S(2)}) copy-start(bf16[9,99,128]{2,1,0:T(8,128)(2,1)} %refs_3_.1) | copy-start | bytes 684292
  3.3 9.5 %collective-permute-start = (bf16[104,1152]{1,0:T(8,128)(2,1)S(1)}, bf16[104,1152]{1,0:T(8,128)(2,1)S(1)}, u32[]{:S(2)}, u32[]{:S(2)}) collective-permute-start(bf16[104,1152]{1,0:T(8,128)(2,1)S(1)} %get-tuple-element.27), channel_id=1, source_target_pairs={{1,0},{2,1},{3,2},{5,4},{6,5},{7,6},{9,8},{10,9},{11,10},{13,12},{... | collective-permute-start | bytes 718856 | tf_op jit(solution)/shard_map/ppermute | solution.py:23
  5.6 5.7 %collective-permute-start.1 = (bf16[104,128]{1,0:T(8,128)(2,1)S(1)}, bf16[104,128]{1,0:T(8,128)(2,1)S(1)}, u32[]{:S(2)}, u32[]{:S(2)}) collective-permute-start(bf16[104,128]{1,0:T(8,128)(2,1)S(1)} %get-tuple-element.28), channel_id=1, source_target_pairs={{0,1},{1,2},{2,3},{4,5},{5,6},{6,7},{8,9},{9,10},{10,11},{12,13},{... | collective-permute-start | bytes 79880 | tf_op jit(solution)/shard_map/ppermute | solution.py:23
  17.0 2.1 %collective-permute-start.4 = (bf16[2,104,1536]{2,1,0:T(8,128)(2,1)S(1)}, bf16[2,104,1536]{2,1,0:T(8,128)(2,1)S(1)}, u32[]{:S(2)}, u32[]{:S(2)}) collective-permute-start(bf16[2,104,1536]{2,1,0:T(8,128)(2,1)S(1)} %get-tuple-element.37), channel_id=1, source_target_pairs={{0,4},{4,0},{8,12},{12,8},{1,5},{5,1},{9,13},{13,9},{2,6},{6,2},{1... | collective-permute-start | bytes 1916936 | tf_op jit(solution)/shard_map/ppermute | solution.py:28
  19.2 10.5 %collective-permute-start.5 = (bf16[1,104,1536]{2,1,0:T(8,128)(2,1)S(1)}, bf16[1,104,1536]{2,1,0:T(8,128)(2,1)S(1)}, u32[]{:S(2)}, u32[]{:S(2)}) collective-permute-start(bf16[1,104,1536]{2,1,0:T(8,128)(2,1)S(1)} %shard_map.115), channel_id=1, source_target_pairs={{0,8},{4,12},{8,0},{12,4},{1,9},{5,13},{9,1},{13,5},{2,10},{6,14},... | collective-permute-start | bytes 958472 | tf_op jit(solution)/shard_map/ppermute | solution.py:28
  19.3 22.0 %collective-permute-start.3 = (bf16[2,112,256]{2,1,0:T(8,128)(2,1)S(1)}, bf16[2,112,256]{2,1,0:T(8,128)(2,1)S(1)}, u32[]{:S(2)}, u32[]{:S(2)}) collective-permute-start(bf16[2,112,256]{2,1,0:T(8,128)(2,1)S(1)} %get-tuple-element.35), channel_id=1, source_target_pairs={{4,0},{8,4},{12,8},{5,1},{9,5},{13,9},{6,2},{10,6},{14,10},{7,3},{... | collective-permute-start | bytes 344072 | tf_op jit(solution)/shard_map/ppermute | solution.py:23
  22.6 27.1 %collective-permute-start.2 = (bf16[2,112,256]{2,1,0:T(8,128)(2,1)S(1)}, bf16[2,112,256]{2,1,0:T(8,128)(2,1)S(1)}, u32[]{:S(2)}, u32[]{:S(2)}) collective-permute-start(bf16[2,112,256]{2,1,0:T(8,128)(2,1)S(1)} %get-tuple-element.30), channel_id=1, source_target_pairs={{0,4},{4,8},{8,12},{1,5},{5,9},{9,13},{2,6},{6,10},{10,14},{3,7},{... | collective-permute-start | bytes 344072 | tf_op jit(solution)/shard_map/ppermute | solution.py:23
  35.4 5.9 %collective-permute-start.6 = (bf16[104,1024]{1,0:T(8,128)(2,1)S(1)}, bf16[104,1024]{1,0:T(8,128)(2,1)S(1)}, u32[]{:S(2)}, u32[]{:S(2)}) collective-permute-start(bf16[104,1024]{1,0:T(8,128)(2,1)S(1)} %shard_map.116.refs_0_), channel_id=1, source_target_pairs={{0,8},{4,12},{8,0},{12,4},{1,9},{5,13},{9,1},{13,5},{2,10},{6,14},... | collective-permute-start | bytes 638984 | tf_op jit(solution)/shard_map/ppermute | solution.py:28
  37.7 7.7 %copy-start.7 = (s32[16,2]{0,1:T(2,128)S(1)}, s32[16,2]{0,1:T(2,128)}, u32[]{:S(2)}) copy-start(s32[16,2]{0,1:T(2,128)} %param.16) | copy-start | bytes 388
  37.7 7.7 %collective-permute-start.7 = (bf16[104,1024]{1,0:T(8,128)(2,1)S(1)}, bf16[104,1024]{1,0:T(8,128)(2,1)S(1)}, u32[]{:S(2)}, u32[]{:S(2)}) collective-permute-start(bf16[104,1024]{1,0:T(8,128)(2,1)S(1)} %shard_map.116.refs_0_), channel_id=1, source_target_pairs={{0,4},{4,0},{8,12},{12,8},{1,5},{5,1},{9,13},{13,9},{2,6},{6,2},{1... | collective-permute-start | bytes 638984 | tf_op jit(solution)/shard_map/ppermute | solution.py:28
  41.4 4.0 %collective-permute-start.8 = (bf16[104,1024]{1,0:T(8,128)(2,1)S(1)}, bf16[104,1024]{1,0:T(8,128)(2,1)S(1)}, u32[]{:S(2)}, u32[]{:S(2)}) collective-permute-start(bf16[104,1024]{1,0:T(8,128)(2,1)S(1)} %collective-permute-done.6.refs_1_), channel_id=1, source_target_pairs={{0,4},{4,0},{8,12},{12,8},{1,5},{5,1},{9,13},{13,9},{2,6},{6,2},{1... | collective-permute-start | bytes 638984 | tf_op jit(solution)/shard_map/ppermute | solution.py:28
  47.5 9.6 %collective-permute-start.9 = (bf16[104,1024]{1,0:T(8,128)(2,1)S(1)}, bf16[104,1024]{1,0:T(8,128)(2,1)S(1)}, u32[]{:S(2)}, u32[]{:S(2)}) collective-permute-start(bf16[104,1024]{1,0:T(8,128)(2,1)S(1)} %get-tuple-element.45), channel_id=1, source_target_pairs={{0,1},{1,2},{2,3},{4,5},{5,6},{6,7},{8,9},{9,10},{10,11},{12,13},{... | collective-permute-start | bytes 638984 | tf_op jit(solution)/shard_map/ppermute | solution.py:23

commit v3 on v2

--- a/solution.py
+++ b/solution.py
@@ -64,13 +64,13 @@
     return jnp.swapaxes(flat[...], 0, 1)
 
 
-def pack(who, anchor, state):
+def pack(who, state):
     channels, rows, cols = state.shape
     padded = -(-channels // 8) * 8
     deep = -(-padded // 16) * 16
     span = -(-rows * REACH // LANES)
 
-    def body(who_ref, at_ref, state_ref, right_ref, left_ref, rows_ref, flat):
+    def body(who_ref, state_ref, right_ref, left_ref, rows_ref, flat):
         turned = turn_rows(state_ref, flat)
         rows_ref[...] = turned
         lane = lane_index((deep, LANES))
@@ -95,10 +95,9 @@
     return run(
         body,
         [like((padded, span * LANES)), like((padded, LANES)), like((rows, deep, cols))],
-        [who, anchor, state],
+        [who, state],
         [pltpu.VMEM((deep, rows, cols), HALF)],
         micros=1.0,
-        scalars=2,
     )
 
 
@@ -165,31 +164,88 @@
     return out[:count], out[count : count + lines], *out[count + lines :]
 
 
-def add_parts(kept, got, keep_odd):
-    count, padded, lanes = kept.shape
-
+def add_parts(kept, got):
     def body(kept_ref, got_ref, out_ref):
-        for k in range(count // 2):
-            out_ref[k] = kept_ref[2 * k + keep_odd] + got_ref[2 * k + keep_odd]
-
-    return run(body, [like((count // 2, padded, lanes))], [kept, got], [], micros=0.3, scalars=0)[0]
-
-
-def extract(who, anchor, turned, right, left, pick, bands, sects):
+        out_ref[...] = kept_ref[...] + got_ref[...]
+
+    return run(body, [like(kept.shape)], [kept, got], [], micros=0.3, scalars=0)[0]
+
+
+def window_tile(picked, t, row0, rows, padded, lanes):
+    zone = lane_index((padded, LANES))
+    total = jnp.zeros((padded, LANES), FULL)
+    for m in range(PER_TILE):
+        r = row0 + t * PER_TILE + m
+        low = jnp.where((r >= 0) & (r < rows), WIDE * m, 2 * LANES)
+        keep = (zone >= low) & (zone < WIDE * (m + 1))
+        value = picked[jnp.clip(r, 0, rows - 1), :padded, lanes]
+        total = jnp.where(keep, value, total)
+    return total.astype(HALF)
+
+
+def batches(bands):
+    size = 4 if bands % 4 == 0 else bands
+    return [range(first, first + size) for first in range(0, bands, size)], size
+
+
+def select_rows(source, pick, picked):
+    rows, deep, _ = source.shape
+    chunk = rows // 2
+
+    def select(c, carry):
+        view = source[pl.ds(c * chunk, chunk)].reshape(chunk * deep, LANES)
+        picked[pl.ds(c * chunk, chunk)] = jnp.dot(
+            view, pick, preferred_element_type=FULL
+        ).reshape(chunk, deep, pick.shape[1])
+        return carry
+
+    lax.fori_loop(0, rows // chunk, select, 0)
+
+
+def extract_own(who, anchor, turned, pick, padded, bands, sects):
+    rows, deep, cols = turned.shape
+    groups, size = batches(bands)
+
+    def body(who_ref, at_ref, rows_ref, pick_ref, out_ref, picked):
+        for group in groups:
+            select_rows(rows_ref, pick_ref[:cols, group[0] * LANES : (group[-1] + 1) * LANES], picked)
+            for j in group:
+                row0 = slot_at(who_ref, at_ref, j, sects, rows, cols)[0] - 2
+                inside = (row0 > -WIDE) & (row0 < rows)
+
+                @pl.when(inside)
+                def _(j=j, row0=row0, at=(j - group[0]) * LANES):
+                    for t in range(TILES):
+                        out_ref[j, :, t * LANES : (t + 1) * LANES] = window_tile(
+                            picked, t, row0, rows, padded, slice(at, at + LANES)
+                        )
+
+                @pl.when(jnp.logical_not(inside))
+                def _(j=j):
+                    out_ref[j] = jnp.zeros((padded, TILES * LANES), HALF)
+
+    return run(
+        body,
+        [like((bands, padded, TILES * LANES))],
+        [who, anchor, turned, pick],
+        [pltpu.VMEM((rows, deep, size * LANES), FULL)],
+        micros=1.5,
+        scalars=2,
+    )[0]
+
+
+def extract_rim(who, anchor, parts, turned, right, left, pick, bands, sects):
     rows, deep, cols = turned.shape
     padded = right.shape[0]
-    width = cols + LANES
-    batch = 4 if bands % 4 == 0 else bands
-    chunk = 4
-
-    def body(who_ref, at_ref, rows_ref, right_ref, left_ref, pick_ref,
-             keep_ref, send_ref, top_ref, low_ref, ext, picked):
+    groups, size = batches(bands)
+
+    def body(who_ref, at_ref, part_ref, rows_ref, right_ref, left_ref, pick_ref,
+             own_ref, low_ref, odd_ref, high_ref, near_ref, cross_ref, ext, picked):
         lane = lane_index((padded, LANES))
-        ext[:, padded:, :] = jnp.zeros((rows, deep - padded, width), HALF)
-        ext[:, :, :cols] = rows_ref[...]
+        none = jnp.zeros((padded, LANES), HALF)
         rim = left_ref[...]
-        none = jnp.zeros((padded, LANES), HALF)
-        for r in range(rows):
+
+        def expand(r):
             at, off = divmod(r * REACH, LANES)
             piece = right_ref[:, at * LANES : (at + 1) * LANES]
             if off:
@@ -197,53 +253,74 @@
             if off + REACH > LANES:
                 after = right_ref[:, (at + 1) * LANES : (at + 2) * LANES]
                 piece = jnp.where(lane < LANES - off, piece, pltpu.roll(after, LANES - off, 1))
-            turned = pltpu.roll(rim, (LANES - 2 - 2 * r) % LANES, 1)
-            piece = jnp.where(lane < REACH, piece, jnp.where(lane >= LANES - 2, turned, none))
-            ext[r, :padded, cols:] = piece
-        top_ref[...] = ext[:2]
-        low_ref[...] = ext[rows - 2 :]
-        for first in range(0, bands, batch):
-            chosen = slice(first * LANES, (first + batch) * LANES)
-
-            def select(c, carry, chosen=chosen):
-                view = ext[pl.ds(c * chunk, chunk)].reshape(chunk * deep, width)
-                picked[pl.ds(c * chunk, chunk)] = jnp.dot(
-                    view, pick_ref[:, chosen], preferred_element_type=FULL
-                ).reshape(chunk, deep, batch * LANES)
-                return carry
-
-            lax.fori_loop(0, rows // chunk, select, 0)
-            for j in range(first, first + batch):
-                out_ref = send_ref if j % 2 else keep_ref
-                row0 = slot_at(who_ref, at_ref, j, sects, rows, cols)[0] - 2
-                inside = (row0 > -WIDE) & (row0 < rows)
-
-                @pl.when(inside)
-                def _(j=j, row0=row0, out_ref=out_ref, first=first):
-                    lanes = slice((j - first) * LANES, (j - first + 1) * LANES)
-                    zone = lane_index((padded, LANES))
-                    for t in range(TILES):
-                        total = jnp.zeros((padded, LANES), FULL)
-                        for m in range(PER_TILE):
-                            r = row0 + t * PER_TILE + m
-                            low = jnp.where((r >= 0) & (r < rows), WIDE * m, width)
-                            keep = (zone >= low) & (zone < WIDE * (m + 1))
-                            value = picked[jnp.clip(r, 0, rows - 1), :padded, lanes]
-                            total = jnp.where(keep, value, total)
-                        out_ref[j // 2, :, t * LANES : (t + 1) * LANES] = total.astype(HALF)
-
-                @pl.when(jnp.logical_not(inside))
-                def _(j=j, out_ref=out_ref):
-                    out_ref[j // 2] = jnp.zeros((padded, TILES * LANES), HALF)
-
-    part = like((bands // 2, padded, TILES * LANES))
-    edge = like((2, deep, width))
+            turn = pltpu.roll(rim, (LANES - 2 - 2 * r) % LANES, 1)
+            ext[r, :padded] = jnp.where(
+                lane < REACH, piece, jnp.where(lane >= LANES - 2, turn, none)
+            )
+
+        ext[:, padded:] = jnp.zeros((rows, deep - padded, LANES), HALF)
+        outer = (0, 1, rows - 2, rows - 1)
+        for r in outer:
+            expand(r)
+        even = jnp.bitwise_and(who_ref[0], 1) == 0
+        for k in range(2):
+            top, low = k, rows - 2 + k
+            near_ref[k, :, :cols] = jnp.where(even, rows_ref[low], rows_ref[top])
+            near_ref[k, :, cols:] = jnp.where(even, ext[low], ext[top])
+            cross_ref[k, :, :cols] = jnp.where(even, rows_ref[top], rows_ref[low])
+            cross_ref[k, :, cols:] = jnp.where(even, ext[top], ext[low])
+
+        def target(j):
+            if j < 2:
+                return (own_ref, odd_ref)[j], 0
+            return (low_ref, high_ref)[j % 2], j // 2 - 1
+
+        crossing = []
+        for j in range(bands):
+            row0, col0 = slot_at(who_ref, at_ref, j, sects, rows, cols)
+            row0 = row0 - 2
+            inside = (row0 > -WIDE) & (row0 < rows)
+            over = inside & ((col0 < 2) | (col0 > cols - REACH))
+            crossing.append((row0, over))
+            out_ref, at = target(j)
+            out_ref[at] = part_ref[j]
+        for group in groups:
+            some = crossing[group[0]][1]
+            for j in group[1:]:
+                some = some | crossing[j][1]
+
+            @pl.when(some)
+            def _(group=group):
+                if group[0] == 0:
+                    for r in range(rows):
+                        if r not in outer:
+                            expand(r)
+                else:
+                    for r in range(rows):
+                        expand(r)
+                select_rows(
+                    ext, pick_ref[cols:, group[0] * LANES : (group[-1] + 1) * LANES], picked
+                )
+                for j in group:
+                    out_ref, at = target(j)
+                    row0, over = crossing[j]
+
+                    @pl.when(over)
+                    def _(j=j, out_ref=out_ref, at=at, row0=row0, first=(j - group[0]) * LANES):
+                        for t in range(TILES):
+                            out_ref[at, :, t * LANES : (t + 1) * LANES] += window_tile(
+                                picked, t, row0, rows, padded, slice(first, first + LANES)
+                            )
+
+    one = like((1, padded, TILES * LANES))
+    rest = like((max(bands // 2 - 1, 1), padded, TILES * LANES))
+    edge = like((2, deep, cols + LANES))
     return run(
         body,
-        [part, part, edge, edge],
-        [who, anchor, turned, right, left, pick],
-        [pltpu.VMEM((rows, deep, width), HALF), pltpu.VMEM((rows, deep, batch * LANES), FULL)],
-        micros=3.0,
+        [one, rest, one, rest, edge, edge],
+        [who, anchor, parts, turned, right, left, pick],
+        [pltpu.VMEM((rows, deep, LANES), HALF), pltpu.VMEM((rows, deep, size * LANES), FULL)],
+        micros=1.5,
         scalars=2,
     )
 
@@ -421,9 +498,9 @@
     )[0]
 
 
-def grid_mean(who, shifted, rim, lower, padded, weights, biases, limits):
+def grid_mean(who, shifted, near, cross, lower, padded, weights, biases, limits):
     rows = 2 * shifted.shape[1]
-    _, deep, width = rim.shape
+    _, deep, width = near.shape
     cols = width - LANES
     loose = cols + 16
     made = rows // 2
@@ -434,7 +511,7 @@
     state_pairs = hidden_pairs + 1
     base = rows - made - 2 if lower else -2
 
-    def body(who_ref, shifted_ref, rim_ref, w_in, w_out, b_in, b_out, out_ref,
+    def body(who_ref, shifted_ref, near_ref, cross_ref, w_in, w_out, b_in, b_out, out_ref,
              line, state_sh, hid, hid_sh):
         row0 = who_ref[0] * rows + base + 1
         col0 = who_ref[1] * cols - 1
@@ -448,9 +525,11 @@
         at = (rows - made) // 2 - 1 if lower else 0
         for b in range(3):
             state_sh[b, skip : skip + given] = shifted_ref[b, at : at + given]
+        pair = jnp.bitwise_and(who_ref[0], 1) == (0 if lower else 1)
         for v in range(2):
+            rim = jnp.where(pair, near_ref[v], cross_ref[v])
             value = jnp.concatenate(
-                [rim_ref[v].astype(FULL), jnp.zeros((LANES - deep, width), FULL)], axis=0
+                [rim.astype(FULL), jnp.zeros((LANES - deep, width), FULL)], axis=0
             ).T
             line[v, 8 : 8 + cols] = value[:cols]
             line[v, 8 + cols :] = value[cols : cols + 16]
@@ -496,7 +575,7 @@
     return run(
         body,
         [like((made, padded, cols))],
-        [who, shifted, rim, *weights, *biases],
+        [who, shifted, near, cross, *weights, *biases],
         [
             pltpu.VMEM((2, loose + 8, LANES), FULL),
             pltpu.VMEM((3, state_pairs, 2, loose, LANES), HALF),
@@ -620,7 +699,7 @@
 
     anchor = patch_anchor.T
 
-    right_rim, left_rim, turned = pack(who, anchor, state_field)
+    right_rim, left_rim, turned = pack(who, state_field)
     right = shift_from(right_rim, "sect", -1)
     left = shift_from(left_rim, "sect", 1)
 
@@ -642,18 +721,25 @@
     )
     biases, step_lines = lines[:3], lines[3]
 
-    kept, sent, top, low = extract(who, anchor, turned, right, left, pick, bands, sects)
-    got = swap(sent, "band", 1)
-    addends = [kept, got]
+    padded = right_rim.shape[0]
+    parts = extract_own(who, anchor, turned, pick, padded, bands, sects)
+    own, kept, own_sent, sent, edge_near, edge_cross = extract_rim(
+        who, anchor, parts, turned, right, left, pick, bands, sects
+    )
+    addends = [own]
+    if bands > 2:
+        got = swap(sent, "band", 1)
+        kept = add_parts(kept, got)
     bit = 2
     while bit < bands:
-        odd = add_parts(kept, got, 1)
-        kept = add_parts(kept, got, 0) if 2 * bit < bands else kept
-        got = swap(odd, "band", bit)
+        got = swap(kept[0::2], "band", bit)
         addends.append(got)
+        kept = kept[1::2] + got[1:]
         bit *= 2
-    above = shift_from(low, "band", 1)
-    below = shift_from(top, "band", -1)
+    addends.append(swap(own_sent, "band", 1))
+    rim_near = swap(edge_near, "band", 1)
+    steps = [(i, i + 1) for i in range(1, bands - 1, 2)]
+    rim_cross = lax.ppermute(edge_cross, "band", steps + [(j, i) for i, j in steps])
     correction = patch_step(who, anchor, addends, noise, made, biases, step_lines, sects, limits)
     pieces = [correction]
     sources = [0]
@@ -667,9 +753,8 @@
         bit //= 2
 
     shifted = spread(turned, right, left)
-    padded = right.shape[0]
-    top_mean = grid_mean(who, shifted, above, False, padded, made[:2], biases[:2], limits)
-    low_mean = grid_mean(who, shifted, below, True, padded, made[:2], biases[:2], limits)
+    top_mean = grid_mean(who, shifted, rim_near, rim_cross, False, padded, made[:2], biases[:2], limits)
+    low_mean = grid_mean(who, shifted, rim_near, rim_cross, True, padded, made[:2], biases[:2], limits)
     spilled, summed, inverse = canvas(
         who, anchor, pieces, sources, place, sects, rows, cols
     )

time: 59.3 us -> 58.4 us (0.985)
  Pallas kernels: 27.4 us -> 29.3 us
  starting transfers between devices: 13.6 us -> 12.6 us
  waiting for transfers between devices: 15.5 us -> 14.7 us
  local copies, waits for them, and re-layouts: 1.94 us -> 1.27 us
    ppermute x5 -> x3, starting transfers between devices: 13.2 us -> 7.77 us  [shift_from(): return lax.ppermute(block, axis, route)]
    ppermute x0 -> x1, starting transfers between devices: none -> 3.82 us  [step(): lax.ppermute(edge_cross, 'band', steps + [(j, i) for i, j in steps])]
    pallas_call x10 -> x11, Pallas kernels: 27.4 us -> 29.3 us  [run(): pl.pallas_call(body, out_shape=outs, in_specs=[smem] * scalars + [vmem] *...]
    ppermute x5 -> x3, waiting for transfers between devices: 4.82 us -> 3.62 us  [shift_from(): return lax.ppermute(block, axis, route)]
    unnamed x25 -> x23, local copies, waits for them, and re-layouts: 1.94 us -> 1.27 us
    ppermute x5 -> x7, starting transfers between devices: 0.36 us -> 0.99 us  [swap(): return lax.ppermute(block, axis, [(i, i ^ bit) for i in range(count)])]
    ppermute x5 -> x7, waiting for transfers between devices: 10.7 us -> 11 us  [swap(): return lax.ppermute(block, axis, [(i, i ^ bit) for i in range(count)])]
  transfers between devices with their start and end apart: 10 -> 11, of which waited for: 6 -> 4; matrix products, arithmetic and copies ran while one was open for 0% -> 0% of each run, Pallas kernels for 34% -> 36%
where the time goes in v3:
time: 58.4 us; the launch traced here: 58.2 us
  Pallas kernels  29.3 us (50%)
  waiting for transfers between devices  14.7 us (25%)
  starting transfers between devices  12.6 us (22%)
  local copies, waits for them, and re-layouts  1.27 us (2%)
    pallas_call x11, Pallas kernels, run(): pl.pallas_call(body, out_shape=outs, in_specs=[smem] * scalars + [vmem] *...  29.3 us
    ppermute x7, waiting for transfers between devices, swap(): return lax.ppermute(block, axis, [(i, i ^ bit) for i in range(count)])  11 us
    ppermute x3, starting transfers between devices, shift_from(): return lax.ppermute(block, axis, route)  7.77 us
    ppermute x1, starting transfers between devices, step(): lax.ppermute(edge_cross, 'band', steps + [(j, i) for i, j in steps])  3.82 us
    ppermute x3, waiting for transfers between devices, shift_from(): return lax.ppermute(block, axis, route)  3.62 us
    unnamed x23, local copies, waits for them, and re-layouts  1.27 us
  transfers between devices with their start and end apart: 11, of which 4 were waited for; matrix products, arithmetic and copies ran while one was open for 0% of the time, Pallas kernels for 36%

profile of v3, /device:TPU:18, one launch (start us, length us, event | category | flops | bytes accessed | tf_op | source)
XLA Modules:
  0.0 58.2 jit_solution(14496160165736010618)
XLA Ops:
  0.0 0.1 pad_add_fusion.who_ref.refs_0_
  0.1 1.1 %copy-done = bf16[99,32,128]{2,1,0:T(8,128)(2,1)S(1)} copy-done((bf16[99,32,128]{2,1,0:T(8,128)(2,1)S(1)}, bf16[99,32,128]{2,1,0:T(8,128)(2,1)}, u32[]{:S(2)}) %copy-start) | copy-done | bytes 811032
  1.2 0.0 copy-start.4
  1.2 0.0 copy-start.5
  1.3 0.0 copy-start.6
  1.3 0.0 copy-start.7
  1.3 0.0 copy-start.8
  1.3 0.0 copy-start.9
  1.3 1.3 %shard_map.109 = (bf16[104,1152]{1,0:T(8,128)(2,1)S(1)}, bf16[104,128]{1,0:T(8,128)(2,1)S(1)}, bf16[32,112,128]{2,1,0:T(8,128)(2,1)S(1)}) custom-call(s32[2]{0:T(128)S(1)} %pad_add_fusion.who_ref.refs_0_, bf16[99,32,128]{2,1,0:T(8,128)(2,1)S(1)} %copy-done), custom_call_target="tpu_custom_call" | custom-call | flops 1150000000 | bytes 1024 | tf_op jit(solution)/shard_map/pallas_call | solution.py:34
  2.6 2.4 %collective-permute-start = (bf16[104,1152]{1,0:T(8,128)(2,1)S(1)}, bf16[104,1152]{1,0:T(8,128)(2,1)S(1)}, u32[]{:S(2)}, u32[]{:S(2)}) collective-permute-start(bf16[104,1152]{1,0:T(8,128)(2,1)S(1)} %get-tuple-element.29), channel_id=1, source_target_pairs={{1,0},{2,1},{3,2},{5,4},{6,5},{7,6},{9,8},{10,9},{11,10},{13,12},{... | collective-permute-start | bytes 718856 | tf_op jit(solution)/shard_map/ppermute | solution.py:23
  5.0 3.5 %collective-permute-start.1 = (bf16[104,128]{1,0:T(8,128)(2,1)S(1)}, bf16[104,128]{1,0:T(8,128)(2,1)S(1)}, u32[]{:S(2)}, u32[]{:S(2)}) collective-permute-start(bf16[104,128]{1,0:T(8,128)(2,1)S(1)} %get-tuple-element.30), channel_id=1, source_target_pairs={{0,1},{1,2},{2,3},{4,5},{5,6},{6,7},{8,9},{9,10},{10,11},{12,13},{... | collective-permute-start | bytes 79880 | tf_op jit(solution)/shard_map/ppermute | solution.py:23
  8.5 0.0 copy-done.10
  8.5 0.1 copy.14
  8.6 0.0 copy-done.1
  8.6 0.0 copy-done.2
  8.6 0.0 copy-done.3
  8.6 0.0 copy-done.4
  8.6 0.0 copy-done.5
  8.6 0.0 copy-done.6
  8.6 2.0 %shard_map.111 = (bf16[1536,256]{1,0:T(8,128)(2,1)S(1)}, bf16[256,1536]{1,0:T(8,128)(2,1)S(1)}, bf16[1536,256]{1,0:T(8,128)(2,1)S(1)}, bf16[256,1536]{1,0:T(8,12...) custom-call(s32[2]{0:T(128)S(1)} %pad_add_fusion.who_ref.refs_0_, ...), custom_call_target="tpu_custom_call" | custom-call | flops 2875000064 | bytes 1024 | tf_op jit(solution)/shard_map/pallas_call | solution.py:34
  10.6 2.6 %shard_map.112.part_ref = bf16[4,104,1536]{2,1,0:T(8,128)(2,1)S(1)} custom-call(s32[2]{0:T(128)S(1)} %pad_add_fusion.who_ref.refs_0_, s32[2,16]{1,0:T(2,128)S(1)} %bitcast.15, bf16[32,112,128]{2,1,0:T(8,128)(2,1)S(1)} %get-tuple-element.28.rows_ref, bf16[256,512]{1,0:T(8,128)(2,1)S(1)} %get-tuple-element.31.pick_ref), custom_call_target="tpu_custom_call" | custom-call | flops 1724999936 | bytes 1024 | tf_op jit(solution)/shard_map/pallas_call | solution.py:34
  13.3 0.0 collective-permute-done.1.left_ref
  13.3 0.0 collective-permute-done.right_ref
  13.3 3.4 %shard_map.113 = (bf16[1,104,1536]{2,1,0:T(8,128)(2,1)S(1)}, bf16[1,104,1536]{2,1,0:T(8,128)(2,1)S(1)}, bf16[1,104,1536]{2,1,0:T(8,128)(2,1)S(1)}, bf16[1,104,15...) custom-call(s32[2]{0:T(128)S(1)} %pad_add_fusion.who_ref.refs_0_, ...), custom_call_target="tpu_custom_call" | custom-call | flops 1724999936 | bytes 1024 | tf_op jit(solution)/shard_map/pallas_call | solution.py:34
  16.7 0.1 collective-permute-start.4
  16.7 0.5 collective-permute-start.6
  17.2 1.1 %collective-permute-done.4.got_ref = bf16[1,104,1536]{2,1,0:T(8,128)(2,1)S(1)} collective-permute-done((bf16[1,104,1536]{2,1,0:T(8,128)(2,1)S(1)}, bf16[1,104,1536]{2,1,0:T(8,128)(2,1)S(1)}, u32[]{:S(2)}, u32[]{:S(2)}) %collective-permute-start.4) | collective-permute-done | bytes 319520 | tf_op jit(solution)/shard_map/ppermute | solution.py:28
  18.4 0.1 collective-permute-start.5
  18.5 0.2 collective-permute-start.2
  18.7 3.8 %collective-permute-start.3 = (bf16[2,112,256]{2,1,0:T(8,128)(2,1)S(1)}, bf16[2,112,256]{2,1,0:T(8,128)(2,1)S(1)}, u32[]{:S(2)}, u32[]{:S(2)}) collective-permute-start(bf16[2,112,256]{2,1,0:T(8,128)(2,1)S(1)} %get-tuple-element.33), channel_id=1, source_target_pairs={{4,8},{8,4},{5,9},{9,5},{6,10},{10,6},{7,11},{11,7},{20,24},{24,20... | collective-permute-start | bytes 344072 | tf_op jit(solution)/shard_map/ppermute | solution.py:742
  22.5 0.0 collective-permute-done.6.refs_4_
  22.5 6.3 %collective-permute-done.5.refs_3_ = bf16[1,104,1536]{2,1,0:T(8,128)(2,1)S(1)} collective-permute-done((bf16[1,104,1536]{2,1,0:T(8,128)(2,1)S(1)}, bf16[1,104,1536]{2,1,0:T(8,128)(2,1)S(1)}, u32[]{:S(2)}, u32[]{:S(2)}) %collective-permute-start.5) | collective-permute-done | bytes 319520 | tf_op jit(solution)/shard_map/ppermute | solution.py:28
  28.9 6.0 %shard_map.117.refs_0_ = bf16[104,1024]{1,0:T(8,128)(2,1)S(1)} custom-call(s32[2]{0:T(128)S(1)} %pad_add_fusion.who_ref.refs_0_, s32[2,16]{1,0:T(2,128)S(1)} %bitcast.17, bf16[1,104,1536]{2,1,0:T(8,128)(2,1)S(1)} %get-tuple-element.38.refs_2_, bf16[1,104,1536]{2,1,0:T(8,128)(2,1)S(1)} %collective-permute-done.5.refs_3_, ...), custom_call_target="tpu_custom_call" | custom-call | flops 9200000000 | bytes 1024 | tf_op jit(solution)/shard_map/pallas_call | solution.py:34
  34.8 0.1 collective-permute-start.7
  34.9 2.2 %shard_map.110.shifted_ref = bf16[3,16,2,144,128]{4,3,2,1,0:T(8,128)(2,1)S(1)} custom-call(bf16[32,112,128]{2,1,0:T(8,128)(2,1)S(1)} %get-tuple-element.28.rows_ref, bf16[104,1152]{1,0:T(8,128)(2,1)S(1)} %collective-permute-done.right_ref, bf16[104,128]{1,0:T(8,128)(2,1)S(1)} %collective-permute-done.1.left_ref), custom_call_target="tpu_custom_call" | custom-call | flops 2875000064 | bytes 1024 | tf_op jit(solution)/shard_map/pallas_call | solution.py:34
  37.1 0.1 collective-permute-start.8
  37.2 3.6 %collective-permute-done.7.refs_1_ = bf16[104,1024]{1,0:T(8,128)(2,1)S(1)} collective-permute-done((bf16[104,1024]{1,0:T(8,128)(2,1)S(1)}, bf16[104,1024]{1,0:T(8,128)(2,1)S(1)}, u32[]{:S(2)}, u32[]{:S(2)}) %collective-permute-start.7) | collective-permute-done | bytes 213024 | tf_op jit(solution)/shard_map/ppermute | solution.py:28
  40.7 0.0 collective-permute-start.9
  40.7 0.0 collective-permute-done.2.near_ref
  40.7 0.0 collective-permute-done.3.cross_ref
  40.7 4.0 %shard_map.115.low_ref = bf16[16,104,128]{2,1,0:T(8,128)(2,1)S(1)} custom-call(s32[2]{0:T(128)S(1)} %pad_add_fusion.who_ref.refs_0_, bf16[3,16,2,144,128]{4,3,2,1,0:T(8,128)(2,1)S(1)} %shard_map.110.shifted_ref, bf16[2,112,256]{2,1,0:T(8,128)(2,1)S(1)} %collective-permute-done.2.near_ref, bf16[2,112,256]{2,1,0:T(8,128)(2,1)S(1)} %collective-permute-done.3.cross_ref, ...), custom_call_target="tpu_custom_call" | custom-call | flops 4024999936 | bytes 1024 | tf_op jit(solution)/shard_map/pallas_call | solution.py:34
  44.8 0.0 collective-permute-done.8.refs_2_
  44.8 0.0 collective-permute-done.9.refs_3_
  44.8 2.1 %shard_map.118 = (bf16[104,1024]{1,0:T(8,128)(2,1)S(1)}, f32[32,104,128]{2,1,0:T(8,128)S(1)}, f32[32,128]{1,0:T(8,128)S(1)}) custom-call(s32[2]{0:T(128)S(1)} %pad_add_fusion.who_ref.refs_0_, s32[2,16]{1,0:T(2,128)S(1)} %bitcast.18, bf16[104,1024]{1,0:T(8,128)(2,1)S(1)} %shard_map.117.refs_0_, bf16[104,1024]{1,0:T(8,128)(2,1)S(1)} %collective-permute-done.7.refs_1_, ...), custom_call_target="tpu_custom_call" | custom-call | flops 1724999936 | bytes 1024 | tf_op jit(solution)/shard_map/pallas_call | solution.py:34
  46.9 1.9 %collective-permute-start.10 = (bf16[104,1024]{1,0:T(8,128)(2,1)S(1)}, bf16[104,1024]{1,0:T(8,128)(2,1)S(1)}, u32[]{:S(2)}, u32[]{:S(2)}) collective-permute-start(bf16[104,1024]{1,0:T(8,128)(2,1)S(1)} %get-tuple-element.49), channel_id=1, source_target_pairs={{0,1},{1,2},{2,3},{4,5},{5,6},{6,7},{8,9},{9,10},{10,11},{12,13},{... | collective-permute-start | bytes 638984 | tf_op jit(solution)/shard_map/ppermute | solution.py:23
  48.8 4.0 %shard_map.114.top_ref = bf16[16,104,128]{2,1,0:T(8,128)(2,1)S(1)} custom-call(s32[2]{0:T(128)S(1)} %pad_add_fusion.who_ref.refs_0_, bf16[3,16,2,144,128]{4,3,2,1,0:T(8,128)(2,1)S(1)} %shard_map.110.shifted_ref, bf16[2,112,256]{2,1,0:T(8,128)(2,1)S(1)} %collective-permute-done.2.near_ref, bf16[2,112,256]{2,1,0:T(8,128)(2,1)S(1)} %collective-permute-done.3.cross_ref, ...), custom_call_target="tpu_custom_call" | custom-call | flops 4024999936 | bytes 1024 | tf_op jit(solution)/shard_map/pallas_call | solution.py:34
  52.9 3.6 %collective-permute-done.10.spill_ref = bf16[104,1024]{1,0:T(8,128)(2,1)S(1)} collective-permute-done((bf16[104,1024]{1,0:T(8,128)(2,1)S(1)}, bf16[104,1024]{1,0:T(8,128)(2,1)S(1)}, u32[]{:S(2)}, u32[]{:S(2)}) %collective-permute-start.10) | collective-permute-done | bytes 213024 | tf_op jit(solution)/shard_map/ppermute | solution.py:23
  56.5 1.7 %shard_map.119 = bf16[99,32,128]{2,1,0:T(8,128)(2,1)} custom-call(bf16[16,104,128]{2,1,0:T(8,128)(2,1)S(1)} %shard_map.114.top_ref, bf16[16,104,128]{2,1,0:T(8,128)(2,1)S(1)} %shard_map.115.low_ref, f32[32,104,128]{2,1,0:T(8,128)S(1)} %get-tuple-element.48.sum_ref, bf16[104,1024]{1,0:T(8,128)(2,1)S(1)} %collective-permute-done.10.spill_ref, ...), custom_call_target="tpu_custom_call" | custom-call | flops 3449999872 | bytes 1024 | tf_op jit(solution)/shard_map/pallas_call | solution.py:34
  (9 shorter events, 0.1 us)
Async XLA Ops:
  0.1 1.1 %copy-start = (bf16[99,32,128]{2,1,0:T(8,128)(2,1)S(1)}, bf16[99,32,128]{2,1,0:T(8,128)(2,1)}, u32[]{:S(2)}) copy-start(bf16[99,32,128]{2,1,0:T(8,128)(2,1)} %state_ref.1) | copy-start | bytes 2433028
  1.2 7.2 %copy-start.10 = (bf16[1,2,99,1024]{3,1,2,0:T(2,128)(2,1)S(1)}, bf16[1,2,99,1024]{3,1,2,0:T(2,128)(2,1)}, u32[]{:S(2)}) copy-start(bf16[1,2,99,1024]{3,1,2,0:T(2,128)(2,1)} %param.17) | copy-start | bytes 1216516
  1.2 7.3 %copy-start.1 = (bf16[9,128,99]{1,2,0:T(8,128)(2,1)S(1)}, bf16[9,128,99]{1,2,0:T(8,128)(2,1)}, u32[]{:S(2)}) copy-start(bf16[9,128,99]{1,2,0:T(8,128)(2,1)} %param.12) | copy-start | bytes 684292
  1.2 7.3 %copy-start.2 = (bf16[9,99,128]{2,1,0:T(8,128)(2,1)S(1)}, bf16[9,99,128]{2,1,0:T(8,128)(2,1)}, u32[]{:S(2)}) copy-start(bf16[9,99,128]{2,1,0:T(8,128)(2,1)} %refs_1_.1) | copy-start | bytes 684292
  1.2 7.4 %copy-start.3 = (bf16[9,128,99]{1,2,0:T(8,128)(2,1)S(1)}, bf16[9,128,99]{1,2,0:T(8,128)(2,1)}, u32[]{:S(2)}) copy-start(bf16[9,128,99]{1,2,0:T(8,128)(2,1)} %param.18) | copy-start | bytes 684292
  1.2 7.4 %copy-start.4 = (bf16[9,99,128]{2,1,0:T(8,128)(2,1)S(1)}, bf16[9,99,128]{2,1,0:T(8,128)(2,1)}, u32[]{:S(2)}) copy-start(bf16[9,99,128]{2,1,0:T(8,128)(2,1)} %refs_3_.1) | copy-start | bytes 684292
  1.2 7.4 %copy-start.5 = (f32[2,128]{1,0:T(2,128)S(1)}, f32[2,128]{1,0:T(2,128)}, u32[]{:S(2)}) copy-start(f32[2,128]{1,0:T(2,128)} %refs_7_.1) | copy-start | bytes 3076
  1.3 7.4 %copy-start.6 = (s32[16,2]{0,1:T(2,128)S(1)}, s32[16,2]{0,1:T(2,128)}, u32[]{:S(2)}) copy-start(s32[16,2]{0,1:T(2,128)} %param.16) | copy-start | bytes 388
  1.3 7.3 %copy-start.7 = (f32[128]{0:T(128)S(1)}, f32[128]{0:T(128)}, u32[]{:S(2)}) copy-start(f32[128]{0:T(128)} %param.13) | copy-start | bytes 1540
  1.3 7.3 %copy-start.8 = (f32[99]{0:T(128)S(1)}, f32[99]{0:T(128)}, u32[]{:S(2)}) copy-start(f32[99]{0:T(128)} %param.15) | copy-start | bytes 1192
  1.3 7.3 %copy-start.9 = (f32[99]{0:T(128)S(1)}, f32[99]{0:T(128)}, u32[]{:S(2)}) copy-start(f32[99]{0:T(128)} %param.21) | copy-start | bytes 1192
  2.6 10.7 %collective-permute-start = (bf16[104,1152]{1,0:T(8,128)(2,1)S(1)}, bf16[104,1152]{1,0:T(8,128)(2,1)S(1)}, u32[]{:S(2)}, u32[]{:S(2)}) collective-permute-start(bf16[104,1152]{1,0:T(8,128)(2,1)S(1)} %get-tuple-element.29), channel_id=1, source_target_pairs={{1,0},{2,1},{3,2},{5,4},{6,5},{7,6},{9,8},{10,9},{11,10},{13,12},{... | collective-permute-start | bytes 718856 | tf_op jit(solution)/shard_map/ppermute | solution.py:23
  5.0 8.3 %collective-permute-start.1 = (bf16[104,128]{1,0:T(8,128)(2,1)S(1)}, bf16[104,128]{1,0:T(8,128)(2,1)S(1)}, u32[]{:S(2)}, u32[]{:S(2)}) collective-permute-start(bf16[104,128]{1,0:T(8,128)(2,1)S(1)} %get-tuple-element.30), channel_id=1, source_target_pairs={{0,1},{1,2},{2,3},{4,5},{5,6},{6,7},{8,9},{9,10},{10,11},{12,13},{... | collective-permute-start | bytes 79880 | tf_op jit(solution)/shard_map/ppermute | solution.py:23
  16.7 1.7 %collective-permute-start.4 = (bf16[1,104,1536]{2,1,0:T(8,128)(2,1)S(1)}, bf16[1,104,1536]{2,1,0:T(8,128)(2,1)S(1)}, u32[]{:S(2)}, u32[]{:S(2)}) collective-permute-start(bf16[1,104,1536]{2,1,0:T(8,128)(2,1)S(1)} %get-tuple-element.40), channel_id=1, source_target_pairs={{0,4},{4,0},{8,12},{12,8},{1,5},{5,1},{9,13},{13,9},{2,6},{6,2},{1... | collective-permute-start | bytes 958472 | tf_op jit(solution)/shard_map/ppermute | solution.py:28
  16.7 5.8 %collective-permute-start.6 = (bf16[1,104,1536]{2,1,0:T(8,128)(2,1)S(1)}, bf16[1,104,1536]{2,1,0:T(8,128)(2,1)S(1)}, u32[]{:S(2)}, u32[]{:S(2)}) collective-permute-start(bf16[1,104,1536]{2,1,0:T(8,128)(2,1)S(1)} %get-tuple-element.41), channel_id=1, source_target_pairs={{0,4},{4,0},{8,12},{12,8},{1,5},{5,1},{9,13},{13,9},{2,6},{6,2},{1... | collective-permute-start | bytes 958472 | tf_op jit(solution)/shard_map/ppermute | solution.py:28
  18.4 10.5 %collective-permute-start.5 = (bf16[1,104,1536]{2,1,0:T(8,128)(2,1)S(1)}, bf16[1,104,1536]{2,1,0:T(8,128)(2,1)S(1)}, u32[]{:S(2)}, u32[]{:S(2)}) collective-permute-start(bf16[1,104,1536]{2,1,0:T(8,128)(2,1)S(1)} %shard_map.116), channel_id=1, source_target_pairs={{0,8},{4,12},{8,0},{12,4},{1,9},{5,13},{9,1},{13,5},{2,10},{6,14},... | collective-permute-start | bytes 958472 | tf_op jit(solution)/shard_map/ppermute | solution.py:28
  18.5 22.3 %collective-permute-start.2 = (bf16[2,112,256]{2,1,0:T(8,128)(2,1)S(1)}, bf16[2,112,256]{2,1,0:T(8,128)(2,1)S(1)}, u32[]{:S(2)}, u32[]{:S(2)}) collective-permute-start(bf16[2,112,256]{2,1,0:T(8,128)(2,1)S(1)} %get-tuple-element.32), channel_id=1, source_target_pairs={{0,4},{4,0},{8,12},{12,8},{1,5},{5,1},{9,13},{13,9},{2,6},{6,2},{1... | collective-permute-start | bytes 344072 | tf_op jit(solution)/shard_map/ppermute | solution.py:28
  18.7 22.1 %collective-permute-start.3 = (bf16[2,112,256]{2,1,0:T(8,128)(2,1)S(1)}, bf16[2,112,256]{2,1,0:T(8,128)(2,1)S(1)}, u32[]{:S(2)}, u32[]{:S(2)}) collective-permute-start(bf16[2,112,256]{2,1,0:T(8,128)(2,1)S(1)} %get-tuple-element.33), channel_id=1, source_target_pairs={{4,8},{8,4},{5,9},{9,5},{6,10},{10,6},{7,11},{11,7},{20,24},{24,20... | collective-permute-start | bytes 344072 | tf_op jit(solution)/shard_map/ppermute | solution.py:742
  34.8 5.9 %collective-permute-start.7 = (bf16[104,1024]{1,0:T(8,128)(2,1)S(1)}, bf16[104,1024]{1,0:T(8,128)(2,1)S(1)}, u32[]{:S(2)}, u32[]{:S(2)}) collective-permute-start(bf16[104,1024]{1,0:T(8,128)(2,1)S(1)} %shard_map.117.refs_0_), channel_id=1, source_target_pairs={{0,8},{4,12},{8,0},{12,4},{1,9},{5,13},{9,1},{13,5},{2,10},{6,14},... | collective-permute-start | bytes 638984 | tf_op jit(solution)/shard_map/ppermute | solution.py:28
  37.1 7.7 %collective-permute-start.8 = (bf16[104,1024]{1,0:T(8,128)(2,1)S(1)}, bf16[104,1024]{1,0:T(8,128)(2,1)S(1)}, u32[]{:S(2)}, u32[]{:S(2)}) collective-permute-start(bf16[104,1024]{1,0:T(8,128)(2,1)S(1)} %shard_map.117.refs_0_), channel_id=1, source_target_pairs={{0,4},{4,0},{8,12},{12,8},{1,5},{5,1},{9,13},{13,9},{2,6},{6,2},{1... | collective-permute-start | bytes 638984 | tf_op jit(solution)/shard_map/ppermute | solution.py:28
  40.7 4.1 %collective-permute-start.9 = (bf16[104,1024]{1,0:T(8,128)(2,1)S(1)}, bf16[104,1024]{1,0:T(8,128)(2,1)S(1)}, u32[]{:S(2)}, u32[]{:S(2)}) collective-permute-start(bf16[104,1024]{1,0:T(8,128)(2,1)S(1)} %collective-permute-done.7.refs_1_), channel_id=1, source_target_pairs={{0,4},{4,0},{8,12},{12,8},{1,5},{5,1},{9,13},{13,9},{2,6},{6,2},{1... | collective-permute-start | bytes 638984 | tf_op jit(solution)/shard_map/ppermute | solution.py:28
  46.9 9.6 %collective-permute-start.10 = (bf16[104,1024]{1,0:T(8,128)(2,1)S(1)}, bf16[104,1024]{1,0:T(8,128)(2,1)S(1)}, u32[]{:S(2)}, u32[]{:S(2)}) collective-permute-start(bf16[104,1024]{1,0:T(8,128)(2,1)S(1)} %get-tuple-element.49), channel_id=1, source_target_pairs={{0,1},{1,2},{2,3},{4,5},{5,6},{6,7},{8,9},{9,10},{10,11},{12,13},{... | collective-permute-start | bytes 638984 | tf_op jit(solution)/shard_map/ppermute | solution.py:23

commit v4 on v3

--- a/solution.py
+++ b/solution.py
@@ -28,13 +28,12 @@
     return lax.ppermute(block, axis, [(i, i ^ bit) for i in range(count)])
 
 
-def run(body, outs, ins, scratch, micros=1.0, scalars=1, limit=16):
-    smem = pl.BlockSpec(memory_space=pltpu.SMEM)
+def run(body, outs, ins, scratch, micros=1.0, limit=16):
     vmem = pl.BlockSpec(memory_space=pltpu.VMEM)
     return pl.pallas_call(
         body,
         out_shape=outs,
-        in_specs=[smem] * scalars + [vmem] * (len(ins) - scalars),
+        in_specs=[vmem] * len(ins),
         out_specs=[vmem] * len(outs),
         scratch_shapes=scratch,
         cost_estimate=pl.CostEstimate(
@@ -44,9 +43,28 @@
     )(*ins)
 
 
-def slot_at(who_ref, at_ref, j, sects, rows, cols):
-    reader = jnp.bitwise_xor(who_ref[0], j) * sects + who_ref[1]
-    return at_ref[0, reader] - who_ref[0] * rows, at_ref[1, reader] - who_ref[1] * cols
+def here():
+    return lax.axis_index("band"), lax.axis_index("sect")
+
+
+def slots_at(at_ref, readers, sects, rows, cols):
+    band, sect = here()
+    count = at_ref.shape[1]
+    bits = (cols * sects - 1).bit_length()
+    both = jnp.left_shift(at_ref[0:1, :], bits) + at_ref[1:2, :]
+    lane = lane_index((1, count))
+    found = []
+    for reader in readers:
+        mine = lane == reader * sects + sect
+        code = jnp.sum(jnp.where(mine, both, 0).astype(FULL)).astype(jnp.int32)
+        row, col = jnp.right_shift(code, bits), jnp.bitwise_and(code, (1 << bits) - 1)
+        found.append((row - band * rows, col - sect * cols))
+    return found
+
+
+def slot_anchors(at_ref, slots, sects, rows, cols):
+    band, _ = here()
+    return slots_at(at_ref, [jnp.bitwise_xor(band, j) for j in slots], sects, rows, cols)
 
 
 def like(shape, dtype=HALF):
@@ -64,13 +82,13 @@
     return jnp.swapaxes(flat[...], 0, 1)
 
 
-def pack(who, state):
+def pack(state):
     channels, rows, cols = state.shape
     padded = -(-channels // 8) * 8
     deep = -(-padded // 16) * 16
     span = -(-rows * REACH // LANES)
 
-    def body(who_ref, state_ref, right_ref, left_ref, rows_ref, flat):
+    def body(state_ref, right_ref, left_ref, rows_ref, flat):
         turned = turn_rows(state_ref, flat)
         rows_ref[...] = turned
         lane = lane_index((deep, LANES))
@@ -95,24 +113,22 @@
     return run(
         body,
         [like((padded, span * LANES)), like((padded, LANES)), like((rows, deep, cols))],
-        [who, state],
+        [state],
         [pltpu.VMEM((deep, rows, cols), HALF)],
         micros=1.0,
     )
 
 
-def prep(who, anchor, weights, biases, noise, bands, sects, rows, cols):
+def prep(weights, biases, noise):
     steps, channels, cells = noise.shape
     count = len(weights)
     tile_rows = LANES // SIDE
     lines = len(biases)
-    width = cols + LANES
-
-    def body(who_ref, at_ref, *refs):
+
+    def body(*refs):
         ins, lines_in, noise_ref = refs[:count], refs[count : count + lines], refs[count + lines]
         outs = refs[count + lines + 1 :]
         lines_out, noise_out = outs[count : count + lines], outs[count + lines]
-        pick_ref, place_ref = outs[count + lines + 1 :]
         for k, (w_ref, o_ref) in enumerate(zip(ins, outs)):
             _, down, across = w_ref.shape
             o_ref[...] = jnp.zeros(o_ref.shape, HALF)
@@ -138,14 +154,28 @@
                     noise_out[
                         k, r // 2 * SIDE : (r // 2 + 1) * SIDE, r % 2 * LANES : (r % 2 + 1) * LANES
                     ] = block[m * SIDE : (m + 1) * SIDE]
+
+    sizes = [(12 * LANES, 2 * LANES), (2 * LANES, 12 * LANES)]
+    made = [like(sizes[k % 2]) for k in range(count)]
+    made += [like((line.shape[0], 2 * LANES), FULL) for line in biases]
+    made += [like((steps, cells // 2, 2 * LANES))]
+    out = run(body, made, [*weights, *biases, noise], [], micros=1.5)
+    return out[:count], out[count : count + lines], out[count + lines]
+
+
+def picks(anchor, bands, sects, rows, cols):
+    width = cols + LANES
+    tile_rows = LANES // SIDE
+
+    def body(at_ref, pick_ref, place_ref):
         source = lax.broadcasted_iota(jnp.int32, (width, LANES), 0)
         inner = lane_index((width, LANES))
         for _ in range(1, PER_TILE):
             inner = jnp.where(inner >= WIDE, inner - WIDE, inner)
         cell = lax.broadcasted_iota(jnp.int32, (LANES, 2 * LANES), 0)
         target = lane_index((LANES, 2 * LANES))
-        for j in range(bands):
-            row0, col0 = slot_at(who_ref, at_ref, j, sects, rows, cols)
+        anchors = slot_anchors(at_ref, range(bands), sects, rows, cols)
+        for j, (row0, col0) in enumerate(anchors):
             want = jnp.bitwise_and(inner + (col0 - 2), width - 1)
             pick_ref[:, j * LANES : (j + 1) * LANES] = jnp.where(source == want, 1.0, 0.0).astype(HALF)
             across = jnp.bitwise_and(cell, SIDE - 1) + col0
@@ -155,20 +185,20 @@
                 hit = (target == there) & (cell >= turn * SIDE) & (cell < (turn + 1) * SIDE)
                 place_ref[m, j * LANES : (j + 1) * LANES] = jnp.where(hit, 1.0, 0.0).astype(HALF)
 
-    sizes = [(12 * LANES, 2 * LANES), (2 * LANES, 12 * LANES)]
-    made = [like(sizes[k % 2]) for k in range(count)]
-    made += [like((line.shape[0], 2 * LANES), FULL) for line in biases]
-    made += [like((steps, cells // 2, 2 * LANES))]
-    made += [like((width, bands * LANES)), like((tile_rows, bands * LANES, 2 * LANES))]
-    out = run(body, made, [who, anchor, *weights, *biases, noise], [], micros=2.5, scalars=2)
-    return out[:count], out[count : count + lines], *out[count + lines :]
+    return run(
+        body,
+        [like((width, bands * LANES)), like((tile_rows, bands * LANES, 2 * LANES))],
+        [anchor],
+        [],
+        micros=1.0,
+    )
 
 
 def add_parts(kept, got):
     def body(kept_ref, got_ref, out_ref):
         out_ref[...] = kept_ref[...] + got_ref[...]
 
-    return run(body, [like(kept.shape)], [kept, got], [], micros=0.3, scalars=0)[0]
+    return run(body, [like(kept.shape)], [kept, got], [], micros=0.3)[0]
 
 
 def window_tile(picked, t, row0, rows, padded, lanes):
@@ -202,15 +232,16 @@
     lax.fori_loop(0, rows // chunk, select, 0)
 
 
-def extract_own(who, anchor, turned, pick, padded, bands, sects):
+def extract_own(anchor, turned, pick, padded, bands, sects):
     rows, deep, cols = turned.shape
     groups, size = batches(bands)
 
-    def body(who_ref, at_ref, rows_ref, pick_ref, out_ref, picked):
+    def body(at_ref, rows_ref, pick_ref, out_ref, picked):
+        anchors = slot_anchors(at_ref, range(bands), sects, rows, cols)
         for group in groups:
             select_rows(rows_ref, pick_ref[:cols, group[0] * LANES : (group[-1] + 1) * LANES], picked)
             for j in group:
-                row0 = slot_at(who_ref, at_ref, j, sects, rows, cols)[0] - 2
+                row0 = anchors[j][0] - 2
                 inside = (row0 > -WIDE) & (row0 < rows)
 
                 @pl.when(inside)
@@ -227,19 +258,18 @@
     return run(
         body,
         [like((bands, padded, TILES * LANES))],
-        [who, anchor, turned, pick],
+        [anchor, turned, pick],
         [pltpu.VMEM((rows, deep, size * LANES), FULL)],
-        micros=1.5,
-        scalars=2,
+        micros=1.5
     )[0]
 
 
-def extract_rim(who, anchor, parts, turned, right, left, pick, bands, sects):
+def extract_rim(anchor, parts, turned, right, left, pick, bands, sects):
     rows, deep, cols = turned.shape
     padded = right.shape[0]
     groups, size = batches(bands)
 
-    def body(who_ref, at_ref, part_ref, rows_ref, right_ref, left_ref, pick_ref,
+    def body(at_ref, part_ref, rows_ref, right_ref, left_ref, pick_ref,
              own_ref, low_ref, odd_ref, high_ref, near_ref, cross_ref, ext, picked):
         lane = lane_index((padded, LANES))
         none = jnp.zeros((padded, LANES), HALF)
@@ -262,7 +292,7 @@
         outer = (0, 1, rows - 2, rows - 1)
         for r in outer:
             expand(r)
-        even = jnp.bitwise_and(who_ref[0], 1) == 0
+        even = jnp.bitwise_and(here()[0], 1) == 0
         for k in range(2):
             top, low = k, rows - 2 + k
             near_ref[k, :, :cols] = jnp.where(even, rows_ref[low], rows_ref[top])
@@ -276,8 +306,8 @@
             return (low_ref, high_ref)[j % 2], j // 2 - 1
 
         crossing = []
-        for j in range(bands):
-            row0, col0 = slot_at(who_ref, at_ref, j, sects, rows, cols)
+        anchors = slot_anchors(at_ref, range(bands), sects, rows, cols)
+        for j, (row0, col0) in enumerate(anchors):
             row0 = row0 - 2
             inside = (row0 > -WIDE) & (row0 < rows)
             over = inside & ((col0 < 2) | (col0 > cols - REACH))
@@ -318,10 +348,9 @@
     return run(
         body,
         [one, rest, one, rest, edge, edge],
-        [who, anchor, parts, turned, right, left, pick],
+        [anchor, parts, turned, right, left, pick],
         [pltpu.VMEM((rows, deep, LANES), HALF), pltpu.VMEM((rows, deep, size * LANES), FULL)],
-        micros=1.5,
-        scalars=2,
+        micros=1.5
     )
 
 
@@ -344,19 +373,20 @@
     return value / (1.0 + jnp.exp(-value))
 
 
-def patch_step(who, anchor, addends, noise, weights, biases, step_bias, sects, limits):
+def patch_step(anchor, addends, noise, weights, biases, step_bias, sects, limits):
     padded = addends[0].shape[1]
     steps = noise.shape[0]
     half = SIDE // 2
     loose = 48
 
     def body(*refs):
-        who_ref, at_ref = refs[:2]
-        parts = refs[2 : 2 + len(addends)]
-        mine = who_ref[0] * sects + who_ref[1]
-        row0, col0 = at_ref[0, mine], at_ref[1, mine]
+        at_ref, parts = refs[0], refs[1 : 1 + len(addends)]
+        band, sect = here()
+        mine = lane_index(at_ref.shape) == band * sects + sect
+        at = jnp.sum(jnp.where(mine, at_ref[...], 0).astype(FULL), axis=1, keepdims=True)
+        row0, col0 = at.astype(jnp.int32)[0:1][None], at.astype(jnp.int32)[1:2][None]
         (noise_ref, w_in, w_out, d_in, d_out, b_in, b_out, b_step, b_den, out_ref,
-         flat, state_sh, hid, hid_sh, pad, pad_sh, corr, state) = refs[2 + len(addends) :]
+         flat, state_sh, hid, hid_sh, pad, pad_sh, corr, state) = refs[1 + len(addends) :]
         for t in range(TILES):
             lanes = slice(t * LANES, (t + 1) * LANES)
             tile = parts[0][0, :, lanes].astype(FULL)
@@ -394,7 +424,7 @@
         state[...] = mean + noise_ref[0].astype(FULL)
         pad[...] = jnp.zeros(pad.shape, FULL)
         deal = half // CHUNKS
-        trips = jnp.where(who_ref[0] >= 0, CHUNKS, 0)
+        trips = jnp.where(band >= 0, CHUNKS, 0)
 
         def fill(source, first, count):
             shaped = source.reshape(count, SIDE, 2 * LANES)
@@ -438,7 +468,7 @@
     return run(
         body,
         [like((padded, SIDE * SIDE))],
-        [who, anchor, *addends, noise, *weights, *biases[:2], step_bias, biases[2]],
+        [anchor, *addends, noise, *weights, *biases[:2], step_bias, biases[2]],
         [
             pltpu.VMEM((TILES * LANES, LANES), FULL),
             pltpu.VMEM((3, WIDE // 2, 2, loose, LANES), HALF),
@@ -449,8 +479,7 @@
             pltpu.VMEM((half, 2, SIDE, LANES), FULL),
             pltpu.VMEM((half * SIDE, 2 * LANES), FULL),
         ],
-        micros=8.0,
-        scalars=2,
+        micros=8.0
     )[0]
 
 
@@ -493,12 +522,11 @@
             pltpu.VMEM((LANES, LANES), FULL),
             pltpu.VMEM((2, loose + 8, LANES), FULL),
         ],
-        micros=2.5,
-        scalars=0,
+        micros=2.5
     )[0]
 
 
-def grid_mean(who, shifted, near, cross, lower, padded, weights, biases, limits):
+def grid_mean(shifted, near, cross, lower, padded, weights, biases, limits):
     rows = 2 * shifted.shape[1]
     _, deep, width = near.shape
     cols = width - LANES
@@ -511,10 +539,11 @@
     state_pairs = hidden_pairs + 1
     base = rows - made - 2 if lower else -2
 
-    def body(who_ref, shifted_ref, near_ref, cross_ref, w_in, w_out, b_in, b_out, out_ref,
+    def body(shifted_ref, near_ref, cross_ref, w_in, w_out, b_in, b_out, out_ref,
              line, state_sh, hid, hid_sh):
-        row0 = who_ref[0] * rows + base + 1
-        col0 = who_ref[1] * cols - 1
+        band, sect = here()
+        row0 = band * rows + base + 1
+        col0 = sect * cols - 1
 
         for pair in range(made // 2 + 2, state_pairs):
             for b in range(3):
@@ -525,7 +554,7 @@
         at = (rows - made) // 2 - 1 if lower else 0
         for b in range(3):
             state_sh[b, skip : skip + given] = shifted_ref[b, at : at + given]
-        pair = jnp.bitwise_and(who_ref[0], 1) == (0 if lower else 1)
+        pair = jnp.bitwise_and(band, 1) == (0 if lower else 1)
         for v in range(2):
             rim = jnp.where(pair, near_ref[v], cross_ref[v])
             value = jnp.concatenate(
@@ -575,7 +604,7 @@
     return run(
         body,
         [like((made, padded, cols))],
-        [who, shifted, near, cross, *weights, *biases],
+        [shifted, near, cross, *weights, *biases],
         [
             pltpu.VMEM((2, loose + 8, LANES), FULL),
             pltpu.VMEM((3, state_pairs, 2, loose, LANES), HALF),
@@ -586,7 +615,7 @@
     )[0]
 
 
-def canvas(who, anchor, pieces, sources, place, sects, rows, cols):
+def canvas(anchor, pieces, sources, place, sects, rows, cols):
     padded = pieces[0].shape[-2]
     deep = -(-padded // 16) * 16
     total = anchor.shape[1]
@@ -594,12 +623,13 @@
     tile_rows = LANES // SIDE
     groups = rows // tile_rows
 
-    def body(who_ref, at_ref, *refs):
+    def body(at_ref, *refs):
+        band, sect = here()
         place_ref, spill_ref, out_ref, inverse_ref, view = refs[slots:]
         none = jnp.zeros((padded, LANES), HALF)
-        for piece, j in zip(refs, sources):
+        anchors = slot_anchors(at_ref, sources, sects, rows, cols)
+        for piece, j, (row0, _) in zip(refs, sources, anchors):
             lanes = slice(j * LANES, (j + 1) * LANES)
-            row0 = slot_at(who_ref, at_ref, j, sects, rows, cols)[0]
             for r in range(rows):
                 i = r - row0
                 tile = jnp.clip(jnp.right_shift(i, tile_rows.bit_length() - 1), 0, SIDE // tile_rows - 1)
@@ -623,15 +653,12 @@
             spilled = part if spilled is None else spilled + part
         for k in range(groups):
             spill_ref[:, k * LANES : (k + 1) * LANES] = spilled[k].astype(HALF)
-        row = lax.broadcasted_iota(jnp.int32, (rows, cols), 0) + who_ref[0] * rows
-        col = lane_index((rows, cols)) + who_ref[1] * cols
-
-        def cover(p, count):
-            down, across = row - at_ref[0, p], col - at_ref[1, p]
-            hit = (down >= 0) & (down < SIDE) & (across >= 0) & (across < SIDE)
-            return count + jnp.where(hit, 1.0, 0.0)
-
-        count = lax.fori_loop(0, total, cover, jnp.zeros((rows, cols), FULL))
+        tall, wide = (rows, total), (total, cols)
+        down = lax.broadcasted_iota(jnp.int32, tall, 0) + band * rows - at_ref[0:1, :]
+        across = lane_index(wide) + sect * cols - at_ref[1:2, :].astype(FULL).T.astype(jnp.int32)
+        down = jnp.where((down >= 0) & (down < SIDE), 1.0, 0.0)
+        across = jnp.where((across >= 0) & (across < SIDE), 1.0, 0.0)
+        count = jnp.dot(down.astype(HALF), across.astype(HALF), preferred_element_type=FULL)
         inverse_ref[...] = 1.0 / jnp.maximum(count, 1.0)
 
     return run(
@@ -641,10 +668,9 @@
             like((rows, padded, cols), FULL),
             like((rows, cols), FULL),
         ],
-        [who, anchor, *pieces, place],
+        [anchor, *pieces, place],
         [pltpu.VMEM((tile_rows, groups, deep, slots * LANES), HALF)],
-        micros=1.5,
-        scalars=2,
+        micros=1.5
     )
 
 
@@ -673,8 +699,7 @@
         [like((channels, rows, cols))],
         [*means, summed, arrived, inverse],
         [pltpu.VMEM((rows, deep, cols), HALF)],
-        micros=3.0,
-        scalars=0,
+        micros=3.0
     )[0]
 
 
@@ -695,17 +720,14 @@
     sects = lax.axis_size("sect")
     channels, rows, cols = state_field.shape
     limits = (rows * bands, cols * sects)
-    who = jnp.stack([lax.axis_index("band"), lax.axis_index("sect")]).astype(jnp.int32)
 
     anchor = patch_anchor.T
 
-    right_rim, left_rim, turned = pack(who, state_field)
+    right_rim, left_rim, turned = pack(state_field)
     right = shift_from(right_rim, "sect", -1)
     left = shift_from(left_rim, "sect", 1)
 
-    made, lines, noise, pick, place = prep(
-        who,
-        anchor,
+    made, lines, noise = prep(
         [
             conv_in_weight.transpose(0, 2, 1),
             conv_out_weight,
@@ -714,17 +736,14 @@
         ],
         [conv_in_bias[None, :], conv_out_bias[None, :], denoise_bias[None, :], step_bias],
         patch_noise[0],
-        bands,
-        sects,
-        rows,
-        cols,
     )
     biases, step_lines = lines[:3], lines[3]
 
     padded = right_rim.shape[0]
-    parts = extract_own(who, anchor, turned, pick, padded, bands, sects)
+    pick, place = picks(anchor, bands, sects, rows, cols)
+    parts = extract_own(anchor, turned, pick, padded, bands, sects)
     own, kept, own_sent, sent, edge_near, edge_cross = extract_rim(
-        who, anchor, parts, turned, right, left, pick, bands, sects
+        anchor, parts, turned, right, left, pick, bands, sects
     )
     addends = [own]
     if bands > 2:
@@ -740,7 +759,9 @@
     rim_near = swap(edge_near, "band", 1)
     steps = [(i, i + 1) for i in range(1, bands - 1, 2)]
     rim_cross = lax.ppermute(edge_cross, "band", steps + [(j, i) for i, j in steps])
-    correction = patch_step(who, anchor, addends, noise, made, biases, step_lines, sects, limits)
+    correction = patch_step(
+        anchor, addends, noise, made, biases, step_lines, sects, limits
+    )
     pieces = [correction]
     sources = [0]
     bit = bands // 2
@@ -753,10 +774,10 @@
         bit //= 2
 
     shifted = spread(turned, right, left)
-    top_mean = grid_mean(who, shifted, rim_near, rim_cross, False, padded, made[:2], biases[:2], limits)
-    low_mean = grid_mean(who, shifted, rim_near, rim_cross, True, padded, made[:2], biases[:2], limits)
+    top_mean = grid_mean(shifted, rim_near, rim_cross, False, padded, made[:2], biases[:2], limits)
+    low_mean = grid_mean(shifted, rim_near, rim_cross, True, padded, made[:2], biases[:2], limits)
     spilled, summed, inverse = canvas(
-        who, anchor, pieces, sources, place, sects, rows, cols
+        anchor, pieces, sources, place, sects, rows, cols
     )
     arrived = shift_from(spilled, "sect", 1)
     return finish([top_mean, low_mean], summed, arrived, inverse, channels)

time: 58.4 us -> 54.4 us (0.932)
  Pallas kernels: 29.3 us -> 25.2 us
    pallas_call x11 -> x12, Pallas kernels: 29.3 us -> 25.2 us  [run(): pl.pallas_call(body, out_shape=outs, in_specs=[vmem] * len(ins), out_spec...]
    ppermute x3, waiting for transfers between devices: 3.62 us -> 4.57 us  [shift_from(): return lax.ppermute(block, axis, route)]
    ppermute x7, waiting for transfers between devices: 11 us -> 10.2 us  [swap(): return lax.ppermute(block, axis, [(i, i ^ bit) for i in range(count)])]
  transfers between devices with their start and end apart: 11 -> 11, of which waited for: 4 -> 5; matrix products, arithmetic and copies ran while one was open for 0% -> 0% of each run, Pallas kernels for 36% -> 34%
where the time goes in v4:
time: 54.4 us; the launch traced here: 54.2 us
  Pallas kernels  25.2 us (46%)
  waiting for transfers between devices  14.7 us (27%)
  starting transfers between devices  12.6 us (23%)
  local copies, waits for them, and re-layouts  1.28 us (2%)
    pallas_call x12, Pallas kernels, run(): pl.pallas_call(body, out_shape=outs, in_specs=[vmem] * len(ins), out_spec...  25.2 us
    ppermute x7, waiting for transfers between devices, swap(): return lax.ppermute(block, axis, [(i, i ^ bit) for i in range(count)])  10.2 us
    ppermute x3, starting transfers between devices, shift_from(): return lax.ppermute(block, axis, route)  7.77 us
    ppermute x3, waiting for transfers between devices, shift_from(): return lax.ppermute(block, axis, route)  4.57 us
    ppermute x1, starting transfers between devices, step(): lax.ppermute(edge_cross, 'band', steps + [(j, i) for i, j in steps])  3.88 us
    unnamed x23, local copies, waits for them, and re-layouts  1.28 us
  transfers between devices with their start and end apart: 11, of which 5 were waited for; matrix products, arithmetic and copies ran while one was open for 0% of the time, Pallas kernels for 34%

profile of v4, /device:TPU:18, one launch (start us, length us, event | category | flops | bytes accessed | tf_op | source)
XLA Modules:
  0.0 54.2 jit_solution(10543723522288429851)
XLA Ops:
  0.0 1.1 %copy-done = bf16[99,32,128]{2,1,0:T(8,128)(2,1)S(1)} copy-done((bf16[99,32,128]{2,1,0:T(8,128)(2,1)S(1)}, bf16[99,32,128]{2,1,0:T(8,128)(2,1)}, u32[]{:S(2)}) %copy-start) | copy-done | bytes 811032
  1.1 0.7 %shard_map.109 = (bf16[104,1152]{1,0:T(8,128)(2,1)S(1)}, bf16[104,128]{1,0:T(8,128)(2,1)S(1)}, bf16[32,112,128]{2,1,0:T(8,128)(2,1)S(1)}) custom-call(bf16[99,32,128]{2,1,0:T(8,128)(2,1)S(1)} %copy-done), custom_call_target="tpu_custom_call" | custom-call | flops 1150000000 | bytes 1024 | tf_op jit(solution)/shard_map/pallas_call | solution.py:33
  1.9 2.4 %collective-permute-start = (bf16[104,1152]{1,0:T(8,128)(2,1)S(1)}, bf16[104,1152]{1,0:T(8,128)(2,1)S(1)}, u32[]{:S(2)}, u32[]{:S(2)}) collective-permute-start(bf16[104,1152]{1,0:T(8,128)(2,1)S(1)} %get-tuple-element.29), channel_id=1, source_target_pairs={{1,0},{2,1},{3,2},{5,4},{6,5},{7,6},{9,8},{10,9},{11,10},{13,12},{... | collective-permute-start | bytes 718856 | tf_op jit(solution)/shard_map/ppermute | solution.py:23
  4.2 3.5 %collective-permute-start.1 = (bf16[104,128]{1,0:T(8,128)(2,1)S(1)}, bf16[104,128]{1,0:T(8,128)(2,1)S(1)}, u32[]{:S(2)}, u32[]{:S(2)}) collective-permute-start(bf16[104,128]{1,0:T(8,128)(2,1)S(1)} %get-tuple-element.30), channel_id=1, source_target_pairs={{0,1},{1,2},{2,3},{4,5},{5,6},{6,7},{8,9},{9,10},{10,11},{12,13},{... | collective-permute-start | bytes 79880 | tf_op jit(solution)/shard_map/ppermute | solution.py:23
  7.8 0.0 copy-done.6
  7.8 0.9 %shard_map.111 = (bf16[256,512]{1,0:T(8,128)(2,1)S(1)}, bf16[4,512,256]{2,1,0:T(8,128)(2,1)S(1)}) custom-call(s32[2,16]{1,0:T(2,128)S(1)} %bitcast.12), custom_call_target="tpu_custom_call" | custom-call | flops 1150000000 | bytes 1024 | tf_op jit(solution)/shard_map/pallas_call | solution.py:33
  8.7 2.2 %shard_map.112.part_ref = bf16[4,104,1536]{2,1,0:T(8,128)(2,1)S(1)} custom-call(s32[2,16]{1,0:T(2,128)S(1)} %bitcast.13, bf16[32,112,128]{2,1,0:T(8,128)(2,1)S(1)} %get-tuple-element.28.rows_ref, bf16[256,512]{1,0:T(8,128)(2,1)S(1)} %get-tuple-element.31.pick_ref), custom_call_target="tpu_custom_call" | custom-call | flops 1724999936 | bytes 1024 | tf_op jit(solution)/shard_map/pallas_call | solution.py:33
  10.9 0.0 copy-start.10
  10.9 0.0 collective-permute-done.1.left_ref
  10.9 0.4 collective-permute-done.right_ref
  11.3 2.8 %shard_map.113 = (bf16[1,104,1536]{2,1,0:T(8,128)(2,1)S(1)}, bf16[1,104,1536]{2,1,0:T(8,128)(2,1)S(1)}, bf16[1,104,1536]{2,1,0:T(8,128)(2,1)S(1)}, bf16[1,104,15...) custom-call(s32[2,16]{1,0:T(2,128)S(1)} %bitcast.14, ...), custom_call_target="tpu_custom_call" | custom-call | flops 1724999936 | bytes 1024 | tf_op jit(solution)/shard_map/pallas_call | solution.py:33
  14.2 0.0 copy-start.1
  14.2 0.0 copy-start.2
  14.2 0.0 copy-start.3
  14.2 0.0 copy-start.4
  14.2 0.0 copy-start.5
  14.2 0.0 copy-start.7
  14.2 0.0 copy-start.8
  14.3 0.0 copy-start.9
  14.3 0.1 collective-permute-start.4
  14.3 0.5 collective-permute-start.6
  14.8 1.1 %collective-permute-done.4.got_ref = bf16[1,104,1536]{2,1,0:T(8,128)(2,1)S(1)} collective-permute-done((bf16[1,104,1536]{2,1,0:T(8,128)(2,1)S(1)}, bf16[1,104,1536]{2,1,0:T(8,128)(2,1)S(1)}, u32[]{:S(2)}, u32[]{:S(2)}) %collective-permute-start.4) | collective-permute-done | bytes 319520 | tf_op jit(solution)/shard_map/ppermute | solution.py:28
  16.0 0.1 collective-permute-start.5
  16.1 0.0 copy-done.10
  16.1 0.1 copy.14
  16.2 0.0 copy-done.1
  16.2 0.0 copy-done.2
  16.2 0.6 %shard_map.114 = (bf16[1536,256]{1,0:T(8,128)(2,1)S(1)}, bf16[256,1536]{1,0:T(8,128)(2,1)S(1)}, bf16[1536,256]{1,0:T(8,128)(2,1)S(1)}, bf16[256,1536]{1,0:T(8,12...) custom-call(bf16[9,99,128]{2,1,0:T(8,128)(2,1)S(1)} %bitcast.10, ...), custom_call_target="tpu_custom_call" | custom-call | flops 1724999936 | bytes 1024 | tf_op jit(solution)/shard_map/pallas_call | solution.py:33
  16.9 0.2 collective-permute-start.2
  17.1 3.9 %collective-permute-start.3 = (bf16[2,112,256]{2,1,0:T(8,128)(2,1)S(1)}, bf16[2,112,256]{2,1,0:T(8,128)(2,1)S(1)}, u32[]{:S(2)}, u32[]{:S(2)}) collective-permute-start(bf16[2,112,256]{2,1,0:T(8,128)(2,1)S(1)} %get-tuple-element.33), channel_id=1, source_target_pairs={{4,8},{8,4},{5,9},{9,5},{6,10},{10,6},{7,11},{11,7},{20,24},{24,20... | collective-permute-start | bytes 344072 | tf_op jit(solution)/shard_map/ppermute | solution.py:761
  21.0 0.0 collective-permute-done.6.refs_3_
  21.0 5.5 %collective-permute-done.5.refs_2_ = bf16[1,104,1536]{2,1,0:T(8,128)(2,1)S(1)} collective-permute-done((bf16[1,104,1536]{2,1,0:T(8,128)(2,1)S(1)}, bf16[1,104,1536]{2,1,0:T(8,128)(2,1)S(1)}, u32[]{:S(2)}, u32[]{:S(2)}) %collective-permute-start.5) | collective-permute-done | bytes 319520 | tf_op jit(solution)/shard_map/ppermute | solution.py:28
  26.5 5.4 %shard_map.118.refs_0_ = bf16[104,1024]{1,0:T(8,128)(2,1)S(1)} custom-call(s32[2,16]{1,0:T(2,128)S(1)} %bitcast.15, bf16[1,104,1536]{2,1,0:T(8,128)(2,1)S(1)} %get-tuple-element.38.refs_1_, bf16[1,104,1536]{2,1,0:T(8,128)(2,1)S(1)} %collective-permute-done.5.refs_2_, bf16[1,104,1536]{2,1,0:T(8,128)(2,1)S(1)} %collective-permute-done.6.refs_3_, ...), custom_call_target="tpu_custom_call" | custom-call | flops 9200000000 | bytes 1024 | tf_op jit(solution)/shard_map/pallas_call | solution.py:33
  31.9 0.1 collective-permute-start.7
  32.0 2.2 %shard_map.110.shifted_ref = bf16[3,16,2,144,128]{4,3,2,1,0:T(8,128)(2,1)S(1)} custom-call(bf16[32,112,128]{2,1,0:T(8,128)(2,1)S(1)} %get-tuple-element.28.rows_ref, bf16[104,1152]{1,0:T(8,128)(2,1)S(1)} %collective-permute-done.right_ref, bf16[104,128]{1,0:T(8,128)(2,1)S(1)} %collective-permute-done.1.left_ref), custom_call_target="tpu_custom_call" | custom-call | flops 2875000064 | bytes 1024 | tf_op jit(solution)/shard_map/pallas_call | solution.py:33
  34.1 0.1 collective-permute-start.8
  34.2 3.6 %collective-permute-done.7.refs_1_ = bf16[104,1024]{1,0:T(8,128)(2,1)S(1)} collective-permute-done((bf16[104,1024]{1,0:T(8,128)(2,1)S(1)}, bf16[104,1024]{1,0:T(8,128)(2,1)S(1)}, u32[]{:S(2)}, u32[]{:S(2)}) %collective-permute-start.7) | collective-permute-done | bytes 213024 | tf_op jit(solution)/shard_map/ppermute | solution.py:28
  37.8 0.0 collective-permute-start.9
  37.8 0.0 collective-permute-done.2.near_ref
  37.8 0.0 collective-permute-done.3.cross_ref
  37.8 3.5 %shard_map.116.low_ref = bf16[16,104,128]{2,1,0:T(8,128)(2,1)S(1)} custom-call(bf16[3,16,2,144,128]{4,3,2,1,0:T(8,128)(2,1)S(1)} %shard_map.110.shifted_ref, bf16[2,112,256]{2,1,0:T(8,128)(2,1)S(1)} %collective-permute-done.2.near_ref, bf16[2,112,256]{2,1,0:T(8,128)(2,1)S(1)} %collective-permute-done.3.cross_ref, ...), custom_call_target="tpu_custom_call" | custom-call | flops 4024999936 | bytes 1024 | tf_op jit(solution)/shard_map/pallas_call | solution.py:33
  41.3 0.0 collective-permute-done.8.refs_2_
  41.3 0.0 collective-permute-done.9.refs_3_
  41.3 1.6 %shard_map.119 = (bf16[104,1024]{1,0:T(8,128)(2,1)S(1)}, f32[32,104,128]{2,1,0:T(8,128)S(1)}, f32[32,128]{1,0:T(8,128)S(1)}) custom-call(s32[2,16]{1,0:T(2,128)S(1)} %bitcast.16, bf16[104,1024]{1,0:T(8,128)(2,1)S(1)} %shard_map.118.refs_0_, bf16[104,1024]{1,0:T(8,128)(2,1)S(1)} %collective-permute-done.7.refs_1_, ...), custom_call_target="tpu_custom_call" | custom-call | flops 1724999936 | bytes 1024 | tf_op jit(solution)/shard_map/pallas_call | solution.py:33
  43.0 1.9 %collective-permute-start.10 = (bf16[104,1024]{1,0:T(8,128)(2,1)S(1)}, bf16[104,1024]{1,0:T(8,128)(2,1)S(1)}, u32[]{:S(2)}, u32[]{:S(2)}) collective-permute-start(bf16[104,1024]{1,0:T(8,128)(2,1)S(1)} %get-tuple-element.49), channel_id=1, source_target_pairs={{0,1},{1,2},{2,3},{4,5},{5,6},{6,7},{8,9},{9,10},{10,11},{12,13},{... | collective-permute-start | bytes 638984 | tf_op jit(solution)/shard_map/ppermute | solution.py:23
  44.9 3.5 %shard_map.115.top_ref = bf16[16,104,128]{2,1,0:T(8,128)(2,1)S(1)} custom-call(bf16[3,16,2,144,128]{4,3,2,1,0:T(8,128)(2,1)S(1)} %shard_map.110.shifted_ref, bf16[2,112,256]{2,1,0:T(8,128)(2,1)S(1)} %collective-permute-done.2.near_ref, bf16[2,112,256]{2,1,0:T(8,128)(2,1)S(1)} %collective-permute-done.3.cross_ref, ...), custom_call_target="tpu_custom_call" | custom-call | flops 4024999936 | bytes 1024 | tf_op jit(solution)/shard_map/pallas_call | solution.py:33
  48.4 4.1 %collective-permute-done.10.spill_ref = bf16[104,1024]{1,0:T(8,128)(2,1)S(1)} collective-permute-done((bf16[104,1024]{1,0:T(8,128)(2,1)S(1)}, bf16[104,1024]{1,0:T(8,128)(2,1)S(1)}, u32[]{:S(2)}, u32[]{:S(2)}) %collective-permute-start.10) | collective-permute-done | bytes 213024 | tf_op jit(solution)/shard_map/ppermute | solution.py:23
  52.5 1.7 %shard_map.120 = bf16[99,32,128]{2,1,0:T(8,128)(2,1)} custom-call(bf16[16,104,128]{2,1,0:T(8,128)(2,1)S(1)} %shard_map.115.top_ref, bf16[16,104,128]{2,1,0:T(8,128)(2,1)S(1)} %shard_map.116.low_ref, f32[32,104,128]{2,1,0:T(8,128)S(1)} %get-tuple-element.48.sum_ref, bf16[104,1024]{1,0:T(8,128)(2,1)S(1)} %collective-permute-done.10.spill_ref, ...), custom_call_target="tpu_custom_call" | custom-call | flops 3449999872 | bytes 1024 | tf_op jit(solution)/shard_map/pallas_call | solution.py:33
  (9 shorter events, 0.0 us)
Async XLA Ops:
  0.0 1.1 %copy-start = (bf16[99,32,128]{2,1,0:T(8,128)(2,1)S(1)}, bf16[99,32,128]{2,1,0:T(8,128)(2,1)}, u32[]{:S(2)}) copy-start(bf16[99,32,128]{2,1,0:T(8,128)(2,1)} %state_ref.1) | copy-start | bytes 2433028
  1.1 6.6 %copy-start.6 = (s32[16,2]{0,1:T(2,128)S(1)}, s32[16,2]{0,1:T(2,128)}, u32[]{:S(2)}) copy-start(s32[16,2]{0,1:T(2,128)} %param.16) | copy-start | bytes 388
  1.9 9.5 %collective-permute-start = (bf16[104,1152]{1,0:T(8,128)(2,1)S(1)}, bf16[104,1152]{1,0:T(8,128)(2,1)S(1)}, u32[]{:S(2)}, u32[]{:S(2)}) collective-permute-start(bf16[104,1152]{1,0:T(8,128)(2,1)S(1)} %get-tuple-element.29), channel_id=1, source_target_pairs={{1,0},{2,1},{3,2},{5,4},{6,5},{7,6},{9,8},{10,9},{11,10},{13,12},{... | collective-permute-start | bytes 718856 | tf_op jit(solution)/shard_map/ppermute | solution.py:23
  4.2 6.6 %collective-permute-start.1 = (bf16[104,128]{1,0:T(8,128)(2,1)S(1)}, bf16[104,128]{1,0:T(8,128)(2,1)S(1)}, u32[]{:S(2)}, u32[]{:S(2)}) collective-permute-start(bf16[104,128]{1,0:T(8,128)(2,1)S(1)} %get-tuple-element.30), channel_id=1, source_target_pairs={{0,1},{1,2},{2,3},{4,5},{5,6},{6,7},{8,9},{9,10},{10,11},{12,13},{... | collective-permute-start | bytes 79880 | tf_op jit(solution)/shard_map/ppermute | solution.py:23
  10.9 5.2 %copy-start.10 = (bf16[1,2,99,1024]{3,1,2,0:T(2,128)(2,1)S(1)}, bf16[1,2,99,1024]{3,1,2,0:T(2,128)(2,1)}, u32[]{:S(2)}) copy-start(bf16[1,2,99,1024]{3,1,2,0:T(2,128)(2,1)} %param.17) | copy-start | bytes 1216516
  14.2 2.0 %copy-start.1 = (bf16[9,128,99]{1,2,0:T(8,128)(2,1)S(1)}, bf16[9,128,99]{1,2,0:T(8,128)(2,1)}, u32[]{:S(2)}) copy-start(bf16[9,128,99]{1,2,0:T(8,128)(2,1)} %param.12) | copy-start | bytes 684292
  14.2 2.0 %copy-start.2 = (bf16[9,99,128]{2,1,0:T(8,128)(2,1)S(1)}, bf16[9,99,128]{2,1,0:T(8,128)(2,1)}, u32[]{:S(2)}) copy-start(bf16[9,99,128]{2,1,0:T(8,128)(2,1)} %refs_1_.1) | copy-start | bytes 684292
  14.2 2.0 %copy-start.3 = (bf16[9,128,99]{1,2,0:T(8,128)(2,1)S(1)}, bf16[9,128,99]{1,2,0:T(8,128)(2,1)}, u32[]{:S(2)}) copy-start(bf16[9,128,99]{1,2,0:T(8,128)(2,1)} %param.18) | copy-start | bytes 684292
  14.2 2.0 %copy-start.4 = (bf16[9,99,128]{2,1,0:T(8,128)(2,1)S(1)}, bf16[9,99,128]{2,1,0:T(8,128)(2,1)}, u32[]{:S(2)}) copy-start(bf16[9,99,128]{2,1,0:T(8,128)(2,1)} %refs_3_.1) | copy-start | bytes 684292
  14.2 2.0 %copy-start.5 = (f32[2,128]{1,0:T(2,128)S(1)}, f32[2,128]{1,0:T(2,128)}, u32[]{:S(2)}) copy-start(f32[2,128]{1,0:T(2,128)} %refs_7_.1) | copy-start | bytes 3076
  14.2 2.0 %copy-start.7 = (f32[128]{0:T(128)S(1)}, f32[128]{0:T(128)}, u32[]{:S(2)}) copy-start(f32[128]{0:T(128)} %param.13) | copy-start | bytes 1540
  14.2 2.0 %copy-start.8 = (f32[99]{0:T(128)S(1)}, f32[99]{0:T(128)}, u32[]{:S(2)}) copy-start(f32[99]{0:T(128)} %param.15) | copy-start | bytes 1192
  14.3 2.0 %copy-start.9 = (f32[99]{0:T(128)S(1)}, f32[99]{0:T(128)}, u32[]{:S(2)}) copy-start(f32[99]{0:T(128)} %param.21) | copy-start | bytes 1192
  14.3 1.7 %collective-permute-start.4 = (bf16[1,104,1536]{2,1,0:T(8,128)(2,1)S(1)}, bf16[1,104,1536]{2,1,0:T(8,128)(2,1)S(1)}, u32[]{:S(2)}, u32[]{:S(2)}) collective-permute-start(bf16[1,104,1536]{2,1,0:T(8,128)(2,1)S(1)} %get-tuple-element.40), channel_id=1, source_target_pairs={{0,4},{4,0},{8,12},{12,8},{1,5},{5,1},{9,13},{13,9},{2,6},{6,2},{1... | collective-permute-start | bytes 958472 | tf_op jit(solution)/shard_map/ppermute | solution.py:28
  14.3 6.6 %collective-permute-start.6 = (bf16[1,104,1536]{2,1,0:T(8,128)(2,1)S(1)}, bf16[1,104,1536]{2,1,0:T(8,128)(2,1)S(1)}, u32[]{:S(2)}, u32[]{:S(2)}) collective-permute-start(bf16[1,104,1536]{2,1,0:T(8,128)(2,1)S(1)} %get-tuple-element.41), channel_id=1, source_target_pairs={{0,4},{4,0},{8,12},{12,8},{1,5},{5,1},{9,13},{13,9},{2,6},{6,2},{1... | collective-permute-start | bytes 958472 | tf_op jit(solution)/shard_map/ppermute | solution.py:28
  16.0 10.5 %collective-permute-start.5 = (bf16[1,104,1536]{2,1,0:T(8,128)(2,1)S(1)}, bf16[1,104,1536]{2,1,0:T(8,128)(2,1)S(1)}, u32[]{:S(2)}, u32[]{:S(2)}) collective-permute-start(bf16[1,104,1536]{2,1,0:T(8,128)(2,1)S(1)} %shard_map.117), channel_id=1, source_target_pairs={{0,8},{4,12},{8,0},{12,4},{1,9},{5,13},{9,1},{13,5},{2,10},{6,14},... | collective-permute-start | bytes 958472 | tf_op jit(solution)/shard_map/ppermute | solution.py:28
  16.9 20.9 %collective-permute-start.2 = (bf16[2,112,256]{2,1,0:T(8,128)(2,1)S(1)}, bf16[2,112,256]{2,1,0:T(8,128)(2,1)S(1)}, u32[]{:S(2)}, u32[]{:S(2)}) collective-permute-start(bf16[2,112,256]{2,1,0:T(8,128)(2,1)S(1)} %get-tuple-element.32), channel_id=1, source_target_pairs={{0,4},{4,0},{8,12},{12,8},{1,5},{5,1},{9,13},{13,9},{2,6},{6,2},{1... | collective-permute-start | bytes 344072 | tf_op jit(solution)/shard_map/ppermute | solution.py:28
  17.1 20.7 %collective-permute-start.3 = (bf16[2,112,256]{2,1,0:T(8,128)(2,1)S(1)}, bf16[2,112,256]{2,1,0:T(8,128)(2,1)S(1)}, u32[]{:S(2)}, u32[]{:S(2)}) collective-permute-start(bf16[2,112,256]{2,1,0:T(8,128)(2,1)S(1)} %get-tuple-element.33), channel_id=1, source_target_pairs={{4,8},{8,4},{5,9},{9,5},{6,10},{10,6},{7,11},{11,7},{20,24},{24,20... | collective-permute-start | bytes 344072 | tf_op jit(solution)/shard_map/ppermute | solution.py:761
  31.9 5.9 %collective-permute-start.7 = (bf16[104,1024]{1,0:T(8,128)(2,1)S(1)}, bf16[104,1024]{1,0:T(8,128)(2,1)S(1)}, u32[]{:S(2)}, u32[]{:S(2)}) collective-permute-start(bf16[104,1024]{1,0:T(8,128)(2,1)S(1)} %shard_map.118.refs_0_), channel_id=1, source_target_pairs={{0,8},{4,12},{8,0},{12,4},{1,9},{5,13},{9,1},{13,5},{2,10},{6,14},... | collective-permute-start | bytes 638984 | tf_op jit(solution)/shard_map/ppermute | solution.py:28
  34.1 7.2 %collective-permute-start.8 = (bf16[104,1024]{1,0:T(8,128)(2,1)S(1)}, bf16[104,1024]{1,0:T(8,128)(2,1)S(1)}, u32[]{:S(2)}, u32[]{:S(2)}) collective-permute-start(bf16[104,1024]{1,0:T(8,128)(2,1)S(1)} %shard_map.118.refs_0_), channel_id=1, source_target_pairs={{0,4},{4,0},{8,12},{12,8},{1,5},{5,1},{9,13},{13,9},{2,6},{6,2},{1... | collective-permute-start | bytes 638984 | tf_op jit(solution)/shard_map/ppermute | solution.py:28
  37.8 3.5 %collective-permute-start.9 = (bf16[104,1024]{1,0:T(8,128)(2,1)S(1)}, bf16[104,1024]{1,0:T(8,128)(2,1)S(1)}, u32[]{:S(2)}, u32[]{:S(2)}) collective-permute-start(bf16[104,1024]{1,0:T(8,128)(2,1)S(1)} %collective-permute-done.7.refs_1_), channel_id=1, source_target_pairs={{0,4},{4,0},{8,12},{12,8},{1,5},{5,1},{9,13},{13,9},{2,6},{6,2},{1... | collective-permute-start | bytes 638984 | tf_op jit(solution)/shard_map/ppermute | solution.py:28
  43.0 9.6 %collective-permute-start.10 = (bf16[104,1024]{1,0:T(8,128)(2,1)S(1)}, bf16[104,1024]{1,0:T(8,128)(2,1)S(1)}, u32[]{:S(2)}, u32[]{:S(2)}) collective-permute-start(bf16[104,1024]{1,0:T(8,128)(2,1)S(1)} %get-tuple-element.49), channel_id=1, source_target_pairs={{0,1},{1,2},{2,3},{4,5},{5,6},{6,7},{8,9},{9,10},{10,11},{12,13},{... | collective-permute-start | bytes 638984 | tf_op jit(solution)/shard_map/ppermute | solution.py:23

commit v5 on v4

--- a/solution.py
+++ b/solution.py
@@ -17,10 +17,9 @@
 FULL = jnp.float32
 
 
-def shift_from(block, axis, distance):
+def cycle_from(block, axis, distance):
     count = lax.axis_size(axis)
-    route = [(i - distance, i) for i in range(count) if 0 <= i - distance < count]
-    return lax.ppermute(block, axis, route)
+    return lax.ppermute(block, axis, [((i - distance) % count, i) for i in range(count)])
 
 
 def swap(block, axis, bit):
@@ -28,13 +27,12 @@
     return lax.ppermute(block, axis, [(i, i ^ bit) for i in range(count)])
 
 
-def run(body, outs, ins, scratch, micros=1.0, limit=16):
-    vmem = pl.BlockSpec(memory_space=pltpu.VMEM)
+def run(body, outs, ins, scratch, micros=1.0, limit=16, in_space=pltpu.VMEM, out_space=pltpu.VMEM):
     return pl.pallas_call(
         body,
         out_shape=outs,
-        in_specs=[vmem] * len(ins),
-        out_specs=[vmem] * len(outs),
+        in_specs=[pl.BlockSpec(memory_space=in_space)] * len(ins),
+        out_specs=[pl.BlockSpec(memory_space=out_space)] * len(outs),
         scratch_shapes=scratch,
         cost_estimate=pl.CostEstimate(
             flops=int(micros * 1.15e9), bytes_accessed=1024, transcendentals=0
@@ -75,22 +73,31 @@
     return lax.broadcasted_iota(jnp.int32, shape, len(shape) - 1)
 
 
-def turn_rows(state_ref, flat):
-    channels = state_ref.shape[0]
-    flat[:channels] = state_ref[...]
-    flat[channels:] = jnp.zeros((flat.shape[0] - channels,) + flat.shape[1:], HALF)
-    return jnp.swapaxes(flat[...], 0, 1)
-
-
 def pack(state):
     channels, rows, cols = state.shape
     padded = -(-channels // 8) * 8
     deep = -(-padded // 16) * 16
     span = -(-rows * REACH // LANES)
-
-    def body(state_ref, right_ref, left_ref, rows_ref, flat):
-        turned = turn_rows(state_ref, flat)
-        rows_ref[...] = turned
+    chunk = 8
+
+    def body(state_ref, right_ref, left_ref, rows_ref, flat, sems):
+        copies = [
+            pltpu.make_async_copy(
+                state_ref.at[:, pl.ds(first, chunk), :],
+                flat.at[first // chunk, pl.ds(0, channels)],
+                sems.at[first // chunk],
+            )
+            for first in range(0, rows, chunk)
+        ]
+        for copy in copies:
+            copy.start()
+        turned = []
+        for k, copy in enumerate(copies):
+            flat[k, channels:] = jnp.zeros((deep - channels, chunk, cols), HALF)
+            copy.wait()
+            part = jnp.swapaxes(flat[k], 0, 1)
+            rows_ref[k * chunk : (k + 1) * chunk] = part
+            turned += [part[i] for i in range(chunk)]
         lane = lane_index((deep, LANES))
         tiles = [None] * span
         rim = jnp.zeros((deep, LANES), HALF)
@@ -114,8 +121,12 @@
         body,
         [like((padded, span * LANES)), like((padded, LANES)), like((rows, deep, cols))],
         [state],
-        [pltpu.VMEM((deep, rows, cols), HALF)],
+        [
+            pltpu.VMEM((rows // chunk, deep, chunk, cols), HALF),
+            pltpu.SemaphoreType.DMA((rows // chunk,)),
+        ],
         micros=1.0,
+        in_space=pltpu.HBM,
     )
 
 
@@ -267,13 +278,15 @@
 def extract_rim(anchor, parts, turned, right, left, pick, bands, sects):
     rows, deep, cols = turned.shape
     padded = right.shape[0]
-    groups, size = batches(bands)
 
     def body(at_ref, part_ref, rows_ref, right_ref, left_ref, pick_ref,
              own_ref, low_ref, odd_ref, high_ref, near_ref, cross_ref, ext, picked):
         lane = lane_index((padded, LANES))
         none = jnp.zeros((padded, LANES), HALF)
         rim = left_ref[...]
+        sect = here()[1]
+        reach = jnp.where(sect < sects - 1, REACH, 0)
+        start = jnp.where(sect > 0, LANES - 2, LANES)
 
         def expand(r):
             at, off = divmod(r * REACH, LANES)
@@ -285,7 +298,7 @@
                 piece = jnp.where(lane < LANES - off, piece, pltpu.roll(after, LANES - off, 1))
             turn = pltpu.roll(rim, (LANES - 2 - 2 * r) % LANES, 1)
             ext[r, :padded] = jnp.where(
-                lane < REACH, piece, jnp.where(lane >= LANES - 2, turn, none)
+                lane < reach, piece, jnp.where(lane >= start, turn, none)
             )
 
         ext[:, padded:] = jnp.zeros((rows, deep - padded, LANES), HALF)
@@ -314,33 +327,27 @@
             crossing.append((row0, over))
             out_ref, at = target(j)
             out_ref[at] = part_ref[j]
-        for group in groups:
-            some = crossing[group[0]][1]
-            for j in group[1:]:
-                some = some | crossing[j][1]
-
-            @pl.when(some)
-            def _(group=group):
-                if group[0] == 0:
-                    for r in range(rows):
-                        if r not in outer:
-                            expand(r)
-                else:
-                    for r in range(rows):
-                        expand(r)
-                select_rows(
-                    ext, pick_ref[cols:, group[0] * LANES : (group[-1] + 1) * LANES], picked
-                )
-                for j in group:
-                    out_ref, at = target(j)
-                    row0, over = crossing[j]
-
-                    @pl.when(over)
-                    def _(j=j, out_ref=out_ref, at=at, row0=row0, first=(j - group[0]) * LANES):
-                        for t in range(TILES):
-                            out_ref[at, :, t * LANES : (t + 1) * LANES] += window_tile(
-                                picked, t, row0, rows, padded, slice(first, first + LANES)
-                            )
+        some = crossing[0][1]
+        for _, over in crossing[1:]:
+            some = some | over
+
+        @pl.when(some)
+        def _():
+            for r in range(rows):
+                if r not in outer:
+                    expand(r)
+
+        for j in range(bands):
+            out_ref, at = target(j)
+            row0, over = crossing[j]
+
+            @pl.when(over)
+            def _(j=j, out_ref=out_ref, at=at, row0=row0):
+                select_rows(ext, pick_ref[cols:, j * LANES : (j + 1) * LANES], picked)
+                for t in range(TILES):
+                    out_ref[at, :, t * LANES : (t + 1) * LANES] += window_tile(
+                        picked, t, row0, rows, padded, slice(0, LANES)
+                    )
 
     one = like((1, padded, TILES * LANES))
     rest = like((max(bands // 2 - 1, 1), padded, TILES * LANES))
@@ -349,7 +356,7 @@
         body,
         [one, rest, one, rest, edge, edge],
         [anchor, parts, turned, right, left, pick],
-        [pltpu.VMEM((rows, deep, LANES), HALF), pltpu.VMEM((rows, deep, size * LANES), FULL)],
+        [pltpu.VMEM((rows, deep, LANES), HALF), pltpu.VMEM((rows, deep, LANES), FULL)],
         micros=1.5
     )
 
@@ -483,12 +490,14 @@
     )[0]
 
 
-def spread(turned, right, left):
+def spread(turned, right, left, sects):
     rows, _, cols = turned.shape
     span = right.shape[1]
     loose = cols + 16
 
     def body(rows_ref, right_ref, left_ref, out_ref, after, before, line):
+        sect = here()[1]
+
         def upright(value):
             value = value.astype(FULL)
             return jnp.concatenate(
@@ -497,8 +506,8 @@
 
         for t in range(span // LANES):
             lanes = slice(t * LANES, (t + 1) * LANES)
-            after[lanes] = upright(right_ref[:, lanes])
-        before[...] = upright(left_ref[...])
+            after[lanes] = jnp.where(sect < sects - 1, upright(right_ref[:, lanes]), 0.0)
+        before[...] = jnp.where(sect > 0, upright(left_ref[...]), 0.0)
         line[...] = jnp.zeros(line.shape, FULL)
 
         def spread_rows(i, carry):
@@ -678,28 +687,46 @@
     rows, padded, cols = summed.shape
     deep = -(-padded // 16) * 16
     half = means[0].shape[0]
-
-    def body(top_ref, low_ref, sum_ref, spill_ref, inverse_ref, out_ref, flat):
+    chunk = 8
+
+    def body(top_ref, low_ref, sum_ref, spill_ref, inverse_ref, out_ref, flat, ready, sems):
         lane = lane_index((padded, LANES))
         none = jnp.zeros((padded, LANES), HALF)
-        flat[:, padded:] = jnp.zeros((rows, deep - padded, cols), HALF)
-        for r in range(rows):
-            at, low = divmod(r * SIDE, LANES)
-            extra = spill_ref[:, at * LANES : (at + 1) * LANES]
-            if low:
-                extra = pltpu.roll(extra, LANES - low, 1)
-            extra = jnp.where(lane < SIDE, extra, none).astype(FULL)
-            mean = top_ref[r] if r < half else low_ref[r - half]
-            value = mean.astype(FULL) + (sum_ref[r] + extra) * inverse_ref[r : r + 1]
-            flat[r, :padded] = value.astype(HALF)
-        out_ref[...] = jnp.swapaxes(flat[...], 0, 1)[:channels]
+        reach = jnp.where(here()[1] > 0, SIDE, 0)
+        flat[:, padded:] = jnp.zeros((chunk, deep - padded, cols), HALF)
+        copies = []
+        for first in range(0, rows, chunk):
+            for r in range(first, first + chunk):
+                at, low = divmod(r * SIDE, LANES)
+                extra = spill_ref[:, at * LANES : (at + 1) * LANES]
+                if low:
+                    extra = pltpu.roll(extra, LANES - low, 1)
+                extra = jnp.where(lane < reach, extra, none).astype(FULL)
+                mean = top_ref[r] if r < half else low_ref[r - half]
+                value = mean.astype(FULL) + (sum_ref[r] + extra) * inverse_ref[r : r + 1]
+                flat[r - first, :padded] = value.astype(HALF)
+            k = first // chunk
+            ready[k] = jnp.swapaxes(flat[...], 0, 1)[:channels]
+            copies.append(
+                pltpu.make_async_copy(
+                    ready.at[k], out_ref.at[:, pl.ds(first, chunk), :], sems.at[k]
+                )
+            )
+            copies[-1].start()
+        for copy in copies:
+            copy.wait()
 
     return run(
         body,
         [like((channels, rows, cols))],
         [*means, summed, arrived, inverse],
-        [pltpu.VMEM((rows, deep, cols), HALF)],
-        micros=3.0
+        [
+            pltpu.VMEM((chunk, deep, cols), HALF),
+            pltpu.VMEM((rows // chunk, channels, chunk, cols), HALF),
+            pltpu.SemaphoreType.DMA((rows // chunk,)),
+        ],
+        micros=2.0,
+        out_space=pltpu.HBM,
     )[0]
 
 
@@ -724,8 +751,8 @@
     anchor = patch_anchor.T
 
     right_rim, left_rim, turned = pack(state_field)
-    right = shift_from(right_rim, "sect", -1)
-    left = shift_from(left_rim, "sect", 1)
+    right = cycle_from(right_rim, "sect", -1)
+    left = cycle_from(left_rim, "sect", 1)
 
     made, lines, noise = prep(
         [
@@ -773,13 +800,13 @@
         sources += [s ^ bit for s in sources]
         bit //= 2
 
-    shifted = spread(turned, right, left)
+    shifted = spread(turned, right, left, sects)
     top_mean = grid_mean(shifted, rim_near, rim_cross, False, padded, made[:2], biases[:2], limits)
     low_mean = grid_mean(shifted, rim_near, rim_cross, True, padded, made[:2], biases[:2], limits)
     spilled, summed, inverse = canvas(
         anchor, pieces, sources, place, sects, rows, cols
     )
-    arrived = shift_from(spilled, "sect", 1)
+    arrived = cycle_from(spilled, "sect", 1)
     return finish([top_mean, low_mean], summed, arrived, inverse, channels)
 
 

time: 54.4 us -> 55.4 us (1.018)
  the two profiles are of different devices: /device:TPU:18 before, /device:TPU:0 now
where the time goes in v5:
time: 55.4 us; the launch traced here: 55.3 us
  Pallas kernels  21.9 us (40%)
  waiting for transfers between devices  18.3 us (33%)
  starting transfers between devices  13.3 us (24%)
  local copies, waits for them, and re-layouts  1.28 us (2%)
    pallas_call x12, Pallas kernels, run(): pl.pallas_call(body, out_shape=outs, in_specs=[pl.BlockSpec(memory_space=...  21.9 us
    ppermute x7, waiting for transfers between devices, swap(): return lax.ppermute(block, axis, [(i, i ^ bit) for i in range(count)])  9.49 us
    ppermute x3, waiting for transfers between devices, cycle_from(): lax.ppermute(block, axis, [((i - distance) % count, i) for i in range(cou...  8.81 us
    ppermute x3, starting transfers between devices, cycle_from(): lax.ppermute(block, axis, [((i - distance) % count, i) for i in range(cou...  7.98 us
    ppermute x7, starting transfers between devices, swap(): return lax.ppermute(block, axis, [(i, i ^ bit) for i in range(count)])  4.65 us
    unnamed x23, local copies, waits for them, and re-layouts  1.28 us
  transfers between devices with their start and end apart: 11, of which 5 were waited for; matrix products, arithmetic and copies ran while one was open for 0% of the time, Pallas kernels for 32%

profile of v5, /device:TPU:0, one launch (start us, length us, event | category | flops | bytes accessed | tf_op | source)
XLA Modules:
  0.0 55.3 jit_solution(3262433980569721677)
XLA Ops:
  0.0 1.1 %copy-done = bf16[99,32,128]{2,1,0:T(8,128)(2,1)S(1)} copy-done((bf16[99,32,128]{2,1,0:T(8,128)(2,1)S(1)}, bf16[99,32,128]{2,1,0:T(8,128)(2,1)}, u32[]{:S(2)}) %copy-start) | copy-done | bytes 811032
  1.1 1.0 %shard_map.109 = (bf16[104,1152]{1,0:T(8,128)(2,1)S(1)}, bf16[104,128]{1,0:T(8,128)(2,1)S(1)}, bf16[32,112,128]{2,1,0:T(8,128)(2,1)S(1)}) custom-call(bf16[99,32,128]{2,1,0:T(8,128)(2,1)S(1)} %copy-done), custom_call_target="tpu_custom_call" | custom-call | flops 1150000000 | bytes 1024 | tf_op jit(solution)/shard_map/pallas_call | solution.py:31
  2.1 5.1 %collective-permute-start = (bf16[104,1152]{1,0:T(8,128)(2,1)S(1)}, bf16[104,1152]{1,0:T(8,128)(2,1)S(1)}, u32[]{:S(2)}, u32[]{:S(2)}) collective-permute-start(bf16[104,1152]{1,0:T(8,128)(2,1)S(1)} %get-tuple-element.29), channel_id=1, source_target_pairs={{1,0},{2,1},{3,2},{0,3},{5,4},{6,5},{7,6},{4,7},{9,8},{10,9},{11,1... | collective-permute-start | bytes 718856 | tf_op jit(solution)/shard_map/ppermute | solution.py:22
  7.2 0.0 collective-permute-start.1
  7.3 0.0 copy-done.6
  7.3 0.9 %shard_map.111 = (bf16[256,512]{1,0:T(8,128)(2,1)S(1)}, bf16[4,512,256]{2,1,0:T(8,128)(2,1)S(1)}) custom-call(s32[2,16]{1,0:T(2,128)S(1)} %bitcast.12), custom_call_target="tpu_custom_call" | custom-call | flops 1150000000 | bytes 1024 | tf_op jit(solution)/shard_map/pallas_call | solution.py:31
  8.2 1.5 %shard_map.112.part_ref = bf16[4,104,1536]{2,1,0:T(8,128)(2,1)S(1)} custom-call(s32[2,16]{1,0:T(2,128)S(1)} %bitcast.13, bf16[32,112,128]{2,1,0:T(8,128)(2,1)S(1)} %get-tuple-element.28.rows_ref, bf16[256,512]{1,0:T(8,128)(2,1)S(1)} %get-tuple-element.31.pick_ref), custom_call_target="tpu_custom_call" | custom-call | flops 1724999936 | bytes 1024 | tf_op jit(solution)/shard_map/pallas_call | solution.py:31
  9.7 0.0 copy-start.10
  9.7 4.1 %collective-permute-done.1.left_ref = bf16[104,128]{1,0:T(8,128)(2,1)S(1)} collective-permute-done((bf16[104,128]{1,0:T(8,128)(2,1)S(1)}, bf16[104,128]{1,0:T(8,128)(2,1)S(1)}, u32[]{:S(2)}, u32[]{:S(2)}) %collective-permute-start.1) | collective-permute-done | bytes 26656 | tf_op jit(solution)/shard_map/ppermute | solution.py:22
  13.8 0.0 collective-permute-done.right_ref
  13.8 0.2 shard_map.113
  14.1 0.0 copy-start.1
  14.1 0.0 copy-start.2
  14.1 0.0 copy-start.3
  14.1 0.0 copy-start.4
  14.1 0.0 copy-start.5
  14.1 0.0 copy-start.7
  14.1 0.0 copy-start.8
  14.2 0.0 copy-start.9
  14.2 0.1 collective-permute-start.4
  14.2 0.5 collective-permute-start.6
  14.7 1.1 %collective-permute-done.4.got_ref = bf16[1,104,1536]{2,1,0:T(8,128)(2,1)S(1)} collective-permute-done((bf16[1,104,1536]{2,1,0:T(8,128)(2,1)S(1)}, bf16[1,104,1536]{2,1,0:T(8,128)(2,1)S(1)}, u32[]{:S(2)}, u32[]{:S(2)}) %collective-permute-start.4) | collective-permute-done | bytes 319520 | tf_op jit(solution)/shard_map/ppermute | solution.py:27
  15.9 1.6 %collective-permute-start.5 = (bf16[1,104,1536]{2,1,0:T(8,128)(2,1)S(1)}, bf16[1,104,1536]{2,1,0:T(8,128)(2,1)S(1)}, u32[]{:S(2)}, u32[]{:S(2)}) collective-permute-start(bf16[1,104,1536]{2,1,0:T(8,128)(2,1)S(1)} %shard_map.117), channel_id=1, source_target_pairs={{0,8},{4,12},{8,0},{12,4},{1,9},{5,13},{9,1},{13,5},{2,10},{6,14},... | collective-permute-start | bytes 958472 | tf_op jit(solution)/shard_map/ppermute | solution.py:27
  17.4 0.0 copy-done.10
  17.4 0.1 copy.14
  17.5 0.0 copy-done.1
  17.5 0.0 copy-done.2
  17.6 0.6 %shard_map.114 = (bf16[1536,256]{1,0:T(8,128)(2,1)S(1)}, bf16[256,1536]{1,0:T(8,128)(2,1)S(1)}, bf16[1536,256]{1,0:T(8,128)(2,1)S(1)}, bf16[256,1536]{1,0:T(8,12...) custom-call(bf16[9,99,128]{2,1,0:T(8,128)(2,1)S(1)} %bitcast.10, ...), custom_call_target="tpu_custom_call" | custom-call | flops 1724999936 | bytes 1024 | tf_op jit(solution)/shard_map/pallas_call | solution.py:31
  18.2 0.1 collective-permute-start.2
  18.3 0.7 %collective-permute-start.3 = (bf16[2,112,256]{2,1,0:T(8,128)(2,1)S(1)}, bf16[2,112,256]{2,1,0:T(8,128)(2,1)S(1)}, u32[]{:S(2)}, u32[]{:S(2)}) collective-permute-start(bf16[2,112,256]{2,1,0:T(8,128)(2,1)S(1)} %get-tuple-element.33), channel_id=1, source_target_pairs={{4,8},{8,4},{5,9},{9,5},{6,10},{10,6},{7,11},{11,7},{20,24},{24,20... | collective-permute-start | bytes 344072 | tf_op jit(solution)/shard_map/ppermute | solution.py:788
  19.0 0.0 collective-permute-done.6.refs_3_
  19.0 6.5 %collective-permute-done.5.refs_2_ = bf16[1,104,1536]{2,1,0:T(8,128)(2,1)S(1)} collective-permute-done((bf16[1,104,1536]{2,1,0:T(8,128)(2,1)S(1)}, bf16[1,104,1536]{2,1,0:T(8,128)(2,1)S(1)}, u32[]{:S(2)}, u32[]{:S(2)}) %collective-permute-start.5) | collective-permute-done | bytes 319520 | tf_op jit(solution)/shard_map/ppermute | solution.py:27
  25.5 5.4 %shard_map.118.refs_0_ = bf16[104,1024]{1,0:T(8,128)(2,1)S(1)} custom-call(s32[2,16]{1,0:T(2,128)S(1)} %bitcast.15, bf16[1,104,1536]{2,1,0:T(8,128)(2,1)S(1)} %get-tuple-element.38.refs_1_, bf16[1,104,1536]{2,1,0:T(8,128)(2,1)S(1)} %collective-permute-done.5.refs_2_, bf16[1,104,1536]{2,1,0:T(8,128)(2,1)S(1)} %collective-permute-done.6.refs_3_, ...), custom_call_target="tpu_custom_call" | custom-call | flops 9200000000 | bytes 1024 | tf_op jit(solution)/shard_map/pallas_call | solution.py:31
  30.9 2.4 %collective-permute-start.7 = (bf16[104,1024]{1,0:T(8,128)(2,1)S(1)}, bf16[104,1024]{1,0:T(8,128)(2,1)S(1)}, u32[]{:S(2)}, u32[]{:S(2)}) collective-permute-start(bf16[104,1024]{1,0:T(8,128)(2,1)S(1)} %shard_map.118.refs_0_), channel_id=1, source_target_pairs={{0,8},{4,12},{8,0},{12,4},{1,9},{5,13},{9,1},{13,5},{2,10},{6,14},... | collective-permute-start | bytes 638984 | tf_op jit(solution)/shard_map/ppermute | solution.py:27
  33.3 2.2 %shard_map.110.shifted_ref = bf16[3,16,2,144,128]{4,3,2,1,0:T(8,128)(2,1)S(1)} custom-call(bf16[32,112,128]{2,1,0:T(8,128)(2,1)S(1)} %get-tuple-element.28.rows_ref, bf16[104,1152]{1,0:T(8,128)(2,1)S(1)} %collective-permute-done.right_ref, bf16[104,128]{1,0:T(8,128)(2,1)S(1)} %collective-permute-done.1.left_ref), custom_call_target="tpu_custom_call" | custom-call | flops 2875000064 | bytes 1024 | tf_op jit(solution)/shard_map/pallas_call | solution.py:31
  35.5 0.1 collective-permute-start.8
  35.6 1.9 %collective-permute-done.7.refs_1_ = bf16[104,1024]{1,0:T(8,128)(2,1)S(1)} collective-permute-done((bf16[104,1024]{1,0:T(8,128)(2,1)S(1)}, bf16[104,1024]{1,0:T(8,128)(2,1)S(1)}, u32[]{:S(2)}, u32[]{:S(2)}) %collective-permute-start.7) | collective-permute-done | bytes 213024 | tf_op jit(solution)/shard_map/ppermute | solution.py:27
  37.5 0.0 collective-permute-start.9
  37.5 0.0 collective-permute-done.2.near_ref
  37.5 0.0 collective-permute-done.3.cross_ref
  37.5 3.5 %shard_map.116.low_ref = bf16[16,104,128]{2,1,0:T(8,128)(2,1)S(1)} custom-call(bf16[3,16,2,144,128]{4,3,2,1,0:T(8,128)(2,1)S(1)} %shard_map.110.shifted_ref, bf16[2,112,256]{2,1,0:T(8,128)(2,1)S(1)} %collective-permute-done.2.near_ref, bf16[2,112,256]{2,1,0:T(8,128)(2,1)S(1)} %collective-permute-done.3.cross_ref, ...), custom_call_target="tpu_custom_call" | custom-call | flops 4024999936 | bytes 1024 | tf_op jit(solution)/shard_map/pallas_call | solution.py:31
  41.0 0.0 collective-permute-done.8.refs_2_
  41.0 0.0 collective-permute-done.9.refs_3_
  41.0 1.6 %shard_map.119 = (bf16[104,1024]{1,0:T(8,128)(2,1)S(1)}, f32[32,104,128]{2,1,0:T(8,128)S(1)}, f32[32,128]{1,0:T(8,128)S(1)}) custom-call(s32[2,16]{1,0:T(2,128)S(1)} %bitcast.16, bf16[104,1024]{1,0:T(8,128)(2,1)S(1)} %shard_map.118.refs_0_, bf16[104,1024]{1,0:T(8,128)(2,1)S(1)} %collective-permute-done.7.refs_1_, ...), custom_call_target="tpu_custom_call" | custom-call | flops 1724999936 | bytes 1024 | tf_op jit(solution)/shard_map/pallas_call | solution.py:31
  42.6 2.8 %collective-permute-start.10 = (bf16[104,1024]{1,0:T(8,128)(2,1)S(1)}, bf16[104,1024]{1,0:T(8,128)(2,1)S(1)}, u32[]{:S(2)}, u32[]{:S(2)}) collective-permute-start(bf16[104,1024]{1,0:T(8,128)(2,1)S(1)} %get-tuple-element.49), channel_id=1, source_target_pairs={{3,0},{0,1},{1,2},{2,3},{7,4},{4,5},{5,6},{6,7},{11,8},{8,9},{9,10... | collective-permute-start | bytes 638984 | tf_op jit(solution)/shard_map/ppermute | solution.py:22
  45.4 3.5 %shard_map.115.top_ref = bf16[16,104,128]{2,1,0:T(8,128)(2,1)S(1)} custom-call(bf16[3,16,2,144,128]{4,3,2,1,0:T(8,128)(2,1)S(1)} %shard_map.110.shifted_ref, bf16[2,112,256]{2,1,0:T(8,128)(2,1)S(1)} %collective-permute-done.2.near_ref, bf16[2,112,256]{2,1,0:T(8,128)(2,1)S(1)} %collective-permute-done.3.cross_ref, ...), custom_call_target="tpu_custom_call" | custom-call | flops 4024999936 | bytes 1024 | tf_op jit(solution)/shard_map/pallas_call | solution.py:31
  48.9 4.7 %collective-permute-done.10.spill_ref = bf16[104,1024]{1,0:T(8,128)(2,1)S(1)} collective-permute-done((bf16[104,1024]{1,0:T(8,128)(2,1)S(1)}, bf16[104,1024]{1,0:T(8,128)(2,1)S(1)}, u32[]{:S(2)}, u32[]{:S(2)}) %collective-permute-start.10) | collective-permute-done | bytes 213024 | tf_op jit(solution)/shard_map/ppermute | solution.py:22
  53.6 1.5 %shard_map.120 = bf16[99,32,128]{2,1,0:T(8,128)(2,1)} custom-call(bf16[16,104,128]{2,1,0:T(8,128)(2,1)S(1)} %shard_map.115.top_ref, bf16[16,104,128]{2,1,0:T(8,128)(2,1)S(1)} %shard_map.116.low_ref, f32[32,104,128]{2,1,0:T(8,128)S(1)} %get-tuple-element.48.sum_ref, bf16[104,1024]{1,0:T(8,128)(2,1)S(1)} %collective-permute-done.10.spill_ref, ...), custom_call_target="tpu_custom_call" | custom-call | flops 2300000000 | bytes 1024 | tf_op jit(solution)/shard_map/pallas_call | solution.py:31
  (9 shorter events, 0.0 us)
Async XLA Ops:
  0.0 1.1 %copy-start = (bf16[99,32,128]{2,1,0:T(8,128)(2,1)S(1)}, bf16[99,32,128]{2,1,0:T(8,128)(2,1)}, u32[]{:S(2)}) copy-start(bf16[99,32,128]{2,1,0:T(8,128)(2,1)} %state_ref.1) | copy-start | bytes 2433028
  1.1 6.1 %copy-start.6 = (s32[16,2]{0,1:T(2,128)S(1)}, s32[16,2]{0,1:T(2,128)}, u32[]{:S(2)}) copy-start(s32[16,2]{0,1:T(2,128)} %param.16) | copy-start | bytes 388
  2.1 11.7 %collective-permute-start = (bf16[104,1152]{1,0:T(8,128)(2,1)S(1)}, bf16[104,1152]{1,0:T(8,128)(2,1)S(1)}, u32[]{:S(2)}, u32[]{:S(2)}) collective-permute-start(bf16[104,1152]{1,0:T(8,128)(2,1)S(1)} %get-tuple-element.29), channel_id=1, source_target_pairs={{1,0},{2,1},{3,2},{0,3},{5,4},{6,5},{7,6},{4,7},{9,8},{10,9},{11,1... | collective-permute-start | bytes 718856 | tf_op jit(solution)/shard_map/ppermute | solution.py:22
  7.2 6.6 %collective-permute-start.1 = (bf16[104,128]{1,0:T(8,128)(2,1)S(1)}, bf16[104,128]{1,0:T(8,128)(2,1)S(1)}, u32[]{:S(2)}, u32[]{:S(2)}) collective-permute-start(bf16[104,128]{1,0:T(8,128)(2,1)S(1)} %get-tuple-element.30), channel_id=1, source_target_pairs={{3,0},{0,1},{1,2},{2,3},{7,4},{4,5},{5,6},{6,7},{11,8},{8,9},{9,10... | collective-permute-start | bytes 79880 | tf_op jit(solution)/shard_map/ppermute | solution.py:22
  9.7 7.8 %copy-start.10 = (bf16[1,2,99,1024]{3,1,2,0:T(2,128)(2,1)S(1)}, bf16[1,2,99,1024]{3,1,2,0:T(2,128)(2,1)}, u32[]{:S(2)}) copy-start(bf16[1,2,99,1024]{3,1,2,0:T(2,128)(2,1)} %param.17) | copy-start | bytes 1216516
  14.1 3.5 %copy-start.1 = (bf16[9,128,99]{1,2,0:T(8,128)(2,1)S(1)}, bf16[9,128,99]{1,2,0:T(8,128)(2,1)}, u32[]{:S(2)}) copy-start(bf16[9,128,99]{1,2,0:T(8,128)(2,1)} %param.12) | copy-start | bytes 684292
  14.1 3.5 %copy-start.2 = (bf16[9,99,128]{2,1,0:T(8,128)(2,1)S(1)}, bf16[9,99,128]{2,1,0:T(8,128)(2,1)}, u32[]{:S(2)}) copy-start(bf16[9,99,128]{2,1,0:T(8,128)(2,1)} %refs_1_.1) | copy-start | bytes 684292
  14.1 3.5 %copy-start.3 = (bf16[9,128,99]{1,2,0:T(8,128)(2,1)S(1)}, bf16[9,128,99]{1,2,0:T(8,128)(2,1)}, u32[]{:S(2)}) copy-start(bf16[9,128,99]{1,2,0:T(8,128)(2,1)} %param.18) | copy-start | bytes 684292
  14.1 3.5 %copy-start.4 = (bf16[9,99,128]{2,1,0:T(8,128)(2,1)S(1)}, bf16[9,99,128]{2,1,0:T(8,128)(2,1)}, u32[]{:S(2)}) copy-start(bf16[9,99,128]{2,1,0:T(8,128)(2,1)} %refs_3_.1) | copy-start | bytes 684292
  14.1 3.5 %copy-start.5 = (f32[2,128]{1,0:T(2,128)S(1)}, f32[2,128]{1,0:T(2,128)}, u32[]{:S(2)}) copy-start(f32[2,128]{1,0:T(2,128)} %refs_7_.1) | copy-start | bytes 3076
  14.1 3.5 %copy-start.7 = (f32[128]{0:T(128)S(1)}, f32[128]{0:T(128)}, u32[]{:S(2)}) copy-start(f32[128]{0:T(128)} %param.13) | copy-start | bytes 1540
  14.1 3.5 %copy-start.8 = (f32[99]{0:T(128)S(1)}, f32[99]{0:T(128)}, u32[]{:S(2)}) copy-start(f32[99]{0:T(128)} %param.15) | copy-start | bytes 1192
  14.2 3.5 %copy-start.9 = (f32[99]{0:T(128)S(1)}, f32[99]{0:T(128)}, u32[]{:S(2)}) copy-start(f32[99]{0:T(128)} %param.21) | copy-start | bytes 1192
  14.2 1.7 %collective-permute-start.4 = (bf16[1,104,1536]{2,1,0:T(8,128)(2,1)S(1)}, bf16[1,104,1536]{2,1,0:T(8,128)(2,1)S(1)}, u32[]{:S(2)}, u32[]{:S(2)}) collective-permute-start(bf16[1,104,1536]{2,1,0:T(8,128)(2,1)S(1)} %get-tuple-element.40), channel_id=1, source_target_pairs={{0,4},{4,0},{8,12},{12,8},{1,5},{5,1},{9,13},{13,9},{2,6},{6,2},{1... | collective-permute-start | bytes 958472 | tf_op jit(solution)/shard_map/ppermute | solution.py:27
  14.2 4.8 %collective-permute-start.6 = (bf16[1,104,1536]{2,1,0:T(8,128)(2,1)S(1)}, bf16[1,104,1536]{2,1,0:T(8,128)(2,1)S(1)}, u32[]{:S(2)}, u32[]{:S(2)}) collective-permute-start(bf16[1,104,1536]{2,1,0:T(8,128)(2,1)S(1)} %get-tuple-element.41), channel_id=1, source_target_pairs={{0,4},{4,0},{8,12},{12,8},{1,5},{5,1},{9,13},{13,9},{2,6},{6,2},{1... | collective-permute-start | bytes 958472 | tf_op jit(solution)/shard_map/ppermute | solution.py:27
  15.9 9.6 %collective-permute-start.5 = (bf16[1,104,1536]{2,1,0:T(8,128)(2,1)S(1)}, bf16[1,104,1536]{2,1,0:T(8,128)(2,1)S(1)}, u32[]{:S(2)}, u32[]{:S(2)}) collective-permute-start(bf16[1,104,1536]{2,1,0:T(8,128)(2,1)S(1)} %shard_map.117), channel_id=1, source_target_pairs={{0,8},{4,12},{8,0},{12,4},{1,9},{5,13},{9,1},{13,5},{2,10},{6,14},... | collective-permute-start | bytes 958472 | tf_op jit(solution)/shard_map/ppermute | solution.py:27
  18.2 19.2 %collective-permute-start.2 = (bf16[2,112,256]{2,1,0:T(8,128)(2,1)S(1)}, bf16[2,112,256]{2,1,0:T(8,128)(2,1)S(1)}, u32[]{:S(2)}, u32[]{:S(2)}) collective-permute-start(bf16[2,112,256]{2,1,0:T(8,128)(2,1)S(1)} %get-tuple-element.32), channel_id=1, source_target_pairs={{0,4},{4,0},{8,12},{12,8},{1,5},{5,1},{9,13},{13,9},{2,6},{6,2},{1... | collective-permute-start | bytes 344072 | tf_op jit(solution)/shard_map/ppermute | solution.py:27
  18.3 19.1 %collective-permute-start.3 = (bf16[2,112,256]{2,1,0:T(8,128)(2,1)S(1)}, bf16[2,112,256]{2,1,0:T(8,128)(2,1)S(1)}, u32[]{:S(2)}, u32[]{:S(2)}) collective-permute-start(bf16[2,112,256]{2,1,0:T(8,128)(2,1)S(1)} %get-tuple-element.33), channel_id=1, source_target_pairs={{4,8},{8,4},{5,9},{9,5},{6,10},{10,6},{7,11},{11,7},{20,24},{24,20... | collective-permute-start | bytes 344072 | tf_op jit(solution)/shard_map/ppermute | solution.py:788
  30.9 6.5 %collective-permute-start.7 = (bf16[104,1024]{1,0:T(8,128)(2,1)S(1)}, bf16[104,1024]{1,0:T(8,128)(2,1)S(1)}, u32[]{:S(2)}, u32[]{:S(2)}) collective-permute-start(bf16[104,1024]{1,0:T(8,128)(2,1)S(1)} %shard_map.118.refs_0_), channel_id=1, source_target_pairs={{0,8},{4,12},{8,0},{12,4},{1,9},{5,13},{9,1},{13,5},{2,10},{6,14},... | collective-permute-start | bytes 638984 | tf_op jit(solution)/shard_map/ppermute | solution.py:27
  35.5 5.5 %collective-permute-start.8 = (bf16[104,1024]{1,0:T(8,128)(2,1)S(1)}, bf16[104,1024]{1,0:T(8,128)(2,1)S(1)}, u32[]{:S(2)}, u32[]{:S(2)}) collective-permute-start(bf16[104,1024]{1,0:T(8,128)(2,1)S(1)} %shard_map.118.refs_0_), channel_id=1, source_target_pairs={{0,4},{4,0},{8,12},{12,8},{1,5},{5,1},{9,13},{13,9},{2,6},{6,2},{1... | collective-permute-start | bytes 638984 | tf_op jit(solution)/shard_map/ppermute | solution.py:27
  37.5 3.5 %collective-permute-start.9 = (bf16[104,1024]{1,0:T(8,128)(2,1)S(1)}, bf16[104,1024]{1,0:T(8,128)(2,1)S(1)}, u32[]{:S(2)}, u32[]{:S(2)}) collective-permute-start(bf16[104,1024]{1,0:T(8,128)(2,1)S(1)} %collective-permute-done.7.refs_1_), channel_id=1, source_target_pairs={{0,4},{4,0},{8,12},{12,8},{1,5},{5,1},{9,13},{13,9},{2,6},{6,2},{1... | collective-permute-start | bytes 638984 | tf_op jit(solution)/shard_map/ppermute | solution.py:27
  42.6 11.0 %collective-permute-start.10 = (bf16[104,1024]{1,0:T(8,128)(2,1)S(1)}, bf16[104,1024]{1,0:T(8,128)(2,1)S(1)}, u32[]{:S(2)}, u32[]{:S(2)}) collective-permute-start(bf16[104,1024]{1,0:T(8,128)(2,1)S(1)} %get-tuple-element.49), channel_id=1, source_target_pairs={{3,0},{0,1},{1,2},{2,3},{7,4},{4,5},{5,6},{6,7},{11,8},{8,9},{9,10... | collective-permute-start | bytes 638984 | tf_op jit(solution)/shard_map/ppermute | solution.py:22

commit v6 on v5

--- a/solution.py
+++ b/solution.py
@@ -17,9 +17,10 @@
 FULL = jnp.float32
 
 
-def cycle_from(block, axis, distance):
+def shift_from(block, axis, distance):
     count = lax.axis_size(axis)
-    return lax.ppermute(block, axis, [((i - distance) % count, i) for i in range(count)])
+    route = [(i - distance, i) for i in range(count) if 0 <= i - distance < count]
+    return lax.ppermute(block, axis, route)
 
 
 def swap(block, axis, bit):
@@ -27,11 +28,11 @@
     return lax.ppermute(block, axis, [(i, i ^ bit) for i in range(count)])
 
 
-def run(body, outs, ins, scratch, micros=1.0, limit=16, in_space=pltpu.VMEM, out_space=pltpu.VMEM):
+def run(body, outs, ins, scratch, micros=1.0, limit=16, out_space=pltpu.VMEM):
     return pl.pallas_call(
         body,
         out_shape=outs,
-        in_specs=[pl.BlockSpec(memory_space=in_space)] * len(ins),
+        in_specs=[pl.BlockSpec(memory_space=pltpu.VMEM)] * len(ins),
         out_specs=[pl.BlockSpec(memory_space=out_space)] * len(outs),
         scratch_shapes=scratch,
         cost_estimate=pl.CostEstimate(
@@ -39,6 +40,14 @@
         ),
         compiler_params=pltpu.CompilerParams(vmem_limit_bytes=limit * 1024 * 1024),
     )(*ins)
+
+
+def arrival(bands):
+    slots, bit = [0], bands // 2
+    while bit:
+        slots += [slot ^ bit for slot in slots]
+        bit //= 2
+    return slots
 
 
 def here():
@@ -73,31 +82,22 @@
     return lax.broadcasted_iota(jnp.int32, shape, len(shape) - 1)
 
 
+def turn_rows(state_ref, flat):
+    channels = state_ref.shape[0]
+    flat[:channels] = state_ref[...]
+    flat[channels:] = jnp.zeros((flat.shape[0] - channels,) + flat.shape[1:], HALF)
+    return jnp.swapaxes(flat[...], 0, 1)
+
+
 def pack(state):
     channels, rows, cols = state.shape
     padded = -(-channels // 8) * 8
     deep = -(-padded // 16) * 16
     span = -(-rows * REACH // LANES)
-    chunk = 8
-
-    def body(state_ref, right_ref, left_ref, rows_ref, flat, sems):
-        copies = [
-            pltpu.make_async_copy(
-                state_ref.at[:, pl.ds(first, chunk), :],
-                flat.at[first // chunk, pl.ds(0, channels)],
-                sems.at[first // chunk],
-            )
-            for first in range(0, rows, chunk)
-        ]
-        for copy in copies:
-            copy.start()
-        turned = []
-        for k, copy in enumerate(copies):
-            flat[k, channels:] = jnp.zeros((deep - channels, chunk, cols), HALF)
-            copy.wait()
-            part = jnp.swapaxes(flat[k], 0, 1)
-            rows_ref[k * chunk : (k + 1) * chunk] = part
-            turned += [part[i] for i in range(chunk)]
+
+    def body(state_ref, right_ref, left_ref, rows_ref, flat):
+        turned = turn_rows(state_ref, flat)
+        rows_ref[...] = turned
         lane = lane_index((deep, LANES))
         tiles = [None] * span
         rim = jnp.zeros((deep, LANES), HALF)
@@ -121,25 +121,22 @@
         body,
         [like((padded, span * LANES)), like((padded, LANES)), like((rows, deep, cols))],
         [state],
-        [
-            pltpu.VMEM((rows // chunk, deep, chunk, cols), HALF),
-            pltpu.SemaphoreType.DMA((rows // chunk,)),
-        ],
+        [pltpu.VMEM((deep, rows, cols), HALF)],
         micros=1.0,
-        in_space=pltpu.HBM,
-    )
-
-
-def prep(weights, biases, noise):
+    )
+
+
+def prep(anchor, weights, biases, noise, bands, sects, rows, cols):
     steps, channels, cells = noise.shape
     count = len(weights)
     tile_rows = LANES // SIDE
     lines = len(biases)
 
-    def body(*refs):
+    def body(at_ref, *refs):
         ins, lines_in, noise_ref = refs[:count], refs[count : count + lines], refs[count + lines]
         outs = refs[count + lines + 1 :]
         lines_out, noise_out = outs[count : count + lines], outs[count + lines]
+        place_ref = outs[count + lines + 1]
         for k, (w_ref, o_ref) in enumerate(zip(ins, outs)):
             _, down, across = w_ref.shape
             o_ref[...] = jnp.zeros(o_ref.shape, HALF)
@@ -165,30 +162,10 @@
                     noise_out[
                         k, r // 2 * SIDE : (r // 2 + 1) * SIDE, r % 2 * LANES : (r % 2 + 1) * LANES
                     ] = block[m * SIDE : (m + 1) * SIDE]
-
-    sizes = [(12 * LANES, 2 * LANES), (2 * LANES, 12 * LANES)]
-    made = [like(sizes[k % 2]) for k in range(count)]
-    made += [like((line.shape[0], 2 * LANES), FULL) for line in biases]
-    made += [like((steps, cells // 2, 2 * LANES))]
-    out = run(body, made, [*weights, *biases, noise], [], micros=1.5)
-    return out[:count], out[count : count + lines], out[count + lines]
-
-
-def picks(anchor, bands, sects, rows, cols):
-    width = cols + LANES
-    tile_rows = LANES // SIDE
-
-    def body(at_ref, pick_ref, place_ref):
-        source = lax.broadcasted_iota(jnp.int32, (width, LANES), 0)
-        inner = lane_index((width, LANES))
-        for _ in range(1, PER_TILE):
-            inner = jnp.where(inner >= WIDE, inner - WIDE, inner)
         cell = lax.broadcasted_iota(jnp.int32, (LANES, 2 * LANES), 0)
         target = lane_index((LANES, 2 * LANES))
-        anchors = slot_anchors(at_ref, range(bands), sects, rows, cols)
+        anchors = slot_anchors(at_ref, arrival(bands), sects, rows, cols)
         for j, (row0, col0) in enumerate(anchors):
-            want = jnp.bitwise_and(inner + (col0 - 2), width - 1)
-            pick_ref[:, j * LANES : (j + 1) * LANES] = jnp.where(source == want, 1.0, 0.0).astype(HALF)
             across = jnp.bitwise_and(cell, SIDE - 1) + col0
             for m in range(tile_rows):
                 turn = jnp.bitwise_and(m - row0, tile_rows - 1)
@@ -196,13 +173,29 @@
                 hit = (target == there) & (cell >= turn * SIDE) & (cell < (turn + 1) * SIDE)
                 place_ref[m, j * LANES : (j + 1) * LANES] = jnp.where(hit, 1.0, 0.0).astype(HALF)
 
-    return run(
-        body,
-        [like((width, bands * LANES)), like((tile_rows, bands * LANES, 2 * LANES))],
-        [anchor],
-        [],
-        micros=1.0,
-    )
+    sizes = [(12 * LANES, 2 * LANES), (2 * LANES, 12 * LANES)]
+    made = [like(sizes[k % 2]) for k in range(count)]
+    made += [like((line.shape[0], 2 * LANES), FULL) for line in biases]
+    made += [like((steps, cells // 2, 2 * LANES))]
+    made += [like((tile_rows, bands * LANES, 2 * LANES))]
+    out = run(body, made, [anchor, *weights, *biases, noise], [], micros=1.5)
+    return out[:count], out[count : count + lines], *out[count + lines :]
+
+
+def picks(anchor, bands, sects, rows, cols):
+    width = cols + LANES
+
+    def body(at_ref, pick_ref):
+        source = lax.broadcasted_iota(jnp.int32, (width, LANES), 0)
+        inner = lane_index((width, LANES))
+        for _ in range(1, PER_TILE):
+            inner = jnp.where(inner >= WIDE, inner - WIDE, inner)
+        anchors = slot_anchors(at_ref, range(bands), sects, rows, cols)
+        for j, (row0, col0) in enumerate(anchors):
+            want = jnp.bitwise_and(inner + (col0 - 2), width - 1)
+            pick_ref[:, j * LANES : (j + 1) * LANES] = jnp.where(source == want, 1.0, 0.0).astype(HALF)
+
+    return run(body, [like((width, bands * LANES))], [anchor], [], micros=0.4)[0]
 
 
 def add_parts(kept, got):
@@ -284,9 +277,6 @@
         lane = lane_index((padded, LANES))
         none = jnp.zeros((padded, LANES), HALF)
         rim = left_ref[...]
-        sect = here()[1]
-        reach = jnp.where(sect < sects - 1, REACH, 0)
-        start = jnp.where(sect > 0, LANES - 2, LANES)
 
         def expand(r):
             at, off = divmod(r * REACH, LANES)
@@ -298,7 +288,7 @@
                 piece = jnp.where(lane < LANES - off, piece, pltpu.roll(after, LANES - off, 1))
             turn = pltpu.roll(rim, (LANES - 2 - 2 * r) % LANES, 1)
             ext[r, :padded] = jnp.where(
-                lane < reach, piece, jnp.where(lane >= start, turn, none)
+                lane < REACH, piece, jnp.where(lane >= LANES - 2, turn, none)
             )
 
         ext[:, padded:] = jnp.zeros((rows, deep - padded, LANES), HALF)
@@ -490,14 +480,12 @@
     )[0]
 
 
-def spread(turned, right, left, sects):
+def spread(turned, right, left):
     rows, _, cols = turned.shape
     span = right.shape[1]
     loose = cols + 16
 
     def body(rows_ref, right_ref, left_ref, out_ref, after, before, line):
-        sect = here()[1]
-
         def upright(value):
             value = value.astype(FULL)
             return jnp.concatenate(
@@ -506,8 +494,8 @@
 
         for t in range(span // LANES):
             lanes = slice(t * LANES, (t + 1) * LANES)
-            after[lanes] = jnp.where(sect < sects - 1, upright(right_ref[:, lanes]), 0.0)
-        before[...] = jnp.where(sect > 0, upright(left_ref[...]), 0.0)
+            after[lanes] = upright(right_ref[:, lanes])
+        before[...] = upright(left_ref[...])
         line[...] = jnp.zeros(line.shape, FULL)
 
         def spread_rows(i, carry):
@@ -624,7 +612,41 @@
     )[0]
 
 
-def canvas(anchor, pieces, sources, place, sects, rows, cols):
+def fill_view(view, at_ref, pieces, sources, sects, rows, cols):
+    padded = pieces[0].shape[-2]
+    tile_rows = view.shape[0]
+    none = jnp.zeros((padded, LANES), HALF)
+    anchors = slot_anchors(at_ref, sources, sects, rows, cols)
+    for at, (piece, (row0, _)) in enumerate(zip(pieces, anchors)):
+        lanes = slice(at * LANES, (at + 1) * LANES)
+        for r in range(rows):
+            i = r - row0
+            tile = jnp.clip(
+                jnp.right_shift(i, tile_rows.bit_length() - 1), 0, SIDE // tile_rows - 1
+            )
+            value = piece[:, pl.ds(pl.multiple_of(tile * LANES, LANES), LANES)]
+            inside = (i >= 0) & (i < SIDE)
+            view[r % tile_rows, r // tile_rows, :padded, lanes] = jnp.where(inside, value, none)
+    view[:, :, padded:, :] = jnp.zeros(
+        view.shape[:2] + (view.shape[2] - padded, view.shape[3]), HALF
+    )
+
+
+def view_shape(pieces, rows):
+    tile_rows = LANES // SIDE
+    deep = -(-pieces[0].shape[-2] // 16) * 16
+    return (tile_rows, rows // tile_rows, deep, len(pieces) * LANES)
+
+
+def gather_view(anchor, pieces, sources, sects, rows, cols):
+    def body(at_ref, *refs):
+        fill_view(refs[-1], at_ref, refs[:-1], sources, sects, rows, cols)
+
+    shape = view_shape(pieces, rows)
+    return run(body, [like(shape)], [anchor, *pieces], [], micros=0.8)[0]
+
+
+def canvas(anchor, early, pieces, sources, place, sects, rows, cols):
     padded = pieces[0].shape[-2]
     deep = -(-padded // 16) * 16
     total = anchor.shape[1]
@@ -634,26 +656,13 @@
 
     def body(at_ref, *refs):
         band, sect = here()
-        place_ref, spill_ref, out_ref, inverse_ref, view = refs[slots:]
-        none = jnp.zeros((padded, LANES), HALF)
-        anchors = slot_anchors(at_ref, sources, sects, rows, cols)
-        for piece, j, (row0, _) in zip(refs, sources, anchors):
-            lanes = slice(j * LANES, (j + 1) * LANES)
-            for r in range(rows):
-                i = r - row0
-                tile = jnp.clip(jnp.right_shift(i, tile_rows.bit_length() - 1), 0, SIDE // tile_rows - 1)
-                value = piece[:, pl.ds(pl.multiple_of(tile * LANES, LANES), LANES)]
-                inside = (i >= 0) & (i < SIDE)
-                view[r % tile_rows, r // tile_rows, :padded, lanes] = jnp.where(
-                    inside, value, none
-                )
-        view[:, :, padded:, :] = jnp.zeros(
-            (tile_rows, groups, deep - padded, slots * LANES), HALF
-        )
+        early_ref, place_ref, spill_ref, out_ref, inverse_ref, view = refs[slots:]
+        fill_view(view, at_ref, refs[:slots], sources, sects, rows, cols)
         spilled = None
         for m in range(tile_rows):
+            both = jnp.concatenate([early_ref[m], view[m]], axis=-1)
             value = jnp.dot(
-                view[m].reshape(groups * deep, slots * LANES), place_ref[m],
+                both.reshape(groups * deep, both.shape[-1]), place_ref[m],
                 preferred_element_type=FULL,
             ).reshape(groups, deep, 2 * LANES)
             for k in range(groups):
@@ -677,8 +686,8 @@
             like((rows, padded, cols), FULL),
             like((rows, cols), FULL),
         ],
-        [anchor, *pieces, place],
-        [pltpu.VMEM((tile_rows, groups, deep, slots * LANES), HALF)],
+        [anchor, *pieces, early, place],
+        [pltpu.VMEM(view_shape(pieces, rows), HALF)],
         micros=1.5
     )
 
@@ -692,7 +701,6 @@
     def body(top_ref, low_ref, sum_ref, spill_ref, inverse_ref, out_ref, flat, ready, sems):
         lane = lane_index((padded, LANES))
         none = jnp.zeros((padded, LANES), HALF)
-        reach = jnp.where(here()[1] > 0, SIDE, 0)
         flat[:, padded:] = jnp.zeros((chunk, deep - padded, cols), HALF)
         copies = []
         for first in range(0, rows, chunk):
@@ -701,7 +709,7 @@
                 extra = spill_ref[:, at * LANES : (at + 1) * LANES]
                 if low:
                     extra = pltpu.roll(extra, LANES - low, 1)
-                extra = jnp.where(lane < reach, extra, none).astype(FULL)
+                extra = jnp.where(lane < SIDE, extra, none).astype(FULL)
                 mean = top_ref[r] if r < half else low_ref[r - half]
                 value = mean.astype(FULL) + (sum_ref[r] + extra) * inverse_ref[r : r + 1]
                 flat[r - first, :padded] = value.astype(HALF)
@@ -751,10 +759,11 @@
     anchor = patch_anchor.T
 
     right_rim, left_rim, turned = pack(state_field)
-    right = cycle_from(right_rim, "sect", -1)
-    left = cycle_from(left_rim, "sect", 1)
-
-    made, lines, noise = prep(
+    right = shift_from(right_rim, "sect", -1)
+    left = shift_from(left_rim, "sect", 1)
+
+    made, lines, noise, place = prep(
+        anchor,
         [
             conv_in_weight.transpose(0, 2, 1),
             conv_out_weight,
@@ -763,11 +772,15 @@
         ],
         [conv_in_bias[None, :], conv_out_bias[None, :], denoise_bias[None, :], step_bias],
         patch_noise[0],
+        bands,
+        sects,
+        rows,
+        cols,
     )
     biases, step_lines = lines[:3], lines[3]
 
     padded = right_rim.shape[0]
-    pick, place = picks(anchor, bands, sects, rows, cols)
+    pick = picks(anchor, bands, sects, rows, cols)
     parts = extract_own(anchor, turned, pick, padded, bands, sects)
     own, kept, own_sent, sent, edge_near, edge_cross = extract_rim(
         anchor, parts, turned, right, left, pick, bands, sects
@@ -790,23 +803,23 @@
         anchor, addends, noise, made, biases, step_lines, sects, limits
     )
     pieces = [correction]
-    sources = [0]
+    sources = arrival(bands)
     bit = bands // 2
     while bit:
         fresh = []
         for piece in pieces:
             fresh.append(swap(piece, "band", bit))
         pieces += fresh
-        sources += [s ^ bit for s in sources]
         bit //= 2
 
-    shifted = spread(turned, right, left, sects)
+    shifted = spread(turned, right, left)
     top_mean = grid_mean(shifted, rim_near, rim_cross, False, padded, made[:2], biases[:2], limits)
     low_mean = grid_mean(shifted, rim_near, rim_cross, True, padded, made[:2], biases[:2], limits)
+    early = gather_view(anchor, pieces[:-1], sources[:-1], sects, rows, cols)
     spilled, summed, inverse = canvas(
-        anchor, pieces, sources, place, sects, rows, cols
-    )
-    arrived = cycle_from(spilled, "sect", 1)
+        anchor, early, pieces[-1:], sources[-1:], place, sects, rows, cols
+    )
+    arrived = shift_from(spilled, "sect", 1)
     return finish([top_mean, low_mean], summed, arrived, inverse, channels)
 
 

time: 55.4 us -> 54.7 us (0.987)
  the two profiles are of different devices: /device:TPU:0 before, /device:TPU:18 now
where the time goes in v6:
time: 54.7 us; the launch traced here: 54.5 us
  Pallas kernels  25.5 us (47%)
  waiting for transfers between devices  14.6 us (27%)
  starting transfers between devices  12.6 us (23%)
  local copies, waits for them, and re-layouts  1.28 us (2%)
    pallas_call x13, Pallas kernels, run(): pl.pallas_call(body, out_shape=outs, in_specs=[pl.BlockSpec(memory_space=...  25.5 us
    ppermute x7, waiting for transfers between devices, swap(): return lax.ppermute(block, axis, [(i, i ^ bit) for i in range(count)])  9.46 us
    ppermute x3, starting transfers between devices, shift_from(): return lax.ppermute(block, axis, route)  7.77 us
    ppermute x3, waiting for transfers between devices, shift_from(): return lax.ppermute(block, axis, route)  5.15 us
    ppermute x1, starting transfers between devices, step(): lax.ppermute(edge_cross, 'band', steps + [(j, i) for i, j in steps])  3.88 us
    unnamed x23, local copies, waits for them, and re-layouts  1.28 us
  transfers between devices with their start and end apart: 11, of which 5 were waited for; matrix products, arithmetic and copies ran while one was open for 0% of the time, Pallas kernels for 35%

profile of v6, /device:TPU:18, one launch (start us, length us, event | category | flops | bytes accessed | tf_op | source)
XLA Modules:
  0.0 54.5 jit_solution(17121999717799633658)
XLA Ops:
  0.0 1.1 %copy-done = bf16[99,32,128]{2,1,0:T(8,128)(2,1)S(1)} copy-done((bf16[99,32,128]{2,1,0:T(8,128)(2,1)S(1)}, bf16[99,32,128]{2,1,0:T(8,128)(2,1)}, u32[]{:S(2)}) %copy-start) | copy-done | bytes 811032
  1.1 0.7 %shard_map.109 = (bf16[104,1152]{1,0:T(8,128)(2,1)S(1)}, bf16[104,128]{1,0:T(8,128)(2,1)S(1)}, bf16[32,112,128]{2,1,0:T(8,128)(2,1)S(1)}) custom-call(bf16[99,32,128]{2,1,0:T(8,128)(2,1)S(1)} %copy-done), custom_call_target="tpu_custom_call" | custom-call | flops 1150000000 | bytes 1024 | tf_op jit(solution)/shard_map/pallas_call | solution.py:32
  1.9 2.4 %collective-permute-start = (bf16[104,1152]{1,0:T(8,128)(2,1)S(1)}, bf16[104,1152]{1,0:T(8,128)(2,1)S(1)}, u32[]{:S(2)}, u32[]{:S(2)}) collective-permute-start(bf16[104,1152]{1,0:T(8,128)(2,1)S(1)} %get-tuple-element.28), channel_id=1, source_target_pairs={{1,0},{2,1},{3,2},{5,4},{6,5},{7,6},{9,8},{10,9},{11,10},{13,12},{... | collective-permute-start | bytes 718856 | tf_op jit(solution)/shard_map/ppermute | solution.py:23
  4.2 3.5 %collective-permute-start.1 = (bf16[104,128]{1,0:T(8,128)(2,1)S(1)}, bf16[104,128]{1,0:T(8,128)(2,1)S(1)}, u32[]{:S(2)}, u32[]{:S(2)}) collective-permute-start(bf16[104,128]{1,0:T(8,128)(2,1)S(1)} %get-tuple-element.29), channel_id=1, source_target_pairs={{0,1},{1,2},{2,3},{4,5},{5,6},{6,7},{8,9},{9,10},{10,11},{12,13},{... | collective-permute-start | bytes 79880 | tf_op jit(solution)/shard_map/ppermute | solution.py:23
  7.8 0.0 copy-done.6
  7.8 0.2 shard_map.111.pick_ref
  8.0 2.2 %shard_map.112.part_ref = bf16[4,104,1536]{2,1,0:T(8,128)(2,1)S(1)} custom-call(s32[2,16]{1,0:T(2,128)S(1)} %bitcast.13, bf16[32,112,128]{2,1,0:T(8,128)(2,1)S(1)} %get-tuple-element.27.rows_ref, bf16[256,512]{1,0:T(8,128)(2,1)S(1)} %shard_map.111.pick_ref), custom_call_target="tpu_custom_call" | custom-call | flops 1724999936 | bytes 1024 | tf_op jit(solution)/shard_map/pallas_call | solution.py:32
  10.2 0.0 copy-start.10
  10.2 0.0 copy-start.1
  10.2 0.0 copy-start.2
  10.2 0.0 copy-start.3
  10.2 0.0 copy-start.4
  10.2 0.0 copy-start.5
  10.3 0.0 copy-start.7
  10.3 0.0 copy-start.8
  10.3 0.0 copy-start.9
  10.3 0.0 collective-permute-done.1.left_ref
  10.3 1.0 %collective-permute-done.right_ref = bf16[104,1152]{1,0:T(8,128)(2,1)S(1)} collective-permute-done((bf16[104,1152]{1,0:T(8,128)(2,1)S(1)}, bf16[104,1152]{1,0:T(8,128)(2,1)S(1)}, u32[]{:S(2)}, u32[]{:S(2)}) %collective-permute-start) | collective-permute-done | bytes 239648 | tf_op jit(solution)/shard_map/ppermute | solution.py:23
  11.3 2.9 %shard_map.113 = (bf16[1,104,1536]{2,1,0:T(8,128)(2,1)S(1)}, bf16[1,104,1536]{2,1,0:T(8,128)(2,1)S(1)}, bf16[1,104,1536]{2,1,0:T(8,128)(2,1)S(1)}, bf16[1,104,15...) custom-call(s32[2,16]{1,0:T(2,128)S(1)} %bitcast.14, ...), custom_call_target="tpu_custom_call" | custom-call | flops 1724999936 | bytes 1024 | tf_op jit(solution)/shard_map/pallas_call | solution.py:32
  14.2 0.1 collective-permute-start.4
  14.3 0.5 collective-permute-start.6
  14.8 1.1 %collective-permute-done.4.got_ref = bf16[1,104,1536]{2,1,0:T(8,128)(2,1)S(1)} collective-permute-done((bf16[1,104,1536]{2,1,0:T(8,128)(2,1)S(1)}, bf16[1,104,1536]{2,1,0:T(8,128)(2,1)S(1)}, u32[]{:S(2)}, u32[]{:S(2)}) %collective-permute-start.4) | collective-permute-done | bytes 319520 | tf_op jit(solution)/shard_map/ppermute | solution.py:28
  15.9 0.1 collective-permute-start.5
  16.0 0.0 copy-done.10
  16.0 0.1 copy.14
  16.1 0.0 copy-done.1
  16.2 1.3 %shard_map.114 = (bf16[1536,256]{1,0:T(8,128)(2,1)S(1)}, bf16[256,1536]{1,0:T(8,128)(2,1)S(1)}, bf16[1536,256]{1,0:T(8,128)(2,1)S(1)}, bf16[256,1536]{1,0:T(8,12...) custom-call(s32[2,16]{1,0:T(2,128)S(1)} %bitcast.15, ...), custom_call_target="tpu_custom_call" | custom-call | flops 1724999936 | bytes 1024 | tf_op jit(solution)/shard_map/pallas_call | solution.py:32
  17.5 0.2 collective-permute-start.2
  17.7 3.9 %collective-permute-start.3 = (bf16[2,112,256]{2,1,0:T(8,128)(2,1)S(1)}, bf16[2,112,256]{2,1,0:T(8,128)(2,1)S(1)}, u32[]{:S(2)}, u32[]{:S(2)}) collective-permute-start(bf16[2,112,256]{2,1,0:T(8,128)(2,1)S(1)} %get-tuple-element.31), channel_id=1, source_target_pairs={{4,8},{8,4},{5,9},{9,5},{6,10},{10,6},{7,11},{11,7},{20,24},{24,20... | collective-permute-start | bytes 344072 | tf_op jit(solution)/shard_map/ppermute | solution.py:801
  21.6 0.0 collective-permute-done.6.refs_3_
  21.6 4.8 %collective-permute-done.5.refs_2_ = bf16[1,104,1536]{2,1,0:T(8,128)(2,1)S(1)} collective-permute-done((bf16[1,104,1536]{2,1,0:T(8,128)(2,1)S(1)}, bf16[1,104,1536]{2,1,0:T(8,128)(2,1)S(1)}, u32[]{:S(2)}, u32[]{:S(2)}) %collective-permute-start.5) | collective-permute-done | bytes 319520 | tf_op jit(solution)/shard_map/ppermute | solution.py:28
  26.4 5.4 %shard_map.118.refs_0_ = bf16[104,1024]{1,0:T(8,128)(2,1)S(1)} custom-call(s32[2,16]{1,0:T(2,128)S(1)} %bitcast.16, bf16[1,104,1536]{2,1,0:T(8,128)(2,1)S(1)} %get-tuple-element.36.refs_1_, bf16[1,104,1536]{2,1,0:T(8,128)(2,1)S(1)} %collective-permute-done.5.refs_2_, bf16[1,104,1536]{2,1,0:T(8,128)(2,1)S(1)} %collective-permute-done.6.refs_3_, ...), custom_call_target="tpu_custom_call" | custom-call | flops 9200000000 | bytes 1024 | tf_op jit(solution)/shard_map/pallas_call | solution.py:32
  31.8 0.1 collective-permute-start.7
  31.9 2.2 %shard_map.110.shifted_ref = bf16[3,16,2,144,128]{4,3,2,1,0:T(8,128)(2,1)S(1)} custom-call(bf16[32,112,128]{2,1,0:T(8,128)(2,1)S(1)} %get-tuple-element.27.rows_ref, bf16[104,1152]{1,0:T(8,128)(2,1)S(1)} %collective-permute-done.right_ref, bf16[104,128]{1,0:T(8,128)(2,1)S(1)} %collective-permute-done.1.left_ref), custom_call_target="tpu_custom_call" | custom-call | flops 2875000064 | bytes 1024 | tf_op jit(solution)/shard_map/pallas_call | solution.py:32
  34.1 0.1 collective-permute-start.9
  34.2 3.6 %collective-permute-done.7.refs_1_ = bf16[104,1024]{1,0:T(8,128)(2,1)S(1)} collective-permute-done((bf16[104,1024]{1,0:T(8,128)(2,1)S(1)}, bf16[104,1024]{1,0:T(8,128)(2,1)S(1)}, u32[]{:S(2)}, u32[]{:S(2)}) %collective-permute-start.7) | collective-permute-done | bytes 213024 | tf_op jit(solution)/shard_map/ppermute | solution.py:28
  37.8 0.0 collective-permute-start.8
  37.8 0.0 collective-permute-done.2.near_ref
  37.8 0.0 collective-permute-done.3.cross_ref
  37.8 3.5 %shard_map.116.low_ref = bf16[16,104,128]{2,1,0:T(8,128)(2,1)S(1)} custom-call(bf16[3,16,2,144,128]{4,3,2,1,0:T(8,128)(2,1)S(1)} %shard_map.110.shifted_ref, bf16[2,112,256]{2,1,0:T(8,128)(2,1)S(1)} %collective-permute-done.2.near_ref, bf16[2,112,256]{2,1,0:T(8,128)(2,1)S(1)} %collective-permute-done.3.cross_ref, ...), custom_call_target="tpu_custom_call" | custom-call | flops 4024999936 | bytes 1024 | tf_op jit(solution)/shard_map/pallas_call | solution.py:32
  41.3 0.0 collective-permute-done.9.refs_2_
  41.3 0.8 %shard_map.119.refs_1_ = bf16[4,8,112,384]{3,2,1,0:T(8,128)(2,1)S(1)} custom-call(s32[2,16]{1,0:T(2,128)S(1)} %bitcast.17, bf16[104,1024]{1,0:T(8,128)(2,1)S(1)} %shard_map.118.refs_0_, bf16[104,1024]{1,0:T(8,128)(2,1)S(1)} %collective-permute-done.7.refs_1_, bf16[104,1024]{1,0:T(8,128)(2,1)S(1)} %collective-permute-done.9.refs_2_), custom_call_target="tpu_custom_call" | custom-call | flops 920000000 | bytes 1024 | tf_op jit(solution)/shard_map/pallas_call | solution.py:32
  42.1 0.0 collective-permute-done.8.refs_0_
  42.1 1.2 %shard_map.120 = (bf16[104,1024]{1,0:T(8,128)(2,1)S(1)}, f32[32,104,128]{2,1,0:T(8,128)S(1)}, f32[32,128]{1,0:T(8,128)S(1)}) custom-call(s32[2,16]{1,0:T(2,128)S(1)} %bitcast.18, bf16[104,1024]{1,0:T(8,128)(2,1)S(1)} %collective-permute-done.8.refs_0_, bf16[4,8,112,384]{3,2,1,0:T(8,128)(2,1)S(1)} %shard_map.119.refs_1_, ...), custom_call_target="tpu_custom_call" | custom-call | flops 1724999936 | bytes 1024 | tf_op jit(solution)/shard_map/pallas_call | solution.py:32
  43.3 1.9 %collective-permute-start.10 = (bf16[104,1024]{1,0:T(8,128)(2,1)S(1)}, bf16[104,1024]{1,0:T(8,128)(2,1)S(1)}, u32[]{:S(2)}, u32[]{:S(2)}) collective-permute-start(bf16[104,1024]{1,0:T(8,128)(2,1)S(1)} %get-tuple-element.47), channel_id=1, source_target_pairs={{0,1},{1,2},{2,3},{4,5},{5,6},{6,7},{8,9},{9,10},{10,11},{12,13},{... | collective-permute-start | bytes 638984 | tf_op jit(solution)/shard_map/ppermute | solution.py:23
  45.2 3.5 %shard_map.115.top_ref = bf16[16,104,128]{2,1,0:T(8,128)(2,1)S(1)} custom-call(bf16[3,16,2,144,128]{4,3,2,1,0:T(8,128)(2,1)S(1)} %shard_map.110.shifted_ref, bf16[2,112,256]{2,1,0:T(8,128)(2,1)S(1)} %collective-permute-done.2.near_ref, bf16[2,112,256]{2,1,0:T(8,128)(2,1)S(1)} %collective-permute-done.3.cross_ref, ...), custom_call_target="tpu_custom_call" | custom-call | flops 4024999936 | bytes 1024 | tf_op jit(solution)/shard_map/pallas_call | solution.py:32
  48.7 4.1 %collective-permute-done.10.spill_ref = bf16[104,1024]{1,0:T(8,128)(2,1)S(1)} collective-permute-done((bf16[104,1024]{1,0:T(8,128)(2,1)S(1)}, bf16[104,1024]{1,0:T(8,128)(2,1)S(1)}, u32[]{:S(2)}, u32[]{:S(2)}) %collective-permute-start.10) | collective-permute-done | bytes 213024 | tf_op jit(solution)/shard_map/ppermute | solution.py:23
  52.9 1.5 %shard_map.121 = bf16[99,32,128]{2,1,0:T(8,128)(2,1)} custom-call(bf16[16,104,128]{2,1,0:T(8,128)(2,1)S(1)} %shard_map.115.top_ref, bf16[16,104,128]{2,1,0:T(8,128)(2,1)S(1)} %shard_map.116.low_ref, f32[32,104,128]{2,1,0:T(8,128)S(1)} %get-tuple-element.46.sum_ref, bf16[104,1024]{1,0:T(8,128)(2,1)S(1)} %collective-permute-done.10.spill_ref, ...), custom_call_target="tpu_custom_call" | custom-call | flops 2300000000 | bytes 1024 | tf_op jit(solution)/shard_map/pallas_call | solution.py:32
  (10 shorter events, 0.1 us)
Async XLA Ops:
  0.0 1.1 %copy-start = (bf16[99,32,128]{2,1,0:T(8,128)(2,1)S(1)}, bf16[99,32,128]{2,1,0:T(8,128)(2,1)}, u32[]{:S(2)}) copy-start(bf16[99,32,128]{2,1,0:T(8,128)(2,1)} %state_ref.1) | copy-start | bytes 2433028
  1.1 6.6 %copy-start.6 = (s32[16,2]{0,1:T(2,128)S(1)}, s32[16,2]{0,1:T(2,128)}, u32[]{:S(2)}) copy-start(s32[16,2]{0,1:T(2,128)} %param.16) | copy-start | bytes 388
  1.9 9.5 %collective-permute-start = (bf16[104,1152]{1,0:T(8,128)(2,1)S(1)}, bf16[104,1152]{1,0:T(8,128)(2,1)S(1)}, u32[]{:S(2)}, u32[]{:S(2)}) collective-permute-start(bf16[104,1152]{1,0:T(8,128)(2,1)S(1)} %get-tuple-element.28), channel_id=1, source_target_pairs={{1,0},{2,1},{3,2},{5,4},{6,5},{7,6},{9,8},{10,9},{11,10},{13,12},{... | collective-permute-start | bytes 718856 | tf_op jit(solution)/shard_map/ppermute | solution.py:23
  4.2 6.1 %collective-permute-start.1 = (bf16[104,128]{1,0:T(8,128)(2,1)S(1)}, bf16[104,128]{1,0:T(8,128)(2,1)S(1)}, u32[]{:S(2)}, u32[]{:S(2)}) collective-permute-start(bf16[104,128]{1,0:T(8,128)(2,1)S(1)} %get-tuple-element.29), channel_id=1, source_target_pairs={{0,1},{1,2},{2,3},{4,5},{5,6},{6,7},{8,9},{9,10},{10,11},{12,13},{... | collective-permute-start | bytes 79880 | tf_op jit(solution)/shard_map/ppermute | solution.py:23
  10.2 5.8 %copy-start.10 = (bf16[1,2,99,1024]{3,1,2,0:T(2,128)(2,1)S(1)}, bf16[1,2,99,1024]{3,1,2,0:T(2,128)(2,1)}, u32[]{:S(2)}) copy-start(bf16[1,2,99,1024]{3,1,2,0:T(2,128)(2,1)} %param.17) | copy-start | bytes 1216516
  10.2 5.9 %copy-start.1 = (bf16[9,128,99]{1,2,0:T(8,128)(2,1)S(1)}, bf16[9,128,99]{1,2,0:T(8,128)(2,1)}, u32[]{:S(2)}) copy-start(bf16[9,128,99]{1,2,0:T(8,128)(2,1)} %param.12) | copy-start | bytes 684292
  10.2 5.9 %copy-start.2 = (bf16[9,99,128]{2,1,0:T(8,128)(2,1)S(1)}, bf16[9,99,128]{2,1,0:T(8,128)(2,1)}, u32[]{:S(2)}) copy-start(bf16[9,99,128]{2,1,0:T(8,128)(2,1)} %refs_1_.1) | copy-start | bytes 684292
  10.2 5.9 %copy-start.3 = (bf16[9,128,99]{1,2,0:T(8,128)(2,1)S(1)}, bf16[9,128,99]{1,2,0:T(8,128)(2,1)}, u32[]{:S(2)}) copy-start(bf16[9,128,99]{1,2,0:T(8,128)(2,1)} %param.18) | copy-start | bytes 684292
  10.2 5.9 %copy-start.4 = (bf16[9,99,128]{2,1,0:T(8,128)(2,1)S(1)}, bf16[9,99,128]{2,1,0:T(8,128)(2,1)}, u32[]{:S(2)}) copy-start(bf16[9,99,128]{2,1,0:T(8,128)(2,1)} %refs_3_.1) | copy-start | bytes 684292
  10.2 5.9 %copy-start.5 = (f32[2,128]{1,0:T(2,128)S(1)}, f32[2,128]{1,0:T(2,128)}, u32[]{:S(2)}) copy-start(f32[2,128]{1,0:T(2,128)} %refs_7_.1) | copy-start | bytes 3076
  10.3 5.9 %copy-start.7 = (f32[128]{0:T(128)S(1)}, f32[128]{0:T(128)}, u32[]{:S(2)}) copy-start(f32[128]{0:T(128)} %param.13) | copy-start | bytes 1540
  10.3 5.9 %copy-start.8 = (f32[99]{0:T(128)S(1)}, f32[99]{0:T(128)}, u32[]{:S(2)}) copy-start(f32[99]{0:T(128)} %param.15) | copy-start | bytes 1192
  10.3 5.9 %copy-start.9 = (f32[99]{0:T(128)S(1)}, f32[99]{0:T(128)}, u32[]{:S(2)}) copy-start(f32[99]{0:T(128)} %param.21) | copy-start | bytes 1192
  14.2 1.7 %collective-permute-start.4 = (bf16[1,104,1536]{2,1,0:T(8,128)(2,1)S(1)}, bf16[1,104,1536]{2,1,0:T(8,128)(2,1)S(1)}, u32[]{:S(2)}, u32[]{:S(2)}) collective-permute-start(bf16[1,104,1536]{2,1,0:T(8,128)(2,1)S(1)} %get-tuple-element.38), channel_id=1, source_target_pairs={{0,4},{4,0},{8,12},{12,8},{1,5},{5,1},{9,13},{13,9},{2,6},{6,2},{1... | collective-permute-start | bytes 958472 | tf_op jit(solution)/shard_map/ppermute | solution.py:28
  14.3 7.3 %collective-permute-start.6 = (bf16[1,104,1536]{2,1,0:T(8,128)(2,1)S(1)}, bf16[1,104,1536]{2,1,0:T(8,128)(2,1)S(1)}, u32[]{:S(2)}, u32[]{:S(2)}) collective-permute-start(bf16[1,104,1536]{2,1,0:T(8,128)(2,1)S(1)} %get-tuple-element.39), channel_id=1, source_target_pairs={{0,4},{4,0},{8,12},{12,8},{1,5},{5,1},{9,13},{13,9},{2,6},{6,2},{1... | collective-permute-start | bytes 958472 | tf_op jit(solution)/shard_map/ppermute | solution.py:28
  15.9 10.5 %collective-permute-start.5 = (bf16[1,104,1536]{2,1,0:T(8,128)(2,1)S(1)}, bf16[1,104,1536]{2,1,0:T(8,128)(2,1)S(1)}, u32[]{:S(2)}, u32[]{:S(2)}) collective-permute-start(bf16[1,104,1536]{2,1,0:T(8,128)(2,1)S(1)} %shard_map.117), channel_id=1, source_target_pairs={{0,8},{4,12},{8,0},{12,4},{1,9},{5,13},{9,1},{13,5},{2,10},{6,14},... | collective-permute-start | bytes 958472 | tf_op jit(solution)/shard_map/ppermute | solution.py:28
  17.5 20.2 %collective-permute-start.2 = (bf16[2,112,256]{2,1,0:T(8,128)(2,1)S(1)}, bf16[2,112,256]{2,1,0:T(8,128)(2,1)S(1)}, u32[]{:S(2)}, u32[]{:S(2)}) collective-permute-start(bf16[2,112,256]{2,1,0:T(8,128)(2,1)S(1)} %get-tuple-element.30), channel_id=1, source_target_pairs={{0,4},{4,0},{8,12},{12,8},{1,5},{5,1},{9,13},{13,9},{2,6},{6,2},{1... | collective-permute-start | bytes 344072 | tf_op jit(solution)/shard_map/ppermute | solution.py:28
  17.7 20.0 %collective-permute-start.3 = (bf16[2,112,256]{2,1,0:T(8,128)(2,1)S(1)}, bf16[2,112,256]{2,1,0:T(8,128)(2,1)S(1)}, u32[]{:S(2)}, u32[]{:S(2)}) collective-permute-start(bf16[2,112,256]{2,1,0:T(8,128)(2,1)S(1)} %get-tuple-element.31), channel_id=1, source_target_pairs={{4,8},{8,4},{5,9},{9,5},{6,10},{10,6},{7,11},{11,7},{20,24},{24,20... | collective-permute-start | bytes 344072 | tf_op jit(solution)/shard_map/ppermute | solution.py:801
  31.8 5.9 %collective-permute-start.7 = (bf16[104,1024]{1,0:T(8,128)(2,1)S(1)}, bf16[104,1024]{1,0:T(8,128)(2,1)S(1)}, u32[]{:S(2)}, u32[]{:S(2)}) collective-permute-start(bf16[104,1024]{1,0:T(8,128)(2,1)S(1)} %shard_map.118.refs_0_), channel_id=1, source_target_pairs={{0,8},{4,12},{8,0},{12,4},{1,9},{5,13},{9,1},{13,5},{2,10},{6,14},... | collective-permute-start | bytes 638984 | tf_op jit(solution)/shard_map/ppermute | solution.py:28
  34.1 7.2 %collective-permute-start.9 = (bf16[104,1024]{1,0:T(8,128)(2,1)S(1)}, bf16[104,1024]{1,0:T(8,128)(2,1)S(1)}, u32[]{:S(2)}, u32[]{:S(2)}) collective-permute-start(bf16[104,1024]{1,0:T(8,128)(2,1)S(1)} %shard_map.118.refs_0_), channel_id=1, source_target_pairs={{0,4},{4,0},{8,12},{12,8},{1,5},{5,1},{9,13},{13,9},{2,6},{6,2},{1... | collective-permute-start | bytes 638984 | tf_op jit(solution)/shard_map/ppermute | solution.py:28
  37.8 4.4 %collective-permute-start.8 = (bf16[104,1024]{1,0:T(8,128)(2,1)S(1)}, bf16[104,1024]{1,0:T(8,128)(2,1)S(1)}, u32[]{:S(2)}, u32[]{:S(2)}) collective-permute-start(bf16[104,1024]{1,0:T(8,128)(2,1)S(1)} %collective-permute-done.7.refs_1_), channel_id=1, source_target_pairs={{0,4},{4,0},{8,12},{12,8},{1,5},{5,1},{9,13},{13,9},{2,6},{6,2},{1... | collective-permute-start | bytes 638984 | tf_op jit(solution)/shard_map/ppermute | solution.py:28
  43.3 9.5 %collective-permute-start.10 = (bf16[104,1024]{1,0:T(8,128)(2,1)S(1)}, bf16[104,1024]{1,0:T(8,128)(2,1)S(1)}, u32[]{:S(2)}, u32[]{:S(2)}) collective-permute-start(bf16[104,1024]{1,0:T(8,128)(2,1)S(1)} %get-tuple-element.47), channel_id=1, source_target_pairs={{0,1},{1,2},{2,3},{4,5},{5,6},{6,7},{8,9},{9,10},{10,11},{12,13},{... | collective-permute-start | bytes 638984 | tf_op jit(solution)/shard_map/ppermute | solution.py:23

commit v7 on v6

--- a/solution.py
+++ b/solution.py
@@ -8,9 +8,9 @@
 
 SIDE = 32
 WIDE = SIDE + 4
-PER_TILE = 3
-TILES = WIDE // PER_TILE
 LANES = 128
+PER_PAIR = 2 * LANES // WIDE
+TILES = -(-(WIDE // PER_PAIR * 2 * LANES + WIDE % PER_PAIR * WIDE) // LANES)
 REACH = SIDE + 2
 CHUNKS = 1
 HALF = jnp.bfloat16
@@ -187,15 +187,21 @@
 
     def body(at_ref, pick_ref):
         source = lax.broadcasted_iota(jnp.int32, (width, LANES), 0)
-        inner = lane_index((width, LANES))
-        for _ in range(1, PER_TILE):
-            inner = jnp.where(inner >= WIDE, inner - WIDE, inner)
+        lane = lane_index((width, LANES))
+        inners = []
+        for half in range(2):
+            inner = lane + half * LANES
+            for _ in range(PER_PAIR):
+                inner = jnp.where(inner >= WIDE, inner - WIDE, inner)
+            inners.append(inner)
         anchors = slot_anchors(at_ref, range(bands), sects, rows, cols)
         for j, (row0, col0) in enumerate(anchors):
-            want = jnp.bitwise_and(inner + (col0 - 2), width - 1)
-            pick_ref[:, j * LANES : (j + 1) * LANES] = jnp.where(source == want, 1.0, 0.0).astype(HALF)
-
-    return run(body, [like((width, bands * LANES))], [anchor], [], micros=0.4)[0]
+            for half, inner in enumerate(inners):
+                want = jnp.bitwise_and(inner + (col0 - 2), width - 1)
+                at = (2 * j + half) * LANES
+                pick_ref[:, at : at + LANES] = jnp.where(source == want, 1.0, 0.0).astype(HALF)
+
+    return run(body, [like((width, 2 * bands * LANES))], [anchor], [], micros=0.4)[0]
 
 
 def add_parts(kept, got):
@@ -205,20 +211,26 @@
     return run(body, [like(kept.shape)], [kept, got], [], micros=0.3)[0]
 
 
-def window_tile(picked, t, row0, rows, padded, lanes):
+def window_tile(picked, t, row0, rows, padded, at):
     zone = lane_index((padded, LANES))
     total = jnp.zeros((padded, LANES), FULL)
-    for m in range(PER_TILE):
-        r = row0 + t * PER_TILE + m
-        low = jnp.where((r >= 0) & (r < rows), WIDE * m, 2 * LANES)
-        keep = (zone >= low) & (zone < WIDE * (m + 1))
+    pair, half = divmod(t, 2)
+    lanes = slice(at + half * LANES, at + (half + 1) * LANES)
+    for k in range(PER_PAIR):
+        i = pair * PER_PAIR + k
+        low, high = k * WIDE - half * LANES, (k + 1) * WIDE - half * LANES
+        if i >= WIDE or low >= LANES or high <= 0:
+            continue
+        r = row0 + i
+        start = jnp.where((r >= 0) & (r < rows), low, 2 * LANES)
+        keep = (zone >= start) & (zone < high)
         value = picked[jnp.clip(r, 0, rows - 1), :padded, lanes]
         total = jnp.where(keep, value, total)
     return total.astype(HALF)
 
 
 def batches(bands):
-    size = 4 if bands % 4 == 0 else bands
+    size = 2 if bands % 2 == 0 else bands
     return [range(first, first + size) for first in range(0, bands, size)], size
 
 
@@ -228,9 +240,10 @@
 
     def select(c, carry):
         view = source[pl.ds(c * chunk, chunk)].reshape(chunk * deep, LANES)
-        picked[pl.ds(c * chunk, chunk)] = jnp.dot(
-            view, pick, preferred_element_type=FULL
-        ).reshape(chunk, deep, pick.shape[1])
+        for at in range(0, pick.shape[1], LANES):
+            picked[pl.ds(c * chunk, chunk), :, at : at + LANES] = jnp.dot(
+                view, pick[:, at : at + LANES], preferred_element_type=FULL
+            ).reshape(chunk, deep, LANES)
         return carry
 
     lax.fori_loop(0, rows // chunk, select, 0)
@@ -243,16 +256,18 @@
     def body(at_ref, rows_ref, pick_ref, out_ref, picked):
         anchors = slot_anchors(at_ref, range(bands), sects, rows, cols)
         for group in groups:
-            select_rows(rows_ref, pick_ref[:cols, group[0] * LANES : (group[-1] + 1) * LANES], picked)
+            select_rows(
+                rows_ref, pick_ref[:cols, 2 * group[0] * LANES : 2 * (group[-1] + 1) * LANES], picked
+            )
             for j in group:
                 row0 = anchors[j][0] - 2
                 inside = (row0 > -WIDE) & (row0 < rows)
 
                 @pl.when(inside)
-                def _(j=j, row0=row0, at=(j - group[0]) * LANES):
+                def _(j=j, row0=row0, at=2 * (j - group[0]) * LANES):
                     for t in range(TILES):
                         out_ref[j, :, t * LANES : (t + 1) * LANES] = window_tile(
-                            picked, t, row0, rows, padded, slice(at, at + LANES)
+                            picked, t, row0, rows, padded, at
                         )
 
                 @pl.when(jnp.logical_not(inside))
@@ -263,7 +278,7 @@
         body,
         [like((bands, padded, TILES * LANES))],
         [anchor, turned, pick],
-        [pltpu.VMEM((rows, deep, size * LANES), FULL)],
+        [pltpu.VMEM((rows, deep, 2 * size * LANES), FULL)],
         micros=1.5
     )[0]
 
@@ -333,10 +348,10 @@
 
             @pl.when(over)
             def _(j=j, out_ref=out_ref, at=at, row0=row0):
-                select_rows(ext, pick_ref[cols:, j * LANES : (j + 1) * LANES], picked)
+                select_rows(ext, pick_ref[cols:, 2 * j * LANES : 2 * (j + 1) * LANES], picked)
                 for t in range(TILES):
                     out_ref[at, :, t * LANES : (t + 1) * LANES] += window_tile(
-                        picked, t, row0, rows, padded, slice(0, LANES)
+                        picked, t, row0, rows, padded, 0
                     )
 
     one = like((1, padded, TILES * LANES))
@@ -346,7 +361,7 @@
         body,
         [one, rest, one, rest, edge, edge],
         [anchor, parts, turned, right, left, pick],
-        [pltpu.VMEM((rows, deep, LANES), HALF), pltpu.VMEM((rows, deep, LANES), FULL)],
+        [pltpu.VMEM((rows, deep, LANES), HALF), pltpu.VMEM((rows, deep, 2 * LANES), FULL)],
         micros=1.5
     )
 
@@ -392,8 +407,8 @@
             tile = jnp.concatenate([tile, jnp.zeros((LANES - padded, LANES), FULL)], axis=0)
             flat[lanes, :] = tile.T
         for i in range(WIDE):
-            t, m = divmod(i, PER_TILE)
-            off = t * LANES + m * WIDE
+            pair, k = divmod(i, PER_PAIR)
+            off = pair * 2 * LANES + k * WIDE
             for b in range(3):
                 state_sh[b, i // 2, i % 2] = flat[off + b : off + b + loose, :].astype(HALF)
         pairs = half + 1
@@ -552,8 +567,10 @@
         for b in range(3):
             state_sh[b, skip : skip + given] = shifted_ref[b, at : at + given]
         pair = jnp.bitwise_and(band, 1) == (0 if lower else 1)
+        beyond = band == (limits[0] // rows - 1 if lower else 0)
+        none = jnp.zeros((deep, width), HALF)
         for v in range(2):
-            rim = jnp.where(pair, near_ref[v], cross_ref[v])
+            rim = jnp.where(beyond, none, jnp.where(pair, near_ref[v], cross_ref[v]))
             value = jnp.concatenate(
                 [rim.astype(FULL), jnp.zeros((LANES - deep, width), FULL)], axis=0
             ).T
@@ -798,7 +815,8 @@
     addends.append(swap(own_sent, "band", 1))
     rim_near = swap(edge_near, "band", 1)
     steps = [(i, i + 1) for i in range(1, bands - 1, 2)]
-    rim_cross = lax.ppermute(edge_cross, "band", steps + [(j, i) for i, j in steps])
+    alone = [(i, i) for i in range(bands) if all(i not in step for step in steps)]
+    rim_cross = lax.ppermute(edge_cross, "band", steps + [(j, i) for i, j in steps] + alone)
     correction = patch_step(
         anchor, addends, noise, made, biases, step_lines, sects, limits
     )

time: 54.7 us -> 55.1 us (level)
  Pallas kernels: 25.5 us -> 27.5 us
  waiting for transfers between devices: 14.6 us -> 13 us
    pallas_call x13, Pallas kernels: 25.5 us -> 27.5 us  [run(): pl.pallas_call(body, out_shape=outs, in_specs=[pl.BlockSpec(memory_space=...]
    ppermute x3, waiting for transfers between devices: 5.15 us -> 4.12 us  [shift_from(): return lax.ppermute(block, axis, route)]
    ppermute x7, waiting for transfers between devices: 9.46 us -> 8.86 us  [swap(): return lax.ppermute(block, axis, [(i, i ^ bit) for i in range(count)])]
  transfers between devices with their start and end apart: 11 -> 11, of which waited for: 5 -> 4; matrix products, arithmetic and copies ran while one was open for 0% -> 0% of each run, Pallas kernels for 35% -> 37%
where the time goes in v7:
time: 55.1 us; the launch traced here: 54.9 us
  Pallas kernels  27.5 us (50%)
  waiting for transfers between devices  13 us (24%)
  starting transfers between devices  12.6 us (23%)
  local copies, waits for them, and re-layouts  1.28 us (2%)
    pallas_call x13, Pallas kernels, run(): pl.pallas_call(body, out_shape=outs, in_specs=[pl.BlockSpec(memory_space=...  27.5 us
    ppermute x7, waiting for transfers between devices, swap(): return lax.ppermute(block, axis, [(i, i ^ bit) for i in range(count)])  8.86 us
    ppermute x3, starting transfers between devices, shift_from(): return lax.ppermute(block, axis, route)  7.77 us
    ppermute x3, waiting for transfers between devices, shift_from(): return lax.ppermute(block, axis, route)  4.12 us
    ppermute x1, starting transfers between devices, step(): lax.ppermute(edge_cross, 'band', steps + [(j, i) for i, j in steps] + alone)  3.88 us
    unnamed x23, local copies, waits for them, and re-layouts  1.28 us
  transfers between devices with their start and end apart: 11, of which 4 were waited for; matrix products, arithmetic and copies ran while one was open for 0% of the time, Pallas kernels for 37%

profile of v7, /device:TPU:18, one launch (start us, length us, event | category | flops | bytes accessed | tf_op | source)
XLA Modules:
  0.0 54.9 jit_solution(10375322648392049417)
XLA Ops:
  0.0 1.1 %copy-done = bf16[99,32,128]{2,1,0:T(8,128)(2,1)S(1)} copy-done((bf16[99,32,128]{2,1,0:T(8,128)(2,1)S(1)}, bf16[99,32,128]{2,1,0:T(8,128)(2,1)}, u32[]{:S(2)}) %copy-start) | copy-done | bytes 811032
  1.1 0.7 %shard_map.109 = (bf16[104,1152]{1,0:T(8,128)(2,1)S(1)}, bf16[104,128]{1,0:T(8,128)(2,1)S(1)}, bf16[32,112,128]{2,1,0:T(8,128)(2,1)S(1)}) custom-call(bf16[99,32,128]{2,1,0:T(8,128)(2,1)S(1)} %copy-done), custom_call_target="tpu_custom_call" | custom-call | flops 1150000000 | bytes 1024 | tf_op jit(solution)/shard_map/pallas_call | solution.py:32
  1.9 2.4 %collective-permute-start = (bf16[104,1152]{1,0:T(8,128)(2,1)S(1)}, bf16[104,1152]{1,0:T(8,128)(2,1)S(1)}, u32[]{:S(2)}, u32[]{:S(2)}) collective-permute-start(bf16[104,1152]{1,0:T(8,128)(2,1)S(1)} %get-tuple-element.28), channel_id=1, source_target_pairs={{1,0},{2,1},{3,2},{5,4},{6,5},{7,6},{9,8},{10,9},{11,10},{13,12},{... | collective-permute-start | bytes 718856 | tf_op jit(solution)/shard_map/ppermute | solution.py:23
  4.2 3.5 %collective-permute-start.1 = (bf16[104,128]{1,0:T(8,128)(2,1)S(1)}, bf16[104,128]{1,0:T(8,128)(2,1)S(1)}, u32[]{:S(2)}, u32[]{:S(2)}) collective-permute-start(bf16[104,128]{1,0:T(8,128)(2,1)S(1)} %get-tuple-element.29), channel_id=1, source_target_pairs={{0,1},{1,2},{2,3},{4,5},{5,6},{6,7},{8,9},{9,10},{10,11},{12,13},{... | collective-permute-start | bytes 79880 | tf_op jit(solution)/shard_map/ppermute | solution.py:23
  7.8 0.0 copy-done.6
  7.8 0.4 shard_map.111.pick_ref
  8.1 3.3 %shard_map.112.part_ref = bf16[4,104,1408]{2,1,0:T(8,128)(2,1)S(1)} custom-call(s32[2,16]{1,0:T(2,128)S(1)} %bitcast.13, bf16[32,112,128]{2,1,0:T(8,128)(2,1)S(1)} %get-tuple-element.27.rows_ref, bf16[256,1024]{1,0:T(8,128)(2,1)S(1)} %shard_map.111.pick_ref), custom_call_target="tpu_custom_call" | custom-call | flops 1724999936 | bytes 1024 | tf_op jit(solution)/shard_map/pallas_call | solution.py:32
  11.4 0.0 copy-start.10
  11.5 0.0 copy-start.1
  11.5 0.0 copy-start.2
  11.5 0.0 copy-start.3
  11.5 0.0 copy-start.4
  11.5 0.0 copy-start.5
  11.5 0.0 copy-start.7
  11.5 0.0 copy-start.8
  11.5 0.0 copy-start.9
  11.5 0.0 collective-permute-done.1.left_ref
  11.6 0.0 collective-permute-done.right_ref
  11.6 3.7 %shard_map.113 = (bf16[1,104,1408]{2,1,0:T(8,128)(2,1)S(1)}, bf16[1,104,1408]{2,1,0:T(8,128)(2,1)S(1)}, bf16[1,104,1408]{2,1,0:T(8,128)(2,1)S(1)}, bf16[1,104,14...) custom-call(s32[2,16]{1,0:T(2,128)S(1)} %bitcast.14, ...), custom_call_target="tpu_custom_call" | custom-call | flops 1724999936 | bytes 1024 | tf_op jit(solution)/shard_map/pallas_call | solution.py:32
  15.3 0.1 collective-permute-start.4
  15.3 0.5 collective-permute-start.6
  15.8 1.1 %collective-permute-done.4.got_ref = bf16[1,104,1408]{2,1,0:T(8,128)(2,1)S(1)} collective-permute-done((bf16[1,104,1408]{2,1,0:T(8,128)(2,1)S(1)}, bf16[1,104,1408]{2,1,0:T(8,128)(2,1)S(1)}, u32[]{:S(2)}, u32[]{:S(2)}) %collective-permute-start.4) | collective-permute-done | bytes 292896 | tf_op jit(solution)/shard_map/ppermute | solution.py:28
  16.9 0.1 collective-permute-start.5
  17.0 0.0 copy-done.10
  17.0 0.1 copy.14
  17.1 0.0 copy-done.1
  17.2 1.3 %shard_map.114 = (bf16[1536,256]{1,0:T(8,128)(2,1)S(1)}, bf16[256,1536]{1,0:T(8,128)(2,1)S(1)}, bf16[1536,256]{1,0:T(8,128)(2,1)S(1)}, bf16[256,1536]{1,0:T(8,12...) custom-call(s32[2,16]{1,0:T(2,128)S(1)} %bitcast.15, ...), custom_call_target="tpu_custom_call" | custom-call | flops 1724999936 | bytes 1024 | tf_op jit(solution)/shard_map/pallas_call | solution.py:32
  18.5 0.2 collective-permute-start.2
  18.7 3.9 %collective-permute-start.3 = (bf16[2,112,256]{2,1,0:T(8,128)(2,1)S(1)}, bf16[2,112,256]{2,1,0:T(8,128)(2,1)S(1)}, u32[]{:S(2)}, u32[]{:S(2)}) collective-permute-start(bf16[2,112,256]{2,1,0:T(8,128)(2,1)S(1)} %get-tuple-element.31), channel_id=1, source_target_pairs={{4,8},{8,4},{0,0},{12,12},{5,9},{9,5},{1,1},{13,13},{6,10},{10,6},... | collective-permute-start | bytes 344072 | tf_op jit(solution)/shard_map/ppermute | solution.py:819
  22.6 0.0 collective-permute-done.6.refs_3_
  22.6 4.2 %collective-permute-done.5.refs_2_ = bf16[1,104,1408]{2,1,0:T(8,128)(2,1)S(1)} collective-permute-done((bf16[1,104,1408]{2,1,0:T(8,128)(2,1)S(1)}, bf16[1,104,1408]{2,1,0:T(8,128)(2,1)S(1)}, u32[]{:S(2)}, u32[]{:S(2)}) %collective-permute-start.5) | collective-permute-done | bytes 292896 | tf_op jit(solution)/shard_map/ppermute | solution.py:28
  26.8 5.4 %shard_map.118.refs_0_ = bf16[104,1024]{1,0:T(8,128)(2,1)S(1)} custom-call(s32[2,16]{1,0:T(2,128)S(1)} %bitcast.16, bf16[1,104,1408]{2,1,0:T(8,128)(2,1)S(1)} %get-tuple-element.36.refs_1_, bf16[1,104,1408]{2,1,0:T(8,128)(2,1)S(1)} %collective-permute-done.5.refs_2_, bf16[1,104,1408]{2,1,0:T(8,128)(2,1)S(1)} %collective-permute-done.6.refs_3_, ...), custom_call_target="tpu_custom_call" | custom-call | flops 9200000000 | bytes 1024 | tf_op jit(solution)/shard_map/pallas_call | solution.py:32
  32.2 0.1 collective-permute-start.7
  32.3 2.2 %shard_map.110.shifted_ref = bf16[3,16,2,144,128]{4,3,2,1,0:T(8,128)(2,1)S(1)} custom-call(bf16[32,112,128]{2,1,0:T(8,128)(2,1)S(1)} %get-tuple-element.27.rows_ref, bf16[104,1152]{1,0:T(8,128)(2,1)S(1)} %collective-permute-done.right_ref, bf16[104,128]{1,0:T(8,128)(2,1)S(1)} %collective-permute-done.1.left_ref), custom_call_target="tpu_custom_call" | custom-call | flops 2875000064 | bytes 1024 | tf_op jit(solution)/shard_map/pallas_call | solution.py:32
  34.5 0.1 collective-permute-start.9
  34.6 3.6 %collective-permute-done.7.refs_1_ = bf16[104,1024]{1,0:T(8,128)(2,1)S(1)} collective-permute-done((bf16[104,1024]{1,0:T(8,128)(2,1)S(1)}, bf16[104,1024]{1,0:T(8,128)(2,1)S(1)}, u32[]{:S(2)}, u32[]{:S(2)}) %collective-permute-start.7) | collective-permute-done | bytes 213024 | tf_op jit(solution)/shard_map/ppermute | solution.py:28
  38.2 0.0 collective-permute-start.8
  38.2 0.0 collective-permute-done.2.near_ref
  38.2 0.0 collective-permute-done.3.cross_ref
  38.2 3.5 %shard_map.116.low_ref = bf16[16,104,128]{2,1,0:T(8,128)(2,1)S(1)} custom-call(bf16[3,16,2,144,128]{4,3,2,1,0:T(8,128)(2,1)S(1)} %shard_map.110.shifted_ref, bf16[2,112,256]{2,1,0:T(8,128)(2,1)S(1)} %collective-permute-done.2.near_ref, bf16[2,112,256]{2,1,0:T(8,128)(2,1)S(1)} %collective-permute-done.3.cross_ref, ...), custom_call_target="tpu_custom_call" | custom-call | flops 4024999936 | bytes 1024 | tf_op jit(solution)/shard_map/pallas_call | solution.py:32
  41.7 0.0 collective-permute-done.9.refs_2_
  41.7 0.8 %shard_map.119.refs_1_ = bf16[4,8,112,384]{3,2,1,0:T(8,128)(2,1)S(1)} custom-call(s32[2,16]{1,0:T(2,128)S(1)} %bitcast.17, bf16[104,1024]{1,0:T(8,128)(2,1)S(1)} %shard_map.118.refs_0_, bf16[104,1024]{1,0:T(8,128)(2,1)S(1)} %collective-permute-done.7.refs_1_, bf16[104,1024]{1,0:T(8,128)(2,1)S(1)} %collective-permute-done.9.refs_2_), custom_call_target="tpu_custom_call" | custom-call | flops 920000000 | bytes 1024 | tf_op jit(solution)/shard_map/pallas_call | solution.py:32
  42.5 0.0 collective-permute-done.8.refs_0_
  42.5 1.2 %shard_map.120 = (bf16[104,1024]{1,0:T(8,128)(2,1)S(1)}, f32[32,104,128]{2,1,0:T(8,128)S(1)}, f32[32,128]{1,0:T(8,128)S(1)}) custom-call(s32[2,16]{1,0:T(2,128)S(1)} %bitcast.18, bf16[104,1024]{1,0:T(8,128)(2,1)S(1)} %collective-permute-done.8.refs_0_, bf16[4,8,112,384]{3,2,1,0:T(8,128)(2,1)S(1)} %shard_map.119.refs_1_, ...), custom_call_target="tpu_custom_call" | custom-call | flops 1724999936 | bytes 1024 | tf_op jit(solution)/shard_map/pallas_call | solution.py:32
  43.7 1.9 %collective-permute-start.10 = (bf16[104,1024]{1,0:T(8,128)(2,1)S(1)}, bf16[104,1024]{1,0:T(8,128)(2,1)S(1)}, u32[]{:S(2)}, u32[]{:S(2)}) collective-permute-start(bf16[104,1024]{1,0:T(8,128)(2,1)S(1)} %get-tuple-element.47), channel_id=1, source_target_pairs={{0,1},{1,2},{2,3},{4,5},{5,6},{6,7},{8,9},{9,10},{10,11},{12,13},{... | collective-permute-start | bytes 638984 | tf_op jit(solution)/shard_map/ppermute | solution.py:23
  45.6 3.5 %shard_map.115.top_ref = bf16[16,104,128]{2,1,0:T(8,128)(2,1)S(1)} custom-call(bf16[3,16,2,144,128]{4,3,2,1,0:T(8,128)(2,1)S(1)} %shard_map.110.shifted_ref, bf16[2,112,256]{2,1,0:T(8,128)(2,1)S(1)} %collective-permute-done.2.near_ref, bf16[2,112,256]{2,1,0:T(8,128)(2,1)S(1)} %collective-permute-done.3.cross_ref, ...), custom_call_target="tpu_custom_call" | custom-call | flops 4024999936 | bytes 1024 | tf_op jit(solution)/shard_map/pallas_call | solution.py:32
  49.2 4.1 %collective-permute-done.10.spill_ref = bf16[104,1024]{1,0:T(8,128)(2,1)S(1)} collective-permute-done((bf16[104,1024]{1,0:T(8,128)(2,1)S(1)}, bf16[104,1024]{1,0:T(8,128)(2,1)S(1)}, u32[]{:S(2)}, u32[]{:S(2)}) %collective-permute-start.10) | collective-permute-done | bytes 213024 | tf_op jit(solution)/shard_map/ppermute | solution.py:23
  53.3 1.5 %shard_map.121 = bf16[99,32,128]{2,1,0:T(8,128)(2,1)} custom-call(bf16[16,104,128]{2,1,0:T(8,128)(2,1)S(1)} %shard_map.115.top_ref, bf16[16,104,128]{2,1,0:T(8,128)(2,1)S(1)} %shard_map.116.low_ref, f32[32,104,128]{2,1,0:T(8,128)S(1)} %get-tuple-element.46.sum_ref, bf16[104,1024]{1,0:T(8,128)(2,1)S(1)} %collective-permute-done.10.spill_ref, ...), custom_call_target="tpu_custom_call" | custom-call | flops 2300000000 | bytes 1024 | tf_op jit(solution)/shard_map/pallas_call | solution.py:32
  (10 shorter events, 0.1 us)
Async XLA Ops:
  0.0 1.1 %copy-start = (bf16[99,32,128]{2,1,0:T(8,128)(2,1)S(1)}, bf16[99,32,128]{2,1,0:T(8,128)(2,1)}, u32[]{:S(2)}) copy-start(bf16[99,32,128]{2,1,0:T(8,128)(2,1)} %state_ref.1) | copy-start | bytes 2433028
  1.1 6.6 %copy-start.6 = (s32[16,2]{0,1:T(2,128)S(1)}, s32[16,2]{0,1:T(2,128)}, u32[]{:S(2)}) copy-start(s32[16,2]{0,1:T(2,128)} %param.16) | copy-start | bytes 388
  1.9 9.7 %collective-permute-start = (bf16[104,1152]{1,0:T(8,128)(2,1)S(1)}, bf16[104,1152]{1,0:T(8,128)(2,1)S(1)}, u32[]{:S(2)}, u32[]{:S(2)}) collective-permute-start(bf16[104,1152]{1,0:T(8,128)(2,1)S(1)} %get-tuple-element.28), channel_id=1, source_target_pairs={{1,0},{2,1},{3,2},{5,4},{6,5},{7,6},{9,8},{10,9},{11,10},{13,12},{... | collective-permute-start | bytes 718856 | tf_op jit(solution)/shard_map/ppermute | solution.py:23
  4.2 7.3 %collective-permute-start.1 = (bf16[104,128]{1,0:T(8,128)(2,1)S(1)}, bf16[104,128]{1,0:T(8,128)(2,1)S(1)}, u32[]{:S(2)}, u32[]{:S(2)}) collective-permute-start(bf16[104,128]{1,0:T(8,128)(2,1)S(1)} %get-tuple-element.29), channel_id=1, source_target_pairs={{0,1},{1,2},{2,3},{4,5},{5,6},{6,7},{8,9},{9,10},{10,11},{12,13},{... | collective-permute-start | bytes 79880 | tf_op jit(solution)/shard_map/ppermute | solution.py:23
  11.4 5.6 %copy-start.10 = (bf16[1,2,99,1024]{3,1,2,0:T(2,128)(2,1)S(1)}, bf16[1,2,99,1024]{3,1,2,0:T(2,128)(2,1)}, u32[]{:S(2)}) copy-start(bf16[1,2,99,1024]{3,1,2,0:T(2,128)(2,1)} %param.17) | copy-start | bytes 1216516
  11.5 5.7 %copy-start.1 = (bf16[9,128,99]{1,2,0:T(8,128)(2,1)S(1)}, bf16[9,128,99]{1,2,0:T(8,128)(2,1)}, u32[]{:S(2)}) copy-start(bf16[9,128,99]{1,2,0:T(8,128)(2,1)} %param.12) | copy-start | bytes 684292
  11.5 5.7 %copy-start.2 = (bf16[9,99,128]{2,1,0:T(8,128)(2,1)S(1)}, bf16[9,99,128]{2,1,0:T(8,128)(2,1)}, u32[]{:S(2)}) copy-start(bf16[9,99,128]{2,1,0:T(8,128)(2,1)} %refs_1_.1) | copy-start | bytes 684292
  11.5 5.7 %copy-start.3 = (bf16[9,128,99]{1,2,0:T(8,128)(2,1)S(1)}, bf16[9,128,99]{1,2,0:T(8,128)(2,1)}, u32[]{:S(2)}) copy-start(bf16[9,128,99]{1,2,0:T(8,128)(2,1)} %param.18) | copy-start | bytes 684292
  11.5 5.7 %copy-start.4 = (bf16[9,99,128]{2,1,0:T(8,128)(2,1)S(1)}, bf16[9,99,128]{2,1,0:T(8,128)(2,1)}, u32[]{:S(2)}) copy-start(bf16[9,99,128]{2,1,0:T(8,128)(2,1)} %refs_3_.1) | copy-start | bytes 684292
  11.5 5.7 %copy-start.5 = (f32[2,128]{1,0:T(2,128)S(1)}, f32[2,128]{1,0:T(2,128)}, u32[]{:S(2)}) copy-start(f32[2,128]{1,0:T(2,128)} %refs_7_.1) | copy-start | bytes 3076
  11.5 5.7 %copy-start.7 = (f32[128]{0:T(128)S(1)}, f32[128]{0:T(128)}, u32[]{:S(2)}) copy-start(f32[128]{0:T(128)} %param.13) | copy-start | bytes 1540
  11.5 5.7 %copy-start.8 = (f32[99]{0:T(128)S(1)}, f32[99]{0:T(128)}, u32[]{:S(2)}) copy-start(f32[99]{0:T(128)} %param.15) | copy-start | bytes 1192
  11.5 5.7 %copy-start.9 = (f32[99]{0:T(128)S(1)}, f32[99]{0:T(128)}, u32[]{:S(2)}) copy-start(f32[99]{0:T(128)} %param.21) | copy-start | bytes 1192
  15.3 1.6 %collective-permute-start.4 = (bf16[1,104,1408]{2,1,0:T(8,128)(2,1)S(1)}, bf16[1,104,1408]{2,1,0:T(8,128)(2,1)S(1)}, u32[]{:S(2)}, u32[]{:S(2)}) collective-permute-start(bf16[1,104,1408]{2,1,0:T(8,128)(2,1)S(1)} %get-tuple-element.38), channel_id=1, source_target_pairs={{0,4},{4,0},{8,12},{12,8},{1,5},{5,1},{9,13},{13,9},{2,6},{6,2},{1... | collective-permute-start | bytes 878600 | tf_op jit(solution)/shard_map/ppermute | solution.py:28
  15.3 7.3 %collective-permute-start.6 = (bf16[1,104,1408]{2,1,0:T(8,128)(2,1)S(1)}, bf16[1,104,1408]{2,1,0:T(8,128)(2,1)S(1)}, u32[]{:S(2)}, u32[]{:S(2)}) collective-permute-start(bf16[1,104,1408]{2,1,0:T(8,128)(2,1)S(1)} %get-tuple-element.39), channel_id=1, source_target_pairs={{0,4},{4,0},{8,12},{12,8},{1,5},{5,1},{9,13},{13,9},{2,6},{6,2},{1... | collective-permute-start | bytes 878600 | tf_op jit(solution)/shard_map/ppermute | solution.py:28
  16.9 9.9 %collective-permute-start.5 = (bf16[1,104,1408]{2,1,0:T(8,128)(2,1)S(1)}, bf16[1,104,1408]{2,1,0:T(8,128)(2,1)S(1)}, u32[]{:S(2)}, u32[]{:S(2)}) collective-permute-start(bf16[1,104,1408]{2,1,0:T(8,128)(2,1)S(1)} %shard_map.117), channel_id=1, source_target_pairs={{0,8},{4,12},{8,0},{12,4},{1,9},{5,13},{9,1},{13,5},{2,10},{6,14},... | collective-permute-start | bytes 878600 | tf_op jit(solution)/shard_map/ppermute | solution.py:28
  18.5 19.6 %collective-permute-start.2 = (bf16[2,112,256]{2,1,0:T(8,128)(2,1)S(1)}, bf16[2,112,256]{2,1,0:T(8,128)(2,1)S(1)}, u32[]{:S(2)}, u32[]{:S(2)}) collective-permute-start(bf16[2,112,256]{2,1,0:T(8,128)(2,1)S(1)} %get-tuple-element.30), channel_id=1, source_target_pairs={{0,4},{4,0},{8,12},{12,8},{1,5},{5,1},{9,13},{13,9},{2,6},{6,2},{1... | collective-permute-start | bytes 344072 | tf_op jit(solution)/shard_map/ppermute | solution.py:28
  18.7 19.4 %collective-permute-start.3 = (bf16[2,112,256]{2,1,0:T(8,128)(2,1)S(1)}, bf16[2,112,256]{2,1,0:T(8,128)(2,1)S(1)}, u32[]{:S(2)}, u32[]{:S(2)}) collective-permute-start(bf16[2,112,256]{2,1,0:T(8,128)(2,1)S(1)} %get-tuple-element.31), channel_id=1, source_target_pairs={{4,8},{8,4},{0,0},{12,12},{5,9},{9,5},{1,1},{13,13},{6,10},{10,6},... | collective-permute-start | bytes 344072 | tf_op jit(solution)/shard_map/ppermute | solution.py:819
  32.2 5.9 %collective-permute-start.7 = (bf16[104,1024]{1,0:T(8,128)(2,1)S(1)}, bf16[104,1024]{1,0:T(8,128)(2,1)S(1)}, u32[]{:S(2)}, u32[]{:S(2)}) collective-permute-start(bf16[104,1024]{1,0:T(8,128)(2,1)S(1)} %shard_map.118.refs_0_), channel_id=1, source_target_pairs={{0,8},{4,12},{8,0},{12,4},{1,9},{5,13},{9,1},{13,5},{2,10},{6,14},... | collective-permute-start | bytes 638984 | tf_op jit(solution)/shard_map/ppermute | solution.py:28
  34.5 7.2 %collective-permute-start.9 = (bf16[104,1024]{1,0:T(8,128)(2,1)S(1)}, bf16[104,1024]{1,0:T(8,128)(2,1)S(1)}, u32[]{:S(2)}, u32[]{:S(2)}) collective-permute-start(bf16[104,1024]{1,0:T(8,128)(2,1)S(1)} %shard_map.118.refs_0_), channel_id=1, source_target_pairs={{0,4},{4,0},{8,12},{12,8},{1,5},{5,1},{9,13},{13,9},{2,6},{6,2},{1... | collective-permute-start | bytes 638984 | tf_op jit(solution)/shard_map/ppermute | solution.py:28
  38.2 4.4 %collective-permute-start.8 = (bf16[104,1024]{1,0:T(8,128)(2,1)S(1)}, bf16[104,1024]{1,0:T(8,128)(2,1)S(1)}, u32[]{:S(2)}, u32[]{:S(2)}) collective-permute-start(bf16[104,1024]{1,0:T(8,128)(2,1)S(1)} %collective-permute-done.7.refs_1_), channel_id=1, source_target_pairs={{0,4},{4,0},{8,12},{12,8},{1,5},{5,1},{9,13},{13,9},{2,6},{6,2},{1... | collective-permute-start | bytes 638984 | tf_op jit(solution)/shard_map/ppermute | solution.py:28
  43.7 9.5 %collective-permute-start.10 = (bf16[104,1024]{1,0:T(8,128)(2,1)S(1)}, bf16[104,1024]{1,0:T(8,128)(2,1)S(1)}, u32[]{:S(2)}, u32[]{:S(2)}) collective-permute-start(bf16[104,1024]{1,0:T(8,128)(2,1)S(1)} %get-tuple-element.47), channel_id=1, source_target_pairs={{0,1},{1,2},{2,3},{4,5},{5,6},{6,7},{8,9},{9,10},{10,11},{12,13},{... | collective-permute-start | bytes 638984 | tf_op jit(solution)/shard_map/ppermute | solution.py:23

commit v8 on v7

--- a/solution.py
+++ b/solution.py
@@ -182,28 +182,6 @@
     return out[:count], out[count : count + lines], *out[count + lines :]
 
 
-def picks(anchor, bands, sects, rows, cols):
-    width = cols + LANES
-
-    def body(at_ref, pick_ref):
-        source = lax.broadcasted_iota(jnp.int32, (width, LANES), 0)
-        lane = lane_index((width, LANES))
-        inners = []
-        for half in range(2):
-            inner = lane + half * LANES
-            for _ in range(PER_PAIR):
-                inner = jnp.where(inner >= WIDE, inner - WIDE, inner)
-            inners.append(inner)
-        anchors = slot_anchors(at_ref, range(bands), sects, rows, cols)
-        for j, (row0, col0) in enumerate(anchors):
-            for half, inner in enumerate(inners):
-                want = jnp.bitwise_and(inner + (col0 - 2), width - 1)
-                at = (2 * j + half) * LANES
-                pick_ref[:, at : at + LANES] = jnp.where(source == want, 1.0, 0.0).astype(HALF)
-
-    return run(body, [like((width, 2 * bands * LANES))], [anchor], [], micros=0.4)[0]
-
-
 def add_parts(kept, got):
     def body(kept_ref, got_ref, out_ref):
         out_ref[...] = kept_ref[...] + got_ref[...]
@@ -211,84 +189,54 @@
     return run(body, [like(kept.shape)], [kept, got], [], micros=0.3)[0]
 
 
-def window_tile(picked, t, row0, rows, padded, at):
-    zone = lane_index((padded, LANES))
-    total = jnp.zeros((padded, LANES), FULL)
+def window_tile(source, t, row0, col0, low, high, rows, padded):
+    lane = lane_index((1, LANES))
+    total = jnp.zeros((padded, LANES), HALF)
     pair, half = divmod(t, 2)
-    lanes = slice(at + half * LANES, at + (half + 1) * LANES)
     for k in range(PER_PAIR):
         i = pair * PER_PAIR + k
-        low, high = k * WIDE - half * LANES, (k + 1) * WIDE - half * LANES
-        if i >= WIDE or low >= LANES or high <= 0:
+        zone = k * WIDE - half * LANES
+        if i >= WIDE or zone >= LANES or zone + WIDE <= 0:
             continue
         r = row0 + i
-        start = jnp.where((r >= 0) & (r < rows), low, 2 * LANES)
-        keep = (zone >= start) & (zone < high)
-        value = picked[jnp.clip(r, 0, rows - 1), :padded, lanes]
-        total = jnp.where(keep, value, total)
-    return total.astype(HALF)
-
-
-def batches(bands):
-    size = 2 if bands % 2 == 0 else bands
-    return [range(first, first + size) for first in range(0, bands, size)], size
-
-
-def select_rows(source, pick, picked):
-    rows, deep, _ = source.shape
-    chunk = rows // 2
-
-    def select(c, carry):
-        view = source[pl.ds(c * chunk, chunk)].reshape(chunk * deep, LANES)
-        for at in range(0, pick.shape[1], LANES):
-            picked[pl.ds(c * chunk, chunk), :, at : at + LANES] = jnp.dot(
-                view, pick[:, at : at + LANES], preferred_element_type=FULL
-            ).reshape(chunk, deep, LANES)
-        return carry
-
-    lax.fori_loop(0, rows // chunk, select, 0)
-
-
-def extract_own(anchor, turned, pick, padded, bands, sects):
-    rows, deep, cols = turned.shape
-    groups, size = batches(bands)
-
-    def body(at_ref, rows_ref, pick_ref, out_ref, picked):
+        first = jnp.where((r >= 0) & (r < rows), zone + low, 2 * LANES)
+        keep = jnp.where((lane >= first) & (lane < zone + high), 1.0, 0.0).astype(HALF)
+        turn = jnp.bitwise_and(zone + 2 - col0, LANES - 1)
+        value = pltpu.roll(source[jnp.clip(r, 0, rows - 1), :padded], turn, 1)
+        total = total + value * keep
+    return total
+
+
+def extract_own(anchor, turned, padded, bands, sects):
+    rows, _, cols = turned.shape
+
+    def body(at_ref, rows_ref, out_ref):
         anchors = slot_anchors(at_ref, range(bands), sects, rows, cols)
-        for group in groups:
-            select_rows(
-                rows_ref, pick_ref[:cols, 2 * group[0] * LANES : 2 * (group[-1] + 1) * LANES], picked
-            )
-            for j in group:
-                row0 = anchors[j][0] - 2
-                inside = (row0 > -WIDE) & (row0 < rows)
-
-                @pl.when(inside)
-                def _(j=j, row0=row0, at=2 * (j - group[0]) * LANES):
-                    for t in range(TILES):
-                        out_ref[j, :, t * LANES : (t + 1) * LANES] = window_tile(
-                            picked, t, row0, rows, padded, at
-                        )
-
-                @pl.when(jnp.logical_not(inside))
-                def _(j=j):
-                    out_ref[j] = jnp.zeros((padded, TILES * LANES), HALF)
-
-    return run(
-        body,
-        [like((bands, padded, TILES * LANES))],
-        [anchor, turned, pick],
-        [pltpu.VMEM((rows, deep, 2 * size * LANES), FULL)],
-        micros=1.5
-    )[0]
-
-
-def extract_rim(anchor, parts, turned, right, left, pick, bands, sects):
+        for j, (row0, col0) in enumerate(anchors):
+            row0 = row0 - 2
+            inside = (row0 > -WIDE) & (row0 < rows)
+            low, high = jnp.maximum(2 - col0, 0), jnp.minimum(cols + 2 - col0, WIDE)
+
+            @pl.when(inside)
+            def _(j=j, row0=row0, col0=col0, low=low, high=high):
+                for t in range(TILES):
+                    out_ref[j, :, t * LANES : (t + 1) * LANES] = window_tile(
+                        rows_ref, t, row0, col0, low, high, rows, padded
+                    )
+
+            @pl.when(jnp.logical_not(inside))
+            def _(j=j):
+                out_ref[j] = jnp.zeros((padded, TILES * LANES), HALF)
+
+    return run(body, [like((bands, padded, TILES * LANES))], [anchor, turned], [], micros=1.5)[0]
+
+
+def extract_rim(anchor, parts, turned, right, left, bands, sects):
     rows, deep, cols = turned.shape
     padded = right.shape[0]
 
-    def body(at_ref, part_ref, rows_ref, right_ref, left_ref, pick_ref,
-             own_ref, low_ref, odd_ref, high_ref, near_ref, cross_ref, ext, picked):
+    def body(at_ref, part_ref, rows_ref, right_ref, left_ref,
+             own_ref, low_ref, odd_ref, high_ref, near_ref, cross_ref, ext):
         lane = lane_index((padded, LANES))
         none = jnp.zeros((padded, LANES), HALF)
         rim = left_ref[...]
@@ -329,11 +277,13 @@
             row0 = row0 - 2
             inside = (row0 > -WIDE) & (row0 < rows)
             over = inside & ((col0 < 2) | (col0 > cols - REACH))
-            crossing.append((row0, over))
+            low = jnp.where(col0 < 2, 0, cols + 2 - col0)
+            high = jnp.where(col0 < 2, 2 - col0, WIDE)
+            crossing.append((over, row0, col0, low, high))
             out_ref, at = target(j)
             out_ref[at] = part_ref[j]
-        some = crossing[0][1]
-        for _, over in crossing[1:]:
+        some = crossing[0][0]
+        for over, *_ in crossing[1:]:
             some = some | over
 
         @pl.when(some)
@@ -342,16 +292,14 @@
                 if r not in outer:
                     expand(r)
 
-        for j in range(bands):
+        for j, (over, *where) in enumerate(crossing):
             out_ref, at = target(j)
-            row0, over = crossing[j]
 
             @pl.when(over)
-            def _(j=j, out_ref=out_ref, at=at, row0=row0):
-                select_rows(ext, pick_ref[cols:, 2 * j * LANES : 2 * (j + 1) * LANES], picked)
+            def _(out_ref=out_ref, at=at, where=where):
                 for t in range(TILES):
                     out_ref[at, :, t * LANES : (t + 1) * LANES] += window_tile(
-                        picked, t, row0, rows, padded, 0
+                        ext, t, *where, rows, padded
                     )
 
     one = like((1, padded, TILES * LANES))
@@ -360,8 +308,8 @@
     return run(
         body,
         [one, rest, one, rest, edge, edge],
-        [anchor, parts, turned, right, left, pick],
-        [pltpu.VMEM((rows, deep, LANES), HALF), pltpu.VMEM((rows, deep, 2 * LANES), FULL)],
+        [anchor, parts, turned, right, left],
+        [pltpu.VMEM((rows, deep, LANES), HALF)],
         micros=1.5
     )
 
@@ -797,10 +745,9 @@
     biases, step_lines = lines[:3], lines[3]
 
     padded = right_rim.shape[0]
-    pick = picks(anchor, bands, sects, rows, cols)
-    parts = extract_own(anchor, turned, pick, padded, bands, sects)
+    parts = extract_own(anchor, turned, padded, bands, sects)
     own, kept, own_sent, sent, edge_near, edge_cross = extract_rim(
-        anchor, parts, turned, right, left, pick, bands, sects
+        anchor, parts, turned, right, left, bands, sects
     )
     addends = [own]
     if bands > 2:

time: 55.1 us -> 53.1 us (0.964)
  Pallas kernels: 27.5 us -> 23.4 us
  waiting for transfers between devices: 13 us -> 15.1 us
    pallas_call x13 -> x12, Pallas kernels: 27.5 us -> 23.4 us  [run(): pl.pallas_call(body, out_shape=outs, in_specs=[pl.BlockSpec(memory_space=...]
    ppermute x3, waiting for transfers between devices: 4.12 us -> 6.25 us  [shift_from(): return lax.ppermute(block, axis, route)]
  transfers between devices with their start and end apart: 11 -> 11, of which waited for: 4 -> 6; matrix products, arithmetic and copies ran while one was open for 0% -> 0% of each run, Pallas kernels for 37% -> 34%
where the time goes in v8:
time: 53.1 us; the launch traced here: 52.9 us
  Pallas kernels  23.4 us (44%)
  waiting for transfers between devices  15.1 us (28%)
  starting transfers between devices  12.6 us (24%)
  local copies, waits for them, and re-layouts  1.28 us (2%)
    pallas_call x12, Pallas kernels, run(): pl.pallas_call(body, out_shape=outs, in_specs=[pl.BlockSpec(memory_space=...  23.4 us
    ppermute x7, waiting for transfers between devices, swap(): return lax.ppermute(block, axis, [(i, i ^ bit) for i in range(count)])  8.85 us
    ppermute x3, starting transfers between devices, shift_from(): return lax.ppermute(block, axis, route)  7.77 us
    ppermute x3, waiting for transfers between devices, shift_from(): return lax.ppermute(block, axis, route)  6.25 us
    ppermute x1, starting transfers between devices, step(): lax.ppermute(edge_cross, 'band', steps + [(j, i) for i, j in steps] + alone)  3.88 us
    unnamed x23, local copies, waits for them, and re-layouts  1.28 us
  transfers between devices with their start and end apart: 11, of which 6 were waited for; matrix products, arithmetic and copies ran while one was open for 0% of the time, Pallas kernels for 34%

profile of v8, /device:TPU:18, one launch (start us, length us, event | category | flops | bytes accessed | tf_op | source)
XLA Modules:
  0.0 52.9 jit_solution(16816832856554469332)
XLA Ops:
  0.0 1.1 %copy-done = bf16[99,32,128]{2,1,0:T(8,128)(2,1)S(1)} copy-done((bf16[99,32,128]{2,1,0:T(8,128)(2,1)S(1)}, bf16[99,32,128]{2,1,0:T(8,128)(2,1)}, u32[]{:S(2)}) %copy-start) | copy-done | bytes 811032
  1.1 0.7 %shard_map.109 = (bf16[104,1152]{1,0:T(8,128)(2,1)S(1)}, bf16[104,128]{1,0:T(8,128)(2,1)S(1)}, bf16[32,112,128]{2,1,0:T(8,128)(2,1)S(1)}) custom-call(bf16[99,32,128]{2,1,0:T(8,128)(2,1)S(1)} %copy-done), custom_call_target="tpu_custom_call" | custom-call | flops 1150000000 | bytes 1024 | tf_op jit(solution)/shard_map/pallas_call | solution.py:32
  1.9 2.4 %collective-permute-start = (bf16[104,1152]{1,0:T(8,128)(2,1)S(1)}, bf16[104,1152]{1,0:T(8,128)(2,1)S(1)}, u32[]{:S(2)}, u32[]{:S(2)}) collective-permute-start(bf16[104,1152]{1,0:T(8,128)(2,1)S(1)} %get-tuple-element.28), channel_id=1, source_target_pairs={{1,0},{2,1},{3,2},{5,4},{6,5},{7,6},{9,8},{10,9},{11,10},{13,12},{... | collective-permute-start | bytes 718856 | tf_op jit(solution)/shard_map/ppermute | solution.py:23
  4.2 3.5 %collective-permute-start.1 = (bf16[104,128]{1,0:T(8,128)(2,1)S(1)}, bf16[104,128]{1,0:T(8,128)(2,1)S(1)}, u32[]{:S(2)}, u32[]{:S(2)}) collective-permute-start(bf16[104,128]{1,0:T(8,128)(2,1)S(1)} %get-tuple-element.29), channel_id=1, source_target_pairs={{0,1},{1,2},{2,3},{4,5},{5,6},{6,7},{8,9},{9,10},{10,11},{12,13},{... | collective-permute-start | bytes 79880 | tf_op jit(solution)/shard_map/ppermute | solution.py:23
  7.8 0.0 copy-done.6
  7.8 1.3 %shard_map.111.part_ref = bf16[4,104,1408]{2,1,0:T(8,128)(2,1)S(1)} custom-call(s32[2,16]{1,0:T(2,128)S(1)} %bitcast.12, bf16[32,112,128]{2,1,0:T(8,128)(2,1)S(1)} %get-tuple-element.27.rows_ref), custom_call_target="tpu_custom_call" | custom-call | flops 1724999936 | bytes 1024 | tf_op jit(solution)/shard_map/pallas_call | solution.py:32
  9.1 0.0 copy-start.10
  9.1 0.0 copy-start.1
  9.1 0.0 copy-start.2
  9.1 0.0 copy-start.3
  9.1 0.0 copy-start.4
  9.2 0.0 copy-start.5
  9.2 0.0 copy-start.7
  9.2 0.0 copy-start.8
  9.2 0.0 copy-start.9
  9.2 0.8 %collective-permute-done.1.left_ref = bf16[104,128]{1,0:T(8,128)(2,1)S(1)} collective-permute-done((bf16[104,128]{1,0:T(8,128)(2,1)S(1)}, bf16[104,128]{1,0:T(8,128)(2,1)S(1)}, u32[]{:S(2)}, u32[]{:S(2)}) %collective-permute-start.1) | collective-permute-done | bytes 26656 | tf_op jit(solution)/shard_map/ppermute | solution.py:23
  10.0 1.3 %collective-permute-done.right_ref = bf16[104,1152]{1,0:T(8,128)(2,1)S(1)} collective-permute-done((bf16[104,1152]{1,0:T(8,128)(2,1)S(1)}, bf16[104,1152]{1,0:T(8,128)(2,1)S(1)}, u32[]{:S(2)}, u32[]{:S(2)}) %collective-permute-start) | collective-permute-done | bytes 239648 | tf_op jit(solution)/shard_map/ppermute | solution.py:23
  11.3 1.9 %shard_map.112 = (bf16[1,104,1408]{2,1,0:T(8,128)(2,1)S(1)}, bf16[1,104,1408]{2,1,0:T(8,128)(2,1)S(1)}, bf16[1,104,1408]{2,1,0:T(8,128)(2,1)S(1)}, bf16[1,104,14...) custom-call(s32[2,16]{1,0:T(2,128)S(1)} %bitcast.13, ...), custom_call_target="tpu_custom_call" | custom-call | flops 1724999936 | bytes 1024 | tf_op jit(solution)/shard_map/pallas_call | solution.py:32
  13.3 0.1 collective-permute-start.4
  13.3 0.5 collective-permute-start.6
  13.8 1.1 %collective-permute-done.4.got_ref = bf16[1,104,1408]{2,1,0:T(8,128)(2,1)S(1)} collective-permute-done((bf16[1,104,1408]{2,1,0:T(8,128)(2,1)S(1)}, bf16[1,104,1408]{2,1,0:T(8,128)(2,1)S(1)}, u32[]{:S(2)}, u32[]{:S(2)}) %collective-permute-start.4) | collective-permute-done | bytes 292896 | tf_op jit(solution)/shard_map/ppermute | solution.py:28
  14.9 0.1 collective-permute-start.5
  15.0 0.0 copy-done.10
  15.0 0.1 copy.14
  15.1 0.0 copy-done.1
  15.1 0.0 copy-done.2
  15.2 1.3 %shard_map.113 = (bf16[1536,256]{1,0:T(8,128)(2,1)S(1)}, bf16[256,1536]{1,0:T(8,128)(2,1)S(1)}, bf16[1536,256]{1,0:T(8,128)(2,1)S(1)}, bf16[256,1536]{1,0:T(8,12...) custom-call(s32[2,16]{1,0:T(2,128)S(1)} %bitcast.14, ...), custom_call_target="tpu_custom_call" | custom-call | flops 1724999936 | bytes 1024 | tf_op jit(solution)/shard_map/pallas_call | solution.py:32
  16.5 0.2 collective-permute-start.2
  16.7 3.9 %collective-permute-start.3 = (bf16[2,112,256]{2,1,0:T(8,128)(2,1)S(1)}, bf16[2,112,256]{2,1,0:T(8,128)(2,1)S(1)}, u32[]{:S(2)}, u32[]{:S(2)}) collective-permute-start(bf16[2,112,256]{2,1,0:T(8,128)(2,1)S(1)} %get-tuple-element.31), channel_id=1, source_target_pairs={{4,8},{8,4},{0,0},{12,12},{5,9},{9,5},{1,1},{13,13},{6,10},{10,6},... | collective-permute-start | bytes 344072 | tf_op jit(solution)/shard_map/ppermute | solution.py:766
  20.6 0.0 collective-permute-done.6.refs_3_
  20.6 4.2 %collective-permute-done.5.refs_2_ = bf16[1,104,1408]{2,1,0:T(8,128)(2,1)S(1)} collective-permute-done((bf16[1,104,1408]{2,1,0:T(8,128)(2,1)S(1)}, bf16[1,104,1408]{2,1,0:T(8,128)(2,1)S(1)}, u32[]{:S(2)}, u32[]{:S(2)}) %collective-permute-start.5) | collective-permute-done | bytes 292896 | tf_op jit(solution)/shard_map/ppermute | solution.py:28
  24.8 5.4 %shard_map.117.refs_0_ = bf16[104,1024]{1,0:T(8,128)(2,1)S(1)} custom-call(s32[2,16]{1,0:T(2,128)S(1)} %bitcast.15, bf16[1,104,1408]{2,1,0:T(8,128)(2,1)S(1)} %get-tuple-element.36.refs_1_, bf16[1,104,1408]{2,1,0:T(8,128)(2,1)S(1)} %collective-permute-done.5.refs_2_, bf16[1,104,1408]{2,1,0:T(8,128)(2,1)S(1)} %collective-permute-done.6.refs_3_, ...), custom_call_target="tpu_custom_call" | custom-call | flops 9200000000 | bytes 1024 | tf_op jit(solution)/shard_map/pallas_call | solution.py:32
  30.3 0.1 collective-permute-start.7
  30.3 2.2 %shard_map.110.shifted_ref = bf16[3,16,2,144,128]{4,3,2,1,0:T(8,128)(2,1)S(1)} custom-call(bf16[32,112,128]{2,1,0:T(8,128)(2,1)S(1)} %get-tuple-element.27.rows_ref, bf16[104,1152]{1,0:T(8,128)(2,1)S(1)} %collective-permute-done.right_ref, bf16[104,128]{1,0:T(8,128)(2,1)S(1)} %collective-permute-done.1.left_ref), custom_call_target="tpu_custom_call" | custom-call | flops 2875000064 | bytes 1024 | tf_op jit(solution)/shard_map/pallas_call | solution.py:32
  32.5 0.1 collective-permute-start.9
  32.6 3.6 %collective-permute-done.7.refs_1_ = bf16[104,1024]{1,0:T(8,128)(2,1)S(1)} collective-permute-done((bf16[104,1024]{1,0:T(8,128)(2,1)S(1)}, bf16[104,1024]{1,0:T(8,128)(2,1)S(1)}, u32[]{:S(2)}, u32[]{:S(2)}) %collective-permute-start.7) | collective-permute-done | bytes 213024 | tf_op jit(solution)/shard_map/ppermute | solution.py:28
  36.2 0.0 collective-permute-start.8
  36.2 0.0 collective-permute-done.2.near_ref
  36.2 0.0 collective-permute-done.3.cross_ref
  36.2 3.5 %shard_map.115.low_ref = bf16[16,104,128]{2,1,0:T(8,128)(2,1)S(1)} custom-call(bf16[3,16,2,144,128]{4,3,2,1,0:T(8,128)(2,1)S(1)} %shard_map.110.shifted_ref, bf16[2,112,256]{2,1,0:T(8,128)(2,1)S(1)} %collective-permute-done.2.near_ref, bf16[2,112,256]{2,1,0:T(8,128)(2,1)S(1)} %collective-permute-done.3.cross_ref, ...), custom_call_target="tpu_custom_call" | custom-call | flops 4024999936 | bytes 1024 | tf_op jit(solution)/shard_map/pallas_call | solution.py:32
  39.7 0.0 collective-permute-done.9.refs_2_
  39.7 0.8 %shard_map.118.refs_1_ = bf16[4,8,112,384]{3,2,1,0:T(8,128)(2,1)S(1)} custom-call(s32[2,16]{1,0:T(2,128)S(1)} %bitcast.16, bf16[104,1024]{1,0:T(8,128)(2,1)S(1)} %shard_map.117.refs_0_, bf16[104,1024]{1,0:T(8,128)(2,1)S(1)} %collective-permute-done.7.refs_1_, bf16[104,1024]{1,0:T(8,128)(2,1)S(1)} %collective-permute-done.9.refs_2_), custom_call_target="tpu_custom_call" | custom-call | flops 920000000 | bytes 1024 | tf_op jit(solution)/shard_map/pallas_call | solution.py:32
  40.5 0.0 collective-permute-done.8.refs_0_
  40.5 1.2 %shard_map.119 = (bf16[104,1024]{1,0:T(8,128)(2,1)S(1)}, f32[32,104,128]{2,1,0:T(8,128)S(1)}, f32[32,128]{1,0:T(8,128)S(1)}) custom-call(s32[2,16]{1,0:T(2,128)S(1)} %bitcast.17, bf16[104,1024]{1,0:T(8,128)(2,1)S(1)} %collective-permute-done.8.refs_0_, bf16[4,8,112,384]{3,2,1,0:T(8,128)(2,1)S(1)} %shard_map.118.refs_1_, ...), custom_call_target="tpu_custom_call" | custom-call | flops 1724999936 | bytes 1024 | tf_op jit(solution)/shard_map/pallas_call | solution.py:32
  41.7 1.9 %collective-permute-start.10 = (bf16[104,1024]{1,0:T(8,128)(2,1)S(1)}, bf16[104,1024]{1,0:T(8,128)(2,1)S(1)}, u32[]{:S(2)}, u32[]{:S(2)}) collective-permute-start(bf16[104,1024]{1,0:T(8,128)(2,1)S(1)} %get-tuple-element.47), channel_id=1, source_target_pairs={{0,1},{1,2},{2,3},{4,5},{5,6},{6,7},{8,9},{9,10},{10,11},{12,13},{... | collective-permute-start | bytes 638984 | tf_op jit(solution)/shard_map/ppermute | solution.py:23
  43.7 3.5 %shard_map.114.top_ref = bf16[16,104,128]{2,1,0:T(8,128)(2,1)S(1)} custom-call(bf16[3,16,2,144,128]{4,3,2,1,0:T(8,128)(2,1)S(1)} %shard_map.110.shifted_ref, bf16[2,112,256]{2,1,0:T(8,128)(2,1)S(1)} %collective-permute-done.2.near_ref, bf16[2,112,256]{2,1,0:T(8,128)(2,1)S(1)} %collective-permute-done.3.cross_ref, ...), custom_call_target="tpu_custom_call" | custom-call | flops 4024999936 | bytes 1024 | tf_op jit(solution)/shard_map/pallas_call | solution.py:32
  47.2 4.1 %collective-permute-done.10.spill_ref = bf16[104,1024]{1,0:T(8,128)(2,1)S(1)} collective-permute-done((bf16[104,1024]{1,0:T(8,128)(2,1)S(1)}, bf16[104,1024]{1,0:T(8,128)(2,1)S(1)}, u32[]{:S(2)}, u32[]{:S(2)}) %collective-permute-start.10) | collective-permute-done | bytes 213024 | tf_op jit(solution)/shard_map/ppermute | solution.py:23
  51.3 1.5 %shard_map.120 = bf16[99,32,128]{2,1,0:T(8,128)(2,1)} custom-call(bf16[16,104,128]{2,1,0:T(8,128)(2,1)S(1)} %shard_map.114.top_ref, bf16[16,104,128]{2,1,0:T(8,128)(2,1)S(1)} %shard_map.115.low_ref, f32[32,104,128]{2,1,0:T(8,128)S(1)} %get-tuple-element.46.sum_ref, bf16[104,1024]{1,0:T(8,128)(2,1)S(1)} %collective-permute-done.10.spill_ref, ...), custom_call_target="tpu_custom_call" | custom-call | flops 2300000000 | bytes 1024 | tf_op jit(solution)/shard_map/pallas_call | solution.py:32
  (9 shorter events, 0.0 us)
Async XLA Ops:
  0.0 1.1 %copy-start = (bf16[99,32,128]{2,1,0:T(8,128)(2,1)S(1)}, bf16[99,32,128]{2,1,0:T(8,128)(2,1)}, u32[]{:S(2)}) copy-start(bf16[99,32,128]{2,1,0:T(8,128)(2,1)} %state_ref.1) | copy-start | bytes 2433028
  1.1 6.6 %copy-start.6 = (s32[16,2]{0,1:T(2,128)S(1)}, s32[16,2]{0,1:T(2,128)}, u32[]{:S(2)}) copy-start(s32[16,2]{0,1:T(2,128)} %param.16) | copy-start | bytes 388
  1.9 9.5 %collective-permute-start = (bf16[104,1152]{1,0:T(8,128)(2,1)S(1)}, bf16[104,1152]{1,0:T(8,128)(2,1)S(1)}, u32[]{:S(2)}, u32[]{:S(2)}) collective-permute-start(bf16[104,1152]{1,0:T(8,128)(2,1)S(1)} %get-tuple-element.28), channel_id=1, source_target_pairs={{1,0},{2,1},{3,2},{5,4},{6,5},{7,6},{9,8},{10,9},{11,10},{13,12},{... | collective-permute-start | bytes 718856 | tf_op jit(solution)/shard_map/ppermute | solution.py:23
  4.2 5.7 %collective-permute-start.1 = (bf16[104,128]{1,0:T(8,128)(2,1)S(1)}, bf16[104,128]{1,0:T(8,128)(2,1)S(1)}, u32[]{:S(2)}, u32[]{:S(2)}) collective-permute-start(bf16[104,128]{1,0:T(8,128)(2,1)S(1)} %get-tuple-element.29), channel_id=1, source_target_pairs={{0,1},{1,2},{2,3},{4,5},{5,6},{6,7},{8,9},{9,10},{10,11},{12,13},{... | collective-permute-start | bytes 79880 | tf_op jit(solution)/shard_map/ppermute | solution.py:23
  9.1 5.9 %copy-start.10 = (bf16[1,2,99,1024]{3,1,2,0:T(2,128)(2,1)S(1)}, bf16[1,2,99,1024]{3,1,2,0:T(2,128)(2,1)}, u32[]{:S(2)}) copy-start(bf16[1,2,99,1024]{3,1,2,0:T(2,128)(2,1)} %param.17) | copy-start | bytes 1216516
  9.1 6.0 %copy-start.1 = (bf16[9,128,99]{1,2,0:T(8,128)(2,1)S(1)}, bf16[9,128,99]{1,2,0:T(8,128)(2,1)}, u32[]{:S(2)}) copy-start(bf16[9,128,99]{1,2,0:T(8,128)(2,1)} %param.12) | copy-start | bytes 684292
  9.1 6.0 %copy-start.2 = (bf16[9,99,128]{2,1,0:T(8,128)(2,1)S(1)}, bf16[9,99,128]{2,1,0:T(8,128)(2,1)}, u32[]{:S(2)}) copy-start(bf16[9,99,128]{2,1,0:T(8,128)(2,1)} %refs_1_.1) | copy-start | bytes 684292
  9.1 6.0 %copy-start.3 = (bf16[9,128,99]{1,2,0:T(8,128)(2,1)S(1)}, bf16[9,128,99]{1,2,0:T(8,128)(2,1)}, u32[]{:S(2)}) copy-start(bf16[9,128,99]{1,2,0:T(8,128)(2,1)} %param.18) | copy-start | bytes 684292
  9.1 6.0 %copy-start.4 = (bf16[9,99,128]{2,1,0:T(8,128)(2,1)S(1)}, bf16[9,99,128]{2,1,0:T(8,128)(2,1)}, u32[]{:S(2)}) copy-start(bf16[9,99,128]{2,1,0:T(8,128)(2,1)} %refs_3_.1) | copy-start | bytes 684292
  9.2 6.0 %copy-start.5 = (f32[2,128]{1,0:T(2,128)S(1)}, f32[2,128]{1,0:T(2,128)}, u32[]{:S(2)}) copy-start(f32[2,128]{1,0:T(2,128)} %refs_7_.1) | copy-start | bytes 3076
  9.2 6.0 %copy-start.7 = (f32[128]{0:T(128)S(1)}, f32[128]{0:T(128)}, u32[]{:S(2)}) copy-start(f32[128]{0:T(128)} %param.13) | copy-start | bytes 1540
  9.2 6.0 %copy-start.8 = (f32[99]{0:T(128)S(1)}, f32[99]{0:T(128)}, u32[]{:S(2)}) copy-start(f32[99]{0:T(128)} %param.15) | copy-start | bytes 1192
  9.2 6.0 %copy-start.9 = (f32[99]{0:T(128)S(1)}, f32[99]{0:T(128)}, u32[]{:S(2)}) copy-start(f32[99]{0:T(128)} %param.21) | copy-start | bytes 1192
  13.3 1.6 %collective-permute-start.4 = (bf16[1,104,1408]{2,1,0:T(8,128)(2,1)S(1)}, bf16[1,104,1408]{2,1,0:T(8,128)(2,1)S(1)}, u32[]{:S(2)}, u32[]{:S(2)}) collective-permute-start(bf16[1,104,1408]{2,1,0:T(8,128)(2,1)S(1)} %get-tuple-element.38), channel_id=1, source_target_pairs={{0,4},{4,0},{8,12},{12,8},{1,5},{5,1},{9,13},{13,9},{2,6},{6,2},{1... | collective-permute-start | bytes 878600 | tf_op jit(solution)/shard_map/ppermute | solution.py:28
  13.3 7.3 %collective-permute-start.6 = (bf16[1,104,1408]{2,1,0:T(8,128)(2,1)S(1)}, bf16[1,104,1408]{2,1,0:T(8,128)(2,1)S(1)}, u32[]{:S(2)}, u32[]{:S(2)}) collective-permute-start(bf16[1,104,1408]{2,1,0:T(8,128)(2,1)S(1)} %get-tuple-element.39), channel_id=1, source_target_pairs={{0,4},{4,0},{8,12},{12,8},{1,5},{5,1},{9,13},{13,9},{2,6},{6,2},{1... | collective-permute-start | bytes 878600 | tf_op jit(solution)/shard_map/ppermute | solution.py:28
  14.9 9.9 %collective-permute-start.5 = (bf16[1,104,1408]{2,1,0:T(8,128)(2,1)S(1)}, bf16[1,104,1408]{2,1,0:T(8,128)(2,1)S(1)}, u32[]{:S(2)}, u32[]{:S(2)}) collective-permute-start(bf16[1,104,1408]{2,1,0:T(8,128)(2,1)S(1)} %shard_map.116), channel_id=1, source_target_pairs={{0,8},{4,12},{8,0},{12,4},{1,9},{5,13},{9,1},{13,5},{2,10},{6,14},... | collective-permute-start | bytes 878600 | tf_op jit(solution)/shard_map/ppermute | solution.py:28
  16.5 19.6 %collective-permute-start.2 = (bf16[2,112,256]{2,1,0:T(8,128)(2,1)S(1)}, bf16[2,112,256]{2,1,0:T(8,128)(2,1)S(1)}, u32[]{:S(2)}, u32[]{:S(2)}) collective-permute-start(bf16[2,112,256]{2,1,0:T(8,128)(2,1)S(1)} %get-tuple-element.30), channel_id=1, source_target_pairs={{0,4},{4,0},{8,12},{12,8},{1,5},{5,1},{9,13},{13,9},{2,6},{6,2},{1... | collective-permute-start | bytes 344072 | tf_op jit(solution)/shard_map/ppermute | solution.py:28
  16.7 19.4 %collective-permute-start.3 = (bf16[2,112,256]{2,1,0:T(8,128)(2,1)S(1)}, bf16[2,112,256]{2,1,0:T(8,128)(2,1)S(1)}, u32[]{:S(2)}, u32[]{:S(2)}) collective-permute-start(bf16[2,112,256]{2,1,0:T(8,128)(2,1)S(1)} %get-tuple-element.31), channel_id=1, source_target_pairs={{4,8},{8,4},{0,0},{12,12},{5,9},{9,5},{1,1},{13,13},{6,10},{10,6},... | collective-permute-start | bytes 344072 | tf_op jit(solution)/shard_map/ppermute | solution.py:766
  30.3 5.9 %collective-permute-start.7 = (bf16[104,1024]{1,0:T(8,128)(2,1)S(1)}, bf16[104,1024]{1,0:T(8,128)(2,1)S(1)}, u32[]{:S(2)}, u32[]{:S(2)}) collective-permute-start(bf16[104,1024]{1,0:T(8,128)(2,1)S(1)} %shard_map.117.refs_0_), channel_id=1, source_target_pairs={{0,8},{4,12},{8,0},{12,4},{1,9},{5,13},{9,1},{13,5},{2,10},{6,14},... | collective-permute-start | bytes 638984 | tf_op jit(solution)/shard_map/ppermute | solution.py:28
  32.5 7.2 %collective-permute-start.9 = (bf16[104,1024]{1,0:T(8,128)(2,1)S(1)}, bf16[104,1024]{1,0:T(8,128)(2,1)S(1)}, u32[]{:S(2)}, u32[]{:S(2)}) collective-permute-start(bf16[104,1024]{1,0:T(8,128)(2,1)S(1)} %shard_map.117.refs_0_), channel_id=1, source_target_pairs={{0,4},{4,0},{8,12},{12,8},{1,5},{5,1},{9,13},{13,9},{2,6},{6,2},{1... | collective-permute-start | bytes 638984 | tf_op jit(solution)/shard_map/ppermute | solution.py:28
  36.2 4.4 %collective-permute-start.8 = (bf16[104,1024]{1,0:T(8,128)(2,1)S(1)}, bf16[104,1024]{1,0:T(8,128)(2,1)S(1)}, u32[]{:S(2)}, u32[]{:S(2)}) collective-permute-start(bf16[104,1024]{1,0:T(8,128)(2,1)S(1)} %collective-permute-done.7.refs_1_), channel_id=1, source_target_pairs={{0,4},{4,0},{8,12},{12,8},{1,5},{5,1},{9,13},{13,9},{2,6},{6,2},{1... | collective-permute-start | bytes 638984 | tf_op jit(solution)/shard_map/ppermute | solution.py:28
  41.7 9.5 %collective-permute-start.10 = (bf16[104,1024]{1,0:T(8,128)(2,1)S(1)}, bf16[104,1024]{1,0:T(8,128)(2,1)S(1)}, u32[]{:S(2)}, u32[]{:S(2)}) collective-permute-start(bf16[104,1024]{1,0:T(8,128)(2,1)S(1)} %get-tuple-element.47), channel_id=1, source_target_pairs={{0,1},{1,2},{2,3},{4,5},{5,6},{6,7},{8,9},{9,10},{10,11},{12,13},{... | collective-permute-start | bytes 638984 | tf_op jit(solution)/shard_map/ppermute | solution.py:23

commit v9 on v8

--- a/solution.py
+++ b/solution.py
@@ -134,18 +134,23 @@
 
     def body(at_ref, *refs):
         ins, lines_in, noise_ref = refs[:count], refs[count : count + lines], refs[count + lines]
-        outs = refs[count + lines + 1 :]
+        outs, square = refs[count + lines + 1 : -1], refs[-1]
         lines_out, noise_out = outs[count : count + lines], outs[count + lines]
         place_ref = outs[count + lines + 1]
+        square[...] = jnp.zeros(square.shape, FULL)
         for k, (w_ref, o_ref) in enumerate(zip(ins, outs)):
             _, down, across = w_ref.shape
             o_ref[...] = jnp.zeros(o_ref.shape, HALF)
-            for v in range(2):
-                for a in range(3):
-                    for b in range(3):
+            for a in range(3):
+                for b in range(3):
+                    weight = w_ref[3 * a + b]
+                    if k % 2 == 0:
+                        square[:down, :across] = weight.astype(FULL)
+                        weight = square[...].T.astype(HALF)
+                    deep, wide = weight.shape
+                    for v in range(2):
                         tap = (3 * (a + v) + b) * LANES
-                        row, col = (v * LANES, tap) if k % 2 else (tap, v * LANES)
-                        o_ref[row : row + down, col : col + across] = w_ref[3 * a + b]
+                        o_ref[v * LANES : v * LANES + deep, tap : tap + wide] = weight
         for line_ref, o_ref in zip(lines_in, lines_out):
             used = line_ref.shape[1]
             o_ref[...] = jnp.zeros(o_ref.shape, FULL)
@@ -173,12 +178,12 @@
                 hit = (target == there) & (cell >= turn * SIDE) & (cell < (turn + 1) * SIDE)
                 place_ref[m, j * LANES : (j + 1) * LANES] = jnp.where(hit, 1.0, 0.0).astype(HALF)
 
-    sizes = [(12 * LANES, 2 * LANES), (2 * LANES, 12 * LANES)]
-    made = [like(sizes[k % 2]) for k in range(count)]
+    made = [like((2 * LANES, 12 * LANES))] * count
     made += [like((line.shape[0], 2 * LANES), FULL) for line in biases]
     made += [like((steps, cells // 2, 2 * LANES))]
     made += [like((tile_rows, bands * LANES, 2 * LANES))]
-    out = run(body, made, [anchor, *weights, *biases, noise], [], micros=1.5)
+    scratch = [pltpu.VMEM((LANES, LANES), FULL)]
+    out = run(body, made, [anchor, *weights, *biases, noise], scratch, micros=1.5)
     return out[:count], out[count : count + lines], *out[count + lines :]
 
 
@@ -315,9 +320,8 @@
 
 
 def product(view, weight):
-    turned = weight.shape[0] == 2 * LANES
     return lax.dot_general(
-        view, weight, (((1,), (1 if turned else 0,)), ((), ())), preferred_element_type=FULL
+        view, weight, (((1,), (1,)), ((), ())), preferred_element_type=FULL
     )
 
 
@@ -492,7 +496,7 @@
     cols = width - LANES
     loose = cols + 16
     made = rows // 2
-    pairs_in, pairs_out = made // 4 + 1, made // 4
+    pairs_in, pairs_out = 3, made // 4
     hidden_pairs = made // 2 + 1
     if hidden_pairs % pairs_in:
         hidden_pairs += pairs_in - hidden_pairs % pairs_in

time: 53.1 us -> 53.3 us (level)
  transfers between devices with their start and end apart: 11 -> 11, of which waited for: 6 -> 6; matrix products, arithmetic and copies ran while one was open for 0% -> 0% of each run, Pallas kernels for 34% -> 35%
where the time goes in v9:
time: 53.3 us; the launch traced here: 53.1 us
  Pallas kernels  23.7 us (44%)
  waiting for transfers between devices  15 us (28%)
  starting transfers between devices  12.6 us (24%)
  local copies, waits for them, and re-layouts  1.28 us (2%)
    pallas_call x12, Pallas kernels, run(): pl.pallas_call(body, out_shape=outs, in_specs=[pl.BlockSpec(memory_space=...  23.7 us
    ppermute x7, waiting for transfers between devices, swap(): return lax.ppermute(block, axis, [(i, i ^ bit) for i in range(count)])  8.75 us
    ppermute x3, starting transfers between devices, shift_from(): return lax.ppermute(block, axis, route)  7.77 us
    ppermute x3, waiting for transfers between devices, shift_from(): return lax.ppermute(block, axis, route)  6.2 us
    ppermute x1, starting transfers between devices, step(): lax.ppermute(edge_cross, 'band', steps + [(j, i) for i, j in steps] + alone)  3.88 us
    unnamed x23, local copies, waits for them, and re-layouts  1.28 us
  transfers between devices with their start and end apart: 11, of which 6 were waited for; matrix products, arithmetic and copies ran while one was open for 0% of the time, Pallas kernels for 35%

profile of v9, /device:TPU:18, one launch (start us, length us, event | category | flops | bytes accessed | tf_op | source)
XLA Modules:
  0.0 53.1 jit_solution(17067299454401812741)
XLA Ops:
  0.0 1.1 %copy-done = bf16[99,32,128]{2,1,0:T(8,128)(2,1)S(1)} copy-done((bf16[99,32,128]{2,1,0:T(8,128)(2,1)S(1)}, bf16[99,32,128]{2,1,0:T(8,128)(2,1)}, u32[]{:S(2)}) %copy-start) | copy-done | bytes 811032
  1.1 0.7 %shard_map.109 = (bf16[104,1152]{1,0:T(8,128)(2,1)S(1)}, bf16[104,128]{1,0:T(8,128)(2,1)S(1)}, bf16[32,112,128]{2,1,0:T(8,128)(2,1)S(1)}) custom-call(bf16[99,32,128]{2,1,0:T(8,128)(2,1)S(1)} %copy-done), custom_call_target="tpu_custom_call" | custom-call | flops 1150000000 | bytes 1024 | tf_op jit(solution)/shard_map/pallas_call | solution.py:32
  1.9 2.4 %collective-permute-start = (bf16[104,1152]{1,0:T(8,128)(2,1)S(1)}, bf16[104,1152]{1,0:T(8,128)(2,1)S(1)}, u32[]{:S(2)}, u32[]{:S(2)}) collective-permute-start(bf16[104,1152]{1,0:T(8,128)(2,1)S(1)} %get-tuple-element.28), channel_id=1, source_target_pairs={{1,0},{2,1},{3,2},{5,4},{6,5},{7,6},{9,8},{10,9},{11,10},{13,12},{... | collective-permute-start | bytes 718856 | tf_op jit(solution)/shard_map/ppermute | solution.py:23
  4.2 3.5 %collective-permute-start.1 = (bf16[104,128]{1,0:T(8,128)(2,1)S(1)}, bf16[104,128]{1,0:T(8,128)(2,1)S(1)}, u32[]{:S(2)}, u32[]{:S(2)}) collective-permute-start(bf16[104,128]{1,0:T(8,128)(2,1)S(1)} %get-tuple-element.29), channel_id=1, source_target_pairs={{0,1},{1,2},{2,3},{4,5},{5,6},{6,7},{8,9},{9,10},{10,11},{12,13},{... | collective-permute-start | bytes 79880 | tf_op jit(solution)/shard_map/ppermute | solution.py:23
  7.8 0.0 copy-done.6
  7.8 1.3 %shard_map.111.part_ref = bf16[4,104,1408]{2,1,0:T(8,128)(2,1)S(1)} custom-call(s32[2,16]{1,0:T(2,128)S(1)} %bitcast.12, bf16[32,112,128]{2,1,0:T(8,128)(2,1)S(1)} %get-tuple-element.27.rows_ref), custom_call_target="tpu_custom_call" | custom-call | flops 1724999936 | bytes 1024 | tf_op jit(solution)/shard_map/pallas_call | solution.py:32
  9.1 0.0 copy-start.10
  9.1 0.0 copy-start.1
  9.1 0.0 copy-start.2
  9.1 0.0 copy-start.3
  9.1 0.0 copy-start.4
  9.2 0.0 copy-start.5
  9.2 0.0 copy-start.7
  9.2 0.0 copy-start.8
  9.2 0.0 copy-start.9
  9.2 0.8 %collective-permute-done.1.left_ref = bf16[104,128]{1,0:T(8,128)(2,1)S(1)} collective-permute-done((bf16[104,128]{1,0:T(8,128)(2,1)S(1)}, bf16[104,128]{1,0:T(8,128)(2,1)S(1)}, u32[]{:S(2)}, u32[]{:S(2)}) %collective-permute-start.1) | collective-permute-done | bytes 26656 | tf_op jit(solution)/shard_map/ppermute | solution.py:23
  10.0 1.3 %collective-permute-done.right_ref = bf16[104,1152]{1,0:T(8,128)(2,1)S(1)} collective-permute-done((bf16[104,1152]{1,0:T(8,128)(2,1)S(1)}, bf16[104,1152]{1,0:T(8,128)(2,1)S(1)}, u32[]{:S(2)}, u32[]{:S(2)}) %collective-permute-start) | collective-permute-done | bytes 239648 | tf_op jit(solution)/shard_map/ppermute | solution.py:23
  11.3 1.9 %shard_map.112 = (bf16[1,104,1408]{2,1,0:T(8,128)(2,1)S(1)}, bf16[1,104,1408]{2,1,0:T(8,128)(2,1)S(1)}, bf16[1,104,1408]{2,1,0:T(8,128)(2,1)S(1)}, bf16[1,104,14...) custom-call(s32[2,16]{1,0:T(2,128)S(1)} %bitcast.13, ...), custom_call_target="tpu_custom_call" | custom-call | flops 1724999936 | bytes 1024 | tf_op jit(solution)/shard_map/pallas_call | solution.py:32
  13.3 0.1 collective-permute-start.4
  13.3 0.5 collective-permute-start.6
  13.8 1.1 %collective-permute-done.4.got_ref = bf16[1,104,1408]{2,1,0:T(8,128)(2,1)S(1)} collective-permute-done((bf16[1,104,1408]{2,1,0:T(8,128)(2,1)S(1)}, bf16[1,104,1408]{2,1,0:T(8,128)(2,1)S(1)}, u32[]{:S(2)}, u32[]{:S(2)}) %collective-permute-start.4) | collective-permute-done | bytes 292896 | tf_op jit(solution)/shard_map/ppermute | solution.py:28
  14.9 0.1 collective-permute-start.5
  15.0 0.0 copy-done.10
  15.0 0.1 copy.14
  15.1 0.0 copy-done.1
  15.1 0.0 copy-done.2
  15.2 1.4 %shard_map.113 = (bf16[256,1536]{1,0:T(8,128)(2,1)S(1)}, bf16[256,1536]{1,0:T(8,128)(2,1)S(1)}, bf16[256,1536]{1,0:T(8,128)(2,1)S(1)}, bf16[256,1536]{1,0:T(8,12...) custom-call(s32[2,16]{1,0:T(2,128)S(1)} %bitcast.14, ...), custom_call_target="tpu_custom_call" | custom-call | flops 1724999936 | bytes 1024 | tf_op jit(solution)/shard_map/pallas_call | solution.py:32
  16.6 0.2 collective-permute-start.2
  16.8 3.9 %collective-permute-start.3 = (bf16[2,112,256]{2,1,0:T(8,128)(2,1)S(1)}, bf16[2,112,256]{2,1,0:T(8,128)(2,1)S(1)}, u32[]{:S(2)}, u32[]{:S(2)}) collective-permute-start(bf16[2,112,256]{2,1,0:T(8,128)(2,1)S(1)} %get-tuple-element.31), channel_id=1, source_target_pairs={{4,8},{8,4},{0,0},{12,12},{5,9},{9,5},{1,1},{13,13},{6,10},{10,6},... | collective-permute-start | bytes 344072 | tf_op jit(solution)/shard_map/ppermute | solution.py:770
  20.7 0.0 collective-permute-done.6.refs_3_
  20.7 4.1 %collective-permute-done.5.refs_2_ = bf16[1,104,1408]{2,1,0:T(8,128)(2,1)S(1)} collective-permute-done((bf16[1,104,1408]{2,1,0:T(8,128)(2,1)S(1)}, bf16[1,104,1408]{2,1,0:T(8,128)(2,1)S(1)}, u32[]{:S(2)}, u32[]{:S(2)}) %collective-permute-start.5) | collective-permute-done | bytes 292896 | tf_op jit(solution)/shard_map/ppermute | solution.py:28
  24.8 5.5 %shard_map.117.refs_0_ = bf16[104,1024]{1,0:T(8,128)(2,1)S(1)} custom-call(s32[2,16]{1,0:T(2,128)S(1)} %bitcast.15, bf16[1,104,1408]{2,1,0:T(8,128)(2,1)S(1)} %get-tuple-element.36.refs_1_, bf16[1,104,1408]{2,1,0:T(8,128)(2,1)S(1)} %collective-permute-done.5.refs_2_, bf16[1,104,1408]{2,1,0:T(8,128)(2,1)S(1)} %collective-permute-done.6.refs_3_, ...), custom_call_target="tpu_custom_call" | custom-call | flops 9200000000 | bytes 1024 | tf_op jit(solution)/shard_map/pallas_call | solution.py:32
  30.3 0.1 collective-permute-start.7
  30.4 2.2 %shard_map.110.shifted_ref = bf16[3,16,2,144,128]{4,3,2,1,0:T(8,128)(2,1)S(1)} custom-call(bf16[32,112,128]{2,1,0:T(8,128)(2,1)S(1)} %get-tuple-element.27.rows_ref, bf16[104,1152]{1,0:T(8,128)(2,1)S(1)} %collective-permute-done.right_ref, bf16[104,128]{1,0:T(8,128)(2,1)S(1)} %collective-permute-done.1.left_ref), custom_call_target="tpu_custom_call" | custom-call | flops 2875000064 | bytes 1024 | tf_op jit(solution)/shard_map/pallas_call | solution.py:32
  32.6 0.1 collective-permute-start.9
  32.7 3.6 %collective-permute-done.7.refs_1_ = bf16[104,1024]{1,0:T(8,128)(2,1)S(1)} collective-permute-done((bf16[104,1024]{1,0:T(8,128)(2,1)S(1)}, bf16[104,1024]{1,0:T(8,128)(2,1)S(1)}, u32[]{:S(2)}, u32[]{:S(2)}) %collective-permute-start.7) | collective-permute-done | bytes 213024 | tf_op jit(solution)/shard_map/ppermute | solution.py:28
  36.2 0.0 collective-permute-start.8
  36.2 0.0 collective-permute-done.2.near_ref
  36.2 0.0 collective-permute-done.3.cross_ref
  36.2 3.6 %shard_map.115.low_ref = bf16[16,104,128]{2,1,0:T(8,128)(2,1)S(1)} custom-call(bf16[3,16,2,144,128]{4,3,2,1,0:T(8,128)(2,1)S(1)} %shard_map.110.shifted_ref, bf16[2,112,256]{2,1,0:T(8,128)(2,1)S(1)} %collective-permute-done.2.near_ref, bf16[2,112,256]{2,1,0:T(8,128)(2,1)S(1)} %collective-permute-done.3.cross_ref, ...), custom_call_target="tpu_custom_call" | custom-call | flops 4024999936 | bytes 1024 | tf_op jit(solution)/shard_map/pallas_call | solution.py:32
  39.8 0.0 collective-permute-done.9.refs_2_
  39.8 0.8 %shard_map.118.refs_1_ = bf16[4,8,112,384]{3,2,1,0:T(8,128)(2,1)S(1)} custom-call(s32[2,16]{1,0:T(2,128)S(1)} %bitcast.16, bf16[104,1024]{1,0:T(8,128)(2,1)S(1)} %shard_map.117.refs_0_, bf16[104,1024]{1,0:T(8,128)(2,1)S(1)} %collective-permute-done.7.refs_1_, bf16[104,1024]{1,0:T(8,128)(2,1)S(1)} %collective-permute-done.9.refs_2_), custom_call_target="tpu_custom_call" | custom-call | flops 920000000 | bytes 1024 | tf_op jit(solution)/shard_map/pallas_call | solution.py:32
  40.7 0.0 collective-permute-done.8.refs_0_
  40.7 1.2 %shard_map.119 = (bf16[104,1024]{1,0:T(8,128)(2,1)S(1)}, f32[32,104,128]{2,1,0:T(8,128)S(1)}, f32[32,128]{1,0:T(8,128)S(1)}) custom-call(s32[2,16]{1,0:T(2,128)S(1)} %bitcast.17, bf16[104,1024]{1,0:T(8,128)(2,1)S(1)} %collective-permute-done.8.refs_0_, bf16[4,8,112,384]{3,2,1,0:T(8,128)(2,1)S(1)} %shard_map.118.refs_1_, ...), custom_call_target="tpu_custom_call" | custom-call | flops 1724999936 | bytes 1024 | tf_op jit(solution)/shard_map/pallas_call | solution.py:32
  41.9 1.9 %collective-permute-start.10 = (bf16[104,1024]{1,0:T(8,128)(2,1)S(1)}, bf16[104,1024]{1,0:T(8,128)(2,1)S(1)}, u32[]{:S(2)}, u32[]{:S(2)}) collective-permute-start(bf16[104,1024]{1,0:T(8,128)(2,1)S(1)} %get-tuple-element.47), channel_id=1, source_target_pairs={{0,1},{1,2},{2,3},{4,5},{5,6},{6,7},{8,9},{9,10},{10,11},{12,13},{... | collective-permute-start | bytes 638984 | tf_op jit(solution)/shard_map/ppermute | solution.py:23
  43.8 3.6 %shard_map.114.top_ref = bf16[16,104,128]{2,1,0:T(8,128)(2,1)S(1)} custom-call(bf16[3,16,2,144,128]{4,3,2,1,0:T(8,128)(2,1)S(1)} %shard_map.110.shifted_ref, bf16[2,112,256]{2,1,0:T(8,128)(2,1)S(1)} %collective-permute-done.2.near_ref, bf16[2,112,256]{2,1,0:T(8,128)(2,1)S(1)} %collective-permute-done.3.cross_ref, ...), custom_call_target="tpu_custom_call" | custom-call | flops 4024999936 | bytes 1024 | tf_op jit(solution)/shard_map/pallas_call | solution.py:32
  47.4 4.1 %collective-permute-done.10.spill_ref = bf16[104,1024]{1,0:T(8,128)(2,1)S(1)} collective-permute-done((bf16[104,1024]{1,0:T(8,128)(2,1)S(1)}, bf16[104,1024]{1,0:T(8,128)(2,1)S(1)}, u32[]{:S(2)}, u32[]{:S(2)}) %collective-permute-start.10) | collective-permute-done | bytes 213024 | tf_op jit(solution)/shard_map/ppermute | solution.py:23
  51.4 1.5 %shard_map.120 = bf16[99,32,128]{2,1,0:T(8,128)(2,1)} custom-call(bf16[16,104,128]{2,1,0:T(8,128)(2,1)S(1)} %shard_map.114.top_ref, bf16[16,104,128]{2,1,0:T(8,128)(2,1)S(1)} %shard_map.115.low_ref, f32[32,104,128]{2,1,0:T(8,128)S(1)} %get-tuple-element.46.sum_ref, bf16[104,1024]{1,0:T(8,128)(2,1)S(1)} %collective-permute-done.10.spill_ref, ...), custom_call_target="tpu_custom_call" | custom-call | flops 2300000000 | bytes 1024 | tf_op jit(solution)/shard_map/pallas_call | solution.py:32
  (9 shorter events, 0.0 us)
Async XLA Ops:
  0.0 1.1 %copy-start = (bf16[99,32,128]{2,1,0:T(8,128)(2,1)S(1)}, bf16[99,32,128]{2,1,0:T(8,128)(2,1)}, u32[]{:S(2)}) copy-start(bf16[99,32,128]{2,1,0:T(8,128)(2,1)} %state_ref.1) | copy-start | bytes 2433028
  1.1 6.6 %copy-start.6 = (s32[16,2]{0,1:T(2,128)S(1)}, s32[16,2]{0,1:T(2,128)}, u32[]{:S(2)}) copy-start(s32[16,2]{0,1:T(2,128)} %param.16) | copy-start | bytes 388
  1.9 9.5 %collective-permute-start = (bf16[104,1152]{1,0:T(8,128)(2,1)S(1)}, bf16[104,1152]{1,0:T(8,128)(2,1)S(1)}, u32[]{:S(2)}, u32[]{:S(2)}) collective-permute-start(bf16[104,1152]{1,0:T(8,128)(2,1)S(1)} %get-tuple-element.28), channel_id=1, source_target_pairs={{1,0},{2,1},{3,2},{5,4},{6,5},{7,6},{9,8},{10,9},{11,10},{13,12},{... | collective-permute-start | bytes 718856 | tf_op jit(solution)/shard_map/ppermute | solution.py:23
  4.2 5.7 %collective-permute-start.1 = (bf16[104,128]{1,0:T(8,128)(2,1)S(1)}, bf16[104,128]{1,0:T(8,128)(2,1)S(1)}, u32[]{:S(2)}, u32[]{:S(2)}) collective-permute-start(bf16[104,128]{1,0:T(8,128)(2,1)S(1)} %get-tuple-element.29), channel_id=1, source_target_pairs={{0,1},{1,2},{2,3},{4,5},{5,6},{6,7},{8,9},{9,10},{10,11},{12,13},{... | collective-permute-start | bytes 79880 | tf_op jit(solution)/shard_map/ppermute | solution.py:23
  9.1 5.9 %copy-start.10 = (bf16[1,2,99,1024]{3,1,2,0:T(2,128)(2,1)S(1)}, bf16[1,2,99,1024]{3,1,2,0:T(2,128)(2,1)}, u32[]{:S(2)}) copy-start(bf16[1,2,99,1024]{3,1,2,0:T(2,128)(2,1)} %param.17) | copy-start | bytes 1216516
  9.1 6.0 %copy-start.1 = (bf16[9,128,99]{1,2,0:T(8,128)(2,1)S(1)}, bf16[9,128,99]{1,2,0:T(8,128)(2,1)}, u32[]{:S(2)}) copy-start(bf16[9,128,99]{1,2,0:T(8,128)(2,1)} %param.12) | copy-start | bytes 684292
  9.1 6.0 %copy-start.2 = (bf16[9,99,128]{2,1,0:T(8,128)(2,1)S(1)}, bf16[9,99,128]{2,1,0:T(8,128)(2,1)}, u32[]{:S(2)}) copy-start(bf16[9,99,128]{2,1,0:T(8,128)(2,1)} %refs_1_.1) | copy-start | bytes 684292
  9.1 6.0 %copy-start.3 = (bf16[9,128,99]{1,2,0:T(8,128)(2,1)S(1)}, bf16[9,128,99]{1,2,0:T(8,128)(2,1)}, u32[]{:S(2)}) copy-start(bf16[9,128,99]{1,2,0:T(8,128)(2,1)} %param.18) | copy-start | bytes 684292
  9.1 6.0 %copy-start.4 = (bf16[9,99,128]{2,1,0:T(8,128)(2,1)S(1)}, bf16[9,99,128]{2,1,0:T(8,128)(2,1)}, u32[]{:S(2)}) copy-start(bf16[9,99,128]{2,1,0:T(8,128)(2,1)} %refs_3_.1) | copy-start | bytes 684292
  9.2 6.0 %copy-start.5 = (f32[2,128]{1,0:T(2,128)S(1)}, f32[2,128]{1,0:T(2,128)}, u32[]{:S(2)}) copy-start(f32[2,128]{1,0:T(2,128)} %refs_7_.1) | copy-start | bytes 3076
  9.2 6.0 %copy-start.7 = (f32[128]{0:T(128)S(1)}, f32[128]{0:T(128)}, u32[]{:S(2)}) copy-start(f32[128]{0:T(128)} %param.13) | copy-start | bytes 1540
  9.2 6.0 %copy-start.8 = (f32[99]{0:T(128)S(1)}, f32[99]{0:T(128)}, u32[]{:S(2)}) copy-start(f32[99]{0:T(128)} %param.15) | copy-start | bytes 1192
  9.2 6.0 %copy-start.9 = (f32[99]{0:T(128)S(1)}, f32[99]{0:T(128)}, u32[]{:S(2)}) copy-start(f32[99]{0:T(128)} %param.21) | copy-start | bytes 1192
  13.3 1.6 %collective-permute-start.4 = (bf16[1,104,1408]{2,1,0:T(8,128)(2,1)S(1)}, bf16[1,104,1408]{2,1,0:T(8,128)(2,1)S(1)}, u32[]{:S(2)}, u32[]{:S(2)}) collective-permute-start(bf16[1,104,1408]{2,1,0:T(8,128)(2,1)S(1)} %get-tuple-element.38), channel_id=1, source_target_pairs={{0,4},{4,0},{8,12},{12,8},{1,5},{5,1},{9,13},{13,9},{2,6},{6,2},{1... | collective-permute-start | bytes 878600 | tf_op jit(solution)/shard_map/ppermute | solution.py:28
  13.3 7.4 %collective-permute-start.6 = (bf16[1,104,1408]{2,1,0:T(8,128)(2,1)S(1)}, bf16[1,104,1408]{2,1,0:T(8,128)(2,1)S(1)}, u32[]{:S(2)}, u32[]{:S(2)}) collective-permute-start(bf16[1,104,1408]{2,1,0:T(8,128)(2,1)S(1)} %get-tuple-element.39), channel_id=1, source_target_pairs={{0,4},{4,0},{8,12},{12,8},{1,5},{5,1},{9,13},{13,9},{2,6},{6,2},{1... | collective-permute-start | bytes 878600 | tf_op jit(solution)/shard_map/ppermute | solution.py:28
  14.9 9.9 %collective-permute-start.5 = (bf16[1,104,1408]{2,1,0:T(8,128)(2,1)S(1)}, bf16[1,104,1408]{2,1,0:T(8,128)(2,1)S(1)}, u32[]{:S(2)}, u32[]{:S(2)}) collective-permute-start(bf16[1,104,1408]{2,1,0:T(8,128)(2,1)S(1)} %shard_map.116), channel_id=1, source_target_pairs={{0,8},{4,12},{8,0},{12,4},{1,9},{5,13},{9,1},{13,5},{2,10},{6,14},... | collective-permute-start | bytes 878600 | tf_op jit(solution)/shard_map/ppermute | solution.py:28
  16.6 19.6 %collective-permute-start.2 = (bf16[2,112,256]{2,1,0:T(8,128)(2,1)S(1)}, bf16[2,112,256]{2,1,0:T(8,128)(2,1)S(1)}, u32[]{:S(2)}, u32[]{:S(2)}) collective-permute-start(bf16[2,112,256]{2,1,0:T(8,128)(2,1)S(1)} %get-tuple-element.30), channel_id=1, source_target_pairs={{0,4},{4,0},{8,12},{12,8},{1,5},{5,1},{9,13},{13,9},{2,6},{6,2},{1... | collective-permute-start | bytes 344072 | tf_op jit(solution)/shard_map/ppermute | solution.py:28
  16.8 19.4 %collective-permute-start.3 = (bf16[2,112,256]{2,1,0:T(8,128)(2,1)S(1)}, bf16[2,112,256]{2,1,0:T(8,128)(2,1)S(1)}, u32[]{:S(2)}, u32[]{:S(2)}) collective-permute-start(bf16[2,112,256]{2,1,0:T(8,128)(2,1)S(1)} %get-tuple-element.31), channel_id=1, source_target_pairs={{4,8},{8,4},{0,0},{12,12},{5,9},{9,5},{1,1},{13,13},{6,10},{10,6},... | collective-permute-start | bytes 344072 | tf_op jit(solution)/shard_map/ppermute | solution.py:770
  30.3 5.9 %collective-permute-start.7 = (bf16[104,1024]{1,0:T(8,128)(2,1)S(1)}, bf16[104,1024]{1,0:T(8,128)(2,1)S(1)}, u32[]{:S(2)}, u32[]{:S(2)}) collective-permute-start(bf16[104,1024]{1,0:T(8,128)(2,1)S(1)} %shard_map.117.refs_0_), channel_id=1, source_target_pairs={{0,8},{4,12},{8,0},{12,4},{1,9},{5,13},{9,1},{13,5},{2,10},{6,14},... | collective-permute-start | bytes 638984 | tf_op jit(solution)/shard_map/ppermute | solution.py:28
  32.6 7.2 %collective-permute-start.9 = (bf16[104,1024]{1,0:T(8,128)(2,1)S(1)}, bf16[104,1024]{1,0:T(8,128)(2,1)S(1)}, u32[]{:S(2)}, u32[]{:S(2)}) collective-permute-start(bf16[104,1024]{1,0:T(8,128)(2,1)S(1)} %shard_map.117.refs_0_), channel_id=1, source_target_pairs={{0,4},{4,0},{8,12},{12,8},{1,5},{5,1},{9,13},{13,9},{2,6},{6,2},{1... | collective-permute-start | bytes 638984 | tf_op jit(solution)/shard_map/ppermute | solution.py:28
  36.2 4.4 %collective-permute-start.8 = (bf16[104,1024]{1,0:T(8,128)(2,1)S(1)}, bf16[104,1024]{1,0:T(8,128)(2,1)S(1)}, u32[]{:S(2)}, u32[]{:S(2)}) collective-permute-start(bf16[104,1024]{1,0:T(8,128)(2,1)S(1)} %collective-permute-done.7.refs_1_), channel_id=1, source_target_pairs={{0,4},{4,0},{8,12},{12,8},{1,5},{5,1},{9,13},{13,9},{2,6},{6,2},{1... | collective-permute-start | bytes 638984 | tf_op jit(solution)/shard_map/ppermute | solution.py:28
  41.9 9.6 %collective-permute-start.10 = (bf16[104,1024]{1,0:T(8,128)(2,1)S(1)}, bf16[104,1024]{1,0:T(8,128)(2,1)S(1)}, u32[]{:S(2)}, u32[]{:S(2)}) collective-permute-start(bf16[104,1024]{1,0:T(8,128)(2,1)S(1)} %get-tuple-element.47), channel_id=1, source_target_pairs={{0,1},{1,2},{2,3},{4,5},{5,6},{6,7},{8,9},{9,10},{10,11},{12,13},{... | collective-permute-start | bytes 638984 | tf_op jit(solution)/shard_map/ppermute | solution.py:23

commit v10 on v9

--- a/solution.py
+++ b/solution.py
@@ -95,12 +95,11 @@
     deep = -(-padded // 16) * 16
     span = -(-rows * REACH // LANES)
 
-    def body(state_ref, right_ref, left_ref, rows_ref, flat):
+    def body(state_ref, right_ref, rows_ref, flat):
         turned = turn_rows(state_ref, flat)
         rows_ref[...] = turned
         lane = lane_index((deep, LANES))
         tiles = [None] * span
-        rim = jnp.zeros((deep, LANES), HALF)
         for r in range(rows):
             row = turned[r]
             at, off = divmod(r * REACH, LANES)
@@ -111,19 +110,30 @@
                 tiles[at] = jnp.where(lane >= off, moved, tiles[at])
             if off + REACH > LANES:
                 tiles[at + 1] = moved
-            moved = pltpu.roll(row, (2 * r + 2) % LANES, 1)
-            rim = jnp.where((lane >= 2 * r) & (lane < 2 * r + 2), moved, rim)
         for at in range(span):
             right_ref[:, at * LANES : (at + 1) * LANES] = tiles[at][:padded]
-        left_ref[...] = rim[:padded]
 
     return run(
         body,
-        [like((padded, span * LANES)), like((padded, LANES)), like((rows, deep, cols))],
+        [like((padded, span * LANES)), like((rows, deep, cols))],
         [state],
         [pltpu.VMEM((deep, rows, cols), HALF)],
         micros=1.0,
     )
+
+
+def pack_left(turned, padded):
+    rows, deep, _ = turned.shape
+
+    def body(rows_ref, left_ref):
+        lane = lane_index((deep, LANES))
+        rim = jnp.zeros((deep, LANES), HALF)
+        for r in range(rows):
+            moved = pltpu.roll(rows_ref[r], (2 * r + 2) % LANES, 1)
+            rim = jnp.where((lane >= 2 * r) & (lane < 2 * r + 2), moved, rim)
+        left_ref[...] = rim[:padded]
+
+    return run(body, [like((padded, LANES))], [turned], [], micros=0.3)[0]
 
 
 def prep(anchor, weights, biases, noise, bands, sects, rows, cols):
@@ -496,7 +506,7 @@
     cols = width - LANES
     loose = cols + 16
     made = rows // 2
-    pairs_in, pairs_out = 3, made // 4
+    pairs_in, pairs_out = made // 4 + 1, made // 4
     hidden_pairs = made // 2 + 1
     if hidden_pairs % pairs_in:
         hidden_pairs += pairs_in - hidden_pairs % pairs_in
@@ -727,7 +737,9 @@
 
     anchor = patch_anchor.T
 
-    right_rim, left_rim, turned = pack(state_field)
+    right_rim, turned = pack(state_field)
+    padded = right_rim.shape[0]
+    left_rim = pack_left(turned, padded)
     right = shift_from(right_rim, "sect", -1)
     left = shift_from(left_rim, "sect", 1)
 

time: 53.3 us -> 53.1 us (level)
  waiting for transfers between devices: 15 us -> 14.4 us
    pallas_call x12 -> x13, Pallas kernels: 23.7 us -> 23.9 us  [run(): pl.pallas_call(body, out_shape=outs, in_specs=[pl.BlockSpec(memory_space=...]
where the time goes in v10:
time: 53.1 us; the launch traced here: 52.9 us
  Pallas kernels  23.9 us (45%)
  waiting for transfers between devices  14.4 us (27%)
  starting transfers between devices  12.8 us (24%)
  local copies, waits for them, and re-layouts  1.28 us (2%)
    pallas_call x13, Pallas kernels, run(): pl.pallas_call(body, out_shape=outs, in_specs=[pl.BlockSpec(memory_space=...  23.9 us
    ppermute x7, waiting for transfers between devices, swap(): return lax.ppermute(block, axis, [(i, i ^ bit) for i in range(count)])  8.75 us
    ppermute x3, starting transfers between devices, shift_from(): return lax.ppermute(block, axis, route)  7.93 us
    ppermute x3, waiting for transfers between devices, shift_from(): return lax.ppermute(block, axis, route)  5.69 us
    ppermute x1, starting transfers between devices, step(): lax.ppermute(edge_cross, 'band', steps + [(j, i) for i, j in steps] + alone)  3.88 us
    unnamed x23, local copies, waits for them, and re-layouts  1.28 us
  transfers between devices with their start and end apart: 11, of which 6 were waited for; matrix products, arithmetic and copies ran while one was open for 0% of the time, Pallas kernels for 35%

profile of v10, /device:TPU:18, one launch (start us, length us, event | category | flops | bytes accessed | tf_op | source)
XLA Modules:
  0.0 52.9 jit_solution(2409957139424731522)
XLA Ops:
  0.0 1.1 %copy-done = bf16[99,32,128]{2,1,0:T(8,128)(2,1)S(1)} copy-done((bf16[99,32,128]{2,1,0:T(8,128)(2,1)S(1)}, bf16[99,32,128]{2,1,0:T(8,128)(2,1)}, u32[]{:S(2)}) %copy-start) | copy-done | bytes 811032
  1.1 0.6 %shard_map.109 = (bf16[104,1152]{1,0:T(8,128)(2,1)S(1)}, bf16[32,112,128]{2,1,0:T(8,128)(2,1)S(1)}) custom-call(bf16[99,32,128]{2,1,0:T(8,128)(2,1)S(1)} %copy-done), custom_call_target="tpu_custom_call" | custom-call | flops 1150000000 | bytes 1024 | tf_op jit(solution)/shard_map/pallas_call | solution.py:32
  1.7 2.4 %collective-permute-start = (bf16[104,1152]{1,0:T(8,128)(2,1)S(1)}, bf16[104,1152]{1,0:T(8,128)(2,1)S(1)}, u32[]{:S(2)}, u32[]{:S(2)}) collective-permute-start(bf16[104,1152]{1,0:T(8,128)(2,1)S(1)} %get-tuple-element.27), channel_id=1, source_target_pairs={{1,0},{2,1},{3,2},{5,4},{6,5},{7,6},{9,8},{10,9},{11,10},{13,12},{... | collective-permute-start | bytes 718856 | tf_op jit(solution)/shard_map/ppermute | solution.py:23
  4.1 0.3 shard_map.110
  4.4 3.5 %collective-permute-start.1 = (bf16[104,128]{1,0:T(8,128)(2,1)S(1)}, bf16[104,128]{1,0:T(8,128)(2,1)S(1)}, u32[]{:S(2)}, u32[]{:S(2)}) collective-permute-start(bf16[104,128]{1,0:T(8,128)(2,1)S(1)} %shard_map.110), channel_id=1, source_target_pairs={{0,1},{1,2},{2,3},{4,5},{5,6},{6,7},{8,9},{9,10},{10,11},{12,13},{... | collective-permute-start | bytes 79880 | tf_op jit(solution)/shard_map/ppermute | solution.py:23
  7.9 0.0 copy-done.6
  7.9 1.3 %shard_map.112.part_ref = bf16[4,104,1408]{2,1,0:T(8,128)(2,1)S(1)} custom-call(s32[2,16]{1,0:T(2,128)S(1)} %bitcast.12, bf16[32,112,128]{2,1,0:T(8,128)(2,1)S(1)} %get-tuple-element.26.rows_ref), custom_call_target="tpu_custom_call" | custom-call | flops 1724999936 | bytes 1024 | tf_op jit(solution)/shard_map/pallas_call | solution.py:32
  9.2 0.0 copy-start.10
  9.2 0.0 copy-start.1
  9.2 0.0 copy-start.2
  9.3 0.0 copy-start.3
  9.3 0.0 copy-start.4
  9.3 0.0 copy-start.5
  9.3 0.0 copy-start.7
  9.3 0.0 copy-start.8
  9.3 0.0 copy-start.9
  9.3 0.8 %collective-permute-done.1.left_ref = bf16[104,128]{1,0:T(8,128)(2,1)S(1)} collective-permute-done((bf16[104,128]{1,0:T(8,128)(2,1)S(1)}, bf16[104,128]{1,0:T(8,128)(2,1)S(1)}, u32[]{:S(2)}, u32[]{:S(2)}) %collective-permute-start.1) | collective-permute-done | bytes 26656 | tf_op jit(solution)/shard_map/ppermute | solution.py:23
  10.1 1.0 %collective-permute-done.right_ref = bf16[104,1152]{1,0:T(8,128)(2,1)S(1)} collective-permute-done((bf16[104,1152]{1,0:T(8,128)(2,1)S(1)}, bf16[104,1152]{1,0:T(8,128)(2,1)S(1)}, u32[]{:S(2)}, u32[]{:S(2)}) %collective-permute-start) | collective-permute-done | bytes 239648 | tf_op jit(solution)/shard_map/ppermute | solution.py:23
  11.2 1.9 %shard_map.113 = (bf16[1,104,1408]{2,1,0:T(8,128)(2,1)S(1)}, bf16[1,104,1408]{2,1,0:T(8,128)(2,1)S(1)}, bf16[1,104,1408]{2,1,0:T(8,128)(2,1)S(1)}, bf16[1,104,14...) custom-call(s32[2,16]{1,0:T(2,128)S(1)} %bitcast.13, ...), custom_call_target="tpu_custom_call" | custom-call | flops 1724999936 | bytes 1024 | tf_op jit(solution)/shard_map/pallas_call | solution.py:32
  13.1 0.1 collective-permute-start.4
  13.2 0.5 collective-permute-start.6
  13.7 1.1 %collective-permute-done.4.got_ref = bf16[1,104,1408]{2,1,0:T(8,128)(2,1)S(1)} collective-permute-done((bf16[1,104,1408]{2,1,0:T(8,128)(2,1)S(1)}, bf16[1,104,1408]{2,1,0:T(8,128)(2,1)S(1)}, u32[]{:S(2)}, u32[]{:S(2)}) %collective-permute-start.4) | collective-permute-done | bytes 292896 | tf_op jit(solution)/shard_map/ppermute | solution.py:28
  14.8 0.1 collective-permute-start.5
  14.8 0.0 copy-done.10
  14.8 0.1 copy.14
  14.9 0.0 copy-done.1
  15.0 1.4 %shard_map.114 = (bf16[256,1536]{1,0:T(8,128)(2,1)S(1)}, bf16[256,1536]{1,0:T(8,128)(2,1)S(1)}, bf16[256,1536]{1,0:T(8,128)(2,1)S(1)}, bf16[256,1536]{1,0:T(8,12...) custom-call(s32[2,16]{1,0:T(2,128)S(1)} %bitcast.14, ...), custom_call_target="tpu_custom_call" | custom-call | flops 1724999936 | bytes 1024 | tf_op jit(solution)/shard_map/pallas_call | solution.py:32
  16.5 0.2 collective-permute-start.2
  16.7 3.9 %collective-permute-start.3 = (bf16[2,112,256]{2,1,0:T(8,128)(2,1)S(1)}, bf16[2,112,256]{2,1,0:T(8,128)(2,1)S(1)}, u32[]{:S(2)}, u32[]{:S(2)}) collective-permute-start(bf16[2,112,256]{2,1,0:T(8,128)(2,1)S(1)} %get-tuple-element.29), channel_id=1, source_target_pairs={{4,8},{8,4},{0,0},{12,12},{5,9},{9,5},{1,1},{13,13},{6,10},{10,6},... | collective-permute-start | bytes 344072 | tf_op jit(solution)/shard_map/ppermute | solution.py:782
  20.5 0.0 collective-permute-done.6.refs_3_
  20.6 4.1 %collective-permute-done.5.refs_2_ = bf16[1,104,1408]{2,1,0:T(8,128)(2,1)S(1)} collective-permute-done((bf16[1,104,1408]{2,1,0:T(8,128)(2,1)S(1)}, bf16[1,104,1408]{2,1,0:T(8,128)(2,1)S(1)}, u32[]{:S(2)}, u32[]{:S(2)}) %collective-permute-start.5) | collective-permute-done | bytes 292896 | tf_op jit(solution)/shard_map/ppermute | solution.py:28
  24.7 5.5 %shard_map.118.refs_0_ = bf16[104,1024]{1,0:T(8,128)(2,1)S(1)} custom-call(s32[2,16]{1,0:T(2,128)S(1)} %bitcast.15, bf16[1,104,1408]{2,1,0:T(8,128)(2,1)S(1)} %get-tuple-element.34.refs_1_, bf16[1,104,1408]{2,1,0:T(8,128)(2,1)S(1)} %collective-permute-done.5.refs_2_, bf16[1,104,1408]{2,1,0:T(8,128)(2,1)S(1)} %collective-permute-done.6.refs_3_, ...), custom_call_target="tpu_custom_call" | custom-call | flops 9200000000 | bytes 1024 | tf_op jit(solution)/shard_map/pallas_call | solution.py:32
  30.2 0.1 collective-permute-start.7
  30.2 2.2 %shard_map.111.shifted_ref = bf16[3,16,2,144,128]{4,3,2,1,0:T(8,128)(2,1)S(1)} custom-call(bf16[32,112,128]{2,1,0:T(8,128)(2,1)S(1)} %get-tuple-element.26.rows_ref, bf16[104,1152]{1,0:T(8,128)(2,1)S(1)} %collective-permute-done.right_ref, bf16[104,128]{1,0:T(8,128)(2,1)S(1)} %collective-permute-done.1.left_ref), custom_call_target="tpu_custom_call" | custom-call | flops 2875000064 | bytes 1024 | tf_op jit(solution)/shard_map/pallas_call | solution.py:32
  32.4 0.1 collective-permute-start.9
  32.5 3.6 %collective-permute-done.7.refs_1_ = bf16[104,1024]{1,0:T(8,128)(2,1)S(1)} collective-permute-done((bf16[104,1024]{1,0:T(8,128)(2,1)S(1)}, bf16[104,1024]{1,0:T(8,128)(2,1)S(1)}, u32[]{:S(2)}, u32[]{:S(2)}) %collective-permute-start.7) | collective-permute-done | bytes 213024 | tf_op jit(solution)/shard_map/ppermute | solution.py:28
  36.1 0.0 collective-permute-start.8
  36.1 0.0 collective-permute-done.2.near_ref
  36.1 0.0 collective-permute-done.3.cross_ref
  36.1 3.6 %shard_map.116.low_ref = bf16[16,104,128]{2,1,0:T(8,128)(2,1)S(1)} custom-call(bf16[3,16,2,144,128]{4,3,2,1,0:T(8,128)(2,1)S(1)} %shard_map.111.shifted_ref, bf16[2,112,256]{2,1,0:T(8,128)(2,1)S(1)} %collective-permute-done.2.near_ref, bf16[2,112,256]{2,1,0:T(8,128)(2,1)S(1)} %collective-permute-done.3.cross_ref, ...), custom_call_target="tpu_custom_call" | custom-call | flops 4024999936 | bytes 1024 | tf_op jit(solution)/shard_map/pallas_call | solution.py:32
  39.7 0.0 collective-permute-done.9.refs_2_
  39.7 0.8 %shard_map.119.refs_1_ = bf16[4,8,112,384]{3,2,1,0:T(8,128)(2,1)S(1)} custom-call(s32[2,16]{1,0:T(2,128)S(1)} %bitcast.16, bf16[104,1024]{1,0:T(8,128)(2,1)S(1)} %shard_map.118.refs_0_, bf16[104,1024]{1,0:T(8,128)(2,1)S(1)} %collective-permute-done.7.refs_1_, bf16[104,1024]{1,0:T(8,128)(2,1)S(1)} %collective-permute-done.9.refs_2_), custom_call_target="tpu_custom_call" | custom-call | flops 920000000 | bytes 1024 | tf_op jit(solution)/shard_map/pallas_call | solution.py:32
  40.5 0.0 collective-permute-done.8.refs_0_
  40.5 1.2 %shard_map.120 = (bf16[104,1024]{1,0:T(8,128)(2,1)S(1)}, f32[32,104,128]{2,1,0:T(8,128)S(1)}, f32[32,128]{1,0:T(8,128)S(1)}) custom-call(s32[2,16]{1,0:T(2,128)S(1)} %bitcast.17, bf16[104,1024]{1,0:T(8,128)(2,1)S(1)} %collective-permute-done.8.refs_0_, bf16[4,8,112,384]{3,2,1,0:T(8,128)(2,1)S(1)} %shard_map.119.refs_1_, ...), custom_call_target="tpu_custom_call" | custom-call | flops 1724999936 | bytes 1024 | tf_op jit(solution)/shard_map/pallas_call | solution.py:32
  41.7 2.1 %collective-permute-start.10 = (bf16[104,1024]{1,0:T(8,128)(2,1)S(1)}, bf16[104,1024]{1,0:T(8,128)(2,1)S(1)}, u32[]{:S(2)}, u32[]{:S(2)}) collective-permute-start(bf16[104,1024]{1,0:T(8,128)(2,1)S(1)} %get-tuple-element.45), channel_id=1, source_target_pairs={{0,1},{1,2},{2,3},{4,5},{5,6},{6,7},{8,9},{9,10},{10,11},{12,13},{... | collective-permute-start | bytes 638984 | tf_op jit(solution)/shard_map/ppermute | solution.py:23
  43.8 3.6 %shard_map.115.top_ref = bf16[16,104,128]{2,1,0:T(8,128)(2,1)S(1)} custom-call(bf16[3,16,2,144,128]{4,3,2,1,0:T(8,128)(2,1)S(1)} %shard_map.111.shifted_ref, bf16[2,112,256]{2,1,0:T(8,128)(2,1)S(1)} %collective-permute-done.2.near_ref, bf16[2,112,256]{2,1,0:T(8,128)(2,1)S(1)} %collective-permute-done.3.cross_ref, ...), custom_call_target="tpu_custom_call" | custom-call | flops 4024999936 | bytes 1024 | tf_op jit(solution)/shard_map/pallas_call | solution.py:32
  47.4 3.9 %collective-permute-done.10.spill_ref = bf16[104,1024]{1,0:T(8,128)(2,1)S(1)} collective-permute-done((bf16[104,1024]{1,0:T(8,128)(2,1)S(1)}, bf16[104,1024]{1,0:T(8,128)(2,1)S(1)}, u32[]{:S(2)}, u32[]{:S(2)}) %collective-permute-start.10) | collective-permute-done | bytes 213024 | tf_op jit(solution)/shard_map/ppermute | solution.py:23
  51.2 1.5 %shard_map.121 = bf16[99,32,128]{2,1,0:T(8,128)(2,1)} custom-call(bf16[16,104,128]{2,1,0:T(8,128)(2,1)S(1)} %shard_map.115.top_ref, bf16[16,104,128]{2,1,0:T(8,128)(2,1)S(1)} %shard_map.116.low_ref, f32[32,104,128]{2,1,0:T(8,128)S(1)} %get-tuple-element.44.sum_ref, bf16[104,1024]{1,0:T(8,128)(2,1)S(1)} %collective-permute-done.10.spill_ref, ...), custom_call_target="tpu_custom_call" | custom-call | flops 2300000000 | bytes 1024 | tf_op jit(solution)/shard_map/pallas_call | solution.py:32
  (10 shorter events, 0.1 us)
Async XLA Ops:
  0.0 1.1 %copy-start = (bf16[99,32,128]{2,1,0:T(8,128)(2,1)S(1)}, bf16[99,32,128]{2,1,0:T(8,128)(2,1)}, u32[]{:S(2)}) copy-start(bf16[99,32,128]{2,1,0:T(8,128)(2,1)} %state_ref.1) | copy-start | bytes 2433028
  1.1 6.7 %copy-start.6 = (s32[16,2]{0,1:T(2,128)S(1)}, s32[16,2]{0,1:T(2,128)}, u32[]{:S(2)}) copy-start(s32[16,2]{0,1:T(2,128)} %param.16) | copy-start | bytes 388
  1.7 9.5 %collective-permute-start = (bf16[104,1152]{1,0:T(8,128)(2,1)S(1)}, bf16[104,1152]{1,0:T(8,128)(2,1)S(1)}, u32[]{:S(2)}, u32[]{:S(2)}) collective-permute-start(bf16[104,1152]{1,0:T(8,128)(2,1)S(1)} %get-tuple-element.27), channel_id=1, source_target_pairs={{1,0},{2,1},{3,2},{5,4},{6,5},{7,6},{9,8},{10,9},{11,10},{13,12},{... | collective-permute-start | bytes 718856 | tf_op jit(solution)/shard_map/ppermute | solution.py:23
  4.4 5.7 %collective-permute-start.1 = (bf16[104,128]{1,0:T(8,128)(2,1)S(1)}, bf16[104,128]{1,0:T(8,128)(2,1)S(1)}, u32[]{:S(2)}, u32[]{:S(2)}) collective-permute-start(bf16[104,128]{1,0:T(8,128)(2,1)S(1)} %shard_map.110), channel_id=1, source_target_pairs={{0,1},{1,2},{2,3},{4,5},{5,6},{6,7},{8,9},{9,10},{10,11},{12,13},{... | collective-permute-start | bytes 79880 | tf_op jit(solution)/shard_map/ppermute | solution.py:23
  9.2 5.6 %copy-start.10 = (bf16[1,2,99,1024]{3,1,2,0:T(2,128)(2,1)S(1)}, bf16[1,2,99,1024]{3,1,2,0:T(2,128)(2,1)}, u32[]{:S(2)}) copy-start(bf16[1,2,99,1024]{3,1,2,0:T(2,128)(2,1)} %param.17) | copy-start | bytes 1216516
  9.2 5.7 %copy-start.1 = (bf16[9,128,99]{1,2,0:T(8,128)(2,1)S(1)}, bf16[9,128,99]{1,2,0:T(8,128)(2,1)}, u32[]{:S(2)}) copy-start(bf16[9,128,99]{1,2,0:T(8,128)(2,1)} %param.12) | copy-start | bytes 684292
  9.2 5.7 %copy-start.2 = (bf16[9,99,128]{2,1,0:T(8,128)(2,1)S(1)}, bf16[9,99,128]{2,1,0:T(8,128)(2,1)}, u32[]{:S(2)}) copy-start(bf16[9,99,128]{2,1,0:T(8,128)(2,1)} %refs_1_.1) | copy-start | bytes 684292
  9.3 5.7 %copy-start.3 = (bf16[9,128,99]{1,2,0:T(8,128)(2,1)S(1)}, bf16[9,128,99]{1,2,0:T(8,128)(2,1)}, u32[]{:S(2)}) copy-start(bf16[9,128,99]{1,2,0:T(8,128)(2,1)} %param.18) | copy-start | bytes 684292
  9.3 5.7 %copy-start.4 = (bf16[9,99,128]{2,1,0:T(8,128)(2,1)S(1)}, bf16[9,99,128]{2,1,0:T(8,128)(2,1)}, u32[]{:S(2)}) copy-start(bf16[9,99,128]{2,1,0:T(8,128)(2,1)} %refs_3_.1) | copy-start | bytes 684292
  9.3 5.7 %copy-start.5 = (f32[2,128]{1,0:T(2,128)S(1)}, f32[2,128]{1,0:T(2,128)}, u32[]{:S(2)}) copy-start(f32[2,128]{1,0:T(2,128)} %refs_7_.1) | copy-start | bytes 3076
  9.3 5.7 %copy-start.7 = (f32[128]{0:T(128)S(1)}, f32[128]{0:T(128)}, u32[]{:S(2)}) copy-start(f32[128]{0:T(128)} %param.13) | copy-start | bytes 1540
  9.3 5.7 %copy-start.8 = (f32[99]{0:T(128)S(1)}, f32[99]{0:T(128)}, u32[]{:S(2)}) copy-start(f32[99]{0:T(128)} %param.15) | copy-start | bytes 1192
  9.3 5.7 %copy-start.9 = (f32[99]{0:T(128)S(1)}, f32[99]{0:T(128)}, u32[]{:S(2)}) copy-start(f32[99]{0:T(128)} %param.21) | copy-start | bytes 1192
  13.1 1.6 %collective-permute-start.4 = (bf16[1,104,1408]{2,1,0:T(8,128)(2,1)S(1)}, bf16[1,104,1408]{2,1,0:T(8,128)(2,1)S(1)}, u32[]{:S(2)}, u32[]{:S(2)}) collective-permute-start(bf16[1,104,1408]{2,1,0:T(8,128)(2,1)S(1)} %get-tuple-element.36), channel_id=1, source_target_pairs={{0,4},{4,0},{8,12},{12,8},{1,5},{5,1},{9,13},{13,9},{2,6},{6,2},{1... | collective-permute-start | bytes 878600 | tf_op jit(solution)/shard_map/ppermute | solution.py:28
  13.2 7.4 %collective-permute-start.6 = (bf16[1,104,1408]{2,1,0:T(8,128)(2,1)S(1)}, bf16[1,104,1408]{2,1,0:T(8,128)(2,1)S(1)}, u32[]{:S(2)}, u32[]{:S(2)}) collective-permute-start(bf16[1,104,1408]{2,1,0:T(8,128)(2,1)S(1)} %get-tuple-element.37), channel_id=1, source_target_pairs={{0,4},{4,0},{8,12},{12,8},{1,5},{5,1},{9,13},{13,9},{2,6},{6,2},{1... | collective-permute-start | bytes 878600 | tf_op jit(solution)/shard_map/ppermute | solution.py:28
  14.8 9.9 %collective-permute-start.5 = (bf16[1,104,1408]{2,1,0:T(8,128)(2,1)S(1)}, bf16[1,104,1408]{2,1,0:T(8,128)(2,1)S(1)}, u32[]{:S(2)}, u32[]{:S(2)}) collective-permute-start(bf16[1,104,1408]{2,1,0:T(8,128)(2,1)S(1)} %shard_map.117), channel_id=1, source_target_pairs={{0,8},{4,12},{8,0},{12,4},{1,9},{5,13},{9,1},{13,5},{2,10},{6,14},... | collective-permute-start | bytes 878600 | tf_op jit(solution)/shard_map/ppermute | solution.py:28
  16.5 19.6 %collective-permute-start.2 = (bf16[2,112,256]{2,1,0:T(8,128)(2,1)S(1)}, bf16[2,112,256]{2,1,0:T(8,128)(2,1)S(1)}, u32[]{:S(2)}, u32[]{:S(2)}) collective-permute-start(bf16[2,112,256]{2,1,0:T(8,128)(2,1)S(1)} %get-tuple-element.28), channel_id=1, source_target_pairs={{0,4},{4,0},{8,12},{12,8},{1,5},{5,1},{9,13},{13,9},{2,6},{6,2},{1... | collective-permute-start | bytes 344072 | tf_op jit(solution)/shard_map/ppermute | solution.py:28
  16.7 19.4 %collective-permute-start.3 = (bf16[2,112,256]{2,1,0:T(8,128)(2,1)S(1)}, bf16[2,112,256]{2,1,0:T(8,128)(2,1)S(1)}, u32[]{:S(2)}, u32[]{:S(2)}) collective-permute-start(bf16[2,112,256]{2,1,0:T(8,128)(2,1)S(1)} %get-tuple-element.29), channel_id=1, source_target_pairs={{4,8},{8,4},{0,0},{12,12},{5,9},{9,5},{1,1},{13,13},{6,10},{10,6},... | collective-permute-start | bytes 344072 | tf_op jit(solution)/shard_map/ppermute | solution.py:782
  30.2 5.9 %collective-permute-start.7 = (bf16[104,1024]{1,0:T(8,128)(2,1)S(1)}, bf16[104,1024]{1,0:T(8,128)(2,1)S(1)}, u32[]{:S(2)}, u32[]{:S(2)}) collective-permute-start(bf16[104,1024]{1,0:T(8,128)(2,1)S(1)} %shard_map.118.refs_0_), channel_id=1, source_target_pairs={{0,8},{4,12},{8,0},{12,4},{1,9},{5,13},{9,1},{13,5},{2,10},{6,14},... | collective-permute-start | bytes 638984 | tf_op jit(solution)/shard_map/ppermute | solution.py:28
  32.4 7.2 %collective-permute-start.9 = (bf16[104,1024]{1,0:T(8,128)(2,1)S(1)}, bf16[104,1024]{1,0:T(8,128)(2,1)S(1)}, u32[]{:S(2)}, u32[]{:S(2)}) collective-permute-start(bf16[104,1024]{1,0:T(8,128)(2,1)S(1)} %shard_map.118.refs_0_), channel_id=1, source_target_pairs={{0,4},{4,0},{8,12},{12,8},{1,5},{5,1},{9,13},{13,9},{2,6},{6,2},{1... | collective-permute-start | bytes 638984 | tf_op jit(solution)/shard_map/ppermute | solution.py:28
  36.1 4.4 %collective-permute-start.8 = (bf16[104,1024]{1,0:T(8,128)(2,1)S(1)}, bf16[104,1024]{1,0:T(8,128)(2,1)S(1)}, u32[]{:S(2)}, u32[]{:S(2)}) collective-permute-start(bf16[104,1024]{1,0:T(8,128)(2,1)S(1)} %collective-permute-done.7.refs_1_), channel_id=1, source_target_pairs={{0,4},{4,0},{8,12},{12,8},{1,5},{5,1},{9,13},{13,9},{2,6},{6,2},{1... | collective-permute-start | bytes 638984 | tf_op jit(solution)/shard_map/ppermute | solution.py:28
  41.7 9.5 %collective-permute-start.10 = (bf16[104,1024]{1,0:T(8,128)(2,1)S(1)}, bf16[104,1024]{1,0:T(8,128)(2,1)S(1)}, u32[]{:S(2)}, u32[]{:S(2)}) collective-permute-start(bf16[104,1024]{1,0:T(8,128)(2,1)S(1)} %get-tuple-element.45), channel_id=1, source_target_pairs={{0,1},{1,2},{2,3},{4,5},{5,6},{6,7},{8,9},{9,10},{10,11},{12,13},{... | collective-permute-start | bytes 638984 | tf_op jit(solution)/shard_map/ppermute | solution.py:23
